TPU v7x, 512 devices: a whole 4x4x16 slice. The times are simulated.
512 devices in a mesh: ctx: 32 (over x, z_lo), tp: 16 (over y, z_hi, core).
Axes of the slice: x: 4, y: 4, z: 16 (z_hi: 2, z_lo: 8; z = z_hi * 8 + z_lo), core: 2. Of those that a mesh axis runs over, the one named last changes fastest.
Arguments:
- queries: bfloat16 [4096, 4096], P('ctx', 'tp'), may hold values from -5 to 5
- key_states: bfloat16 [4096, 4096], P('ctx', 'tp'), may hold values from -5 to 5
- value_states: bfloat16 [4096, 4096], P('ctx', 'tp'), may hold values from -6 to 6
- attn_output: bfloat16 [4096, 4096], P('ctx', 'tp'), may hold values from -6 to 6
- output_grad: bfloat16 [4096, 4096], P('ctx', 'tp'), may hold values from -6 to 6
- block_map: int32 [32, 32], replicated, may hold values from 0 to 1, as said below
- w_query: bfloat16 [8192, 4096], P('ctx', 'tp'), may hold values from -0.09375 to 0.09375
- w_key: bfloat16 [8192, 4096], P('ctx', 'tp'), may hold values from -0.09375 to 0.09375
- w_value: bfloat16 [8192, 4096], P('ctx', 'tp'), may hold values from -0.09375 to 0.09375
Outputs:
- grad_input: bfloat16 [4096, 8192], P('tp', 'ctx')
Inputs may be any that keep to these rules, and one draw needn't show every extreme that they name: block_map[i, j] is 1 wherever |i - j| <= 1; elsewhere each row is 1 on a share of its entries that differs from row to row.
All inputs are finite; a program needn't handle non-finite values.
Results may differ from a plain program's by a relative error of at most 0.014.
Values may be sent and summed in bfloat16 or wider, within the bound.
No kernel may reach another device: no remote copies, remote signals or barrier semaphores. Data moves between devices by JAX's collectives and lax.ppermute only.
A program may use at most 64 MiB of HBM per device.

v0:
```python
import math

import jax
import jax.numpy as jnp
from jax import lax
from jax.sharding import PartitionSpec as P

HD = 128
BLK = 128


NEG_FILL = -1e30


def block_mask(block_map, row_offset, row_count, col_offset, col_count):
    tiles = lax.dynamic_slice(
        block_map, (row_offset // BLK, col_offset // BLK), (row_count // BLK, col_count // BLK)
    )
    spread = jnp.broadcast_to(
        tiles[:, None, :, None], (row_count // BLK, BLK, col_count // BLK, BLK)
    )
    return spread.reshape(row_count, col_count) > 0


def resolved_rows(values):
    return lax.optimization_barrier(values.astype(jnp.bfloat16)).astype(jnp.float32)


def stat_update(state, query_heads, key_block, allowed, score_scale):
    row_max, row_sum = state
    scores = (
        jnp.einsum("qhd,khd->hqk", query_heads, key_block, preferred_element_type=jnp.float32)
        * score_scale
    )
    masked = jnp.where(allowed[None], scores, NEG_FILL)
    new_max = jnp.maximum(row_max, jnp.max(masked, axis=2))
    kept = jnp.where(allowed[None], jnp.exp(masked - new_max[:, :, None]), 0.0)
    return (new_max, row_sum * jnp.exp(row_max - new_max) + jnp.sum(kept, axis=2))


def gradient_block(
    query_heads, grad_heads, key_block, value_block, log_total, row_delta, allowed, score_scale
):
    scores = (
        jnp.einsum("qhd,khd->hqk", query_heads, key_block, preferred_element_type=jnp.float32)
        * score_scale
    )
    masked = jnp.where(allowed[None], scores, NEG_FILL)
    probs = jnp.where(allowed[None], jnp.exp(masked - log_total[:, :, None]), 0.0)
    probs_low = probs.astype(jnp.bfloat16)
    dprobs = jnp.einsum("qhd,khd->hqk", grad_heads, value_block, preferred_element_type=jnp.float32)
    score_gradient = (probs * (dprobs - row_delta[:, :, None]) * score_scale).astype(jnp.bfloat16)
    return (probs_low, score_gradient)


def per_device(
    queries, key_states, value_states, attn_output, output_grad, block_map, w_query, w_key, w_value
):
    slab_rows, width = queries.shape
    head_count = width // HD
    context_count = lax.axis_size("ctx")
    score_scale = 1.0 / math.sqrt(HD)
    row_offset = lax.axis_index("ctx") * slab_rows
    query_heads = queries.reshape(slab_rows, head_count, HD)
    grad_heads = output_grad.reshape(slab_rows, head_count, HD)
    output_heads = attn_output.reshape(slab_rows, head_count, HD)
    row_delta = jnp.sum(grad_heads.astype(jnp.float32) * output_heads.astype(jnp.float32), axis=2).T
    start_state = (
        jnp.full((head_count, slab_rows), NEG_FILL, jnp.float32),
        jnp.zeros((head_count, slab_rows), jnp.float32),
    )
    full_keys, full_values = (
        lax.all_gather(key_states, "ctx", axis=0, tiled=True),
        lax.all_gather(value_states, "ctx", axis=0, tiled=True),
    )
    group_size = min(context_count, max(1, 512 // slab_rows))
    key_span = slab_rows * group_size
    total_block_count = context_count // group_size
    key_blocks = full_keys.reshape(total_block_count, key_span, head_count, HD)
    value_blocks = full_values.reshape(total_block_count, key_span, head_count, HD)
    block_ids = jnp.arange(total_block_count, dtype=jnp.int32)

    def stat_step(state, inputs):
        key_block, block_index = inputs
        allowed = block_mask(block_map, row_offset, slab_rows, block_index * key_span, key_span)

        def stat_active_step(previous):
            return stat_update(previous, query_heads, key_block, allowed, score_scale)

        return (
            lax.cond(jnp.any(allowed), stat_active_step, lambda previous: previous, state),
            None,
        )

    (row_max, row_sum), _ = lax.scan(stat_step, start_state, (key_blocks, block_ids))
    log_total = row_max + jnp.log(row_sum)

    def back_step(dq_total, inputs):
        key_block, value_block, block_index = inputs
        allowed = block_mask(block_map, row_offset, slab_rows, block_index * key_span, key_span)

        def back_active_step(previous):
            probs_low, score_gradient = gradient_block(
                query_heads,
                grad_heads,
                key_block,
                value_block,
                log_total,
                row_delta,
                allowed,
                score_scale,
            )
            dv_part = jnp.einsum(
                "hqk,qhd->khd", probs_low, grad_heads, preferred_element_type=jnp.float32
            ).astype(jnp.bfloat16)
            dk_part = jnp.einsum(
                "hqk,qhd->khd", score_gradient, query_heads, preferred_element_type=jnp.float32
            ).astype(jnp.bfloat16)
            per_slab = jnp.einsum(
                "hqgk,gkhd->gqhd",
                score_gradient.reshape(head_count, slab_rows, group_size, slab_rows),
                key_block.reshape(group_size, slab_rows, head_count, HD),
                preferred_element_type=jnp.float32,
            )
            joined = jnp.concatenate(
                [dk_part.reshape(key_span, width), dv_part.reshape(key_span, width)], axis=1
            )
            return (previous + jnp.sum(resolved_rows(per_slab), axis=0), joined)

        def empty_step(previous):
            return (previous, jnp.zeros((key_span, 2 * width), jnp.bfloat16))

        return lax.cond(jnp.any(allowed), back_active_step, empty_step, dq_total)

    dq_total, joined_blocks = lax.scan(
        back_step,
        jnp.zeros((slab_rows, head_count, HD), jnp.float32),
        (key_blocks, value_blocks, block_ids),
    )
    local_grads = dq_total.astype(jnp.bfloat16).reshape(slab_rows, width)
    part_grads = joined_blocks.reshape(context_count * slab_rows, 2 * width)
    part_width = part_grads.shape[1]
    arrived = lax.all_to_all(
        part_grads.reshape(context_count, slab_rows, part_width),
        "ctx",
        split_axis=0,
        concat_axis=0,
        tiled=True,
    )
    finished = jnp.sum(arrived.astype(jnp.float32), axis=0).astype(jnp.bfloat16)
    own_grads = jnp.concatenate([local_grads, finished], axis=1)
    gradients = lax.all_gather(own_grads, "ctx", axis=0, tiled=True)
    projections = jnp.concatenate([w_query, w_key, w_value], axis=1)
    return lax.psum_scatter(
        lax.dot_general(
            gradients, projections, (((1,), (1,)), ((), ())), preferred_element_type=jnp.float32
        ).astype(jnp.bfloat16),
        "tp",
        scatter_dimension=0,
        tiled=True,
    )


def solution(mesh):
    return jax.shard_map(
        per_device,
        mesh=mesh,
        in_specs=(
            P("ctx", "tp"),
            P("ctx", "tp"),
            P("ctx", "tp"),
            P("ctx", "tp"),
            P("ctx", "tp"),
            P(),
            P("ctx", "tp"),
            P("ctx", "tp"),
            P("ctx", "tp"),
        ),
        out_specs=P("tp", "ctx"),
        check_vma=False,
    )
```

profile of v0, /device:TPU:6, one launch (start us, length us, event | category | flops | bytes accessed | tf_op | source)
XLA Modules:
  0.0 1083.6 jit_solution(8561882724283096852)
XLA Ops:
  8.0 1.0 copy.66
  9.1 1.0 copy.70
  10.1 0.9 copy.71
  11.1 211.7 %all-gather.4.cloned.1.call-done = bf16[4096,256]{1,0:T(8,128)(2,1)} async-done(((bf16[128,256]{1,0:T(8,128)(2,1)}), bf16[4096,256]{1,0:T(8,128)(2,1)}) %all-gather.4.cloned.1.call-update) | async-done | bytes 2097168 | tf_op jit(solution)/shard_map/all_gather | solution.py:73
  222.8 4.0 reshape.84
  226.8 2.0 copy.72
  228.8 30.3 %while.33 = (s32[]{:T(128)}, f32[2,128]{1,0:T(2,128)S(1)}, f32[2,128]{1,0:T(2,128)S(1)}, s32[8]{0:T(128)S(1)}, s32[32,32]{1,0:T(8,128)}, /*index=5*/s32[]{:T(128...) while((s32[]{:T(128)}, f32[2,128]{1,0:T(2,128)S(1)}, ...), condition=%wide.region_6.7_spmd, body=%wide.region_0.6_spmd.sunk | while | flops 34406940 | bytes 1391623 | solution.py:95
  230.0 0.8 broadcast_compare_fusion.6
  233.9 0.8 broadcast_compare_fusion.6
  237.7 0.8 broadcast_compare_fusion.6
  244.9 0.8 broadcast_compare_fusion.6
  248.7 0.8 broadcast_compare_fusion.6
  256.5 0.8 broadcast_compare_fusion.6
  259.1 191.5 %all-gather.6.cloned.1.call-done = bf16[4096,256]{1,0:T(8,128)(2,1)} async-done(((bf16[128,256]{1,0:T(8,128)(2,1)}), bf16[4096,256]{1,0:T(8,128)(2,1)}) %all-gather.6.cloned.1.call-update) | async-done | bytes 2097168 | tf_op jit(solution)/shard_map/all_gather | solution.py:74
  450.6 4.0 reshape.85
  454.6 3.3 copy.73
  457.9 52.1 %while.34 = (s32[]{:T(128)}, f32[128,2,128]{2,0,1:T(8,128)S(1)}, bf16[8,512,512]{2,1,0:T(8,128)(2,1)}, s32[8]{0:T(128)S(1)}, s32[32,32]{1,0:T(8,128)}, /*index=5...) while((s32[]{:T(128)}, f32[128,2,128]{2,0,1:T(8,128)S(1)}, ...), condition=%wide.region_13.14_spmd, body=%wide.region_8.13_spmd.sunk | while | flops 170721312 | bytes 8655399 | solution.py:135
  461.2 2.5 conditional.5
  461.6 1.2 fusion.11
  463.9 0.8 constant_dynamic-update-slice_fusion.2
  465.9 0.8 broadcast_compare_fusion.7
  468.0 2.5 conditional.5
  468.5 1.2 fusion.11
  470.7 0.8 constant_dynamic-update-slice_fusion.2
  472.7 0.8 broadcast_compare_fusion.7
  474.8 2.5 conditional.5
  475.3 1.2 fusion.11
  477.5 0.8 constant_dynamic-update-slice_fusion.2
  479.5 0.8 broadcast_compare_fusion.7
  481.9 0.8 constant_dynamic-update-slice_fusion.2
  486.0 2.5 conditional.5
  486.5 1.2 fusion.11
  488.7 0.8 constant_dynamic-update-slice_fusion.2
  492.9 2.5 conditional.5
  493.3 1.2 fusion.11
  495.6 0.9 constant_dynamic-update-slice_fusion.2
  499.7 2.5 conditional.5
  500.1 1.2 fusion.11
  502.4 0.8 constant_dynamic-update-slice_fusion.2
  506.5 2.5 conditional.5
  506.9 1.2 fusion.11
  509.2 0.8 constant_dynamic-update-slice_fusion.2
  510.0 32.3 %all-to-all-start = ((bf16[32,128,512]{2,1,0:T(8,128)(2,1)}), bf16[32,128,512]{2,1,0:T(8,128)(2,1)}, u32[]{:S(2)}, u32[]{:S(2)}) async-start(bf16[32,128,512]{2,1,0:T(8,128)(2,1)} %bitcast.63), calls=%async_computation | async-start | bytes 8388608 | tf_op jit(solution)/shard_map/all_to_all | solution.py:143
  542.7 154.2 %all-to-all-done = bf16[32,128,512]{2,1,0:T(8,128)(2,1)} async-done(((bf16[32,128,512]{2,1,0:T(8,128)(2,1)}), bf16[32,128,512]{2,1,0:T(8,128)(2,1)}, u32[]{:S(2)}, u32[]{:S(2)}) %all-to-all-start) | async-done | bytes 4194336 | tf_op jit(solution)/shard_map/all_to_all | solution.py:143
  696.9 2.8 reduce_sum.43
  700.5 233.9 %all-gather.8.cloned.1.call-done = bf16[4096,768]{1,0:T(8,128)(2,1)} async-done(((bf16[128,768]{1,0:T(8,128)(2,1)}), bf16[4096,768]{1,0:T(8,128)(2,1)}) %all-gather.8.cloned.1.call-update) | async-done | bytes 6291472 | tf_op jit(solution)/shard_map/all_gather | solution.py:152
  934.4 6.0 convolution_convert_fusion.3
  940.4 136.7 %reduce-scatter.2.cloned.1.call-done = bf16[256,256]{1,0:T(8,128)(2,1)} async-done(((bf16[4096,256]{1,0:T(8,128)(2,1)}), bf16[256,256]{1,0:T(8,128)(2,1)}) %reduce-scatter.2.cloned.1.call-update) | async-done | bytes 131088 | tf_op jit(solution)/shard_map/reduce_scatter | solution.py:154
  (202 shorter events, 47.1 us)
Async XLA Ops:
  6.5 216.3 %all-gather.4.cloned.1.call-start = ((), (), s32[]{:S(2)}) async-start(), calls=%async_computation.2 | async-start | bytes 2162688 | tf_op jit(solution)/shard_map/all_gather | solution.py:73
  7.3 443.3 %all-gather.6.cloned.1.call-start = ((), (), s32[]{:S(2)}) async-start(), calls=%async_computation.3 | async-start | bytes 2162688 | tf_op jit(solution)/shard_map/all_gather | solution.py:74
  510.0 186.9 %all-to-all-start = ((bf16[32,128,512]{2,1,0:T(8,128)(2,1)}), bf16[32,128,512]{2,1,0:T(8,128)(2,1)}, u32[]{:S(2)}, u32[]{:S(2)}) async-start(bf16[32,128,512]{2,1,0:T(8,128)(2,1)} %bitcast.63), calls=%async_computation | async-start | bytes 8388608 | tf_op jit(solution)/shard_map/all_to_all | solution.py:143
  542.4 392.0 %copy-start = (bf16[256,256]{1,0:T(8,128)(2,1)S(1)}, bf16[256,256]{1,0:T(8,128)(2,1)}, u32[]{:S(2)}) copy-start(bf16[256,256]{1,0:T(8,128)(2,1)} %param.25) | copy-start | bytes 393220
  542.4 392.0 %copy-start.1 = (bf16[256,256]{1,0:T(8,128)(2,1)S(1)}, bf16[256,256]{1,0:T(8,128)(2,1)}, u32[]{:S(2)}) copy-start(bf16[256,256]{1,0:T(8,128)(2,1)} %param.24) | copy-start | bytes 393220
  542.4 392.0 %copy-start.2 = (bf16[256,256]{1,0:T(8,128)(2,1)S(1)}, bf16[256,256]{1,0:T(8,128)(2,1)}, u32[]{:S(2)}) copy-start(bf16[256,256]{1,0:T(8,128)(2,1)} %param.23) | copy-start | bytes 393220
  542.4 392.0 %all-gather.8.cloned.1.call-start = ((), (), s32[]{:S(2)}) async-start(), calls=%async_computation.4 | async-start | bytes 6488064 | tf_op jit(solution)/shard_map/all_gather | solution.py:152
  700.4 376.6 %reduce-scatter.2.cloned.1.call-start = ((), (), s32[]{:S(2)}) async-start(), calls=%async_computation.5 | async-start | bytes 2228224 | tf_op jit(solution)/shard_map/reduce_scatter | solution.py:154
Sparse Core Ops, SparseCore 0:
  9.4 213.3 all-gather.3
  224.9 225.6 all-gather.5
  700.6 233.7 all-gather.7
  940.5 136.5 reduce-scatter.1
where the time goes:
time: 1090 us; the launch traced here: 1080 us
  waiting for transfers between devices  929 us (85%)
  local copies, waits for them, and re-layouts  35.4 us (3%)
  starting transfers between devices  32.5 us (3%)
  other arithmetic  30.1 us (3%)
  matrix products  22.9 us (2%)
  loops' own time  20 us (2%)
  between operations  13.3 us (1%)
    all_gather x1, waiting for transfers between devices, per_device(): gradients = lax.all_gather(own_grads, 'ctx', axis=0, tiled=True)  234 us
    all_gather x1, waiting for transfers between devices, per_device(): lax.all_gather(key_states, 'ctx', axis=0, tiled=True)  212 us
    all_gather x1, waiting for transfers between devices, per_device(): lax.all_gather(value_states, 'ctx', axis=0, tiled=True)  191 us
    all_to_all x1, waiting for transfers between devices, per_device(): lax.all_to_all(part_grads.reshape(context_count, slab_rows, part_width),...  154 us
    reduce_scatter x1, waiting for transfers between devices, per_device(): lax.psum_scatter(lax.dot_general(gradients, projections, (((1,), (1,)), (...  137 us
    all_to_all x1, starting transfers between devices, per_device(): lax.all_to_all(part_grads.reshape(context_count, slab_rows, part_width),...  32.3 us
  transfers between devices with their start and end apart: 5, of which 5 were waited for; matrix products, arithmetic and copies ran while one was open for 3% of the time, Pallas kernels for 0%

commit v1 on v0

--- a/solution.py
+++ b/solution.py
@@ -69,10 +69,12 @@
         jnp.full((head_count, slab_rows), NEG_FILL, jnp.float32),
         jnp.zeros((head_count, slab_rows), jnp.float32),
     )
-    full_keys, full_values = (
-        lax.all_gather(key_states, "ctx", axis=0, tiled=True),
-        lax.all_gather(value_states, "ctx", axis=0, tiled=True),
+    key_value = jnp.concatenate([key_states, value_states], axis=1)
+    spread = jnp.broadcast_to(key_value[None], (context_count,) + key_value.shape)
+    gathered = lax.all_to_all(spread, "ctx", 0, 0, tiled=True).reshape(
+        context_count * slab_rows, 2 * width
     )
+    full_keys, full_values = gathered[:, :width], gathered[:, width:]
     group_size = min(context_count, max(1, 512 // slab_rows))
     key_span = slab_rows * group_size
     total_block_count = context_count // group_size

time: 1090 us -> 894 us (0.82)
  waiting for transfers between devices: 929 us -> 724 us
    all_gather x2 -> x0, waiting for transfers between devices: 403 us -> none  [the longest x1 212 us: per_device(): lax.all_gather(key_states, 'ctx', axis=0, tiled=True)]
    all_to_all x0 -> x1, waiting for transfers between devices: none -> 175 us  [per_device(): lax.all_to_all(spread, 'ctx', 0, 0, tiled=True)]
    all_to_all x1, waiting for transfers between devices: 154 us -> 175 us  [per_device(): lax.all_to_all(part_grads.reshape(context_count, slab_rows, part_width),...]
    all_to_all x0 -> x1, starting transfers between devices: none -> 15.8 us  [per_device(): lax.all_to_all(spread, 'ctx', 0, 0, tiled=True)]
  transfers between devices with their start and end apart: 5 -> 4, of which waited for: 5 -> 4; matrix products, arithmetic and copies ran while one was open for 3% -> 0% of each run, Pallas kernels for 0% -> 0%
where the time goes in v1:
time: 894 us; the launch traced here: 892 us
  waiting for transfers between devices  724 us (81%)
  local copies, waits for them, and re-layouts  44 us (5%)
  starting transfers between devices  42.5 us (5%)
  other arithmetic  30.4 us (3%)
  loops' own time  19.8 us (2%)
  matrix products  18.1 us (2%)
  between operations  13.6 us (2%)
    all_gather x1, waiting for transfers between devices, per_device(): gradients = lax.all_gather(own_grads, 'ctx', axis=0, tiled=True)  237 us
    all_to_all x1, waiting for transfers between devices, per_device(): lax.all_to_all(part_grads.reshape(context_count, slab_rows, part_width),...  175 us
    all_to_all x1, waiting for transfers between devices, per_device(): lax.all_to_all(spread, 'ctx', 0, 0, tiled=True)  175 us
    reduce_scatter x1, waiting for transfers between devices, per_device(): lax.psum_scatter(lax.dot_general(gradients, projections, (((1,), (1,)), (...  137 us
    all_to_all x1, starting transfers between devices, per_device(): lax.all_to_all(part_grads.reshape(context_count, slab_rows, part_width),...  26.5 us
  transfers between devices with their start and end apart: 4, of which 4 were waited for; matrix products, arithmetic and copies ran while one was open for 0% of the time, Pallas kernels for 0%

profile of v1, /device:TPU:6, one launch (start us, length us, event | category | flops | bytes accessed | tf_op | source)
XLA Modules:
  0.0 892.0 jit_solution(6560580829469173553)
XLA Ops:
  6.5 0.9 pad_maximum_fusion.1
  7.5 2.9 broadcast_in_dim.103
  10.4 15.8 %all-to-all-start = ((bf16[32,128,512]{1,2,0:T(8,128)(2,1)}), bf16[32,128,512]{1,2,0:T(8,128)(2,1)}, u32[]{:S(2)}, u32[]{:S(2)}) async-start(bf16[32,128,512]{1,2,0:T(8,128)(2,1)} %broadcast_in_dim.103), calls=%async_computation | async-start | bytes 8388608 | tf_op jit(solution)/shard_map/all_to_all | solution.py:74
  26.9 174.8 %all-to-all-done = bf16[32,128,512]{1,2,0:T(8,128)(2,1)} async-done(((bf16[32,128,512]{1,2,0:T(8,128)(2,1)}), bf16[32,128,512]{1,2,0:T(8,128)(2,1)}, u32[]{:S(2)}, u32[]{:S(2)}) %all-to-all-start) | async-done | bytes 4194336 | tf_op jit(solution)/shard_map/all_to_all | solution.py:74
  201.7 6.5 copy.66
  208.2 3.8 fusion.27
  212.0 2.1 reshape.89
  214.1 2.0 copy.74
  216.1 29.2 %while.33 = (s32[]{:T(128)}, f32[2,128]{1,0:T(2,128)S(1)}, f32[2,128]{1,0:T(2,128)S(1)}, s32[8]{0:T(128)S(1)}, s32[32,32]{1,0:T(8,128)}, /*index=5*/s32[]{:T(128...) while((s32[]{:T(128)}, f32[2,128]{1,0:T(2,128)S(1)}, ...), condition=%wide.region_6.7_spmd, body=%wide.region_0.6_spmd.sunk | while | flops 34406940 | bytes 1391623 | solution.py:97
  217.3 0.8 broadcast_compare_fusion.6
  220.6 0.8 broadcast_compare_fusion.6
  224.5 0.8 broadcast_compare_fusion.6
  227.8 0.8 broadcast_compare_fusion.6
  231.1 0.8 broadcast_compare_fusion.6
  235.0 0.8 broadcast_compare_fusion.6
  238.8 0.8 broadcast_compare_fusion.6
  245.3 4.0 reshape.90
  249.4 3.3 copy.75
  252.7 47.2 %while.34 = (s32[]{:T(128)}, f32[128,2,128]{2,0,1:T(8,128)S(1)}, bf16[8,512,512]{2,1,0:T(8,128)(2,1)}, s32[8]{0:T(128)S(1)}, s32[32,32]{1,0:T(8,128)}, /*index=5...) while((s32[]{:T(128)}, f32[128,2,128]{2,0,1:T(8,128)S(1)}, ...), condition=%wide.region_13.14_spmd, body=%wide.region_8.13_spmd.sunk | while | flops 170721312 | bytes 8655399 | solution.py:137
  256.3 0.8 constant_dynamic-update-slice_fusion.2
  258.3 0.8 broadcast_compare_fusion.7
  260.4 2.5 conditional.5
  260.8 1.2 fusion.11
  263.1 0.8 constant_dynamic-update-slice_fusion.2
  265.1 0.8 broadcast_compare_fusion.7
  267.5 0.8 constant_dynamic-update-slice_fusion.2
  269.5 0.8 broadcast_compare_fusion.7
  271.9 0.8 constant_dynamic-update-slice_fusion.2
  276.0 2.5 conditional.5
  276.4 1.2 fusion.11
  278.7 0.8 constant_dynamic-update-slice_fusion.2
  282.8 2.5 conditional.5
  283.2 1.2 fusion.11
  285.5 0.9 constant_dynamic-update-slice_fusion.2
  287.5 0.8 broadcast_compare_fusion.7
  289.6 2.5 conditional.5
  290.0 1.2 fusion.11
  292.3 0.8 constant_dynamic-update-slice_fusion.2
  294.3 0.8 broadcast_compare_fusion.7
  296.4 2.5 conditional.5
  296.8 1.2 fusion.11
  299.1 0.8 constant_dynamic-update-slice_fusion.2
  299.9 26.5 %all-to-all-start.1 = ((bf16[32,128,512]{2,1,0:T(8,128)(2,1)}), bf16[32,128,512]{2,1,0:T(8,128)(2,1)}, u32[]{:S(2)}, u32[]{:S(2)}) async-start(bf16[32,128,512]{2,1,0:T(8,128)(2,1)} %bitcast.65), calls=%async_computation.1 | async-start | bytes 8388608 | tf_op jit(solution)/shard_map/all_to_all | solution.py:145
  326.8 175.2 %all-to-all-done.1 = bf16[32,128,512]{2,1,0:T(8,128)(2,1)} async-done(((bf16[32,128,512]{2,1,0:T(8,128)(2,1)}), bf16[32,128,512]{2,1,0:T(8,128)(2,1)}, u32[]{:S(2)}, u32[]{:S(2)}) %all-to-all-start.1) | async-done | bytes 4194336 | tf_op jit(solution)/shard_map/all_to_all | solution.py:145
  502.1 2.8 reduce_sum.43
  505.6 236.8 %all-gather.2.cloned.1.call-done = bf16[4096,768]{1,0:T(8,128)(2,1)} async-done(((bf16[128,768]{1,0:T(8,128)(2,1)}), bf16[4096,768]{1,0:T(8,128)(2,1)}) %all-gather.2.cloned.1.call-update) | async-done | bytes 6291472 | tf_op jit(solution)/shard_map/all_gather | solution.py:154
  742.5 6.0 convolution_convert_fusion.3
  748.5 136.7 %reduce-scatter.2.cloned.1.call-done = bf16[256,256]{1,0:T(8,128)(2,1)} async-done(((bf16[4096,256]{1,0:T(8,128)(2,1)}), bf16[256,256]{1,0:T(8,128)(2,1)}) %reduce-scatter.2.cloned.1.call-update) | async-done | bytes 131088 | tf_op jit(solution)/shard_map/reduce_scatter | solution.py:156
  (175 shorter events, 39.5 us)
Async XLA Ops:
  10.4 15.9 %copy-start.1 = (bf16[128,256]{1,0:T(8,128)(2,1)S(1)}, bf16[128,256]{1,0:T(8,128)(2,1)}, u32[]{:S(2)}) copy-start(bf16[128,256]{1,0:T(8,128)(2,1)} %param.17) | copy-start | bytes 196612
  10.4 16.2 %copy-start.2 = (bf16[128,256]{1,0:T(8,128)(2,1)S(1)}, bf16[128,256]{1,0:T(8,128)(2,1)}, u32[]{:S(2)}) copy-start(bf16[128,256]{1,0:T(8,128)(2,1)} %param.21) | copy-start | bytes 196612
  10.4 16.3 %copy-start = (bf16[128,256]{1,0:T(8,128)(2,1)S(1)}, bf16[128,256]{1,0:T(8,128)(2,1)}, u32[]{:S(2)}) copy-start(bf16[128,256]{1,0:T(8,128)(2,1)} %param.20) | copy-start | bytes 196612
  10.4 191.3 %all-to-all-start = ((bf16[32,128,512]{1,2,0:T(8,128)(2,1)}), bf16[32,128,512]{1,2,0:T(8,128)(2,1)}, u32[]{:S(2)}, u32[]{:S(2)}) async-start(bf16[32,128,512]{1,2,0:T(8,128)(2,1)} %broadcast_in_dim.103), calls=%async_computation | async-start | bytes 8388608 | tf_op jit(solution)/shard_map/all_to_all | solution.py:74
  299.9 202.1 %all-to-all-start.1 = ((bf16[32,128,512]{2,1,0:T(8,128)(2,1)}), bf16[32,128,512]{2,1,0:T(8,128)(2,1)}, u32[]{:S(2)}, u32[]{:S(2)}) async-start(bf16[32,128,512]{2,1,0:T(8,128)(2,1)} %bitcast.65), calls=%async_computation.1 | async-start | bytes 8388608 | tf_op jit(solution)/shard_map/all_to_all | solution.py:145
  326.5 416.0 %copy-start.3 = (bf16[256,256]{1,0:T(8,128)(2,1)S(1)}, bf16[256,256]{1,0:T(8,128)(2,1)}, u32[]{:S(2)}) copy-start(bf16[256,256]{1,0:T(8,128)(2,1)} %param.25) | copy-start | bytes 393220
  326.5 416.0 %copy-start.4 = (bf16[256,256]{1,0:T(8,128)(2,1)S(1)}, bf16[256,256]{1,0:T(8,128)(2,1)}, u32[]{:S(2)}) copy-start(bf16[256,256]{1,0:T(8,128)(2,1)} %param.24) | copy-start | bytes 393220
  326.5 416.0 %copy-start.5 = (bf16[256,256]{1,0:T(8,128)(2,1)S(1)}, bf16[256,256]{1,0:T(8,128)(2,1)}, u32[]{:S(2)}) copy-start(bf16[256,256]{1,0:T(8,128)(2,1)} %param.23) | copy-start | bytes 393220
  326.5 415.9 %all-gather.2.cloned.1.call-start = ((), (), s32[]{:S(2)}) async-start(), calls=%async_computation.3 | async-start | bytes 6488064 | tf_op jit(solution)/shard_map/all_gather | solution.py:154
  505.6 379.6 %reduce-scatter.2.cloned.1.call-start = ((), (), s32[]{:S(2)}) async-start(), calls=%async_computation.4 | async-start | bytes 2228224 | tf_op jit(solution)/shard_map/reduce_scatter | solution.py:156
Sparse Core Ops, SparseCore 0:
  505.7 236.7 all-gather.1
  748.6 136.5 reduce-scatter.1

commit v2 on v1

v2 whole, which is shorter than its diff:
```python
import functools
import math

import jax
import jax.numpy as jnp
from jax import lax
from jax.experimental import pallas as pl
from jax.experimental.pallas import tpu as pltpu
from jax.sharding import PartitionSpec as P

HD = 128
BLK = 128


NEG_FILL = -1e30


def _nt(a, b):
    return lax.dot_general(a, b, (((1,), (1,)), ((), ())), preferred_element_type=jnp.float32)


def _tn(a, b):
    return lax.dot_general(a, b, (((0,), (0,)), ((), ())), preferred_element_type=jnp.float32)


def attention_kernel(
    head_count, block_count, score_scale,
    row_map, q_ref, do_ref, o_ref, k_ref, v_ref, dq_ref, dkdv_ref, m_ref, l_ref, dq_acc,
):
    width = head_count * HD
    for h in range(head_count):
        cols = slice(h * HD, (h + 1) * HD)
        m_ref[h] = jnp.full((BLK, 1), NEG_FILL, jnp.float32)
        l_ref[h] = jnp.zeros((BLK, 1), jnp.float32)
        dq_acc[:, cols] = jnp.zeros((BLK, HD), jnp.float32)

    def stat_body(j, carry):
        rows = pl.ds(pl.multiple_of(j * BLK, BLK), BLK)

        @pl.when(row_map[j] > 0)
        def _():
            for h in range(head_count):
                cols = slice(h * HD, (h + 1) * HD)
                scores = _nt(q_ref[:, cols], k_ref[rows, cols]) * score_scale
                old_max = m_ref[h]
                new_max = jnp.maximum(old_max, jnp.max(scores, axis=1, keepdims=True))
                kept = jnp.sum(jnp.exp(scores - new_max), axis=1, keepdims=True)
                l_ref[h] = l_ref[h] * jnp.exp(old_max - new_max) + kept
                m_ref[h] = new_max

        return carry

    lax.fori_loop(0, block_count, stat_body, 0)

    def back_body(j, carry):
        rows = pl.ds(pl.multiple_of(j * BLK, BLK), BLK)

        @pl.when(row_map[j] > 0)
        def _():
            for h in range(head_count):
                cols = slice(h * HD, (h + 1) * HD)
                q_h = q_ref[:, cols]
                do_h = do_ref[:, cols]
                k_b = k_ref[rows, cols]
                log_total = m_ref[h] + jnp.log(l_ref[h])
                row_delta = jnp.sum(
                    do_h.astype(jnp.float32) * o_ref[:, cols].astype(jnp.float32),
                    axis=1,
                    keepdims=True,
                )
                scores = _nt(q_h, k_b) * score_scale
                probs = jnp.exp(scores - log_total)
                dprobs = _nt(do_h, v_ref[rows, cols])
                score_gradient = (probs * (dprobs - row_delta) * score_scale).astype(jnp.bfloat16)
                dv = _tn(probs.astype(jnp.bfloat16), do_h)
                dk = _tn(score_gradient, q_h)
                dkdv_ref[rows, cols] = dk.astype(jnp.bfloat16)
                dkdv_ref[rows, pl.ds(width + h * HD, HD)] = dv.astype(jnp.bfloat16)
                part = jnp.dot(score_gradient, k_b, preferred_element_type=jnp.float32)
                dq_acc[:, cols] += part.astype(jnp.bfloat16).astype(jnp.float32)

        @pl.when(row_map[j] == 0)
        def _():
            dkdv_ref[rows, :] = jnp.zeros((BLK, 2 * width), jnp.bfloat16)

        return carry

    lax.fori_loop(0, block_count, back_body, 0)
    dq_ref[...] = dq_acc[...]


def slab_attention(row_map, queries, output_grad, attn_output, full_keys, full_values):
    slab_rows, width = queries.shape
    head_count = width // HD
    key_rows = full_keys.shape[0]
    block_count = key_rows // BLK
    vmem = pl.BlockSpec(memory_space=pltpu.VMEM)
    flops = 2 * slab_rows * key_rows * width * 6
    return pl.pallas_call(
        functools.partial(attention_kernel, head_count, block_count, 1.0 / math.sqrt(HD)),
        out_shape=(
            jax.ShapeDtypeStruct((slab_rows, width), jnp.float32),
            jax.ShapeDtypeStruct((key_rows, 2 * width), jnp.bfloat16),
        ),
        in_specs=[pl.BlockSpec(memory_space=pltpu.SMEM)] + [vmem] * 5,
        out_specs=(vmem, vmem),
        scratch_shapes=[
            pltpu.VMEM((head_count, slab_rows, 1), jnp.float32),
            pltpu.VMEM((head_count, slab_rows, 1), jnp.float32),
            pltpu.VMEM((slab_rows, width), jnp.float32),
        ],
        compiler_params=pltpu.CompilerParams(vmem_limit_bytes=48 * 1024 * 1024),
        cost_estimate=pl.CostEstimate(
            flops=flops,
            transcendentals=2 * slab_rows * key_rows * head_count,
            bytes_accessed=key_rows * width * 2 * 4,
        ),
    )(row_map, queries, output_grad, attn_output, full_keys, full_values)


def per_device(
    queries, key_states, value_states, attn_output, output_grad, block_map, w_query, w_key, w_value
):
    slab_rows, width = queries.shape
    context_count = lax.axis_size("ctx")
    row_map = lax.dynamic_index_in_dim(
        block_map, lax.axis_index("ctx") * slab_rows // BLK, axis=0, keepdims=False
    )
    key_value = jnp.concatenate([key_states, value_states], axis=1)
    spread = jnp.broadcast_to(key_value[None], (context_count,) + key_value.shape)
    gathered = lax.all_to_all(spread, "ctx", 0, 0, tiled=True).reshape(
        context_count * slab_rows, 2 * width
    )
    full_keys, full_values = gathered[:, :width], gathered[:, width:]
    dq_total, part_grads = slab_attention(
        row_map, queries, output_grad, attn_output, full_keys, full_values
    )
    local_grads = dq_total.astype(jnp.bfloat16)
    part_width = part_grads.shape[1]
    arrived = lax.all_to_all(
        part_grads.reshape(context_count, slab_rows, part_width),
        "ctx",
        split_axis=0,
        concat_axis=0,
        tiled=True,
    )
    finished = jnp.sum(arrived.astype(jnp.float32), axis=0).astype(jnp.bfloat16)
    own_grads = jnp.concatenate([local_grads, finished], axis=1)
    gradients = lax.all_gather(own_grads, "ctx", axis=0, tiled=True)
    projections = jnp.concatenate([w_query, w_key, w_value], axis=1)
    return lax.psum_scatter(
        lax.dot_general(
            gradients, projections, (((1,), (1,)), ((), ())), preferred_element_type=jnp.float32
        ).astype(jnp.bfloat16),
        "tp",
        scatter_dimension=0,
        tiled=True,
    )


def solution(mesh):
    return jax.shard_map(
        per_device,
        mesh=mesh,
        in_specs=(
            P("ctx", "tp"),
            P("ctx", "tp"),
            P("ctx", "tp"),
            P("ctx", "tp"),
            P("ctx", "tp"),
            P(),
            P("ctx", "tp"),
            P("ctx", "tp"),
            P("ctx", "tp"),
        ),
        out_specs=P("tp", "ctx"),
        check_vma=False,
    )
```

time: 894 us -> 819 us (0.916)
  local copies, waits for them, and re-layouts: 44 us -> 5.02 us
  other arithmetic: 30.4 us -> 4.39 us
  loops' own time: 19.8 us -> 0 us
  Pallas kernels: 0 us -> 18.6 us
  matrix products: 18.1 us -> 5.97 us
    another operation x18 -> x0, loops' own time: 19.8 us -> none  [the longest x1 9.56 us: per_device(): lax.scan(stat_step, start_state, (key_blocks, block_ids))]
    pallas_call x0 -> x1, Pallas kernels: none -> 18.6 us  [slab_attention(): pl.pallas_call(functools.partial(attention_kernel, head_count, block_coun...]
    gt x26 -> x0, other arithmetic: 12.4 us -> none  [block_mask(): return spread.reshape(row_count, col_count) > 0]
    reduce_or x16 -> x0, other arithmetic: 12.2 us -> none  [the longest x8 6.1 us: stat_step(): jnp.any(allowed)]
    dot_general x30 -> x0, matrix products: 12.1 us -> none  [the longest x5 5.85 us: gradient_block(): jnp.einsum('qhd,khd->hqk', grad_heads, value_block, preferred_element_typ...]
    dynamic_slice x21 -> x0, local copies, waits for them, and re-layouts: 9.36 us -> none  [per_device(): lax.scan(stat_step, start_state, (key_blocks, block_ids))]
where the time goes in v2:
time: 819 us; the launch traced here: 818 us
  waiting for transfers between devices  724 us (88%)
  starting transfers between devices  46.7 us (6%)
  Pallas kernels  18.6 us (2%)
  between operations  13.5 us (2%)
    all_gather x1, waiting for transfers between devices, per_device(): gradients = lax.all_gather(own_grads, 'ctx', axis=0, tiled=True)  237 us
    all_to_all x1, waiting for transfers between devices, per_device(): lax.all_to_all(spread, 'ctx', 0, 0, tiled=True)  175 us
    all_to_all x1, waiting for transfers between devices, per_device(): lax.all_to_all(part_grads.reshape(context_count, slab_rows, part_width),...  175 us
    reduce_scatter x1, waiting for transfers between devices, per_device(): lax.psum_scatter(lax.dot_general(gradients, projections, (((1,), (1,)), (...  137 us
    all_to_all x1, starting transfers between devices, per_device(): lax.all_to_all(part_grads.reshape(context_count, slab_rows, part_width),...  30.9 us
    pallas_call x1, Pallas kernels, slab_attention(): pl.pallas_call(functools.partial(attention_kernel, head_count, block_coun...  18.6 us
  transfers between devices with their start and end apart: 4, of which 4 were waited for; matrix products, arithmetic and copies ran while one was open for 0% of the time, Pallas kernels for 0%

profile of v2, /device:TPU:6, one launch (start us, length us, event | category | flops | bytes accessed | tf_op | source)
XLA Modules:
  0.0 818.3 jit_solution(11544299434880833348)
XLA Ops:
  6.5 0.0 copy-start
  6.5 0.9 pad_maximum_fusion.1
  7.4 2.4 broadcast_in_dim.2
  9.9 15.7 %all-to-all-start = ((bf16[32,128,512]{2,1,0:T(8,128)(2,1)}), bf16[32,128,512]{2,1,0:T(8,128)(2,1)}, u32[]{:S(2)}, u32[]{:S(2)}) async-start(bf16[32,128,512]{2,1,0:T(8,128)(2,1)} %broadcast_in_dim.2), calls=%async_computation | async-start | bytes 8388608 | tf_op jit(solution)/shard_map/all_to_all | solution.py:131
  25.6 0.0 copy-done
  25.7 175.4 %all-to-all-done = bf16[32,128,512]{2,1,0:T(8,128)(2,1)} async-done(((bf16[32,128,512]{2,1,0:T(8,128)(2,1)}), bf16[32,128,512]{2,1,0:T(8,128)(2,1)}, u32[]{:S(2)}, u32[]{:S(2)}) %all-to-all-start) | async-done | bytes 4194336 | tf_op jit(solution)/shard_map/all_to_all | solution.py:131
  201.0 0.0 copy-start.1
  201.0 0.0 copy-start.2
  201.0 0.0 copy-start.3
  201.0 2.5 fusion.6
  203.5 0.0 copy-done.1
  203.6 0.0 copy-done.2
  203.6 0.0 copy-done.3
  203.6 18.6 %shard_map.91 = (f32[128,256]{1,0:T(8,128)S(1)}, bf16[4096,512]{1,0:T(8,128)(2,1)}) custom-call(s32[32]{0:T(128)S(1)} %dynamic-slice_bitcast_fusion.row_map, bf16[128,256]{1,0:T(8,128)(2,1)S(1)} %copy-done.1, bf16[128,256]{1,0:T(8,128)(2,1)S(1)} %copy-done.2, bf16[128,256]{1,0:T(8,128)(2,1)S(1)} %copy-done.3, bf16[4096,256]{1,0:T(8,128)(2,1)S(1)} %get-tuple-element.10.k_ref, ...), custom_call_target="tpu_custom_call" | custom-call | flops 1610612736 | bytes 8388608 | tf_op jit(solution)/shard_map/pallas_call | solution.py:99
  222.2 30.9 %all-to-all-start.1 = ((bf16[32,128,512]{2,1,0:T(8,128)(2,1)}), bf16[32,128,512]{2,1,0:T(8,128)(2,1)}, u32[]{:S(2)}, u32[]{:S(2)}) async-start(bf16[32,128,512]{2,1,0:T(8,128)(2,1)} %bitcast.5), calls=%async_computation.1 | async-start | bytes 8388608 | tf_op jit(solution)/shard_map/all_to_all | solution.py:140
  253.0 0.0 copy-start.4
  253.1 0.0 copy-start.5
  253.1 0.0 copy-start.6
  253.1 0.0 all-gather.2.cloned.1.call-start
  253.1 175.1 %all-to-all-done.1 = bf16[32,128,512]{2,1,0:T(8,128)(2,1)} async-done(((bf16[32,128,512]{2,1,0:T(8,128)(2,1)}), bf16[32,128,512]{2,1,0:T(8,128)(2,1)}, u32[]{:S(2)}, u32[]{:S(2)}) %all-to-all-start.1) | async-done | bytes 4194336 | tf_op jit(solution)/shard_map/all_to_all | solution.py:140
  428.3 2.8 reduce_sum.12
  431.1 0.7 pad_maximum_fusion
  431.8 0.0 all-gather.2.cloned.1.call-update
  431.8 0.0 reduce-scatter.2.cloned.1.call-start
  431.8 236.9 %all-gather.2.cloned.1.call-done = bf16[4096,768]{1,0:T(8,128)(2,1)} async-done(((bf16[128,768]{1,0:T(8,128)(2,1)}), bf16[4096,768]{1,0:T(8,128)(2,1)}) %all-gather.2.cloned.1.call-update) | async-done | bytes 6291472 | tf_op jit(solution)/shard_map/all_gather | solution.py:149
  668.7 0.0 copy-done.4
  668.7 0.0 copy-done.5
  668.8 0.0 copy-done.6
  668.8 6.0 convolution_convert_fusion
  674.7 0.0 reduce-scatter.2.cloned.1.call-update
  674.7 136.7 %reduce-scatter.2.cloned.1.call-done = bf16[256,256]{1,0:T(8,128)(2,1)} async-done(((bf16[4096,256]{1,0:T(8,128)(2,1)}), bf16[256,256]{1,0:T(8,128)(2,1)}) %reduce-scatter.2.cloned.1.call-update) | async-done | bytes 131088 | tf_op jit(solution)/shard_map/reduce_scatter | solution.py:151
  (2 shorter events, 0.0 us)
Async XLA Ops:
  6.5 19.1 %copy-start = (s32[32,32]{1,0:T(8,128)S(1)}, s32[32,32]{1,0:T(8,128)}, u32[]{:S(2)}) copy-start(s32[32,32]{1,0:T(8,128)} %param.14) | copy-start | bytes 12292
  9.9 191.1 %all-to-all-start = ((bf16[32,128,512]{2,1,0:T(8,128)(2,1)}), bf16[32,128,512]{2,1,0:T(8,128)(2,1)}, u32[]{:S(2)}, u32[]{:S(2)}) async-start(bf16[32,128,512]{2,1,0:T(8,128)(2,1)} %broadcast_in_dim.2), calls=%async_computation | async-start | bytes 8388608 | tf_op jit(solution)/shard_map/all_to_all | solution.py:131
  201.0 2.5 copy-start.1
  201.0 2.6 copy-start.2
  201.0 2.6 copy-start.3
  222.2 206.1 %all-to-all-start.1 = ((bf16[32,128,512]{2,1,0:T(8,128)(2,1)}), bf16[32,128,512]{2,1,0:T(8,128)(2,1)}, u32[]{:S(2)}, u32[]{:S(2)}) async-start(bf16[32,128,512]{2,1,0:T(8,128)(2,1)} %bitcast.5), calls=%async_computation.1 | async-start | bytes 8388608 | tf_op jit(solution)/shard_map/all_to_all | solution.py:140
  253.0 415.7 %copy-start.4 = (bf16[256,256]{1,0:T(8,128)(2,1)S(1)}, bf16[256,256]{1,0:T(8,128)(2,1)}, u32[]{:S(2)}) copy-start(bf16[256,256]{1,0:T(8,128)(2,1)} %param.17) | copy-start | bytes 393220
  253.1 415.7 %copy-start.5 = (bf16[256,256]{1,0:T(8,128)(2,1)S(1)}, bf16[256,256]{1,0:T(8,128)(2,1)}, u32[]{:S(2)}) copy-start(bf16[256,256]{1,0:T(8,128)(2,1)} %param.16) | copy-start | bytes 393220
  253.1 415.7 %copy-start.6 = (bf16[256,256]{1,0:T(8,128)(2,1)S(1)}, bf16[256,256]{1,0:T(8,128)(2,1)}, u32[]{:S(2)}) copy-start(bf16[256,256]{1,0:T(8,128)(2,1)} %param.15) | copy-start | bytes 393220
  253.1 415.7 %all-gather.2.cloned.1.call-start = ((), (), s32[]{:S(2)}) async-start(), calls=%async_computation.3 | async-start | bytes 6488064 | tf_op jit(solution)/shard_map/all_gather | solution.py:149
  431.8 379.6 %reduce-scatter.2.cloned.1.call-start = ((), (), s32[]{:S(2)}) async-start(), calls=%async_computation.4 | async-start | bytes 2228224 | tf_op jit(solution)/shard_map/reduce_scatter | solution.py:151
Sparse Core Ops, SparseCore 0:
  431.9 236.7 all-gather.1
  674.9 136.5 reduce-scatter.1

commit v3 on v2

--- a/solution.py
+++ b/solution.py
@@ -13,6 +13,9 @@
 
 
 NEG_FILL = -1e30
+GATHER_ORDER = (4, 2, 16, 8, 1)
+SCATTER_ORDER = (1, 8, 16, 2, 4)
+TP_ORDER = (1, 4, 8, 2)
 
 
 def _nt(a, b):
@@ -118,44 +121,62 @@
     )(row_map, queries, output_grad, attn_output, full_keys, full_values)
 
 
+def tree_gather(x, axis, order):
+    me = lax.axis_index(axis)
+    count = lax.axis_size(axis)
+    held = x
+    for distance in order:
+        other = lax.ppermute(held, axis, [(i, i ^ distance) for i in range(count)])
+        low = (me & distance) == 0
+        held = jnp.where(low, jnp.stack([held, other]), jnp.stack([other, held]))
+    bits = list(reversed(order))
+    perm = sorted(range(len(bits)), key=lambda k: -bits[k])
+    held = jnp.transpose(held, perm + list(range(len(bits), held.ndim)))
+    return held.reshape((count * x.shape[0],) + x.shape[1:])
+
+
+def tree_reduce_scatter(x, axis, order, wire=jnp.bfloat16):
+    me = lax.axis_index(axis)
+    count = lax.axis_size(axis)
+    levels = count.bit_length() - 1
+    block = x.shape[0] // count
+    held = x.astype(jnp.float32).reshape((2,) * levels + (block,) + x.shape[1:])
+    bits = [1 << (levels - 1 - k) for k in range(levels)]
+    for distance in order:
+        dim = bits.index(distance)
+        bits.pop(dim)
+        zero = lax.index_in_dim(held, 0, dim, keepdims=False)
+        one = lax.index_in_dim(held, 1, dim, keepdims=False)
+        low = (me & distance) == 0
+        keep = jnp.where(low, zero, one)
+        send = jnp.where(low, one, zero).astype(wire)
+        other = lax.ppermute(send, axis, [(i, i ^ distance) for i in range(count)])
+        held = keep + other.astype(jnp.float32)
+    return held.reshape((block,) + x.shape[1:])
+
+
 def per_device(
     queries, key_states, value_states, attn_output, output_grad, block_map, w_query, w_key, w_value
 ):
     slab_rows, width = queries.shape
-    context_count = lax.axis_size("ctx")
     row_map = lax.dynamic_index_in_dim(
         block_map, lax.axis_index("ctx") * slab_rows // BLK, axis=0, keepdims=False
     )
     key_value = jnp.concatenate([key_states, value_states], axis=1)
-    spread = jnp.broadcast_to(key_value[None], (context_count,) + key_value.shape)
-    gathered = lax.all_to_all(spread, "ctx", 0, 0, tiled=True).reshape(
-        context_count * slab_rows, 2 * width
-    )
+    gathered = tree_gather(key_value, "ctx", GATHER_ORDER)
     full_keys, full_values = gathered[:, :width], gathered[:, width:]
     dq_total, part_grads = slab_attention(
         row_map, queries, output_grad, attn_output, full_keys, full_values
     )
     local_grads = dq_total.astype(jnp.bfloat16)
-    part_width = part_grads.shape[1]
-    arrived = lax.all_to_all(
-        part_grads.reshape(context_count, slab_rows, part_width),
-        "ctx",
-        split_axis=0,
-        concat_axis=0,
-        tiled=True,
-    )
-    finished = jnp.sum(arrived.astype(jnp.float32), axis=0).astype(jnp.bfloat16)
+    finished = tree_reduce_scatter(part_grads, "ctx", SCATTER_ORDER).astype(jnp.bfloat16)
     own_grads = jnp.concatenate([local_grads, finished], axis=1)
-    gradients = lax.all_gather(own_grads, "ctx", axis=0, tiled=True)
+    gradients = tree_gather(own_grads, "ctx", GATHER_ORDER)
     projections = jnp.concatenate([w_query, w_key, w_value], axis=1)
-    return lax.psum_scatter(
-        lax.dot_general(
-            gradients, projections, (((1,), (1,)), ((), ())), preferred_element_type=jnp.float32
-        ).astype(jnp.bfloat16),
-        "tp",
-        scatter_dimension=0,
-        tiled=True,
-    )
+    term = lax.dot_general(
+        gradients, projections, (((1,), (1,)), ((), ())), preferred_element_type=jnp.float32
+    ).astype(jnp.bfloat16)
+    return tree_reduce_scatter(term, "tp", TP_ORDER).astype(jnp.bfloat16)
 
 
 def solution(mesh):

time: 819 us -> 521 us (0.64)
  waiting for transfers between devices: 724 us -> 360 us
  starting transfers between devices: 46.7 us -> 84.7 us
  other arithmetic: 4.39 us -> 23.2 us
  Pallas kernels: 18.6 us -> 33.4 us
  between operations: 13.5 us -> 0.61 us
    ppermute x0 -> x19, waiting for transfers between devices: none -> 360 us  [the longest x10 240 us: tree_gather(): other = lax.ppermute(held, axis, [(i, i ^ distance) for i in range(count)])]
    all_to_all x2 -> x0, waiting for transfers between devices: 350 us -> none  [the longest x1 175 us: per_device(): lax.all_to_all(spread, 'ctx', 0, 0, tiled=True)]
    all_gather x1 -> x0, waiting for transfers between devices: 237 us -> none  [per_device(): gradients = lax.all_gather(own_grads, 'ctx', axis=0, tiled=True)]
    reduce_scatter x1 -> x0, waiting for transfers between devices: 137 us -> none  [per_device(): lax.psum_scatter(lax.dot_general(gradients, projections, (((1,), (1,)), (...]
    ppermute x0 -> x19, starting transfers between devices: none -> 84.7 us  [the longest x10 46.1 us: tree_gather(): other = lax.ppermute(held, axis, [(i, i ^ distance) for i in range(count)])]
    all_to_all x2 -> x0, starting transfers between devices: 46.6 us -> none  [the longest x1 30.9 us: per_device(): lax.all_to_all(part_grads.reshape(context_count, slab_rows, part_width),...]
    pallas_call x1, Pallas kernels: 18.6 us -> 33.4 us  [slab_attention(): pl.pallas_call(functools.partial(attention_kernel, head_count, block_coun...]
    select_n x0 -> x17, other arithmetic: none -> 10.5 us  [tree_gather(): held = jnp.where(low, jnp.stack([held, other]), jnp.stack([other, held]))]
  transfers between devices with their start and end apart: 4 -> 19, of which waited for: 4 -> 19; matrix products, arithmetic and copies ran while one was open for 0% -> 1% of each run, Pallas kernels for 0% -> 0%
where the time goes in v3:
time: 521 us; the launch traced here: 513 us
  waiting for transfers between devices  360 us (69%)
  starting transfers between devices  84.7 us (16%)
  Pallas kernels  33.4 us (6%)
  other arithmetic  23.2 us (4%)
  local copies, waits for them, and re-layouts  9.06 us (2%)
    ppermute x10, waiting for transfers between devices, tree_gather(): other = lax.ppermute(held, axis, [(i, i ^ distance) for i in range(count)])  240 us
    ppermute x9, waiting for transfers between devices, tree_reduce_scatter(): other = lax.ppermute(send, axis, [(i, i ^ distance) for i in range(count)])  120 us
    ppermute x10, starting transfers between devices, tree_gather(): other = lax.ppermute(held, axis, [(i, i ^ distance) for i in range(count)])  46.1 us
    ppermute x9, starting transfers between devices, tree_reduce_scatter(): other = lax.ppermute(send, axis, [(i, i ^ distance) for i in range(count)])  38.6 us
    pallas_call x1, Pallas kernels, slab_attention(): pl.pallas_call(functools.partial(attention_kernel, head_count, block_coun...  33.4 us
    select_n x17, other arithmetic, tree_gather(): held = jnp.where(low, jnp.stack([held, other]), jnp.stack([other, held]))  10.5 us
  transfers between devices with their start and end apart: 19, of which 19 were waited for; matrix products, arithmetic and copies ran while one was open for 1% of the time, Pallas kernels for 0%

profile of v3, /device:TPU:6, one launch (start us, length us, event | category | flops | bytes accessed | tf_op | source)
XLA Modules:
  0.0 512.8 jit_solution(13609521056549340827)
XLA Ops:
  1.7 9.1 %collective-permute-start = (bf16[128,512]{1,0:T(8,128)(2,1)S(1)}, bf16[128,512]{1,0:T(8,128)(2,1)S(1)}, u32[]{:S(2)}, u32[]{:S(2)}) collective-permute-start(bf16[128,512]{1,0:T(8,128)(2,1)S(1)} %constant_dynamic-update-slice_fusion), channel_id=1, source_target_pairs={{0,64},{16,80},{32,96},{48,112},{64,0},{80,16},{96,32},{112,48},{1... | collective-permute-start | bytes 393224 | tf_op jit(solution)/shard_map/ppermute | solution.py:129
  10.8 11.9 %collective-permute-done = bf16[128,512]{1,0:T(8,128)(2,1)S(1)} collective-permute-done((bf16[128,512]{1,0:T(8,128)(2,1)S(1)}, bf16[128,512]{1,0:T(8,128)(2,1)S(1)}, u32[]{:S(2)}, u32[]{:S(2)}) %collective-permute-start) | collective-permute-done | bytes 131104 | tf_op jit(solution)/shard_map/ppermute | solution.py:129
  22.7 1.9 collective-permute-start.1
  24.7 13.9 %collective-permute-done.1 = bf16[2,128,512]{2,1,0:T(8,128)(2,1)S(1)} collective-permute-done((bf16[2,128,512]{2,1,0:T(8,128)(2,1)S(1)}, bf16[2,128,512]{2,1,0:T(8,128)(2,1)S(1)}, u32[]{:S(2)}, u32[]{:S(2)}) %collective-permute-start.1) | collective-permute-done | bytes 262176 | tf_op jit(solution)/shard_map/ppermute | solution.py:129
  38.7 3.3 collective-permute-start.2
  42.2 13.1 %collective-permute-done.2 = bf16[2,2,128,512]{3,2,1,0:T(8,128)(2,1)S(1)} collective-permute-done((bf16[2,2,128,512]{3,2,1,0:T(8,128)(2,1)S(1)}, bf16[2,2,128,512]{3,2,1,0:T(8,128)(2,1)S(1)}, u32[]{:S(2)}, u32[]{:S(2)}) %collective-permute-start.2) | collective-permute-done | bytes 524320 | tf_op jit(solution)/shard_map/ppermute | solution.py:129
  56.4 2.7 collective-permute-start.3
  59.4 22.6 %collective-permute-done.3 = bf16[2,2,2,128,512]{4,3,2,1,0:T(8,128)(2,1)S(1)} collective-permute-done((bf16[2,2,2,128,512]{4,3,2,1,0:T(8,128)(2,1)}, bf16[2,2,2,128,512]{4,3,2,1,0:T(8,128)(2,1)S(1)}, u32[]{:S(2)}, u32[]{:S(2)}) %collective-permute-start.3) | collective-permute-done | bytes 1048608 | tf_op jit(solution)/shard_map/ppermute | solution.py:129
  82.0 1.7 maximum_select_fusion.4
  83.7 1.9 collective-permute-start.4
  86.2 44.7 %collective-permute-done.4 = bf16[2,2,2,2,128,512]{5,4,3,2,1,0:T(8,128)(2,1)} collective-permute-done((bf16[2,2,2,2,128,512]{5,4,3,2,1,0:T(8,128)(2,1)}, bf16[2,2,2,2,128,512]{5,4,3,2,1,0:T(8,128)(2,1)}, u32[]{:S(2)}, u32[]{:S(2)}) %collective-permute-start.4) | collective-permute-done | bytes 2097184 | tf_op jit(solution)/shard_map/ppermute | solution.py:129
  130.9 2.9 fusion
  135.1 33.4 %shard_map.91 = (f32[128,256]{1,0:T(8,128)S(1)}, bf16[4096,512]{1,0:T(8,128)(2,1)}) custom-call(s32[32]{0:T(128)S(1)} %dynamic-slice_bitcast_fusion.row_map, bf16[128,256]{1,0:T(8,128)(2,1)S(1)} %copy-done.2, bf16[128,256]{1,0:T(8,128)(2,1)S(1)} %copy-done.3, bf16[128,256]{1,0:T(8,128)(2,1)S(1)} %copy-done.4, bf16[4096,256]{1,0:T(8,128)(2,1)S(1)} %get-tuple-element.12.k_ref, ...), custom_call_target="tpu_custom_call" | custom-call | flops 1610612736 | bytes 8388608 | tf_op jit(solution)/shard_map/pallas_call | solution.py:102
  168.5 3.4 fusion.22
  172.2 1.9 collective-permute-start.5
  174.1 44.1 %collective-permute-done.5 = bf16[2,2,2,2,128,512]{5,4,2,3,0,1:T(8,128)(2,1)S(1)} collective-permute-done((bf16[2,2,2,2,128,512]{5,4,2,3,0,1:T(8,128)(2,1)S(1)}, bf16[2,2,2,2,128,512]{5,4,2,3,0,1:T(8,128)(2,1)S(1)}, u32[]{:S(2)}, u32[]{:S(2)}) %collective-permute-start.5) | collective-permute-done | bytes 2097184 | tf_op jit(solution)/shard_map/ppermute | solution.py:153
  219.7 1.9 collective-permute-start.6
  221.6 20.7 %collective-permute-done.6 = bf16[2,2,2,128,512]{4,3,1,2,0:T(8,128)(2,1)S(1)} collective-permute-done((bf16[2,2,2,128,512]{4,3,1,2,0:T(8,128)(2,1)S(1)}, bf16[2,2,2,128,512]{4,3,1,2,0:T(8,128)(2,1)S(1)}, u32[]{:S(2)}, u32[]{:S(2)}) %collective-permute-start.6) | collective-permute-done | bytes 1048608 | tf_op jit(solution)/shard_map/ppermute | solution.py:153
  243.0 5.3 %collective-permute-start.7 = (bf16[2,2,128,512]{3,2,0,1:T(8,128)(2,1)S(1)}, bf16[2,2,128,512]{3,2,0,1:T(8,128)(2,1)S(1)}, u32[]{:S(2)}, u32[]{:S(2)}) collective-permute-start(bf16[2,2,128,512]{3,2,0,1:T(8,128)(2,1)S(1)} %fusion.5), channel_id=1, source_target_pairs={{0,256},{16,272},{32,288},{48,304},{64,320},{80,336},{96,352},{112... | collective-permute-start | bytes 1572872 | tf_op jit(solution)/shard_map/ppermute | solution.py:153
  248.3 8.2 %collective-permute-done.7 = bf16[2,2,128,512]{3,2,0,1:T(8,128)(2,1)S(1)} collective-permute-done((bf16[2,2,128,512]{3,2,0,1:T(8,128)(2,1)S(1)}, bf16[2,2,128,512]{3,2,0,1:T(8,128)(2,1)S(1)}, u32[]{:S(2)}, u32[]{:S(2)}) %collective-permute-start.7) | collective-permute-done | bytes 524320 | tf_op jit(solution)/shard_map/ppermute | solution.py:153
  256.8 8.1 %collective-permute-start.8 = (bf16[2,128,512]{2,1,0:T(8,128)(2,1)S(1)}, bf16[2,128,512]{2,1,0:T(8,128)(2,1)S(1)}, u32[]{:S(2)}, u32[]{:S(2)}) collective-permute-start(bf16[2,128,512]{2,1,0:T(8,128)(2,1)S(1)} %fusion.13), channel_id=1, source_target_pairs={{0,32},{16,48},{32,0},{48,16},{64,96},{80,112},{96,64},{112,80},{1... | collective-permute-start | bytes 786440 | tf_op jit(solution)/shard_map/ppermute | solution.py:153
  265.0 7.1 %collective-permute-done.8 = bf16[2,128,512]{2,1,0:T(8,128)(2,1)S(1)} collective-permute-done((bf16[2,128,512]{2,1,0:T(8,128)(2,1)S(1)}, bf16[2,128,512]{2,1,0:T(8,128)(2,1)S(1)}, u32[]{:S(2)}, u32[]{:S(2)}) %collective-permute-start.8) | collective-permute-done | bytes 262176 | tf_op jit(solution)/shard_map/ppermute | solution.py:153
  272.3 3.9 collective-permute-start.9
  276.2 7.9 %collective-permute-done.9 = bf16[128,512]{1,0:T(8,128)(2,1)S(1)} collective-permute-done((bf16[128,512]{1,0:T(8,128)(2,1)S(1)}, bf16[128,512]{1,0:T(8,128)(2,1)S(1)}, u32[]{:S(2)}, u32[]{:S(2)}) %collective-permute-start.9) | collective-permute-done | bytes 131104 | tf_op jit(solution)/shard_map/ppermute | solution.py:153
  284.2 3.1 collective-permute-start.10
  287.3 12.2 %collective-permute-done.10 = bf16[128,768]{1,0:T(8,128)(2,1)S(1)} collective-permute-done((bf16[128,768]{1,0:T(8,128)(2,1)S(1)}, bf16[128,768]{1,0:T(8,128)(2,1)S(1)}, u32[]{:S(2)}, u32[]{:S(2)}) %collective-permute-start.10) | collective-permute-done | bytes 196640 | tf_op jit(solution)/shard_map/ppermute | solution.py:129
  299.6 1.9 collective-permute-start.11
  301.6 13.9 %collective-permute-done.11 = bf16[2,128,768]{2,1,0:T(8,128)(2,1)S(1)} collective-permute-done((bf16[2,128,768]{2,1,0:T(8,128)(2,1)S(1)}, bf16[2,128,768]{2,1,0:T(8,128)(2,1)S(1)}, u32[]{:S(2)}, u32[]{:S(2)}) %collective-permute-start.11) | collective-permute-done | bytes 393248 | tf_op jit(solution)/shard_map/ppermute | solution.py:129
  315.6 11.5 %collective-permute-start.12 = (bf16[2,2,128,768]{3,2,0,1:T(8,128)(2,1)S(1)}, bf16[2,2,128,768]{3,2,0,1:T(8,128)(2,1)S(1)}, u32[]{:S(2)}, u32[]{:S(2)}) collective-permute-start(bf16[2,2,128,768]{3,2,0,1:T(8,128)(2,1)S(1)} %maximum_select_fusion.8), channel_id=1, source_target_pairs={{0,256},{16,272},{32,288},{48,304},{64,320},{80,336},{96,352},{112... | collective-permute-start | bytes 2359304 | tf_op jit(solution)/shard_map/ppermute | solution.py:129
  327.4 10.2 %collective-permute-done.12 = bf16[2,2,128,768]{3,2,0,1:T(8,128)(2,1)S(1)} collective-permute-done((bf16[2,2,128,768]{3,2,0,1:T(8,128)(2,1)S(1)}, bf16[2,2,128,768]{3,2,0,1:T(8,128)(2,1)S(1)}, u32[]{:S(2)}, u32[]{:S(2)}) %collective-permute-start.12) | collective-permute-done | bytes 786464 | tf_op jit(solution)/shard_map/ppermute | solution.py:129
  337.9 8.5 %collective-permute-start.13 = (bf16[2,2,2,128,768]{4,3,1,2,0:T(8,128)(2,1)S(1)}, bf16[2,2,2,128,768]{4,3,1,2,0:T(8,128)(2,1)S(1)}, u32[]{:S(2)}, u32[]{:S(2)}) collective-permute-start(bf16[2,2,2,128,768]{4,3,1,2,0:T(8,128)(2,1)S(1)} %maximum_select_fusion.5), channel_id=1, source_target_pairs={{0,128},{16,144},{32,160},{48,176},{64,192},{80,208},{96,224},{112... | collective-permute-start | bytes 4718600 | tf_op jit(solution)/shard_map/ppermute | solution.py:129
  346.7 31.8 %collective-permute-done.13 = bf16[2,2,2,128,768]{4,3,1,2,0:T(8,128)(2,1)S(1)} collective-permute-done((bf16[2,2,2,128,768]{4,3,1,2,0:T(8,128)(2,1)S(1)}, bf16[2,2,2,128,768]{4,3,1,2,0:T(8,128)(2,1)S(1)}, u32[]{:S(2)}, u32[]{:S(2)}) %collective-permute-start.13) | collective-permute-done | bytes 1572896 | tf_op jit(solution)/shard_map/ppermute | solution.py:129
  378.6 1.9 maximum_select_fusion.2
  380.4 2.1 collective-permute-start.14
  383.7 65.8 %collective-permute-done.14 = bf16[2,2,2,2,128,768]{5,4,2,3,0,1:T(8,128)(2,1)} collective-permute-done((bf16[2,2,2,2,128,768]{5,4,2,3,0,1:T(8,128)(2,1)}, bf16[2,2,2,2,128,768]{5,4,2,3,0,1:T(8,128)(2,1)}, u32[]{:S(2)}, u32[]{:S(2)}) %collective-permute-start.14) | collective-permute-done | bytes 3145760 | tf_op jit(solution)/shard_map/ppermute | solution.py:129
  449.5 4.0 maximum_select_fusion
  453.6 1.9 convolution_convert_fusion
  457.2 1.9 collective-permute-start.15
  459.1 2.8 collective-permute-done.15
  461.9 2.3 bitcast_add_fusion.1
  464.1 1.3 copy-done.6
  465.6 3.5 collective-permute-start.16
  469.1 12.4 %collective-permute-done.16 = bf16[2,2,256,256]{3,2,1,0:T(8,128)(2,1)S(1)} collective-permute-done((bf16[2,2,256,256]{3,2,1,0:T(8,128)(2,1)S(1)}, bf16[2,2,256,256]{3,2,1,0:T(8,128)(2,1)S(1)}, u32[]{:S(2)}, u32[]{:S(2)}) %collective-permute-start.16) | collective-permute-done | bytes 524320 | tf_op jit(solution)/shard_map/ppermute | solution.py:153
  481.4 1.7 bitcast_add_fusion.3
  483.2 5.1 collective-permute-start.17
  488.3 5.8 %collective-permute-done.17 = bf16[2,256,256]{2,1,0:T(8,128)(2,1)S(1)} collective-permute-done((bf16[2,256,256]{2,1,0:T(8,128)(2,1)S(1)}, bf16[2,256,256]{2,1,0:T(8,128)(2,1)S(1)}, u32[]{:S(2)}, u32[]{:S(2)}) %collective-permute-start.17) | collective-permute-done | bytes 262176 | tf_op jit(solution)/shard_map/ppermute | solution.py:153
  494.3 7.0 %collective-permute-start.18 = (bf16[256,256]{1,0:T(8,128)(2,1)S(1)}, bf16[256,256]{1,0:T(8,128)(2,1)S(1)}, u32[]{:S(2)}, u32[]{:S(2)}) collective-permute-start(bf16[256,256]{1,0:T(8,128)(2,1)S(1)} %fusion.18), channel_id=1, source_target_pairs={{0,2},{1,3},{2,0},{3,1},{4,6},{5,7},{6,4},{7,5},{8,10},{9,11},{10,... | collective-permute-start | bytes 393224 | tf_op jit(solution)/shard_map/ppermute | solution.py:153
  501.3 10.8 %collective-permute-done.18 = bf16[256,256]{1,0:T(8,128)(2,1)S(1)} collective-permute-done((bf16[256,256]{1,0:T(8,128)(2,1)S(1)}, bf16[256,256]{1,0:T(8,128)(2,1)S(1)}, u32[]{:S(2)}, u32[]{:S(2)}) %collective-permute-start.18) | collective-permute-done | bytes 131104 | tf_op jit(solution)/shard_map/ppermute | solution.py:153
  (64 shorter events, 13.2 us)
Async XLA Ops:
  0.0 85.6 %copy-start = (s32[32,32]{1,0:T(8,128)S(1)}, s32[32,32]{1,0:T(8,128)}, u32[]{:S(2)}) copy-start(s32[32,32]{1,0:T(8,128)} %param.14) | copy-start | bytes 12292
  1.7 21.0 %collective-permute-start = (bf16[128,512]{1,0:T(8,128)(2,1)S(1)}, bf16[128,512]{1,0:T(8,128)(2,1)S(1)}, u32[]{:S(2)}, u32[]{:S(2)}) collective-permute-start(bf16[128,512]{1,0:T(8,128)(2,1)S(1)} %constant_dynamic-update-slice_fusion), channel_id=1, source_target_pairs={{0,64},{16,80},{32,96},{48,112},{64,0},{80,16},{96,32},{112,48},{1... | collective-permute-start | bytes 393224 | tf_op jit(solution)/shard_map/ppermute | solution.py:129
  22.7 15.9 %collective-permute-start.1 = (bf16[2,128,512]{2,1,0:T(8,128)(2,1)S(1)}, bf16[2,128,512]{2,1,0:T(8,128)(2,1)S(1)}, u32[]{:S(2)}, u32[]{:S(2)}) collective-permute-start(bf16[2,128,512]{2,1,0:T(8,128)(2,1)S(1)} %maximum_select_fusion.13), channel_id=1, source_target_pairs={{0,32},{16,48},{32,0},{48,16},{64,96},{80,112},{96,64},{112,80},{1... | collective-permute-start | bytes 786440 | tf_op jit(solution)/shard_map/ppermute | solution.py:129
  38.7 16.6 %collective-permute-start.2 = (bf16[2,2,128,512]{3,2,1,0:T(8,128)(2,1)S(1)}, bf16[2,2,128,512]{3,2,1,0:T(8,128)(2,1)S(1)}, u32[]{:S(2)}, u32[]{:S(2)}) collective-permute-start(bf16[2,2,128,512]{3,2,1,0:T(8,128)(2,1)S(1)} %maximum_select_fusion.10), channel_id=1, source_target_pairs={{0,256},{16,272},{32,288},{48,304},{64,320},{80,336},{96,352},{112... | collective-permute-start | bytes 1572872 | tf_op jit(solution)/shard_map/ppermute | solution.py:129
  56.4 25.6 %collective-permute-start.3 = (bf16[2,2,2,128,512]{4,3,2,1,0:T(8,128)(2,1)}, bf16[2,2,2,128,512]{4,3,2,1,0:T(8,128)(2,1)S(1)}, u32[]{:S(2)}, u32[]{:S(2)}) collective-permute-start(bf16[2,2,2,128,512]{4,3,2,1,0:T(8,128)(2,1)} %maximum_select_fusion.7), channel_id=1, source_target_pairs={{0,128},{16,144},{32,160},{48,176},{64,192},{80,208},{96,224},{112... | collective-permute-start | bytes 3145736 | tf_op jit(solution)/shard_map/ppermute | solution.py:129
  83.7 47.2 %collective-permute-start.4 = (bf16[2,2,2,2,128,512]{5,4,3,2,1,0:T(8,128)(2,1)}, bf16[2,2,2,2,128,512]{5,4,3,2,1,0:T(8,128)(2,1)}, u32[]{:S(2)}, u32[]{:S(2)}) collective-permute-start(bf16[2,2,2,2,128,512]{5,4,3,2,1,0:T(8,128)(2,1)} %maximum_select_fusion.4), channel_id=1, source_target_pairs={{0,16},{16,0},{32,48},{48,32},{64,80},{80,64},{96,112},{112,96},{1... | collective-permute-start | bytes 6291464 | tf_op jit(solution)/shard_map/ppermute | solution.py:129
  134.2 0.8 copy-start.2
  134.2 0.9 copy-start.3
  134.2 0.9 copy-start.4
  172.2 46.0 %collective-permute-start.5 = (bf16[2,2,2,2,128,512]{5,4,2,3,0,1:T(8,128)(2,1)S(1)}, bf16[2,2,2,2,128,512]{5,4,2,3,0,1:T(8,128)(2,1)S(1)}, u32[]{:S(2)}, u32[]{:S(2)}) collective-permute-start(bf16[2,2,2,2,128,512]{5,4,2,3,0,1:T(8,128)(2,1)S(1)} %fusion.1), channel_id=1, source_target_pairs={{0,16},{16,0},{32,48},{48,32},{64,80},{80,64},{96,112},{112,96},{1... | collective-permute-start | bytes 6291464 | tf_op jit(solution)/shard_map/ppermute | solution.py:153
  219.7 22.6 %collective-permute-start.6 = (bf16[2,2,2,128,512]{4,3,1,2,0:T(8,128)(2,1)S(1)}, bf16[2,2,2,128,512]{4,3,1,2,0:T(8,128)(2,1)S(1)}, u32[]{:S(2)}, u32[]{:S(2)}) collective-permute-start(bf16[2,2,2,128,512]{4,3,1,2,0:T(8,128)(2,1)S(1)} %fusion.3), channel_id=1, source_target_pairs={{0,128},{16,144},{32,160},{48,176},{64,192},{80,208},{96,224},{112... | collective-permute-start | bytes 3145736 | tf_op jit(solution)/shard_map/ppermute | solution.py:153
  243.0 13.5 %collective-permute-start.7 = (bf16[2,2,128,512]{3,2,0,1:T(8,128)(2,1)S(1)}, bf16[2,2,128,512]{3,2,0,1:T(8,128)(2,1)S(1)}, u32[]{:S(2)}, u32[]{:S(2)}) collective-permute-start(bf16[2,2,128,512]{3,2,0,1:T(8,128)(2,1)S(1)} %fusion.5), channel_id=1, source_target_pairs={{0,256},{16,272},{32,288},{48,304},{64,320},{80,336},{96,352},{112... | collective-permute-start | bytes 1572872 | tf_op jit(solution)/shard_map/ppermute | solution.py:153
  256.8 15.3 %collective-permute-start.8 = (bf16[2,128,512]{2,1,0:T(8,128)(2,1)S(1)}, bf16[2,128,512]{2,1,0:T(8,128)(2,1)S(1)}, u32[]{:S(2)}, u32[]{:S(2)}) collective-permute-start(bf16[2,128,512]{2,1,0:T(8,128)(2,1)S(1)} %fusion.13), channel_id=1, source_target_pairs={{0,32},{16,48},{32,0},{48,16},{64,96},{80,112},{96,64},{112,80},{1... | collective-permute-start | bytes 786440 | tf_op jit(solution)/shard_map/ppermute | solution.py:153
  272.3 11.8 %collective-permute-start.9 = (bf16[128,512]{1,0:T(8,128)(2,1)S(1)}, bf16[128,512]{1,0:T(8,128)(2,1)S(1)}, u32[]{:S(2)}, u32[]{:S(2)}) collective-permute-start(bf16[128,512]{1,0:T(8,128)(2,1)S(1)} %fusion.17), channel_id=1, source_target_pairs={{0,64},{16,80},{32,96},{48,112},{64,0},{80,16},{96,32},{112,48},{1... | collective-permute-start | bytes 393224 | tf_op jit(solution)/shard_map/ppermute | solution.py:153
  284.2 15.3 %collective-permute-start.10 = (bf16[128,768]{1,0:T(8,128)(2,1)S(1)}, bf16[128,768]{1,0:T(8,128)(2,1)S(1)}, u32[]{:S(2)}, u32[]{:S(2)}) collective-permute-start(bf16[128,768]{1,0:T(8,128)(2,1)S(1)} %get-tuple-element.21), channel_id=1, source_target_pairs={{0,64},{16,80},{32,96},{48,112},{64,0},{80,16},{96,32},{112,48},{1... | collective-permute-start | bytes 589832 | tf_op jit(solution)/shard_map/ppermute | solution.py:129
  299.6 15.9 %collective-permute-start.11 = (bf16[2,128,768]{2,1,0:T(8,128)(2,1)S(1)}, bf16[2,128,768]{2,1,0:T(8,128)(2,1)S(1)}, u32[]{:S(2)}, u32[]{:S(2)}) collective-permute-start(bf16[2,128,768]{2,1,0:T(8,128)(2,1)S(1)} %maximum_select_fusion.11), channel_id=1, source_target_pairs={{0,32},{16,48},{32,0},{48,16},{64,96},{80,112},{96,64},{112,80},{1... | collective-permute-start | bytes 1179656 | tf_op jit(solution)/shard_map/ppermute | solution.py:129
  315.6 22.1 %collective-permute-start.12 = (bf16[2,2,128,768]{3,2,0,1:T(8,128)(2,1)S(1)}, bf16[2,2,128,768]{3,2,0,1:T(8,128)(2,1)S(1)}, u32[]{:S(2)}, u32[]{:S(2)}) collective-permute-start(bf16[2,2,128,768]{3,2,0,1:T(8,128)(2,1)S(1)} %maximum_select_fusion.8), channel_id=1, source_target_pairs={{0,256},{16,272},{32,288},{48,304},{64,320},{80,336},{96,352},{112... | collective-permute-start | bytes 2359304 | tf_op jit(solution)/shard_map/ppermute | solution.py:129
  337.9 40.6 %collective-permute-start.13 = (bf16[2,2,2,128,768]{4,3,1,2,0:T(8,128)(2,1)S(1)}, bf16[2,2,2,128,768]{4,3,1,2,0:T(8,128)(2,1)S(1)}, u32[]{:S(2)}, u32[]{:S(2)}) collective-permute-start(bf16[2,2,2,128,768]{4,3,1,2,0:T(8,128)(2,1)S(1)} %maximum_select_fusion.5), channel_id=1, source_target_pairs={{0,128},{16,144},{32,160},{48,176},{64,192},{80,208},{96,224},{112... | collective-permute-start | bytes 4718600 | tf_op jit(solution)/shard_map/ppermute | solution.py:129
  380.4 69.1 %collective-permute-start.14 = (bf16[2,2,2,2,128,768]{5,4,2,3,0,1:T(8,128)(2,1)}, bf16[2,2,2,2,128,768]{5,4,2,3,0,1:T(8,128)(2,1)}, u32[]{:S(2)}, u32[]{:S(2)}) collective-permute-start(bf16[2,2,2,2,128,768]{5,4,2,3,0,1:T(8,128)(2,1)} %maximum_select_fusion.2), channel_id=1, source_target_pairs={{0,16},{16,0},{32,48},{48,32},{64,80},{80,64},{96,112},{112,96},{1... | collective-permute-start | bytes 9437192 | tf_op jit(solution)/shard_map/ppermute | solution.py:129
  449.5 4.0 copy-start.7
  449.5 4.0 copy-start.8
  449.5 4.0 copy-start.9
  455.8 1.3 copy-start.5
  457.2 4.7 collective-permute-start.15
  464.1 1.3 copy-start.6
  465.6 15.9 %collective-permute-start.16 = (bf16[2,2,256,256]{3,2,1,0:T(8,128)(2,1)S(1)}, bf16[2,2,256,256]{3,2,1,0:T(8,128)(2,1)S(1)}, u32[]{:S(2)}, u32[]{:S(2)}) collective-permute-start(bf16[2,2,256,256]{3,2,1,0:T(8,128)(2,1)S(1)} %fusion.6), channel_id=1, source_target_pairs={{0,4},{1,5},{2,6},{3,7},{4,0},{5,1},{6,2},{7,3},{8,12},{9,13},{10,... | collective-permute-start | bytes 1572872 | tf_op jit(solution)/shard_map/ppermute | solution.py:153
  481.4 31.4 %copy-start.1 = (s32[32,32]{1,0:T(8,128)S(1)}, s32[32,32]{1,0:T(8,128)}, u32[]{:S(2)}) copy-start(s32[32,32]{1,0:T(8,128)} %param.14) | copy-start | bytes 12292
  483.2 10.9 %collective-permute-start.17 = (bf16[2,256,256]{2,1,0:T(8,128)(2,1)S(1)}, bf16[2,256,256]{2,1,0:T(8,128)(2,1)S(1)}, u32[]{:S(2)}, u32[]{:S(2)}) collective-permute-start(bf16[2,256,256]{2,1,0:T(8,128)(2,1)S(1)} %fusion.14), channel_id=1, source_target_pairs={{0,8},{1,9},{2,10},{3,11},{4,12},{5,13},{6,14},{7,15},{8,0},{9,1},... | collective-permute-start | bytes 786440 | tf_op jit(solution)/shard_map/ppermute | solution.py:153
  494.3 17.8 %collective-permute-start.18 = (bf16[256,256]{1,0:T(8,128)(2,1)S(1)}, bf16[256,256]{1,0:T(8,128)(2,1)S(1)}, u32[]{:S(2)}, u32[]{:S(2)}) collective-permute-start(bf16[256,256]{1,0:T(8,128)(2,1)S(1)} %fusion.18), channel_id=1, source_target_pairs={{0,2},{1,3},{2,0},{3,1},{4,6},{5,7},{6,4},{7,5},{8,10},{9,11},{10,... | collective-permute-start | bytes 393224 | tf_op jit(solution)/shard_map/ppermute | solution.py:153

commit v4 on v3

--- a/solution.py
+++ b/solution.py
@@ -13,8 +13,8 @@
 
 
 NEG_FILL = -1e30
-GATHER_ORDER = (4, 2, 16, 8, 1)
-SCATTER_ORDER = (1, 8, 16, 2, 4)
+GATHER_ORDERS = ((4, 2, 16, 8, 1), (4, 2, 16, 1, 8))
+SCATTER_ORDERS = ((1, 8, 16, 2, 4), (8, 1, 16, 2, 4))
 TP_ORDER = (1, 4, 8, 2)
 
 
@@ -121,18 +121,62 @@
     )(row_map, queries, output_grad, attn_output, full_keys, full_values)
 
 
-def tree_gather(x, axis, order):
-    me = lax.axis_index(axis)
-    count = lax.axis_size(axis)
+def _pair_permute(value, distances):
+    ctx_count, tp_count = lax.axis_size("ctx"), lax.axis_size("tp")
+    pairs = [
+        (c * tp_count + t, (c ^ distances[t % 2]) * tp_count + t)
+        for c in range(ctx_count)
+        for t in range(tp_count)
+    ]
+    return lax.ppermute(value, ("ctx", "tp"), pairs)
+
+
+def core_tree_gather(x, orders):
+    me = lax.axis_index("ctx")
+    core = lax.axis_index("tp") % 2
+    count = lax.axis_size("ctx")
     held = x
-    for distance in order:
-        other = lax.ppermute(held, axis, [(i, i ^ distance) for i in range(count)])
-        low = (me & distance) == 0
+    for distances in zip(*orders):
+        other = _pair_permute(held, distances)
+        mine = jnp.where(core == 0, distances[0], distances[1])
+        low = (me & mine) == 0
         held = jnp.where(low, jnp.stack([held, other]), jnp.stack([other, held]))
-    bits = list(reversed(order))
-    perm = sorted(range(len(bits)), key=lambda k: -bits[k])
-    held = jnp.transpose(held, perm + list(range(len(bits), held.ndim)))
-    return held.reshape((count * x.shape[0],) + x.shape[1:])
+    results = []
+    for order in orders:
+        bits = list(reversed(order))
+        perm = sorted(range(len(bits)), key=lambda k: -bits[k])
+        results.append(
+            jnp.transpose(held, perm + list(range(len(bits), held.ndim))).reshape(
+                (count * x.shape[0],) + x.shape[1:]
+            )
+        )
+    if tuple(orders[0]) == tuple(orders[1]):
+        return results[0]
+    return jnp.where(core == 0, results[0], results[1])
+
+
+def core_tree_reduce_scatter(x, orders, wire=jnp.bfloat16):
+    me = lax.axis_index("ctx")
+    core = lax.axis_index("tp") % 2
+    count = lax.axis_size("ctx")
+    levels = count.bit_length() - 1
+    block = x.shape[0] // count
+    held = x.astype(jnp.float32).reshape((2,) * levels + (block,) + x.shape[1:])
+    bits = [[1 << (levels - 1 - k) for k in range(levels)] for _ in orders]
+    for distances in zip(*orders):
+        keeps, sends = [], []
+        for k, distance in enumerate(distances):
+            dim = bits[k].index(distance)
+            bits[k].pop(dim)
+            zero = lax.index_in_dim(held, 0, dim, keepdims=False)
+            one = lax.index_in_dim(held, 1, dim, keepdims=False)
+            low = (me & distance) == 0
+            keeps.append(jnp.where(low, zero, one))
+            sends.append(jnp.where(low, one, zero))
+        keep = jnp.where(core == 0, keeps[0], keeps[1])
+        send = jnp.where(core == 0, sends[0], sends[1]).astype(wire)
+        held = keep + _pair_permute(send, distances).astype(jnp.float32)
+    return held.reshape((block,) + x.shape[1:])
 
 
 def tree_reduce_scatter(x, axis, order, wire=jnp.bfloat16):
@@ -163,15 +207,15 @@
         block_map, lax.axis_index("ctx") * slab_rows // BLK, axis=0, keepdims=False
     )
     key_value = jnp.concatenate([key_states, value_states], axis=1)
-    gathered = tree_gather(key_value, "ctx", GATHER_ORDER)
+    gathered = core_tree_gather(key_value, GATHER_ORDERS)
     full_keys, full_values = gathered[:, :width], gathered[:, width:]
     dq_total, part_grads = slab_attention(
         row_map, queries, output_grad, attn_output, full_keys, full_values
     )
     local_grads = dq_total.astype(jnp.bfloat16)
-    finished = tree_reduce_scatter(part_grads, "ctx", SCATTER_ORDER).astype(jnp.bfloat16)
+    finished = core_tree_reduce_scatter(part_grads, SCATTER_ORDERS).astype(jnp.bfloat16)
     own_grads = jnp.concatenate([local_grads, finished], axis=1)
-    gradients = tree_gather(own_grads, "ctx", GATHER_ORDER)
+    gradients = core_tree_gather(own_grads, GATHER_ORDERS)
     projections = jnp.concatenate([w_query, w_key, w_value], axis=1)
     term = lax.dot_general(
         gradients, projections, (((1,), (1,)), ((), ())), preferred_element_type=jnp.float32

time: 521 us -> 436 us (0.84)
  waiting for transfers between devices: 360 us -> 279 us
  Pallas kernels: 33.4 us -> 22.9 us
  other arithmetic: 23.2 us -> 31.8 us
  starting transfers between devices: 84.7 us -> 77.9 us
    ppermute x9 -> x4, waiting for transfers between devices: 120 us -> 35.7 us  [tree_reduce_scatter(): other = lax.ppermute(send, axis, [(i, i ^ distance) for i in range(count)])]
    ppermute x9 -> x4, starting transfers between devices: 38.6 us -> 14 us  [tree_reduce_scatter(): other = lax.ppermute(send, axis, [(i, i ^ distance) for i in range(count)])]
    ppermute x10 -> x15, starting transfers between devices: 46.1 us -> 63.9 us  [_pair_permute(): return lax.ppermute(value, ('ctx', 'tp'), pairs)]
    pallas_call x1, Pallas kernels: 33.4 us -> 22.9 us  [slab_attention(): pl.pallas_call(functools.partial(attention_kernel, head_count, block_coun...]
    slice x0 -> x3, local copies, waits for them, and re-layouts: none -> 7.25 us  [the longest x2 6.65 us: core_tree_reduce_scatter(): zero = lax.index_in_dim(held, 0, dim, keepdims=False)]
    add x0 -> x4, other arithmetic: none -> 5.94 us  [core_tree_reduce_scatter(): held = keep + _pair_permute(send, distances).astype(jnp.float32)]
    ppermute x10 -> x15, waiting for transfers between devices: 240 us -> 243 us  [_pair_permute(): return lax.ppermute(value, ('ctx', 'tp'), pairs)]
    select_n x17 -> x19, other arithmetic: 10.5 us -> 12.4 us  [the longest x17 9.52 us: core_tree_gather(): held = jnp.where(low, jnp.stack([held, other]), jnp.stack([other, held]))]
where the time goes in v4:
time: 436 us; the launch traced here: 427 us
  waiting for transfers between devices  279 us (64%)
  starting transfers between devices  77.9 us (18%)
  other arithmetic  31.8 us (7%)
  Pallas kernels  22.9 us (5%)
  local copies, waits for them, and re-layouts  13.1 us (3%)
    ppermute x15, waiting for transfers between devices, _pair_permute(): return lax.ppermute(value, ('ctx', 'tp'), pairs)  243 us
    ppermute x15, starting transfers between devices, _pair_permute(): return lax.ppermute(value, ('ctx', 'tp'), pairs)  63.9 us
    ppermute x4, waiting for transfers between devices, tree_reduce_scatter(): other = lax.ppermute(send, axis, [(i, i ^ distance) for i in range(count)])  35.7 us
    pallas_call x1, Pallas kernels, slab_attention(): pl.pallas_call(functools.partial(attention_kernel, head_count, block_coun...  22.9 us
    ppermute x4, starting transfers between devices, tree_reduce_scatter(): other = lax.ppermute(send, axis, [(i, i ^ distance) for i in range(count)])  14 us
    select_n x17, other arithmetic, core_tree_gather(): held = jnp.where(low, jnp.stack([held, other]), jnp.stack([other, held]))  9.52 us
  transfers between devices with their start and end apart: 19, of which 19 were waited for; matrix products, arithmetic and copies ran while one was open for 1% of the time, Pallas kernels for 0%

profile of v4, /device:TPU:6, one launch (start us, length us, event | category | flops | bytes accessed | tf_op | source)
XLA Modules:
  0.0 427.3 jit_solution(12217377029854958220)
XLA Ops:
  1.7 9.1 %collective-permute-start = (bf16[128,512]{1,0:T(8,128)(2,1)S(1)}, bf16[128,512]{1,0:T(8,128)(2,1)S(1)}, u32[]{:S(2)}, u32[]{:S(2)}) collective-permute-start(bf16[128,512]{1,0:T(8,128)(2,1)S(1)} %constant_dynamic-update-slice_fusion), channel_id=1, source_target_pairs={{0,64},{1,65},{2,66},{3,67},{4,68},{5,69},{6,70},{7,71},{8,72},{9,... | collective-permute-start | bytes 393224 | tf_op jit(solution)/shard_map/ppermute | solution.py:131
  10.8 11.9 %collective-permute-done = bf16[128,512]{1,0:T(8,128)(2,1)S(1)} collective-permute-done((bf16[128,512]{1,0:T(8,128)(2,1)S(1)}, bf16[128,512]{1,0:T(8,128)(2,1)S(1)}, u32[]{:S(2)}, u32[]{:S(2)}) %collective-permute-start) | collective-permute-done | bytes 131104 | tf_op jit(solution)/shard_map/ppermute | solution.py:131
  22.7 1.9 collective-permute-start.1
  24.7 13.9 %collective-permute-done.1 = bf16[2,128,512]{2,1,0:T(8,128)(2,1)S(1)} collective-permute-done((bf16[2,128,512]{2,1,0:T(8,128)(2,1)S(1)}, bf16[2,128,512]{2,1,0:T(8,128)(2,1)S(1)}, u32[]{:S(2)}, u32[]{:S(2)}) %collective-permute-start.1) | collective-permute-done | bytes 262176 | tf_op jit(solution)/shard_map/ppermute | solution.py:131
  38.7 3.3 collective-permute-start.2
  42.2 13.1 %collective-permute-done.2 = bf16[2,2,128,512]{3,2,1,0:T(8,128)(2,1)S(1)} collective-permute-done((bf16[2,2,128,512]{3,2,1,0:T(8,128)(2,1)S(1)}, bf16[2,2,128,512]{3,2,1,0:T(8,128)(2,1)S(1)}, u32[]{:S(2)}, u32[]{:S(2)}) %collective-permute-start.2) | collective-permute-done | bytes 524320 | tf_op jit(solution)/shard_map/ppermute | solution.py:131
  56.4 2.7 collective-permute-start.3
  59.5 13.9 %collective-permute-done.3 = bf16[2,2,2,128,512]{4,3,2,1,0:T(8,128)(2,1)S(1)} collective-permute-done((bf16[2,2,2,128,512]{4,3,2,1,0:T(8,128)(2,1)}, bf16[2,2,2,128,512]{4,3,2,1,0:T(8,128)(2,1)S(1)}, u32[]{:S(2)}, u32[]{:S(2)}) %collective-permute-start.3) | collective-permute-done | bytes 1048608 | tf_op jit(solution)/shard_map/ppermute | solution.py:131
  75.0 1.9 collective-permute-start.4
  77.5 25.7 %collective-permute-done.4 = bf16[2,2,2,2,128,512]{5,4,3,2,1,0:T(8,128)(2,1)} collective-permute-done((bf16[2,2,2,2,128,512]{5,4,3,2,1,0:T(8,128)(2,1)}, bf16[2,2,2,2,128,512]{5,4,3,2,1,0:T(8,128)(2,1)}, u32[]{:S(2)}, u32[]{:S(2)}) %collective-permute-start.4) | collective-permute-done | bytes 2097184 | tf_op jit(solution)/shard_map/ppermute | solution.py:131
  103.2 2.8 maximum_select_fusion.1
  107.6 22.9 %shard_map.91 = (f32[128,256]{1,0:T(8,128)S(1)}, bf16[4096,512]{1,0:T(8,128)(2,1)}) custom-call(s32[32]{0:T(128)S(1)} %dynamic-slice_bitcast_fusion.row_map, bf16[128,256]{1,0:T(8,128)(2,1)S(1)} %copy-done.2, bf16[128,256]{1,0:T(8,128)(2,1)S(1)} %copy-done.3, bf16[128,256]{1,0:T(8,128)(2,1)S(1)} %copy-done.4, bf16[4096,256]{1,0:T(8,128)(2,1)S(1)} %get-tuple-element.16.k_ref, ...), custom_call_target="tpu_custom_call" | custom-call | flops 1610612736 | bytes 8388608 | tf_op jit(solution)/shard_map/pallas_call | solution.py:102
  130.5 3.5 fusion.26
  134.1 3.1 fusion.25
  137.2 4.3 %fusion = bf16[2,2,2,2,128,512]{5,4,2,3,0,1:T(8,128)(2,1)} fusion(f32[2,1,2,2,2,128,512]{6,5,4,3,2,1,0:T(8,128)S(1)} %get-tuple-element.14, f32[2,1,2,2,2,128,512]{6,5,4,3,2,1,0:T(8,128)S(1)} %get-tuple-element.13, f32[2,2,2,2,1,128,512]{6,5,4,3,2,1,0:T(8,128)} %get-tuple-element.12, f32[2,2,2,2,1,128,512]{6,5,4,3,2,1,0:T(8,128)S(1)} %get-tuple-element.11, ...), kind=kLoop, calls=%fused_computation.5 | loop fusion | flops 3145728 | bytes 18874372 | tf_op jit(solution)/shard_map/convert_element_type | solution.py:177
  141.5 1.9 collective-permute-start.5
  143.4 26.2 %collective-permute-done.5 = bf16[2,2,2,2,128,512]{5,4,2,3,0,1:T(8,128)(2,1)S(1)} collective-permute-done((bf16[2,2,2,2,128,512]{5,4,2,3,0,1:T(8,128)(2,1)}, bf16[2,2,2,2,128,512]{5,4,2,3,0,1:T(8,128)(2,1)S(1)}, u32[]{:S(2)}, u32[]{:S(2)}) %collective-permute-start.5) | collective-permute-done | bytes 2097184 | tf_op jit(solution)/shard_map/ppermute | solution.py:131
  169.6 4.4 %fusion.1 = f32[2,2,2,2,128,512]{5,4,2,3,0,1:T(8,128)S(1)} fusion(bf16[2,2,2,2,128,512]{5,4,2,3,0,1:T(8,128)(2,1)S(1)} %collective-permute-done.5, f32[2,1,2,2,2,128,512]{6,5,4,3,2,1,0:T(8,128)S(1)} %get-tuple-element.14, f32[2,1,2,2,2,128,512]{6,5,4,3,2,1,0:T(8,128)S(1)} %get-tuple-element.13, f32[2,2,2,2,1,128,512]{6,5,4,3,2,1,0:T(8,128)} %get-tuple-element.12, ...), kind=kLoop, calls=%fused_computation.7 | loop fusion | flops 5242880 | bytes 23068676 | tf_op jit(solution)/shard_map/add | solution.py:178
  175.0 10.1 %collective-permute-start.6 = (bf16[2,2,2,128,512]{4,3,1,2,0:T(8,128)(2,1)S(1)}, bf16[2,2,2,128,512]{4,3,1,2,0:T(8,128)(2,1)S(1)}, u32[]{:S(2)}, u32[]{:S(2)}) collective-permute-start(bf16[2,2,2,128,512]{4,3,1,2,0:T(8,128)(2,1)S(1)} %fusion.2), channel_id=1, source_target_pairs={{0,128},{1,17},{2,130},{3,19},{4,132},{5,21},{6,134},{7,23},{8,136... | collective-permute-start | bytes 3145736 | tf_op jit(solution)/shard_map/ppermute | solution.py:131
  185.1 12.8 %collective-permute-done.6 = bf16[2,2,2,128,512]{4,3,1,2,0:T(8,128)(2,1)S(1)} collective-permute-done((bf16[2,2,2,128,512]{4,3,1,2,0:T(8,128)(2,1)S(1)}, bf16[2,2,2,128,512]{4,3,1,2,0:T(8,128)(2,1)S(1)}, u32[]{:S(2)}, u32[]{:S(2)}) %collective-permute-start.6) | collective-permute-done | bytes 1048608 | tf_op jit(solution)/shard_map/ppermute | solution.py:131
  199.1 6.2 %collective-permute-start.7 = (bf16[2,2,128,512]{3,2,0,1:T(8,128)(2,1)S(1)}, bf16[2,2,128,512]{3,2,0,1:T(8,128)(2,1)S(1)}, u32[]{:S(2)}, u32[]{:S(2)}) collective-permute-start(bf16[2,2,128,512]{3,2,0,1:T(8,128)(2,1)S(1)} %fusion.7), channel_id=1, source_target_pairs={{0,256},{1,257},{2,258},{3,259},{4,260},{5,261},{6,262},{7,263},{8... | collective-permute-start | bytes 1572872 | tf_op jit(solution)/shard_map/ppermute | solution.py:131
  205.3 7.9 %collective-permute-done.7 = bf16[2,2,128,512]{3,2,0,1:T(8,128)(2,1)S(1)} collective-permute-done((bf16[2,2,128,512]{3,2,0,1:T(8,128)(2,1)S(1)}, bf16[2,2,128,512]{3,2,0,1:T(8,128)(2,1)S(1)}, u32[]{:S(2)}, u32[]{:S(2)}) %collective-permute-start.7) | collective-permute-done | bytes 524320 | tf_op jit(solution)/shard_map/ppermute | solution.py:131
  213.5 6.9 %collective-permute-start.8 = (bf16[2,128,512]{2,1,0:T(8,128)(2,1)S(1)}, bf16[2,128,512]{2,1,0:T(8,128)(2,1)S(1)}, u32[]{:S(2)}, u32[]{:S(2)}) collective-permute-start(bf16[2,128,512]{2,1,0:T(8,128)(2,1)S(1)} %fusion.15), channel_id=1, source_target_pairs={{0,32},{1,33},{2,34},{3,35},{4,36},{5,37},{6,38},{7,39},{8,40},{9,... | collective-permute-start | bytes 786440 | tf_op jit(solution)/shard_map/ppermute | solution.py:131
  220.4 7.8 %collective-permute-done.8 = bf16[2,128,512]{2,1,0:T(8,128)(2,1)S(1)} collective-permute-done((bf16[2,128,512]{2,1,0:T(8,128)(2,1)S(1)}, bf16[2,128,512]{2,1,0:T(8,128)(2,1)S(1)}, u32[]{:S(2)}, u32[]{:S(2)}) %collective-permute-start.8) | collective-permute-done | bytes 262176 | tf_op jit(solution)/shard_map/ppermute | solution.py:131
  228.3 5.3 %collective-permute-start.9 = (bf16[128,512]{1,0:T(8,128)(2,1)S(1)}, bf16[128,512]{1,0:T(8,128)(2,1)S(1)}, u32[]{:S(2)}, u32[]{:S(2)}) collective-permute-start(bf16[128,512]{1,0:T(8,128)(2,1)S(1)} %fusion.19), channel_id=1, source_target_pairs={{0,64},{1,65},{2,66},{3,67},{4,68},{5,69},{6,70},{7,71},{8,72},{9,... | collective-permute-start | bytes 393224 | tf_op jit(solution)/shard_map/ppermute | solution.py:131
  233.6 20.5 %collective-permute-done.9 = bf16[128,512]{1,0:T(8,128)(2,1)S(1)} collective-permute-done((bf16[128,512]{1,0:T(8,128)(2,1)S(1)}, bf16[128,512]{1,0:T(8,128)(2,1)S(1)}, u32[]{:S(2)}, u32[]{:S(2)}) %collective-permute-start.9) | collective-permute-done | bytes 131104 | tf_op jit(solution)/shard_map/ppermute | solution.py:131
  254.2 1.9 collective-permute-start.10
  256.1 10.7 %collective-permute-done.10 = bf16[128,768]{1,0:T(8,128)(2,1)S(1)} collective-permute-done((bf16[128,768]{1,0:T(8,128)(2,1)S(1)}, bf16[128,768]{1,0:T(8,128)(2,1)S(1)}, u32[]{:S(2)}, u32[]{:S(2)}) %collective-permute-start.10) | collective-permute-done | bytes 196640 | tf_op jit(solution)/shard_map/ppermute | solution.py:131
  266.9 1.9 collective-permute-start.11
  268.9 10.9 %collective-permute-done.11 = bf16[2,128,768]{2,1,0:T(8,128)(2,1)S(1)} collective-permute-done((bf16[2,128,768]{2,1,0:T(8,128)(2,1)S(1)}, bf16[2,128,768]{2,1,0:T(8,128)(2,1)S(1)}, u32[]{:S(2)}, u32[]{:S(2)}) %collective-permute-start.11) | collective-permute-done | bytes 393248 | tf_op jit(solution)/shard_map/ppermute | solution.py:131
  279.9 5.4 %collective-permute-start.12 = (bf16[2,2,128,768]{3,2,0,1:T(8,128)(2,1)S(1)}, bf16[2,2,128,768]{3,2,0,1:T(8,128)(2,1)S(1)}, u32[]{:S(2)}, u32[]{:S(2)}) collective-permute-start(bf16[2,2,128,768]{3,2,0,1:T(8,128)(2,1)S(1)} %maximum_select_fusion.8), channel_id=1, source_target_pairs={{0,256},{1,257},{2,258},{3,259},{4,260},{5,261},{6,262},{7,263},{8... | collective-permute-start | bytes 2359304 | tf_op jit(solution)/shard_map/ppermute | solution.py:131
  285.6 15.3 %collective-permute-done.12 = bf16[2,2,128,768]{3,2,0,1:T(8,128)(2,1)S(1)} collective-permute-done((bf16[2,2,128,768]{3,2,0,1:T(8,128)(2,1)S(1)}, bf16[2,2,128,768]{3,2,0,1:T(8,128)(2,1)S(1)}, u32[]{:S(2)}, u32[]{:S(2)}) %collective-permute-start.12) | collective-permute-done | bytes 786464 | tf_op jit(solution)/shard_map/ppermute | solution.py:131
  301.1 3.5 collective-permute-start.13
  304.9 18.5 %collective-permute-done.13 = bf16[2,2,2,128,768]{4,3,1,2,0:T(8,128)(2,1)S(1)} collective-permute-done((bf16[2,2,2,128,768]{4,3,1,2,0:T(8,128)(2,1)S(1)}, bf16[2,2,2,128,768]{4,3,1,2,0:T(8,128)(2,1)S(1)}, u32[]{:S(2)}, u32[]{:S(2)}) %collective-permute-start.13) | collective-permute-done | bytes 1572896 | tf_op jit(solution)/shard_map/ppermute | solution.py:131
  323.4 2.0 maximum_select_fusion.2
  327.5 2.2 fusion.30
  330.7 34.2 %collective-permute-done.14 = bf16[2,2,2,2,128,768]{5,4,0,2,3,1:T(8,128)(2,1)S(1)} collective-permute-done((bf16[2,2,2,2,128,768]{5,4,0,2,3,1:T(8,128)(2,1)}, bf16[2,2,2,2,128,768]{5,4,0,2,3,1:T(8,128)(2,1)S(1)}, u32[]{:S(2)}, u32[]{:S(2)}) %collective-permute-start.14) | collective-permute-done | bytes 3145760 | tf_op jit(solution)/shard_map/ppermute | solution.py:131
  364.9 2.5 bitcast_select_fusion
  367.5 2.0 convolution_convert_fusion
  371.2 1.9 collective-permute-start.15
  373.1 2.8 collective-permute-done.15
  375.8 2.3 bitcast_add_fusion
  379.6 1.9 collective-permute-start.16
  381.5 13.9 %collective-permute-done.16 = bf16[2,2,256,256]{3,2,1,0:T(8,128)(2,1)S(1)} collective-permute-done((bf16[2,2,256,256]{3,2,1,0:T(8,128)(2,1)S(1)}, bf16[2,2,256,256]{3,2,1,0:T(8,128)(2,1)S(1)}, u32[]{:S(2)}, u32[]{:S(2)}) %collective-permute-start.16) | collective-permute-done | bytes 524320 | tf_op jit(solution)/shard_map/ppermute | solution.py:197
  397.2 1.9 collective-permute-start.17
  399.1 9.0 %collective-permute-done.17 = bf16[2,256,256]{2,1,0:T(8,128)(2,1)S(1)} collective-permute-done((bf16[2,256,256]{2,1,0:T(8,128)(2,1)S(1)}, bf16[2,256,256]{2,1,0:T(8,128)(2,1)S(1)}, u32[]{:S(2)}, u32[]{:S(2)}) %collective-permute-start.17) | collective-permute-done | bytes 262176 | tf_op jit(solution)/shard_map/ppermute | solution.py:197
  408.3 8.3 %collective-permute-start.18 = (bf16[256,256]{1,0:T(8,128)(2,1)S(1)}, bf16[256,256]{1,0:T(8,128)(2,1)S(1)}, u32[]{:S(2)}, u32[]{:S(2)}) collective-permute-start(bf16[256,256]{1,0:T(8,128)(2,1)S(1)} %fusion.20), channel_id=1, source_target_pairs={{0,2},{1,3},{2,0},{3,1},{4,6},{5,7},{6,4},{7,5},{8,10},{9,11},{10,... | collective-permute-start | bytes 393224 | tf_op jit(solution)/shard_map/ppermute | solution.py:197
  416.5 10.0 %collective-permute-done.18 = bf16[256,256]{1,0:T(8,128)(2,1)S(1)} collective-permute-done((bf16[256,256]{1,0:T(8,128)(2,1)S(1)}, bf16[256,256]{1,0:T(8,128)(2,1)S(1)}, u32[]{:S(2)}, u32[]{:S(2)}) %collective-permute-start.18) | collective-permute-done | bytes 131104 | tf_op jit(solution)/shard_map/ppermute | solution.py:197
  (77 shorter events, 19.6 us)
Async XLA Ops:
  0.0 77.0 %copy-start = (s32[32,32]{1,0:T(8,128)S(1)}, s32[32,32]{1,0:T(8,128)}, u32[]{:S(2)}) copy-start(s32[32,32]{1,0:T(8,128)} %param.14) | copy-start | bytes 12292
  1.7 21.0 %collective-permute-start = (bf16[128,512]{1,0:T(8,128)(2,1)S(1)}, bf16[128,512]{1,0:T(8,128)(2,1)S(1)}, u32[]{:S(2)}, u32[]{:S(2)}) collective-permute-start(bf16[128,512]{1,0:T(8,128)(2,1)S(1)} %constant_dynamic-update-slice_fusion), channel_id=1, source_target_pairs={{0,64},{1,65},{2,66},{3,67},{4,68},{5,69},{6,70},{7,71},{8,72},{9,... | collective-permute-start | bytes 393224 | tf_op jit(solution)/shard_map/ppermute | solution.py:131
  22.7 15.9 %collective-permute-start.1 = (bf16[2,128,512]{2,1,0:T(8,128)(2,1)S(1)}, bf16[2,128,512]{2,1,0:T(8,128)(2,1)S(1)}, u32[]{:S(2)}, u32[]{:S(2)}) collective-permute-start(bf16[2,128,512]{2,1,0:T(8,128)(2,1)S(1)} %maximum_select_fusion.13), channel_id=1, source_target_pairs={{0,32},{1,33},{2,34},{3,35},{4,36},{5,37},{6,38},{7,39},{8,40},{9,... | collective-permute-start | bytes 786440 | tf_op jit(solution)/shard_map/ppermute | solution.py:131
  38.7 16.6 %collective-permute-start.2 = (bf16[2,2,128,512]{3,2,1,0:T(8,128)(2,1)S(1)}, bf16[2,2,128,512]{3,2,1,0:T(8,128)(2,1)S(1)}, u32[]{:S(2)}, u32[]{:S(2)}) collective-permute-start(bf16[2,2,128,512]{3,2,1,0:T(8,128)(2,1)S(1)} %maximum_select_fusion.10), channel_id=1, source_target_pairs={{0,256},{1,257},{2,258},{3,259},{4,260},{5,261},{6,262},{7,263},{8... | collective-permute-start | bytes 1572872 | tf_op jit(solution)/shard_map/ppermute | solution.py:131
  56.4 16.9 %collective-permute-start.3 = (bf16[2,2,2,128,512]{4,3,2,1,0:T(8,128)(2,1)}, bf16[2,2,2,128,512]{4,3,2,1,0:T(8,128)(2,1)S(1)}, u32[]{:S(2)}, u32[]{:S(2)}) collective-permute-start(bf16[2,2,2,128,512]{4,3,2,1,0:T(8,128)(2,1)} %maximum_select_fusion.7), channel_id=1, source_target_pairs={{0,128},{1,17},{2,130},{3,19},{4,132},{5,21},{6,134},{7,23},{8,136... | collective-permute-start | bytes 3145736 | tf_op jit(solution)/shard_map/ppermute | solution.py:131
  75.0 28.2 %collective-permute-start.4 = (bf16[2,2,2,2,128,512]{5,4,3,2,1,0:T(8,128)(2,1)}, bf16[2,2,2,2,128,512]{5,4,3,2,1,0:T(8,128)(2,1)}, u32[]{:S(2)}, u32[]{:S(2)}) collective-permute-start(bf16[2,2,2,2,128,512]{5,4,3,2,1,0:T(8,128)(2,1)} %maximum_select_fusion.4), channel_id=1, source_target_pairs={{0,16},{1,129},{2,18},{3,131},{4,20},{5,133},{6,22},{7,135},{8,24}... | collective-permute-start | bytes 6291464 | tf_op jit(solution)/shard_map/ppermute | solution.py:131
  106.7 0.8 copy-start.2
  106.7 0.9 copy-start.3
  106.7 0.9 copy-start.4
  130.5 3.5 copy-start.5
  141.5 28.1 %collective-permute-start.5 = (bf16[2,2,2,2,128,512]{5,4,2,3,0,1:T(8,128)(2,1)}, bf16[2,2,2,2,128,512]{5,4,2,3,0,1:T(8,128)(2,1)S(1)}, u32[]{:S(2)}, u32[]{:S(2)}) collective-permute-start(bf16[2,2,2,2,128,512]{5,4,2,3,0,1:T(8,128)(2,1)} %fusion), channel_id=1, source_target_pairs={{0,16},{1,129},{2,18},{3,131},{4,20},{5,133},{6,22},{7,135},{8,24}... | collective-permute-start | bytes 6291464 | tf_op jit(solution)/shard_map/ppermute | solution.py:131
  175.0 22.9 %collective-permute-start.6 = (bf16[2,2,2,128,512]{4,3,1,2,0:T(8,128)(2,1)S(1)}, bf16[2,2,2,128,512]{4,3,1,2,0:T(8,128)(2,1)S(1)}, u32[]{:S(2)}, u32[]{:S(2)}) collective-permute-start(bf16[2,2,2,128,512]{4,3,1,2,0:T(8,128)(2,1)S(1)} %fusion.2), channel_id=1, source_target_pairs={{0,128},{1,17},{2,130},{3,19},{4,132},{5,21},{6,134},{7,23},{8,136... | collective-permute-start | bytes 3145736 | tf_op jit(solution)/shard_map/ppermute | solution.py:131
  199.1 14.1 %collective-permute-start.7 = (bf16[2,2,128,512]{3,2,0,1:T(8,128)(2,1)S(1)}, bf16[2,2,128,512]{3,2,0,1:T(8,128)(2,1)S(1)}, u32[]{:S(2)}, u32[]{:S(2)}) collective-permute-start(bf16[2,2,128,512]{3,2,0,1:T(8,128)(2,1)S(1)} %fusion.7), channel_id=1, source_target_pairs={{0,256},{1,257},{2,258},{3,259},{4,260},{5,261},{6,262},{7,263},{8... | collective-permute-start | bytes 1572872 | tf_op jit(solution)/shard_map/ppermute | solution.py:131
  213.5 14.6 %collective-permute-start.8 = (bf16[2,128,512]{2,1,0:T(8,128)(2,1)S(1)}, bf16[2,128,512]{2,1,0:T(8,128)(2,1)S(1)}, u32[]{:S(2)}, u32[]{:S(2)}) collective-permute-start(bf16[2,128,512]{2,1,0:T(8,128)(2,1)S(1)} %fusion.15), channel_id=1, source_target_pairs={{0,32},{1,33},{2,34},{3,35},{4,36},{5,37},{6,38},{7,39},{8,40},{9,... | collective-permute-start | bytes 786440 | tf_op jit(solution)/shard_map/ppermute | solution.py:131
  228.3 25.8 %collective-permute-start.9 = (bf16[128,512]{1,0:T(8,128)(2,1)S(1)}, bf16[128,512]{1,0:T(8,128)(2,1)S(1)}, u32[]{:S(2)}, u32[]{:S(2)}) collective-permute-start(bf16[128,512]{1,0:T(8,128)(2,1)S(1)} %fusion.19), channel_id=1, source_target_pairs={{0,64},{1,65},{2,66},{3,67},{4,68},{5,69},{6,70},{7,71},{8,72},{9,... | collective-permute-start | bytes 393224 | tf_op jit(solution)/shard_map/ppermute | solution.py:131
  254.2 12.7 %collective-permute-start.10 = (bf16[128,768]{1,0:T(8,128)(2,1)S(1)}, bf16[128,768]{1,0:T(8,128)(2,1)S(1)}, u32[]{:S(2)}, u32[]{:S(2)}) collective-permute-start(bf16[128,768]{1,0:T(8,128)(2,1)S(1)} %get-tuple-element.25), channel_id=1, source_target_pairs={{0,64},{1,65},{2,66},{3,67},{4,68},{5,69},{6,70},{7,71},{8,72},{9,... | collective-permute-start | bytes 589832 | tf_op jit(solution)/shard_map/ppermute | solution.py:131
  266.9 12.8 %collective-permute-start.11 = (bf16[2,128,768]{2,1,0:T(8,128)(2,1)S(1)}, bf16[2,128,768]{2,1,0:T(8,128)(2,1)S(1)}, u32[]{:S(2)}, u32[]{:S(2)}) collective-permute-start(bf16[2,128,768]{2,1,0:T(8,128)(2,1)S(1)} %maximum_select_fusion.11), channel_id=1, source_target_pairs={{0,32},{1,33},{2,34},{3,35},{4,36},{5,37},{6,38},{7,39},{8,40},{9,... | collective-permute-start | bytes 1179656 | tf_op jit(solution)/shard_map/ppermute | solution.py:131
  279.9 21.0 %collective-permute-start.12 = (bf16[2,2,128,768]{3,2,0,1:T(8,128)(2,1)S(1)}, bf16[2,2,128,768]{3,2,0,1:T(8,128)(2,1)S(1)}, u32[]{:S(2)}, u32[]{:S(2)}) collective-permute-start(bf16[2,2,128,768]{3,2,0,1:T(8,128)(2,1)S(1)} %maximum_select_fusion.8), channel_id=1, source_target_pairs={{0,256},{1,257},{2,258},{3,259},{4,260},{5,261},{6,262},{7,263},{8... | collective-permute-start | bytes 2359304 | tf_op jit(solution)/shard_map/ppermute | solution.py:131
  285.6 19.3 %copy-start.8 = (bf16[1,2,2,128,768]{4,3,1,2,0:T(8,128)(2,1)}, bf16[1,2,2,128,768]{4,3,1,2,0:T(8,128)(2,1)S(1)}, u32[]{:S(2)}) copy-start(bf16[1,2,2,128,768]{4,3,1,2,0:T(8,128)(2,1)S(1)} %copy_select_fusion.1) | copy-start | bytes 2359300
  300.8 4.0 copy-start.9
  301.1 22.3 %collective-permute-start.13 = (bf16[2,2,2,128,768]{4,3,1,2,0:T(8,128)(2,1)S(1)}, bf16[2,2,2,128,768]{4,3,1,2,0:T(8,128)(2,1)S(1)}, u32[]{:S(2)}, u32[]{:S(2)}) collective-permute-start(bf16[2,2,2,128,768]{4,3,1,2,0:T(8,128)(2,1)S(1)} %maximum_select_fusion.5), channel_id=1, source_target_pairs={{0,128},{1,17},{2,130},{3,19},{4,132},{5,21},{6,134},{7,23},{8,136... | collective-permute-start | bytes 4718600 | tf_op jit(solution)/shard_map/ppermute | solution.py:131
  323.4 2.1 copy-start.10
  325.6 39.4 %collective-permute-start.14 = (bf16[2,2,2,2,128,768]{5,4,0,2,3,1:T(8,128)(2,1)}, bf16[2,2,2,2,128,768]{5,4,0,2,3,1:T(8,128)(2,1)S(1)}, u32[]{:S(2)}, u32[]{:S(2)}) collective-permute-start(bf16[2,2,2,2,128,768]{5,4,0,2,3,1:T(8,128)(2,1)} %maximum_select_fusion.2), channel_id=1, source_target_pairs={{0,16},{1,129},{2,18},{3,131},{4,20},{5,133},{6,22},{7,135},{8,24}... | collective-permute-start | bytes 9437192 | tf_op jit(solution)/shard_map/ppermute | solution.py:131
  327.5 2.4 copy-start.11
  364.9 2.5 copy-start.12
  364.9 2.5 copy-start.13
  364.9 2.5 copy-start.14
  369.8 1.4 copy-start.6
  371.2 4.7 %collective-permute-start.15 = (bf16[2,2,2,256,256]{4,3,2,0,1:T(8,128)(2,1)S(1)}, bf16[2,2,2,256,256]{4,3,2,0,1:T(8,128)(2,1)}, u32[]{:S(2)}, u32[]{:S(2)}) collective-permute-start(bf16[2,2,2,256,256]{4,3,2,0,1:T(8,128)(2,1)S(1)} %fusion.6), channel_id=1, source_target_pairs={{0,1},{1,0},{2,3},{3,2},{4,5},{5,4},{6,7},{7,6},{8,9},{9,8},{10,11... | collective-permute-start | bytes 3145736 | tf_op jit(solution)/shard_map/ppermute | solution.py:197
  378.1 1.4 copy-start.7
  379.6 15.9 %collective-permute-start.16 = (bf16[2,2,256,256]{3,2,1,0:T(8,128)(2,1)S(1)}, bf16[2,2,256,256]{3,2,1,0:T(8,128)(2,1)S(1)}, u32[]{:S(2)}, u32[]{:S(2)}) collective-permute-start(bf16[2,2,256,256]{3,2,1,0:T(8,128)(2,1)S(1)} %fusion.8), channel_id=1, source_target_pairs={{0,4},{1,5},{2,6},{3,7},{4,0},{5,1},{6,2},{7,3},{8,12},{9,13},{10,... | collective-permute-start | bytes 1572872 | tf_op jit(solution)/shard_map/ppermute | solution.py:197
  395.4 31.8 %copy-start.1 = (s32[32,32]{1,0:T(8,128)S(1)}, s32[32,32]{1,0:T(8,128)}, u32[]{:S(2)}) copy-start(s32[32,32]{1,0:T(8,128)} %param.14) | copy-start | bytes 12292
  397.2 10.9 %collective-permute-start.17 = (bf16[2,256,256]{2,1,0:T(8,128)(2,1)S(1)}, bf16[2,256,256]{2,1,0:T(8,128)(2,1)S(1)}, u32[]{:S(2)}, u32[]{:S(2)}) collective-permute-start(bf16[2,256,256]{2,1,0:T(8,128)(2,1)S(1)} %fusion.16), channel_id=1, source_target_pairs={{0,8},{1,9},{2,10},{3,11},{4,12},{5,13},{6,14},{7,15},{8,0},{9,1},... | collective-permute-start | bytes 786440 | tf_op jit(solution)/shard_map/ppermute | solution.py:197
  408.3 18.3 %collective-permute-start.18 = (bf16[256,256]{1,0:T(8,128)(2,1)S(1)}, bf16[256,256]{1,0:T(8,128)(2,1)S(1)}, u32[]{:S(2)}, u32[]{:S(2)}) collective-permute-start(bf16[256,256]{1,0:T(8,128)(2,1)S(1)} %fusion.20), channel_id=1, source_target_pairs={{0,2},{1,3},{2,0},{3,1},{4,6},{5,7},{6,4},{7,5},{8,10},{9,11},{10,... | collective-permute-start | bytes 393224 | tf_op jit(solution)/shard_map/ppermute | solution.py:197

commit v5 on v2

v5 whole, which is shorter than its diff:
```python
import functools
import math

import jax
import jax.numpy as jnp
from jax import lax
from jax.experimental import pallas as pl
from jax.experimental.pallas import tpu as pltpu
from jax.sharding import PartitionSpec as P

HD = 128
BLK = 128


NEG_FILL = -1e30
GATHER_ORDERS = ((4, 2, 16, 8, 1), (4, 2, 16, 1, 8))
SCATTER_ORDERS = ((1, 8, 16, 2, 4), (8, 1, 16, 2, 4))
TP_ORDER = (1, 4, 8, 2)


def _nt(a, b):
    return lax.dot_general(a, b, (((1,), (1,)), ((), ())), preferred_element_type=jnp.float32)


def _tn(a, b):
    return lax.dot_general(a, b, (((0,), (0,)), ((), ())), preferred_element_type=jnp.float32)


def attention_kernel(
    head_count, block_count, score_scale,
    tables, q_ref, do_ref, o_ref, kv_ref, dq_ref, dkdv_ref, m_ref, l_ref, dq_acc,
):
    width = head_count * HD
    for h in range(head_count):
        cols = slice(h * HD, (h + 1) * HD)
        m_ref[h] = jnp.full((BLK, 1), NEG_FILL, jnp.float32)
        l_ref[h] = jnp.zeros((BLK, 1), jnp.float32)
        dq_acc[:, cols] = jnp.zeros((BLK, HD), jnp.float32)

    def stat_body(j, carry):
        rows = pl.ds(pl.multiple_of(tables[1, j] * BLK, BLK), BLK)

        @pl.when(tables[0, j] > 0)
        def _():
            for h in range(head_count):
                cols = slice(h * HD, (h + 1) * HD)
                scores = _nt(q_ref[:, cols], kv_ref[rows, cols]) * score_scale
                old_max = m_ref[h]
                new_max = jnp.maximum(old_max, jnp.max(scores, axis=1, keepdims=True))
                kept = jnp.sum(jnp.exp(scores - new_max), axis=1, keepdims=True)
                l_ref[h] = l_ref[h] * jnp.exp(old_max - new_max) + kept
                m_ref[h] = new_max

        return carry

    lax.fori_loop(0, block_count, stat_body, 0)

    def back_body(j, carry):
        rows = pl.ds(pl.multiple_of(tables[1, j] * BLK, BLK), BLK)
        out_rows = pl.ds(pl.multiple_of(tables[2, j] * BLK, BLK), BLK)

        @pl.when(tables[0, j] > 0)
        def _():
            for h in range(head_count):
                cols = slice(h * HD, (h + 1) * HD)
                q_h = q_ref[:, cols]
                do_h = do_ref[:, cols]
                k_b = kv_ref[rows, cols]
                log_total = m_ref[h] + jnp.log(l_ref[h])
                row_delta = jnp.sum(
                    do_h.astype(jnp.float32) * o_ref[:, cols].astype(jnp.float32),
                    axis=1,
                    keepdims=True,
                )
                scores = _nt(q_h, k_b) * score_scale
                probs = jnp.exp(scores - log_total)
                dprobs = _nt(do_h, kv_ref[rows, pl.ds(width + h * HD, HD)])
                score_gradient = (probs * (dprobs - row_delta) * score_scale).astype(jnp.bfloat16)
                dv = _tn(probs.astype(jnp.bfloat16), do_h)
                dk = _tn(score_gradient, q_h)
                dkdv_ref[out_rows, cols] = dk.astype(jnp.bfloat16)
                dkdv_ref[out_rows, pl.ds(width + h * HD, HD)] = dv.astype(jnp.bfloat16)
                part = jnp.dot(score_gradient, k_b, preferred_element_type=jnp.float32)
                dq_acc[:, cols] += part.astype(jnp.bfloat16).astype(jnp.float32)

        @pl.when(tables[0, j] == 0)
        def _():
            dkdv_ref[out_rows, :] = jnp.zeros((BLK, 2 * width), jnp.bfloat16)

        return carry

    lax.fori_loop(0, block_count, back_body, 0)
    dq_ref[...] = dq_acc[...]


def slab_attention(tables, queries, output_grad, attn_output, key_value):
    slab_rows, width = queries.shape
    head_count = width // HD
    key_rows = key_value.shape[0]
    block_count = key_rows // BLK
    vmem = pl.BlockSpec(memory_space=pltpu.VMEM)
    flops = 2 * slab_rows * key_rows * width * 6
    return pl.pallas_call(
        functools.partial(attention_kernel, head_count, block_count, 1.0 / math.sqrt(HD)),
        out_shape=(
            jax.ShapeDtypeStruct((slab_rows, width), jnp.float32),
            jax.ShapeDtypeStruct((key_rows, 2 * width), jnp.bfloat16),
        ),
        in_specs=[pl.BlockSpec(memory_space=pltpu.SMEM)] + [vmem] * 4,
        out_specs=(vmem, vmem),
        scratch_shapes=[
            pltpu.VMEM((head_count, slab_rows, 1), jnp.float32),
            pltpu.VMEM((head_count, slab_rows, 1), jnp.float32),
            pltpu.VMEM((slab_rows, width), jnp.float32),
        ],
        compiler_params=pltpu.CompilerParams(vmem_limit_bytes=48 * 1024 * 1024),
        cost_estimate=pl.CostEstimate(
            flops=flops,
            transcendentals=2 * slab_rows * key_rows * head_count,
            bytes_accessed=key_rows * width * 2 * 4,
        ),
    )(tables, queries, output_grad, attn_output, key_value)


def _pair_permute(value, distances):
    ctx_count, tp_count = lax.axis_size("ctx"), lax.axis_size("tp")
    pairs = [
        (c * tp_count + t, (c ^ distances[t % 2]) * tp_count + t)
        for c in range(ctx_count)
        for t in range(tp_count)
    ]
    return lax.ppermute(value, ("ctx", "tp"), pairs)


def gather_positions(me, distances, count):
    offset = me ^ jnp.arange(count, dtype=jnp.int32)
    return sum(((offset & d) != 0).astype(jnp.int32) << r for r, d in enumerate(distances))


def scatter_positions(me, distances, count):
    offset = me ^ jnp.arange(count, dtype=jnp.int32)
    top = len(distances) - 1
    return sum(((offset & d) == 0).astype(jnp.int32) << (top - r) for r, d in enumerate(distances))


def per_core(core, tables):
    return jnp.where(core == 0, tables[0], tables[1])


def concat_gather(x, orders):
    held = x
    for distances in zip(*orders):
        held = jnp.concatenate([held, _pair_permute(held, distances)], axis=0)
    return held


def halving_reduce(x, orders, wire=jnp.bfloat16):
    held = x
    for distances in zip(*orders):
        half = held.shape[0] // 2
        sent = _pair_permute(held[:half].astype(wire), distances)
        held = held[half:].astype(jnp.float32) + sent.astype(jnp.float32)
    return held


def tp_halving_reduce(x, order, wire=jnp.bfloat16):
    count = lax.axis_size("tp")
    held = x
    for distance in order:
        half = held.shape[0] // 2
        sent = lax.ppermute(
            held[:half].astype(wire), "tp", [(i, i ^ distance) for i in range(count)]
        )
        held = held[half:].astype(jnp.float32) + sent.astype(jnp.float32)
    return held


def per_device(
    queries, key_states, value_states, attn_output, output_grad, block_map, w_query, w_key, w_value
):
    slab_rows, width = queries.shape
    ctx_count, tp_count = lax.axis_size("ctx"), lax.axis_size("tp")
    me = lax.axis_index("ctx")
    me_tp = lax.axis_index("tp")
    core = me_tp % 2
    row_map = lax.dynamic_index_in_dim(block_map, me * slab_rows // BLK, axis=0, keepdims=False)
    gather_at = per_core(core, [gather_positions(me, o, ctx_count) for o in GATHER_ORDERS])
    scatter_at = per_core(core, [scatter_positions(me, o, ctx_count) for o in SCATTER_ORDERS])
    tables = jnp.stack([row_map.astype(jnp.int32), gather_at, scatter_at])
    key_value = jnp.concatenate([key_states, value_states], axis=1)
    gathered = concat_gather(key_value, GATHER_ORDERS)
    dq_total, part_grads = slab_attention(tables, queries, output_grad, attn_output, gathered)
    finished = halving_reduce(part_grads, SCATTER_ORDERS).astype(jnp.bfloat16)
    own_grads = jnp.concatenate([dq_total.astype(jnp.bfloat16), finished], axis=1)
    gradients = concat_gather(own_grads, GATHER_ORDERS)
    projections = jnp.concatenate([w_query, w_key, w_value], axis=1)
    term = lax.dot_general(
        gradients, projections, (((1,), (1,)), ((), ())), preferred_element_type=jnp.float32
    ).astype(jnp.bfloat16)
    tp_at = scatter_positions(me_tp, TP_ORDER, tp_count)
    owner = jnp.argsort(tp_at)
    per_owner = ctx_count // tp_count
    wanted = (owner[:, None] * per_owner + jnp.arange(per_owner)[None, :]).reshape(-1)
    source = gather_at[wanted]
    ordered = jnp.take(term.reshape(ctx_count, slab_rows, -1), source, axis=0)
    return tp_halving_reduce(ordered.reshape(ctx_count * slab_rows, -1), TP_ORDER).astype(
        jnp.bfloat16
    )


def solution(mesh):
    return jax.shard_map(
        per_device,
        mesh=mesh,
        in_specs=(
            P("ctx", "tp"),
            P("ctx", "tp"),
            P("ctx", "tp"),
            P("ctx", "tp"),
            P("ctx", "tp"),
            P(),
            P("ctx", "tp"),
            P("ctx", "tp"),
            P("ctx", "tp"),
        ),
        out_specs=P("tp", "ctx"),
        check_vma=False,
    )
```

time: 819 us -> 414 us (0.51)
  waiting for transfers between devices: 724 us -> 258 us
  starting transfers between devices: 46.7 us -> 99.3 us
  local copies, waits for them, and re-layouts: 5.02 us -> 22.1 us
  between operations: 13.5 us -> 0.45 us
    all_to_all x2 -> x0, waiting for transfers between devices: 350 us -> none  [the longest x1 175 us: per_device(): lax.all_to_all(spread, 'ctx', 0, 0, tiled=True)]
    ppermute x0 -> x19, waiting for transfers between devices: none -> 258 us  [the longest x15 233 us: _pair_permute(): return lax.ppermute(value, ('ctx', 'tp'), pairs)]
    all_gather x1 -> x0, waiting for transfers between devices: 237 us -> none  [per_device(): gradients = lax.all_gather(own_grads, 'ctx', axis=0, tiled=True)]
    reduce_scatter x1 -> x0, waiting for transfers between devices: 137 us -> none  [per_device(): lax.psum_scatter(lax.dot_general(gradients, projections, (((1,), (1,)), (...]
    ppermute x0 -> x19, starting transfers between devices: none -> 99.3 us  [the longest x15 70.3 us: _pair_permute(): return lax.ppermute(value, ('ctx', 'tp'), pairs)]
    all_to_all x2 -> x0, starting transfers between devices: 46.6 us -> none  [the longest x1 30.9 us: per_device(): lax.all_to_all(part_grads.reshape(context_count, slab_rows, part_width),...]
    unnamed x14 -> x28, local copies, waits for them, and re-layouts: 0.03 us -> 12.4 us
  transfers between devices with their start and end apart: 4 -> 19, of which waited for: 4 -> 19; matrix products, arithmetic and copies ran while one was open for 0% -> 2% of each run, Pallas kernels for 0% -> 0%
where the time goes in v5:
time: 414 us; the launch traced here: 409 us
  waiting for transfers between devices  258 us (62%)
  starting transfers between devices  99.3 us (24%)
  local copies, waits for them, and re-layouts  22.1 us (5%)
  Pallas kernels  18.1 us (4%)
  matrix products  6.01 us (1%)
  other arithmetic  5.06 us (1%)
    ppermute x15, waiting for transfers between devices, _pair_permute(): return lax.ppermute(value, ('ctx', 'tp'), pairs)  233 us
    ppermute x15, starting transfers between devices, _pair_permute(): return lax.ppermute(value, ('ctx', 'tp'), pairs)  70.3 us
    ppermute x4, starting transfers between devices, tp_halving_reduce(): lax.ppermute(held[:half].astype(wire), 'tp', [(i, i ^ distance) for i in...  29 us
    ppermute x4, waiting for transfers between devices, tp_halving_reduce(): lax.ppermute(held[:half].astype(wire), 'tp', [(i, i ^ distance) for i in...  25.1 us
    pallas_call x1, Pallas kernels, slab_attention(): pl.pallas_call(functools.partial(attention_kernel, head_count, block_coun...  18.1 us
    unnamed x28, local copies, waits for them, and re-layouts  12.4 us
  transfers between devices with their start and end apart: 19, of which 19 were waited for; matrix products, arithmetic and copies ran while one was open for 2% of the time, Pallas kernels for 0%

profile of v5, /device:TPU:6, one launch (start us, length us, event | category | flops | bytes accessed | tf_op | source)
XLA Modules:
  0.0 409.0 jit_solution(12958600788804210176)
XLA Ops:
  0.0 1.5 constant_dynamic-update-slice_fusion.7
  1.5 1.5 constant_dynamic-update-slice_fusion.6
  3.0 9.1 %collective-permute-start = (bf16[128,512]{1,0:T(8,128)(2,1)S(1)}, bf16[128,512]{1,0:T(8,128)(2,1)S(1)}, u32[]{:S(2)}, u32[]{:S(2)}) collective-permute-start(bf16[128,512]{1,0:T(8,128)(2,1)S(1)} %get-tuple-element.34), channel_id=1, source_target_pairs={{0,64},{1,65},{2,66},{3,67},{4,68},{5,69},{6,70},{7,71},{8,72},{9,... | collective-permute-start | bytes 393224 | tf_op jit(solution)/shard_map/ppermute | solution.py:132
  12.1 11.9 %collective-permute-done = bf16[128,512]{1,0:T(8,128)(2,1)S(1)} collective-permute-done((bf16[128,512]{1,0:T(8,128)(2,1)S(1)}, bf16[128,512]{1,0:T(8,128)(2,1)S(1)}, u32[]{:S(2)}, u32[]{:S(2)}) %collective-permute-start) | collective-permute-done | bytes 131104 | tf_op jit(solution)/shard_map/ppermute | solution.py:132
  24.0 1.9 collective-permute-start.1
  25.9 14.0 %collective-permute-done.1 = bf16[256,512]{1,0:T(8,128)(2,1)S(1)} collective-permute-done((bf16[256,512]{1,0:T(8,128)(2,1)S(1)}, bf16[256,512]{1,0:T(8,128)(2,1)S(1)}, u32[]{:S(2)}, u32[]{:S(2)}) %collective-permute-start.1) | collective-permute-done | bytes 262176 | tf_op jit(solution)/shard_map/ppermute | solution.py:132
  40.0 3.3 collective-permute-start.2
  43.3 13.2 %collective-permute-done.2 = bf16[512,512]{1,0:T(8,128)(2,1)S(1)} collective-permute-done((bf16[512,512]{1,0:T(8,128)(2,1)S(1)}, bf16[512,512]{1,0:T(8,128)(2,1)S(1)}, u32[]{:S(2)}, u32[]{:S(2)}) %collective-permute-start.2) | collective-permute-done | bytes 524320 | tf_op jit(solution)/shard_map/ppermute | solution.py:132
  56.6 2.7 collective-permute-start.3
  61.6 11.6 %collective-permute-done.3 = bf16[1024,512]{1,0:T(8,128)(2,1)S(1)} collective-permute-done((bf16[1024,512]{1,0:T(8,128)(2,1)S(1)}, bf16[1024,512]{1,0:T(8,128)(2,1)S(1)}, u32[]{:S(2)}, u32[]{:S(2)}) %collective-permute-start.3) | collective-permute-done | bytes 1048608 | tf_op jit(solution)/shard_map/ppermute | solution.py:132
  74.4 2.0 copy-done.6
  76.4 1.9 collective-permute-start.4
  78.4 26.1 %collective-permute-done.4 = bf16[2048,512]{1,0:T(8,128)(2,1)S(1)} collective-permute-done((bf16[2048,512]{1,0:T(8,128)(2,1)}, bf16[2048,512]{1,0:T(8,128)(2,1)S(1)}, u32[]{:S(2)}, u32[]{:S(2)}) %collective-permute-start.4) | collective-permute-done | bytes 2097184 | tf_op jit(solution)/shard_map/ppermute | solution.py:132
  104.5 1.5 constant_dynamic-update-slice_fusion.8.kv_ref
  106.0 18.1 %shard_map.91 = (f32[128,256]{1,0:T(8,128)S(1)}, bf16[4096,512]{1,0:T(8,128)(2,1)S(1)}) custom-call(s32[3,32]{1,0:T(4,128)S(1)} %pad_add_fusion.tables, bf16[128,256]{1,0:T(8,128)(2,1)S(1)} %copy-done.2, bf16[128,256]{1,0:T(8,128)(2,1)S(1)} %copy-done.3, bf16[128,256]{1,0:T(8,128)(2,1)S(1)} %copy-done.4, ...), custom_call_target="tpu_custom_call" | custom-call | flops 1610612736 | bytes 8388608 | tf_op jit(solution)/shard_map/pallas_call | solution.py:103
  124.2 1.9 collective-permute-start.5
  126.1 26.0 %collective-permute-done.5 = bf16[2048,512]{1,0:T(8,128)(2,1)S(1)} collective-permute-done((bf16[2048,512]{1,0:T(8,128)(2,1)S(1)}, bf16[2048,512]{1,0:T(8,128)(2,1)S(1)}, u32[]{:S(2)}, u32[]{:S(2)}) %collective-permute-start.5) | collective-permute-done | bytes 2097184 | tf_op jit(solution)/shard_map/ppermute | solution.py:132
  152.9 4.9 %collective-permute-start.6 = (bf16[1024,512]{1,0:T(8,128)(2,1)S(1)}, bf16[1024,512]{1,0:T(8,128)(2,1)S(1)}, u32[]{:S(2)}, u32[]{:S(2)}) collective-permute-start(bf16[1024,512]{1,0:T(8,128)(2,1)S(1)} %slice.123), channel_id=1, source_target_pairs={{0,128},{1,17},{2,130},{3,19},{4,132},{5,21},{6,134},{7,23},{8,136... | collective-permute-start | bytes 3145736 | tf_op jit(solution)/shard_map/ppermute | solution.py:132
  157.7 12.8 %collective-permute-done.6 = bf16[1024,512]{1,0:T(8,128)(2,1)S(1)} collective-permute-done((bf16[1024,512]{1,0:T(8,128)(2,1)S(1)}, bf16[1024,512]{1,0:T(8,128)(2,1)S(1)}, u32[]{:S(2)}, u32[]{:S(2)}) %collective-permute-start.6) | collective-permute-done | bytes 1048608 | tf_op jit(solution)/shard_map/ppermute | solution.py:132
  170.9 17.9 %collective-permute-start.7 = (bf16[512,512]{1,0:T(8,128)(2,1)S(1)}, bf16[512,512]{1,0:T(8,128)(2,1)S(1)}, u32[]{:S(2)}, u32[]{:S(2)}) collective-permute-start(bf16[512,512]{1,0:T(8,128)(2,1)S(1)} %slice.125), channel_id=1, source_target_pairs={{0,256},{1,257},{2,258},{3,259},{4,260},{5,261},{6,262},{7,263},{8... | collective-permute-start | bytes 1572872 | tf_op jit(solution)/shard_map/ppermute | solution.py:132
  188.8 8.2 %collective-permute-done.7 = bf16[512,512]{1,0:T(8,128)(2,1)S(1)} collective-permute-done((bf16[512,512]{1,0:T(8,128)(2,1)S(1)}, bf16[512,512]{1,0:T(8,128)(2,1)S(1)}, u32[]{:S(2)}, u32[]{:S(2)}) %collective-permute-start.7) | collective-permute-done | bytes 524320 | tf_op jit(solution)/shard_map/ppermute | solution.py:132
  197.2 2.0 collective-permute-start.8
  199.2 9.8 %collective-permute-done.8 = bf16[256,512]{1,0:T(8,128)(2,1)S(1)} collective-permute-done((bf16[256,512]{1,0:T(8,128)(2,1)S(1)}, bf16[256,512]{1,0:T(8,128)(2,1)S(1)}, u32[]{:S(2)}, u32[]{:S(2)}) %collective-permute-start.8) | collective-permute-done | bytes 262176 | tf_op jit(solution)/shard_map/ppermute | solution.py:132
  209.1 11.4 %collective-permute-start.9 = (bf16[128,512]{1,0:T(8,128)(2,1)S(1)}, bf16[128,512]{1,0:T(8,128)(2,1)S(1)}, u32[]{:S(2)}, u32[]{:S(2)}) collective-permute-start(bf16[128,512]{1,0:T(8,128)(2,1)S(1)} %slice.129), channel_id=1, source_target_pairs={{0,64},{1,65},{2,66},{3,67},{4,68},{5,69},{6,70},{7,71},{8,72},{9,... | collective-permute-start | bytes 393224 | tf_op jit(solution)/shard_map/ppermute | solution.py:132
  220.5 13.2 %collective-permute-done.9 = bf16[128,512]{1,0:T(8,128)(2,1)S(1)} collective-permute-done((bf16[128,512]{1,0:T(8,128)(2,1)S(1)}, bf16[128,512]{1,0:T(8,128)(2,1)S(1)}, u32[]{:S(2)}, u32[]{:S(2)}) %collective-permute-start.9) | collective-permute-done | bytes 131104 | tf_op jit(solution)/shard_map/ppermute | solution.py:132
  234.5 1.9 collective-permute-start.10
  236.4 9.7 %collective-permute-done.10 = bf16[128,768]{1,0:T(8,128)(2,1)S(1)} collective-permute-done((bf16[128,768]{1,0:T(8,128)(2,1)S(1)}, bf16[128,768]{1,0:T(8,128)(2,1)S(1)}, u32[]{:S(2)}, u32[]{:S(2)}) %collective-permute-start.10) | collective-permute-done | bytes 196640 | tf_op jit(solution)/shard_map/ppermute | solution.py:132
  246.2 1.9 collective-permute-start.11
  248.1 12.9 %collective-permute-done.11 = bf16[256,768]{1,0:T(8,128)(2,1)S(1)} collective-permute-done((bf16[256,768]{1,0:T(8,128)(2,1)S(1)}, bf16[256,768]{1,0:T(8,128)(2,1)S(1)}, u32[]{:S(2)}, u32[]{:S(2)}) %collective-permute-start.11) | collective-permute-done | bytes 393248 | tf_op jit(solution)/shard_map/ppermute | solution.py:132
  261.1 1.9 collective-permute-start.12
  263.0 13.5 %collective-permute-done.12 = bf16[512,768]{1,0:T(8,128)(2,1)S(1)} collective-permute-done((bf16[512,768]{1,0:T(8,128)(2,1)S(1)}, bf16[512,768]{1,0:T(8,128)(2,1)S(1)}, u32[]{:S(2)}, u32[]{:S(2)}) %collective-permute-start.12) | collective-permute-done | bytes 786464 | tf_op jit(solution)/shard_map/ppermute | solution.py:132
  276.6 4.5 %collective-permute-start.13 = (bf16[1024,768]{1,0:T(8,128)(2,1)S(1)}, bf16[1024,768]{1,0:T(8,128)(2,1)S(1)}, u32[]{:S(2)}, u32[]{:S(2)}) collective-permute-start(bf16[1024,768]{1,0:T(8,128)(2,1)S(1)} %pad_maximum_fusion), channel_id=1, source_target_pairs={{0,128},{1,17},{2,130},{3,19},{4,132},{5,21},{6,134},{7,23},{8,136... | collective-permute-start | bytes 4718600 | tf_op jit(solution)/shard_map/ppermute | solution.py:132
  283.6 15.8 %collective-permute-done.13 = bf16[1024,768]{1,0:T(8,128)(2,1)S(1)} collective-permute-done((bf16[1024,768]{1,0:T(8,128)(2,1)S(1)}, bf16[1024,768]{1,0:T(8,128)(2,1)S(1)}, u32[]{:S(2)}, u32[]{:S(2)}) %collective-permute-start.13) | collective-permute-done | bytes 1572896 | tf_op jit(solution)/shard_map/ppermute | solution.py:132
  299.5 1.4 constant_dynamic-update-slice_fusion.15
  300.9 2.6 copy-done.5
  303.5 3.0 collective-permute-start.14
  308.8 34.1 %collective-permute-done.14 = bf16[2048,768]{1,0:T(8,128)(2,1)S(1)} collective-permute-done((bf16[2048,768]{1,0:T(8,128)(2,1)}, bf16[2048,768]{1,0:T(8,128)(2,1)S(1)}, u32[]{:S(2)}, u32[]{:S(2)}) %collective-permute-start.14) | collective-permute-done | bytes 3145760 | tf_op jit(solution)/shard_map/ppermute | solution.py:132
  342.9 1.9 constant_dynamic-update-slice_fusion.20
  344.8 6.0 %convolution_convert_fusion = bf16[4096,256]{1,0:T(8,128)(2,1)} fusion(bf16[4096,768]{1,0:T(8,128)(2,1)} %constant_dynamic-update-slice_fusion.20, bf16[256,256]{1,0:T(8,128)(2,1)S(1)} %copy-done.7, bf16[256,256]{1,0:T(8,128)(2,1)S(1)} %copy-done.8, bf16[256,256]{1,0:T(8,128)(2,1)S(1)} %copy-done.9), kind=kOutput, calls=%fused_computation.2 | convolution fusion | flops 1612840960 | bytes 8781824 | tf_op jit(solution)/shard_map/dot_general | solution.py:197
  350.8 2.3 gather_fusion.1
  353.6 1.9 collective-permute-start.15
  355.5 2.6 collective-permute-done.15
  358.5 3.5 collective-permute-start.16
  362.0 12.4 %collective-permute-done.16 = bf16[1024,256]{1,0:T(8,128)(2,1)S(1)} collective-permute-done((bf16[1024,256]{1,0:T(8,128)(2,1)S(1)}, bf16[1024,256]{1,0:T(8,128)(2,1)S(1)}, u32[]{:S(2)}, u32[]{:S(2)}) %collective-permute-start.16) | collective-permute-done | bytes 524320 | tf_op jit(solution)/shard_map/ppermute | solution.py:171
  374.5 5.1 %collective-permute-start.17 = (bf16[512,256]{1,0:T(8,128)(2,1)S(1)}, bf16[512,256]{1,0:T(8,128)(2,1)S(1)}, u32[]{:S(2)}, u32[]{:S(2)}) collective-permute-start(bf16[512,256]{1,0:T(8,128)(2,1)S(1)} %slice.126), channel_id=1, source_target_pairs={{0,8},{1,9},{2,10},{3,11},{4,12},{5,13},{6,14},{7,15},{8,0},{9,1},... | collective-permute-start | bytes 786440 | tf_op jit(solution)/shard_map/ppermute | solution.py:171
  379.7 5.8 %collective-permute-done.17 = bf16[512,256]{1,0:T(8,128)(2,1)S(1)} collective-permute-done((bf16[512,256]{1,0:T(8,128)(2,1)S(1)}, bf16[512,256]{1,0:T(8,128)(2,1)S(1)}, u32[]{:S(2)}, u32[]{:S(2)}) %collective-permute-start.17) | collective-permute-done | bytes 262176 | tf_op jit(solution)/shard_map/ppermute | solution.py:171
  385.5 18.4 %collective-permute-start.18 = (bf16[256,256]{1,0:T(8,128)(2,1)S(1)}, bf16[256,256]{1,0:T(8,128)(2,1)S(1)}, u32[]{:S(2)}, u32[]{:S(2)}) collective-permute-start(bf16[256,256]{1,0:T(8,128)(2,1)S(1)} %slice.128), channel_id=1, source_target_pairs={{0,2},{1,3},{2,0},{3,1},{4,6},{5,7},{6,4},{7,5},{8,10},{9,11},{10,... | collective-permute-start | bytes 393224 | tf_op jit(solution)/shard_map/ppermute | solution.py:171
  404.0 4.3 %collective-permute-done.18 = bf16[256,256]{1,0:T(8,128)(2,1)S(1)} collective-permute-done((bf16[256,256]{1,0:T(8,128)(2,1)S(1)}, bf16[256,256]{1,0:T(8,128)(2,1)S(1)}, u32[]{:S(2)}, u32[]{:S(2)}) %collective-permute-start.18) | collective-permute-done | bytes 131104 | tf_op jit(solution)/shard_map/ppermute | solution.py:171
  (68 shorter events, 12.5 us)
Async XLA Ops:
  0.0 78.3 %copy-start = (s32[32,32]{1,0:T(8,128)S(1)}, s32[32,32]{1,0:T(8,128)}, u32[]{:S(2)}) copy-start(s32[32,32]{1,0:T(8,128)} %param.14) | copy-start | bytes 12292
  3.0 21.0 %collective-permute-start = (bf16[128,512]{1,0:T(8,128)(2,1)S(1)}, bf16[128,512]{1,0:T(8,128)(2,1)S(1)}, u32[]{:S(2)}, u32[]{:S(2)}) collective-permute-start(bf16[128,512]{1,0:T(8,128)(2,1)S(1)} %get-tuple-element.34), channel_id=1, source_target_pairs={{0,64},{1,65},{2,66},{3,67},{4,68},{5,69},{6,70},{7,71},{8,72},{9,... | collective-permute-start | bytes 393224 | tf_op jit(solution)/shard_map/ppermute | solution.py:132
  24.0 15.9 %collective-permute-start.1 = (bf16[256,512]{1,0:T(8,128)(2,1)S(1)}, bf16[256,512]{1,0:T(8,128)(2,1)S(1)}, u32[]{:S(2)}, u32[]{:S(2)}) collective-permute-start(bf16[256,512]{1,0:T(8,128)(2,1)S(1)} %pad_maximum_fusion.5), channel_id=1, source_target_pairs={{0,32},{1,33},{2,34},{3,35},{4,36},{5,37},{6,38},{7,39},{8,40},{9,... | collective-permute-start | bytes 786440 | tf_op jit(solution)/shard_map/ppermute | solution.py:132
  40.0 16.6 %collective-permute-start.2 = (bf16[512,512]{1,0:T(8,128)(2,1)S(1)}, bf16[512,512]{1,0:T(8,128)(2,1)S(1)}, u32[]{:S(2)}, u32[]{:S(2)}) collective-permute-start(bf16[512,512]{1,0:T(8,128)(2,1)S(1)} %pad_maximum_fusion.3), channel_id=1, source_target_pairs={{0,256},{1,257},{2,258},{3,259},{4,260},{5,261},{6,262},{7,263},{8... | collective-permute-start | bytes 1572872 | tf_op jit(solution)/shard_map/ppermute | solution.py:132
  56.6 16.7 %collective-permute-start.3 = (bf16[1024,512]{1,0:T(8,128)(2,1)S(1)}, bf16[1024,512]{1,0:T(8,128)(2,1)S(1)}, u32[]{:S(2)}, u32[]{:S(2)}) collective-permute-start(bf16[1024,512]{1,0:T(8,128)(2,1)S(1)} %pad_maximum_fusion.1), channel_id=1, source_target_pairs={{0,128},{1,17},{2,130},{3,19},{4,132},{5,21},{6,134},{7,23},{8,136... | collective-permute-start | bytes 3145736 | tf_op jit(solution)/shard_map/ppermute | solution.py:132
  73.3 32.7 %copy-start.2 = (bf16[128,256]{1,0:T(8,128)(2,1)S(1)}, bf16[128,256]{1,0:T(8,128)(2,1)}, u32[]{:S(2)}) copy-start(bf16[128,256]{1,0:T(8,128)(2,1)} %q_ref.1) | copy-start | bytes 196612
  73.3 32.7 %copy-start.3 = (bf16[128,256]{1,0:T(8,128)(2,1)S(1)}, bf16[128,256]{1,0:T(8,128)(2,1)}, u32[]{:S(2)}) copy-start(bf16[128,256]{1,0:T(8,128)(2,1)} %do_ref.1) | copy-start | bytes 196612
  73.3 32.7 %copy-start.4 = (bf16[128,256]{1,0:T(8,128)(2,1)S(1)}, bf16[128,256]{1,0:T(8,128)(2,1)}, u32[]{:S(2)}) copy-start(bf16[128,256]{1,0:T(8,128)(2,1)} %o_ref.1) | copy-start | bytes 196612
  74.4 2.0 copy-start.6
  76.4 28.1 %collective-permute-start.4 = (bf16[2048,512]{1,0:T(8,128)(2,1)}, bf16[2048,512]{1,0:T(8,128)(2,1)S(1)}, u32[]{:S(2)}, u32[]{:S(2)}) collective-permute-start(bf16[2048,512]{1,0:T(8,128)(2,1)} %get-tuple-element.15), channel_id=1, source_target_pairs={{0,16},{1,129},{2,18},{3,131},{4,20},{5,133},{6,22},{7,135},{8,24}... | collective-permute-start | bytes 6291464 | tf_op jit(solution)/shard_map/ppermute | solution.py:132
  124.2 27.9 %collective-permute-start.5 = (bf16[2048,512]{1,0:T(8,128)(2,1)S(1)}, bf16[2048,512]{1,0:T(8,128)(2,1)S(1)}, u32[]{:S(2)}, u32[]{:S(2)}) collective-permute-start(bf16[2048,512]{1,0:T(8,128)(2,1)S(1)} %slice.66), channel_id=1, source_target_pairs={{0,16},{1,129},{2,18},{3,131},{4,20},{5,133},{6,22},{7,135},{8,24}... | collective-permute-start | bytes 6291464 | tf_op jit(solution)/shard_map/ppermute | solution.py:132
  152.9 17.6 %collective-permute-start.6 = (bf16[1024,512]{1,0:T(8,128)(2,1)S(1)}, bf16[1024,512]{1,0:T(8,128)(2,1)S(1)}, u32[]{:S(2)}, u32[]{:S(2)}) collective-permute-start(bf16[1024,512]{1,0:T(8,128)(2,1)S(1)} %slice.123), channel_id=1, source_target_pairs={{0,128},{1,17},{2,130},{3,19},{4,132},{5,21},{6,134},{7,23},{8,136... | collective-permute-start | bytes 3145736 | tf_op jit(solution)/shard_map/ppermute | solution.py:132
  170.9 26.1 %collective-permute-start.7 = (bf16[512,512]{1,0:T(8,128)(2,1)S(1)}, bf16[512,512]{1,0:T(8,128)(2,1)S(1)}, u32[]{:S(2)}, u32[]{:S(2)}) collective-permute-start(bf16[512,512]{1,0:T(8,128)(2,1)S(1)} %slice.125), channel_id=1, source_target_pairs={{0,256},{1,257},{2,258},{3,259},{4,260},{5,261},{6,262},{7,263},{8... | collective-permute-start | bytes 1572872 | tf_op jit(solution)/shard_map/ppermute | solution.py:132
  197.2 11.8 %collective-permute-start.8 = (bf16[256,512]{1,0:T(8,128)(2,1)S(1)}, bf16[256,512]{1,0:T(8,128)(2,1)S(1)}, u32[]{:S(2)}, u32[]{:S(2)}) collective-permute-start(bf16[256,512]{1,0:T(8,128)(2,1)S(1)} %slice.127), channel_id=1, source_target_pairs={{0,32},{1,33},{2,34},{3,35},{4,36},{5,37},{6,38},{7,39},{8,40},{9,... | collective-permute-start | bytes 786440 | tf_op jit(solution)/shard_map/ppermute | solution.py:132
  209.1 24.7 %collective-permute-start.9 = (bf16[128,512]{1,0:T(8,128)(2,1)S(1)}, bf16[128,512]{1,0:T(8,128)(2,1)S(1)}, u32[]{:S(2)}, u32[]{:S(2)}) collective-permute-start(bf16[128,512]{1,0:T(8,128)(2,1)S(1)} %slice.129), channel_id=1, source_target_pairs={{0,64},{1,65},{2,66},{3,67},{4,68},{5,69},{6,70},{7,71},{8,72},{9,... | collective-permute-start | bytes 393224 | tf_op jit(solution)/shard_map/ppermute | solution.py:132
  234.5 11.7 %collective-permute-start.10 = (bf16[128,768]{1,0:T(8,128)(2,1)S(1)}, bf16[128,768]{1,0:T(8,128)(2,1)S(1)}, u32[]{:S(2)}, u32[]{:S(2)}) collective-permute-start(bf16[128,768]{1,0:T(8,128)(2,1)S(1)} %get-tuple-element.29), channel_id=1, source_target_pairs={{0,64},{1,65},{2,66},{3,67},{4,68},{5,69},{6,70},{7,71},{8,72},{9,... | collective-permute-start | bytes 589832 | tf_op jit(solution)/shard_map/ppermute | solution.py:132
  246.2 14.8 %collective-permute-start.11 = (bf16[256,768]{1,0:T(8,128)(2,1)S(1)}, bf16[256,768]{1,0:T(8,128)(2,1)S(1)}, u32[]{:S(2)}, u32[]{:S(2)}) collective-permute-start(bf16[256,768]{1,0:T(8,128)(2,1)S(1)} %pad_maximum_fusion.4), channel_id=1, source_target_pairs={{0,32},{1,33},{2,34},{3,35},{4,36},{5,37},{6,38},{7,39},{8,40},{9,... | collective-permute-start | bytes 1179656 | tf_op jit(solution)/shard_map/ppermute | solution.py:132
  261.1 15.4 %collective-permute-start.12 = (bf16[512,768]{1,0:T(8,128)(2,1)S(1)}, bf16[512,768]{1,0:T(8,128)(2,1)S(1)}, u32[]{:S(2)}, u32[]{:S(2)}) collective-permute-start(bf16[512,768]{1,0:T(8,128)(2,1)S(1)} %pad_maximum_fusion.2), channel_id=1, source_target_pairs={{0,256},{1,257},{2,258},{3,259},{4,260},{5,261},{6,262},{7,263},{8... | collective-permute-start | bytes 2359304 | tf_op jit(solution)/shard_map/ppermute | solution.py:132
  276.6 22.9 %collective-permute-start.13 = (bf16[1024,768]{1,0:T(8,128)(2,1)S(1)}, bf16[1024,768]{1,0:T(8,128)(2,1)S(1)}, u32[]{:S(2)}, u32[]{:S(2)}) collective-permute-start(bf16[1024,768]{1,0:T(8,128)(2,1)S(1)} %pad_maximum_fusion), channel_id=1, source_target_pairs={{0,128},{1,17},{2,130},{3,19},{4,132},{5,21},{6,134},{7,23},{8,136... | collective-permute-start | bytes 4718600 | tf_op jit(solution)/shard_map/ppermute | solution.py:132
  300.9 2.6 copy-start.5
  303.5 39.4 %collective-permute-start.14 = (bf16[2048,768]{1,0:T(8,128)(2,1)}, bf16[2048,768]{1,0:T(8,128)(2,1)S(1)}, u32[]{:S(2)}, u32[]{:S(2)}) collective-permute-start(bf16[2048,768]{1,0:T(8,128)(2,1)} %get-tuple-element.13), channel_id=1, source_target_pairs={{0,16},{1,129},{2,18},{3,131},{4,20},{5,133},{6,22},{7,135},{8,24}... | collective-permute-start | bytes 9437192 | tf_op jit(solution)/shard_map/ppermute | solution.py:132
  342.9 1.9 copy-start.7
  342.9 1.9 copy-start.8
  342.9 1.9 copy-start.9
  353.6 4.6 %collective-permute-start.15 = (bf16[2048,256]{1,0:T(8,128)(2,1)S(1)}, bf16[2048,256]{1,0:T(8,128)(2,1)S(1)}, u32[]{:S(2)}, u32[]{:S(2)}) collective-permute-start(bf16[2048,256]{1,0:T(8,128)(2,1)S(1)} %bitcast.13), channel_id=1, source_target_pairs={{0,1},{1,0},{2,3},{3,2},{4,5},{5,4},{6,7},{7,6},{8,9},{9,8},{10,11... | collective-permute-start | bytes 3145736 | tf_op jit(solution)/shard_map/ppermute | solution.py:171
  358.1 50.8 %copy-start.1 = (s32[32,32]{1,0:T(8,128)S(1)}, s32[32,32]{1,0:T(8,128)}, u32[]{:S(2)}) copy-start(s32[32,32]{1,0:T(8,128)} %param.14) | copy-start | bytes 12292
  358.5 15.9 %collective-permute-start.16 = (bf16[1024,256]{1,0:T(8,128)(2,1)S(1)}, bf16[1024,256]{1,0:T(8,128)(2,1)S(1)}, u32[]{:S(2)}, u32[]{:S(2)}) collective-permute-start(bf16[1024,256]{1,0:T(8,128)(2,1)S(1)} %slice.124), channel_id=1, source_target_pairs={{0,4},{1,5},{2,6},{3,7},{4,0},{5,1},{6,2},{7,3},{8,12},{9,13},{10,... | collective-permute-start | bytes 1572872 | tf_op jit(solution)/shard_map/ppermute | solution.py:171
  374.5 10.9 %collective-permute-start.17 = (bf16[512,256]{1,0:T(8,128)(2,1)S(1)}, bf16[512,256]{1,0:T(8,128)(2,1)S(1)}, u32[]{:S(2)}, u32[]{:S(2)}) collective-permute-start(bf16[512,256]{1,0:T(8,128)(2,1)S(1)} %slice.126), channel_id=1, source_target_pairs={{0,8},{1,9},{2,10},{3,11},{4,12},{5,13},{6,14},{7,15},{8,0},{9,1},... | collective-permute-start | bytes 786440 | tf_op jit(solution)/shard_map/ppermute | solution.py:171
  385.5 22.7 %collective-permute-start.18 = (bf16[256,256]{1,0:T(8,128)(2,1)S(1)}, bf16[256,256]{1,0:T(8,128)(2,1)S(1)}, u32[]{:S(2)}, u32[]{:S(2)}) collective-permute-start(bf16[256,256]{1,0:T(8,128)(2,1)S(1)} %slice.128), channel_id=1, source_target_pairs={{0,2},{1,3},{2,0},{3,1},{4,6},{5,7},{6,4},{7,5},{8,10},{9,11},{10,... | collective-permute-start | bytes 393224 | tf_op jit(solution)/shard_map/ppermute | solution.py:171

commit v6 on v5

v6 whole, which is shorter than its diff:
```python
import functools
import math

import jax
import jax.numpy as jnp
from jax import lax
from jax.experimental import pallas as pl
from jax.experimental.pallas import tpu as pltpu
from jax.sharding import PartitionSpec as P

HD = 128
BLK = 128


NEG_FILL = -1e30
GATHER_ORDERS = ((4, 2, 16, 8, 1), (4, 2, 16, 1, 8))
SCATTER_ORDERS = ((1, 8, 16, 2, 4), (8, 1, 16, 2, 4))
TP_ORDER = (1, 4, 8, 2)


def _nt(a, b):
    return lax.dot_general(a, b, (((1,), (1,)), ((), ())), preferred_element_type=jnp.float32)


def _tn(a, b):
    return lax.dot_general(a, b, (((0,), (0,)), ((), ())), preferred_element_type=jnp.float32)


def attention_kernel(head_count, score_scale, mask_ref, q_ref, do_ref, o_ref, kv_ref, dq_ref, dkdv_ref):
    width = head_count * HD
    key_rows = kv_ref.shape[0]
    block_count = key_rows // BLK
    allowed = mask_ref[0:1, :] > 0
    for h in range(head_count):
        cols = slice(h * HD, (h + 1) * HD)
        q_h = q_ref[:, cols]
        do_h = do_ref[:, cols]
        k_h = kv_ref[:, cols]
        scores = _nt(q_h, k_h) * score_scale
        masked = jnp.where(allowed, scores, NEG_FILL)
        row_max = jnp.max(masked, axis=1, keepdims=True)
        row_sum = jnp.sum(jnp.where(allowed, jnp.exp(masked - row_max), 0.0), axis=1, keepdims=True)
        log_total = row_max + jnp.log(row_sum)
        probs = jnp.where(allowed, jnp.exp(masked - log_total), 0.0)
        row_delta = jnp.sum(
            do_h.astype(jnp.float32) * o_ref[:, cols].astype(jnp.float32), axis=1, keepdims=True
        )
        dprobs = _nt(do_h, kv_ref[:, pl.ds(width + h * HD, HD)])
        score_gradient = (probs * (dprobs - row_delta) * score_scale).astype(jnp.bfloat16)
        dq_ref[:, cols] = jnp.dot(score_gradient, k_h, preferred_element_type=jnp.float32)
        dk = _tn(score_gradient, q_h).astype(jnp.bfloat16)
        dv = _tn(probs.astype(jnp.bfloat16), do_h).astype(jnp.bfloat16)
        for p in range(block_count):
            src = slice(p * BLK, (p + 1) * BLK)
            dst = slice((block_count - 1 - p) * BLK, (block_count - p) * BLK)
            dkdv_ref[dst, cols] = dk[src]
            dkdv_ref[dst, pl.ds(width + h * HD, HD)] = dv[src]


def slab_attention(mask, queries, output_grad, attn_output, key_value):
    slab_rows, width = queries.shape
    head_count = width // HD
    key_rows = key_value.shape[0]
    vmem = pl.BlockSpec(memory_space=pltpu.VMEM)
    flops = 2 * slab_rows * key_rows * width * 5
    return pl.pallas_call(
        functools.partial(attention_kernel, head_count, 1.0 / math.sqrt(HD)),
        out_shape=(
            jax.ShapeDtypeStruct((slab_rows, width), jnp.float32),
            jax.ShapeDtypeStruct((key_rows, 2 * width), jnp.bfloat16),
        ),
        in_specs=[vmem] * 5,
        out_specs=(vmem, vmem),
        compiler_params=pltpu.CompilerParams(vmem_limit_bytes=48 * 1024 * 1024),
        cost_estimate=pl.CostEstimate(
            flops=flops,
            transcendentals=2 * slab_rows * key_rows * head_count,
            bytes_accessed=key_rows * width * 2 * 4,
        ),
    )(mask, queries, output_grad, attn_output, key_value)


def _pair_permute(value, distances):
    ctx_count, tp_count = lax.axis_size("ctx"), lax.axis_size("tp")
    pairs = [
        (c * tp_count + t, (c ^ distances[t % 2]) * tp_count + t)
        for c in range(ctx_count)
        for t in range(tp_count)
    ]
    return lax.ppermute(value, ("ctx", "tp"), pairs)


def gather_positions(me, distances, count):
    offset = me ^ jnp.arange(count, dtype=jnp.int32)
    return sum(((offset & d) != 0).astype(jnp.int32) << r for r, d in enumerate(distances))


def scatter_positions(me, distances, count):
    offset = me ^ jnp.arange(count, dtype=jnp.int32)
    top = len(distances) - 1
    return sum(((offset & d) == 0).astype(jnp.int32) << (top - r) for r, d in enumerate(distances))


def per_core(core, tables):
    return jnp.where(core == 0, tables[0], tables[1])


def concat_gather(x, orders):
    held = x
    for distances in zip(*orders):
        held = jnp.concatenate([held, _pair_permute(held, distances)], axis=0)
    return held


def halving_reduce(x, orders, wire=jnp.bfloat16):
    held = x
    for distances in zip(*orders):
        half = held.shape[0] // 2
        sent = _pair_permute(held[:half].astype(wire), distances)
        held = held[half:].astype(jnp.float32) + sent.astype(jnp.float32)
    return held


def tp_halving_reduce(x, order, wire=jnp.bfloat16):
    count = lax.axis_size("tp")
    held = x
    for distance in order:
        half = held.shape[0] // 2
        sent = lax.ppermute(
            held[:half].astype(wire), "tp", [(i, i ^ distance) for i in range(count)]
        )
        held = held[half:].astype(jnp.float32) + sent.astype(jnp.float32)
    return held


def per_device(
    queries, key_states, value_states, attn_output, output_grad, block_map, w_query, w_key, w_value
):
    slab_rows, width = queries.shape
    ctx_count, tp_count = lax.axis_size("ctx"), lax.axis_size("tp")
    me = lax.axis_index("ctx")
    me_tp = lax.axis_index("tp")
    core = me_tp % 2
    row_map = lax.dynamic_index_in_dim(block_map, me * slab_rows // BLK, axis=0, keepdims=False)
    gather_at = per_core(core, [gather_positions(me, o, ctx_count) for o in GATHER_ORDERS])
    slab_at = jnp.argsort(gather_at)
    mask = jnp.broadcast_to(
        jnp.repeat(row_map[slab_at].astype(jnp.float32), BLK)[None, :], (8, ctx_count * slab_rows)
    )
    key_value = jnp.concatenate([key_states, value_states], axis=1)
    gathered = concat_gather(key_value, GATHER_ORDERS)
    dq_total, part_grads = slab_attention(mask, queries, output_grad, attn_output, gathered)
    finished = halving_reduce(part_grads, SCATTER_ORDERS).astype(jnp.bfloat16)
    own_grads = jnp.concatenate([dq_total.astype(jnp.bfloat16), finished], axis=1)
    gradients = concat_gather(own_grads, GATHER_ORDERS)
    projections = jnp.concatenate([w_query, w_key, w_value], axis=1)
    term = lax.dot_general(
        gradients, projections, (((1,), (1,)), ((), ())), preferred_element_type=jnp.float32
    ).astype(jnp.bfloat16)
    tp_at = scatter_positions(me_tp, TP_ORDER, tp_count)
    owner = jnp.argsort(tp_at)
    per_owner = ctx_count // tp_count
    wanted = (owner[:, None] * per_owner + jnp.arange(per_owner)[None, :]).reshape(-1)
    source = gather_at[wanted]
    ordered = jnp.take(term.reshape(ctx_count, slab_rows, -1), source, axis=0)
    return tp_halving_reduce(ordered.reshape(ctx_count * slab_rows, -1), TP_ORDER).astype(
        jnp.bfloat16
    )


def solution(mesh):
    return jax.shard_map(
        per_device,
        mesh=mesh,
        in_specs=(
            P("ctx", "tp"),
            P("ctx", "tp"),
            P("ctx", "tp"),
            P("ctx", "tp"),
            P("ctx", "tp"),
            P(),
            P("ctx", "tp"),
            P("ctx", "tp"),
            P("ctx", "tp"),
        ),
        out_specs=P("tp", "ctx"),
        check_vma=False,
    )
```

time: 414 us -> 379 us (0.915)
  starting transfers between devices: 99.3 us -> 83 us
  Pallas kernels: 18.1 us -> 7.11 us
  local copies, waits for them, and re-layouts: 22.1 us -> 15.7 us
    pallas_call x1, Pallas kernels: 18.1 us -> 7.11 us  [slab_attention(): pl.pallas_call(functools.partial(attention_kernel, head_count, 1.0 / math...]
    ppermute x15, starting transfers between devices: 70.3 us -> 59.6 us  [_pair_permute(): return lax.ppermute(value, ('ctx', 'tp'), pairs)]
    ppermute x4, starting transfers between devices: 29 us -> 23.4 us  [tp_halving_reduce(): lax.ppermute(held[:half].astype(wire), 'tp', [(i, i ^ distance) for i in...]
    unnamed x28 -> x26, local copies, waits for them, and re-layouts: 12.4 us -> 8.23 us
where the time goes in v6:
time: 379 us; the launch traced here: 372 us
  waiting for transfers between devices  257 us (68%)
  starting transfers between devices  83 us (22%)
  local copies, waits for them, and re-layouts  15.7 us (4%)
  Pallas kernels  7.11 us (2%)
  other arithmetic  5.96 us (2%)
    ppermute x15, waiting for transfers between devices, _pair_permute(): return lax.ppermute(value, ('ctx', 'tp'), pairs)  233 us
    ppermute x15, starting transfers between devices, _pair_permute(): return lax.ppermute(value, ('ctx', 'tp'), pairs)  59.6 us
    ppermute x4, waiting for transfers between devices, tp_halving_reduce(): lax.ppermute(held[:half].astype(wire), 'tp', [(i, i ^ distance) for i in...  24 us
    ppermute x4, starting transfers between devices, tp_halving_reduce(): lax.ppermute(held[:half].astype(wire), 'tp', [(i, i ^ distance) for i in...  23.4 us
    unnamed x26, local copies, waits for them, and re-layouts  8.23 us
  transfers between devices with their start and end apart: 19, of which 19 were waited for; matrix products, arithmetic and copies ran while one was open for 2% of the time, Pallas kernels for 0%

profile of v6, /device:TPU:6, one launch (start us, length us, event | category | flops | bytes accessed | tf_op | source)
XLA Modules:
  0.0 372.1 jit_solution(9634800597346556768)
XLA Ops:
  0.0 1.5 constant_dynamic-update-slice_fusion.7
  1.5 1.5 constant_dynamic-update-slice_fusion.6
  3.0 9.1 %collective-permute-start = (bf16[128,512]{1,0:T(8,128)(2,1)S(1)}, bf16[128,512]{1,0:T(8,128)(2,1)S(1)}, u32[]{:S(2)}, u32[]{:S(2)}) collective-permute-start(bf16[128,512]{1,0:T(8,128)(2,1)S(1)} %get-tuple-element.36), channel_id=1, source_target_pairs={{0,64},{1,65},{2,66},{3,67},{4,68},{5,69},{6,70},{7,71},{8,72},{9,... | collective-permute-start | bytes 393224 | tf_op jit(solution)/shard_map/ppermute | solution.py:90
  12.1 11.9 %collective-permute-done = bf16[128,512]{1,0:T(8,128)(2,1)S(1)} collective-permute-done((bf16[128,512]{1,0:T(8,128)(2,1)S(1)}, bf16[128,512]{1,0:T(8,128)(2,1)S(1)}, u32[]{:S(2)}, u32[]{:S(2)}) %collective-permute-start) | collective-permute-done | bytes 131104 | tf_op jit(solution)/shard_map/ppermute | solution.py:90
  24.0 1.9 collective-permute-start.1
  25.9 14.0 %collective-permute-done.1 = bf16[256,512]{1,0:T(8,128)(2,1)S(1)} collective-permute-done((bf16[256,512]{1,0:T(8,128)(2,1)S(1)}, bf16[256,512]{1,0:T(8,128)(2,1)S(1)}, u32[]{:S(2)}, u32[]{:S(2)}) %collective-permute-start.1) | collective-permute-done | bytes 262176 | tf_op jit(solution)/shard_map/ppermute | solution.py:90
  39.9 3.3 collective-permute-start.2
  43.3 13.2 %collective-permute-done.2 = bf16[512,512]{1,0:T(8,128)(2,1)S(1)} collective-permute-done((bf16[512,512]{1,0:T(8,128)(2,1)S(1)}, bf16[512,512]{1,0:T(8,128)(2,1)S(1)}, u32[]{:S(2)}, u32[]{:S(2)}) %collective-permute-start.2) | collective-permute-done | bytes 524320 | tf_op jit(solution)/shard_map/ppermute | solution.py:90
  56.6 2.7 collective-permute-start.3
  61.6 11.7 %collective-permute-done.3 = bf16[1024,512]{1,0:T(8,128)(2,1)S(1)} collective-permute-done((bf16[1024,512]{1,0:T(8,128)(2,1)S(1)}, bf16[1024,512]{1,0:T(8,128)(2,1)S(1)}, u32[]{:S(2)}, u32[]{:S(2)}) %collective-permute-start.3) | collective-permute-done | bytes 1048608 | tf_op jit(solution)/shard_map/ppermute | solution.py:90
  73.3 1.1 constant_dynamic-update-slice_fusion.2
  74.4 1.9 copy-done.5
  76.3 2.0 collective-permute-start.4
  78.4 1.2 sort.34
  79.9 1.6 sort.35
  83.0 21.6 %collective-permute-done.4 = bf16[2048,512]{1,0:T(8,128)(2,1)S(1)} collective-permute-done((bf16[2048,512]{1,0:T(8,128)(2,1)}, bf16[2048,512]{1,0:T(8,128)(2,1)S(1)}, u32[]{:S(2)}, u32[]{:S(2)}) %collective-permute-start.4) | collective-permute-done | bytes 2097184 | tf_op jit(solution)/shard_map/ppermute | solution.py:90
  104.6 1.4 constant_dynamic-update-slice_fusion.8.kv_ref
  106.1 7.1 %shard_map.91 = (f32[128,256]{1,0:T(8,128)S(1)}, bf16[4096,512]{1,0:T(8,128)(2,1)S(1)}) custom-call(f32[8,4096]{1,0:T(8,128)S(1)} %broadcast_in_dim.30.mask_ref, bf16[128,256]{1,0:T(8,128)(2,1)S(1)} %copy-done.2, bf16[128,256]{1,0:T(8,128)(2,1)S(1)} %copy-done.3, bf16[128,256]{1,0:T(8,128)(2,1)S(1)} %copy-done.4, ...), custom_call_target="tpu_custom_call" | custom-call | flops 1342177280 | bytes 8388608 | tf_op jit(solution)/shard_map/pallas_call | solution.py:66
  113.3 1.9 collective-permute-start.5
  115.3 26.0 %collective-permute-done.5 = bf16[2048,512]{1,0:T(8,128)(2,1)S(1)} collective-permute-done((bf16[2048,512]{1,0:T(8,128)(2,1)S(1)}, bf16[2048,512]{1,0:T(8,128)(2,1)S(1)}, u32[]{:S(2)}, u32[]{:S(2)}) %collective-permute-start.5) | collective-permute-done | bytes 2097184 | tf_op jit(solution)/shard_map/ppermute | solution.py:90
  142.0 2.7 collective-permute-start.6
  144.8 14.6 %collective-permute-done.6 = bf16[1024,512]{1,0:T(8,128)(2,1)S(1)} collective-permute-done((bf16[1024,512]{1,0:T(8,128)(2,1)S(1)}, bf16[1024,512]{1,0:T(8,128)(2,1)S(1)}, u32[]{:S(2)}, u32[]{:S(2)}) %collective-permute-start.6) | collective-permute-done | bytes 1048608 | tf_op jit(solution)/shard_map/ppermute | solution.py:90
  159.8 2.7 collective-permute-start.7
  162.4 9.9 %collective-permute-done.7 = bf16[512,512]{1,0:T(8,128)(2,1)S(1)} collective-permute-done((bf16[512,512]{1,0:T(8,128)(2,1)S(1)}, bf16[512,512]{1,0:T(8,128)(2,1)S(1)}, u32[]{:S(2)}, u32[]{:S(2)}) %collective-permute-start.7) | collective-permute-done | bytes 524320 | tf_op jit(solution)/shard_map/ppermute | solution.py:90
  172.5 2.4 collective-permute-start.8
  174.9 8.8 %collective-permute-done.8 = bf16[256,512]{1,0:T(8,128)(2,1)S(1)} collective-permute-done((bf16[256,512]{1,0:T(8,128)(2,1)S(1)}, bf16[256,512]{1,0:T(8,128)(2,1)S(1)}, u32[]{:S(2)}, u32[]{:S(2)}) %collective-permute-start.8) | collective-permute-done | bytes 262176 | tf_op jit(solution)/shard_map/ppermute | solution.py:90
  183.8 8.9 %collective-permute-start.9 = (bf16[128,512]{1,0:T(8,128)(2,1)S(1)}, bf16[128,512]{1,0:T(8,128)(2,1)S(1)}, u32[]{:S(2)}, u32[]{:S(2)}) collective-permute-start(bf16[128,512]{1,0:T(8,128)(2,1)S(1)} %slice.131), channel_id=1, source_target_pairs={{0,64},{1,65},{2,66},{3,67},{4,68},{5,69},{6,70},{7,71},{8,72},{9,... | collective-permute-start | bytes 393224 | tf_op jit(solution)/shard_map/ppermute | solution.py:90
  192.7 4.8 %collective-permute-done.9 = bf16[128,512]{1,0:T(8,128)(2,1)S(1)} collective-permute-done((bf16[128,512]{1,0:T(8,128)(2,1)S(1)}, bf16[128,512]{1,0:T(8,128)(2,1)S(1)}, u32[]{:S(2)}, u32[]{:S(2)}) %collective-permute-start.9) | collective-permute-done | bytes 131104 | tf_op jit(solution)/shard_map/ppermute | solution.py:90
  197.7 7.4 %collective-permute-start.10 = (bf16[128,768]{1,0:T(8,128)(2,1)S(1)}, bf16[128,768]{1,0:T(8,128)(2,1)S(1)}, u32[]{:S(2)}, u32[]{:S(2)}) collective-permute-start(bf16[128,768]{1,0:T(8,128)(2,1)S(1)} %get-tuple-element.31), channel_id=1, source_target_pairs={{0,64},{1,65},{2,66},{3,67},{4,68},{5,69},{6,70},{7,71},{8,72},{9,... | collective-permute-start | bytes 589832 | tf_op jit(solution)/shard_map/ppermute | solution.py:90
  205.1 5.3 %collective-permute-done.10 = bf16[128,768]{1,0:T(8,128)(2,1)S(1)} collective-permute-done((bf16[128,768]{1,0:T(8,128)(2,1)S(1)}, bf16[128,768]{1,0:T(8,128)(2,1)S(1)}, u32[]{:S(2)}, u32[]{:S(2)}) %collective-permute-start.10) | collective-permute-done | bytes 196640 | tf_op jit(solution)/shard_map/ppermute | solution.py:90
  210.4 6.3 %collective-permute-start.11 = (bf16[256,768]{1,0:T(8,128)(2,1)S(1)}, bf16[256,768]{1,0:T(8,128)(2,1)S(1)}, u32[]{:S(2)}, u32[]{:S(2)}) collective-permute-start(bf16[256,768]{1,0:T(8,128)(2,1)S(1)} %pad_maximum_fusion.4), channel_id=1, source_target_pairs={{0,32},{1,33},{2,34},{3,35},{4,36},{5,37},{6,38},{7,39},{8,40},{9,... | collective-permute-start | bytes 1179656 | tf_op jit(solution)/shard_map/ppermute | solution.py:90
  216.7 14.9 %collective-permute-done.11 = bf16[256,768]{1,0:T(8,128)(2,1)S(1)} collective-permute-done((bf16[256,768]{1,0:T(8,128)(2,1)S(1)}, bf16[256,768]{1,0:T(8,128)(2,1)S(1)}, u32[]{:S(2)}, u32[]{:S(2)}) %collective-permute-start.11) | collective-permute-done | bytes 393248 | tf_op jit(solution)/shard_map/ppermute | solution.py:90
  231.7 3.3 collective-permute-start.12
  235.1 19.5 %collective-permute-done.12 = bf16[512,768]{1,0:T(8,128)(2,1)S(1)} collective-permute-done((bf16[512,768]{1,0:T(8,128)(2,1)S(1)}, bf16[512,768]{1,0:T(8,128)(2,1)S(1)}, u32[]{:S(2)}, u32[]{:S(2)}) %collective-permute-start.12) | collective-permute-done | bytes 786464 | tf_op jit(solution)/shard_map/ppermute | solution.py:90
  254.7 2.7 collective-permute-start.13
  257.6 19.4 %collective-permute-done.13 = bf16[1024,768]{1,0:T(8,128)(2,1)S(1)} collective-permute-done((bf16[1024,768]{1,0:T(8,128)(2,1)S(1)}, bf16[1024,768]{1,0:T(8,128)(2,1)S(1)}, u32[]{:S(2)}, u32[]{:S(2)}) %collective-permute-start.13) | collective-permute-done | bytes 1572896 | tf_op jit(solution)/shard_map/ppermute | solution.py:90
  277.2 2.1 collective-permute-start.14
  279.3 37.0 %collective-permute-done.14 = bf16[2048,768]{1,0:T(8,128)(2,1)S(1)} collective-permute-done((bf16[2048,768]{1,0:T(8,128)(2,1)S(1)}, bf16[2048,768]{1,0:T(8,128)(2,1)S(1)}, u32[]{:S(2)}, u32[]{:S(2)}) %collective-permute-start.14) | collective-permute-done | bytes 3145760 | tf_op jit(solution)/shard_map/ppermute | solution.py:90
  317.4 3.2 convolution_convert_fusion
  320.6 2.3 gather_fusion.2
  323.3 1.9 collective-permute-start.15
  325.3 2.6 collective-permute-done.15
  328.3 3.5 collective-permute-start.16
  331.8 12.4 %collective-permute-done.16 = bf16[1024,256]{1,0:T(8,128)(2,1)S(1)} collective-permute-done((bf16[1024,256]{1,0:T(8,128)(2,1)S(1)}, bf16[1024,256]{1,0:T(8,128)(2,1)S(1)}, u32[]{:S(2)}, u32[]{:S(2)}) %collective-permute-start.16) | collective-permute-done | bytes 524320 | tf_op jit(solution)/shard_map/ppermute | solution.py:129
  344.3 5.1 %collective-permute-start.17 = (bf16[512,256]{1,0:T(8,128)(2,1)S(1)}, bf16[512,256]{1,0:T(8,128)(2,1)S(1)}, u32[]{:S(2)}, u32[]{:S(2)}) collective-permute-start(bf16[512,256]{1,0:T(8,128)(2,1)S(1)} %slice.128), channel_id=1, source_target_pairs={{0,8},{1,9},{2,10},{3,11},{4,12},{5,13},{6,14},{7,15},{8,0},{9,1},... | collective-permute-start | bytes 786440 | tf_op jit(solution)/shard_map/ppermute | solution.py:129
  349.4 5.8 %collective-permute-done.17 = bf16[512,256]{1,0:T(8,128)(2,1)S(1)} collective-permute-done((bf16[512,256]{1,0:T(8,128)(2,1)S(1)}, bf16[512,256]{1,0:T(8,128)(2,1)S(1)}, u32[]{:S(2)}, u32[]{:S(2)}) %collective-permute-start.17) | collective-permute-done | bytes 262176 | tf_op jit(solution)/shard_map/ppermute | solution.py:129
  355.3 12.9 %collective-permute-start.18 = (bf16[256,256]{1,0:T(8,128)(2,1)S(1)}, bf16[256,256]{1,0:T(8,128)(2,1)S(1)}, u32[]{:S(2)}, u32[]{:S(2)}) collective-permute-start(bf16[256,256]{1,0:T(8,128)(2,1)S(1)} %slice.130), channel_id=1, source_target_pairs={{0,2},{1,3},{2,0},{3,1},{4,6},{5,7},{6,4},{7,5},{8,10},{9,11},{10,... | collective-permute-start | bytes 393224 | tf_op jit(solution)/shard_map/ppermute | solution.py:129
  368.2 3.2 collective-permute-done.18
  (71 shorter events, 9.1 us)
Async XLA Ops:
  0.0 82.2 %copy-start = (s32[32,32]{1,0:T(8,128)S(1)}, s32[32,32]{1,0:T(8,128)}, u32[]{:S(2)}) copy-start(s32[32,32]{1,0:T(8,128)} %param.14) | copy-start | bytes 12292
  3.0 21.0 %collective-permute-start = (bf16[128,512]{1,0:T(8,128)(2,1)S(1)}, bf16[128,512]{1,0:T(8,128)(2,1)S(1)}, u32[]{:S(2)}, u32[]{:S(2)}) collective-permute-start(bf16[128,512]{1,0:T(8,128)(2,1)S(1)} %get-tuple-element.36), channel_id=1, source_target_pairs={{0,64},{1,65},{2,66},{3,67},{4,68},{5,69},{6,70},{7,71},{8,72},{9,... | collective-permute-start | bytes 393224 | tf_op jit(solution)/shard_map/ppermute | solution.py:90
  24.0 15.9 %collective-permute-start.1 = (bf16[256,512]{1,0:T(8,128)(2,1)S(1)}, bf16[256,512]{1,0:T(8,128)(2,1)S(1)}, u32[]{:S(2)}, u32[]{:S(2)}) collective-permute-start(bf16[256,512]{1,0:T(8,128)(2,1)S(1)} %pad_maximum_fusion.5), channel_id=1, source_target_pairs={{0,32},{1,33},{2,34},{3,35},{4,36},{5,37},{6,38},{7,39},{8,40},{9,... | collective-permute-start | bytes 786440 | tf_op jit(solution)/shard_map/ppermute | solution.py:90
  39.9 16.6 %collective-permute-start.2 = (bf16[512,512]{1,0:T(8,128)(2,1)S(1)}, bf16[512,512]{1,0:T(8,128)(2,1)S(1)}, u32[]{:S(2)}, u32[]{:S(2)}) collective-permute-start(bf16[512,512]{1,0:T(8,128)(2,1)S(1)} %pad_maximum_fusion.3), channel_id=1, source_target_pairs={{0,256},{1,257},{2,258},{3,259},{4,260},{5,261},{6,262},{7,263},{8... | collective-permute-start | bytes 1572872 | tf_op jit(solution)/shard_map/ppermute | solution.py:90
  56.6 16.7 %collective-permute-start.3 = (bf16[1024,512]{1,0:T(8,128)(2,1)S(1)}, bf16[1024,512]{1,0:T(8,128)(2,1)S(1)}, u32[]{:S(2)}, u32[]{:S(2)}) collective-permute-start(bf16[1024,512]{1,0:T(8,128)(2,1)S(1)} %pad_maximum_fusion.1), channel_id=1, source_target_pairs={{0,128},{1,17},{2,130},{3,19},{4,132},{5,21},{6,134},{7,23},{8,136... | collective-permute-start | bytes 3145736 | tf_op jit(solution)/shard_map/ppermute | solution.py:90
  74.4 1.9 copy-start.5
  76.3 29.7 %copy-start.2 = (bf16[128,256]{1,0:T(8,128)(2,1)S(1)}, bf16[128,256]{1,0:T(8,128)(2,1)}, u32[]{:S(2)}) copy-start(bf16[128,256]{1,0:T(8,128)(2,1)} %q_ref.1) | copy-start | bytes 196612
  76.3 29.7 %copy-start.3 = (bf16[128,256]{1,0:T(8,128)(2,1)S(1)}, bf16[128,256]{1,0:T(8,128)(2,1)}, u32[]{:S(2)}) copy-start(bf16[128,256]{1,0:T(8,128)(2,1)} %do_ref.1) | copy-start | bytes 196612
  76.3 29.7 %copy-start.4 = (bf16[128,256]{1,0:T(8,128)(2,1)S(1)}, bf16[128,256]{1,0:T(8,128)(2,1)}, u32[]{:S(2)}) copy-start(bf16[128,256]{1,0:T(8,128)(2,1)} %o_ref.1) | copy-start | bytes 196612
  76.3 28.3 %collective-permute-start.4 = (bf16[2048,512]{1,0:T(8,128)(2,1)}, bf16[2048,512]{1,0:T(8,128)(2,1)S(1)}, u32[]{:S(2)}, u32[]{:S(2)}) collective-permute-start(bf16[2048,512]{1,0:T(8,128)(2,1)} %get-tuple-element.17), channel_id=1, source_target_pairs={{0,16},{1,129},{2,18},{3,131},{4,20},{5,133},{6,22},{7,135},{8,24}... | collective-permute-start | bytes 6291464 | tf_op jit(solution)/shard_map/ppermute | solution.py:90
  113.3 27.9 %collective-permute-start.5 = (bf16[2048,512]{1,0:T(8,128)(2,1)S(1)}, bf16[2048,512]{1,0:T(8,128)(2,1)S(1)}, u32[]{:S(2)}, u32[]{:S(2)}) collective-permute-start(bf16[2048,512]{1,0:T(8,128)(2,1)S(1)} %slice.66), channel_id=1, source_target_pairs={{0,16},{1,129},{2,18},{3,131},{4,20},{5,133},{6,22},{7,135},{8,24}... | collective-permute-start | bytes 6291464 | tf_op jit(solution)/shard_map/ppermute | solution.py:90
  142.0 17.4 %collective-permute-start.6 = (bf16[1024,512]{1,0:T(8,128)(2,1)S(1)}, bf16[1024,512]{1,0:T(8,128)(2,1)S(1)}, u32[]{:S(2)}, u32[]{:S(2)}) collective-permute-start(bf16[1024,512]{1,0:T(8,128)(2,1)S(1)} %slice.125), channel_id=1, source_target_pairs={{0,128},{1,17},{2,130},{3,19},{4,132},{5,21},{6,134},{7,23},{8,136... | collective-permute-start | bytes 3145736 | tf_op jit(solution)/shard_map/ppermute | solution.py:90
  159.8 12.6 %collective-permute-start.7 = (bf16[512,512]{1,0:T(8,128)(2,1)S(1)}, bf16[512,512]{1,0:T(8,128)(2,1)S(1)}, u32[]{:S(2)}, u32[]{:S(2)}) collective-permute-start(bf16[512,512]{1,0:T(8,128)(2,1)S(1)} %slice.127), channel_id=1, source_target_pairs={{0,256},{1,257},{2,258},{3,259},{4,260},{5,261},{6,262},{7,263},{8... | collective-permute-start | bytes 1572872 | tf_op jit(solution)/shard_map/ppermute | solution.py:90
  172.5 11.2 %collective-permute-start.8 = (bf16[256,512]{1,0:T(8,128)(2,1)S(1)}, bf16[256,512]{1,0:T(8,128)(2,1)S(1)}, u32[]{:S(2)}, u32[]{:S(2)}) collective-permute-start(bf16[256,512]{1,0:T(8,128)(2,1)S(1)} %slice.129), channel_id=1, source_target_pairs={{0,32},{1,33},{2,34},{3,35},{4,36},{5,37},{6,38},{7,39},{8,40},{9,... | collective-permute-start | bytes 786440 | tf_op jit(solution)/shard_map/ppermute | solution.py:90
  183.8 13.8 %collective-permute-start.9 = (bf16[128,512]{1,0:T(8,128)(2,1)S(1)}, bf16[128,512]{1,0:T(8,128)(2,1)S(1)}, u32[]{:S(2)}, u32[]{:S(2)}) collective-permute-start(bf16[128,512]{1,0:T(8,128)(2,1)S(1)} %slice.131), channel_id=1, source_target_pairs={{0,64},{1,65},{2,66},{3,67},{4,68},{5,69},{6,70},{7,71},{8,72},{9,... | collective-permute-start | bytes 393224 | tf_op jit(solution)/shard_map/ppermute | solution.py:90
  197.7 12.7 %collective-permute-start.10 = (bf16[128,768]{1,0:T(8,128)(2,1)S(1)}, bf16[128,768]{1,0:T(8,128)(2,1)S(1)}, u32[]{:S(2)}, u32[]{:S(2)}) collective-permute-start(bf16[128,768]{1,0:T(8,128)(2,1)S(1)} %get-tuple-element.31), channel_id=1, source_target_pairs={{0,64},{1,65},{2,66},{3,67},{4,68},{5,69},{6,70},{7,71},{8,72},{9,... | collective-permute-start | bytes 589832 | tf_op jit(solution)/shard_map/ppermute | solution.py:90
  210.4 21.3 %collective-permute-start.11 = (bf16[256,768]{1,0:T(8,128)(2,1)S(1)}, bf16[256,768]{1,0:T(8,128)(2,1)S(1)}, u32[]{:S(2)}, u32[]{:S(2)}) collective-permute-start(bf16[256,768]{1,0:T(8,128)(2,1)S(1)} %pad_maximum_fusion.4), channel_id=1, source_target_pairs={{0,32},{1,33},{2,34},{3,35},{4,36},{5,37},{6,38},{7,39},{8,40},{9,... | collective-permute-start | bytes 1179656 | tf_op jit(solution)/shard_map/ppermute | solution.py:90
  231.7 22.9 %collective-permute-start.12 = (bf16[512,768]{1,0:T(8,128)(2,1)S(1)}, bf16[512,768]{1,0:T(8,128)(2,1)S(1)}, u32[]{:S(2)}, u32[]{:S(2)}) collective-permute-start(bf16[512,768]{1,0:T(8,128)(2,1)S(1)} %pad_maximum_fusion.2), channel_id=1, source_target_pairs={{0,256},{1,257},{2,258},{3,259},{4,260},{5,261},{6,262},{7,263},{8... | collective-permute-start | bytes 2359304 | tf_op jit(solution)/shard_map/ppermute | solution.py:90
  254.7 22.3 %collective-permute-start.13 = (bf16[1024,768]{1,0:T(8,128)(2,1)S(1)}, bf16[1024,768]{1,0:T(8,128)(2,1)S(1)}, u32[]{:S(2)}, u32[]{:S(2)}) collective-permute-start(bf16[1024,768]{1,0:T(8,128)(2,1)S(1)} %pad_maximum_fusion), channel_id=1, source_target_pairs={{0,128},{1,17},{2,130},{3,19},{4,132},{5,21},{6,134},{7,23},{8,136... | collective-permute-start | bytes 4718600 | tf_op jit(solution)/shard_map/ppermute | solution.py:90
  277.2 39.2 %collective-permute-start.14 = (bf16[2048,768]{1,0:T(8,128)(2,1)S(1)}, bf16[2048,768]{1,0:T(8,128)(2,1)S(1)}, u32[]{:S(2)}, u32[]{:S(2)}) collective-permute-start(bf16[2048,768]{1,0:T(8,128)(2,1)S(1)} %get-tuple-element.15), channel_id=1, source_target_pairs={{0,16},{1,129},{2,18},{3,131},{4,20},{5,133},{6,22},{7,135},{8,24}... | collective-permute-start | bytes 9437192 | tf_op jit(solution)/shard_map/ppermute | solution.py:90
  316.4 0.9 copy-start.6
  316.4 1.0 copy-start.7
  316.4 1.0 copy-start.8
  323.3 4.6 %collective-permute-start.15 = (bf16[2048,256]{1,0:T(8,128)(2,1)S(1)}, bf16[2048,256]{1,0:T(8,128)(2,1)S(1)}, u32[]{:S(2)}, u32[]{:S(2)}) collective-permute-start(bf16[2048,256]{1,0:T(8,128)(2,1)S(1)} %bitcast.17), channel_id=1, source_target_pairs={{0,1},{1,0},{2,3},{3,2},{4,5},{5,4},{6,7},{7,6},{8,9},{9,8},{10,11... | collective-permute-start | bytes 3145736 | tf_op jit(solution)/shard_map/ppermute | solution.py:129
  327.9 44.2 %copy-start.1 = (s32[32,32]{1,0:T(8,128)S(1)}, s32[32,32]{1,0:T(8,128)}, u32[]{:S(2)}) copy-start(s32[32,32]{1,0:T(8,128)} %param.14) | copy-start | bytes 12292
  328.3 15.9 %collective-permute-start.16 = (bf16[1024,256]{1,0:T(8,128)(2,1)S(1)}, bf16[1024,256]{1,0:T(8,128)(2,1)S(1)}, u32[]{:S(2)}, u32[]{:S(2)}) collective-permute-start(bf16[1024,256]{1,0:T(8,128)(2,1)S(1)} %slice.126), channel_id=1, source_target_pairs={{0,4},{1,5},{2,6},{3,7},{4,0},{5,1},{6,2},{7,3},{8,12},{9,13},{10,... | collective-permute-start | bytes 1572872 | tf_op jit(solution)/shard_map/ppermute | solution.py:129
  344.3 10.9 %collective-permute-start.17 = (bf16[512,256]{1,0:T(8,128)(2,1)S(1)}, bf16[512,256]{1,0:T(8,128)(2,1)S(1)}, u32[]{:S(2)}, u32[]{:S(2)}) collective-permute-start(bf16[512,256]{1,0:T(8,128)(2,1)S(1)} %slice.128), channel_id=1, source_target_pairs={{0,8},{1,9},{2,10},{3,11},{4,12},{5,13},{6,14},{7,15},{8,0},{9,1},... | collective-permute-start | bytes 786440 | tf_op jit(solution)/shard_map/ppermute | solution.py:129
  355.3 16.1 %collective-permute-start.18 = (bf16[256,256]{1,0:T(8,128)(2,1)S(1)}, bf16[256,256]{1,0:T(8,128)(2,1)S(1)}, u32[]{:S(2)}, u32[]{:S(2)}) collective-permute-start(bf16[256,256]{1,0:T(8,128)(2,1)S(1)} %slice.130), channel_id=1, source_target_pairs={{0,2},{1,3},{2,0},{3,1},{4,6},{5,7},{6,4},{7,5},{8,10},{9,11},{10,... | collective-permute-start | bytes 393224 | tf_op jit(solution)/shard_map/ppermute | solution.py:129

commit v7 on v6

--- a/solution.py
+++ b/solution.py
@@ -150,9 +150,26 @@
     key_value = jnp.concatenate([key_states, value_states], axis=1)
     gathered = concat_gather(key_value, GATHER_ORDERS)
     dq_total, part_grads = slab_attention(mask, queries, output_grad, attn_output, gathered)
-    finished = halving_reduce(part_grads, SCATTER_ORDERS).astype(jnp.bfloat16)
-    own_grads = jnp.concatenate([dq_total.astype(jnp.bfloat16), finished], axis=1)
-    gradients = concat_gather(own_grads, GATHER_ORDERS)
+    last = tuple(order[-1] for order in SCATTER_ORDERS)
+    assert last == tuple(order[0] for order in GATHER_ORDERS)
+    held = halving_reduce(part_grads, tuple(order[:-1] for order in SCATTER_ORDERS))
+    theirs_part, mine_part = held[:slab_rows], held[slab_rows:]
+    dq_low = dq_total.astype(jnp.bfloat16)
+    payload = jnp.concatenate(
+        [theirs_part.astype(jnp.bfloat16), mine_part.astype(jnp.bfloat16), dq_low], axis=1
+    )
+    arrived = _pair_permute(payload, last)
+    part_width = mine_part.shape[1]
+    mine = mine_part + arrived[:, :part_width].astype(jnp.float32)
+    theirs = theirs_part + arrived[:, part_width : 2 * part_width].astype(jnp.float32)
+    paired = jnp.concatenate(
+        [
+            jnp.concatenate([dq_low, mine.astype(jnp.bfloat16)], axis=1),
+            jnp.concatenate([arrived[:, 2 * part_width :], theirs.astype(jnp.bfloat16)], axis=1),
+        ],
+        axis=0,
+    )
+    gradients = concat_gather(paired, tuple(order[1:] for order in GATHER_ORDERS))
     projections = jnp.concatenate([w_query, w_key, w_value], axis=1)
     term = lax.dot_general(
         gradients, projections, (((1,), (1,)), ((), ())), preferred_element_type=jnp.float32

time: 379 us -> 379 us (level)
  waiting for transfers between devices: 257 us -> 269 us
  starting transfers between devices: 83 us -> 71.4 us
    ppermute x15 -> x14, waiting for transfers between devices: 233 us -> 243 us  [_pair_permute(): return lax.ppermute(value, ('ctx', 'tp'), pairs)]
    ppermute x15 -> x14, starting transfers between devices: 59.6 us -> 50 us  [_pair_permute(): return lax.ppermute(value, ('ctx', 'tp'), pairs)]
    unnamed x26 -> x25, local copies, waits for them, and re-layouts: 8.23 us -> 8.2 us
  transfers between devices with their start and end apart: 19 -> 18, of which waited for: 19 -> 18; matrix products, arithmetic and copies ran while one was open for 2% -> 2% of each run, Pallas kernels for 0% -> 0%
where the time goes in v7:
time: 379 us; the launch traced here: 373 us
  waiting for transfers between devices  269 us (71%)
  starting transfers between devices  71.4 us (19%)
  local copies, waits for them, and re-layouts  15.7 us (4%)
  Pallas kernels  7.12 us (2%)
  other arithmetic  6.05 us (2%)
    ppermute x14, waiting for transfers between devices, _pair_permute(): return lax.ppermute(value, ('ctx', 'tp'), pairs)  243 us
    ppermute x14, starting transfers between devices, _pair_permute(): return lax.ppermute(value, ('ctx', 'tp'), pairs)  50 us
    ppermute x4, waiting for transfers between devices, tp_halving_reduce(): lax.ppermute(held[:half].astype(wire), 'tp', [(i, i ^ distance) for i in...  25.7 us
    ppermute x4, starting transfers between devices, tp_halving_reduce(): lax.ppermute(held[:half].astype(wire), 'tp', [(i, i ^ distance) for i in...  21.4 us
    unnamed x25, local copies, waits for them, and re-layouts  8.2 us
  transfers between devices with their start and end apart: 18, of which 18 were waited for; matrix products, arithmetic and copies ran while one was open for 2% of the time, Pallas kernels for 0%

profile of v7, /device:TPU:6, one launch (start us, length us, event | category | flops | bytes accessed | tf_op | source)
XLA Modules:
  0.0 372.9 jit_solution(17988074563601348010)
XLA Ops:
  0.0 1.5 constant_dynamic-update-slice_fusion.7
  1.5 1.5 constant_dynamic-update-slice_fusion.6
  3.0 9.1 %collective-permute-start = (bf16[128,512]{1,0:T(8,128)(2,1)S(1)}, bf16[128,512]{1,0:T(8,128)(2,1)S(1)}, u32[]{:S(2)}, u32[]{:S(2)}) collective-permute-start(bf16[128,512]{1,0:T(8,128)(2,1)S(1)} %get-tuple-element.39), channel_id=1, source_target_pairs={{0,64},{1,65},{2,66},{3,67},{4,68},{5,69},{6,70},{7,71},{8,72},{9,... | collective-permute-start | bytes 393224 | tf_op jit(solution)/shard_map/ppermute | solution.py:90
  12.1 11.9 %collective-permute-done = bf16[128,512]{1,0:T(8,128)(2,1)S(1)} collective-permute-done((bf16[128,512]{1,0:T(8,128)(2,1)S(1)}, bf16[128,512]{1,0:T(8,128)(2,1)S(1)}, u32[]{:S(2)}, u32[]{:S(2)}) %collective-permute-start) | collective-permute-done | bytes 131104 | tf_op jit(solution)/shard_map/ppermute | solution.py:90
  24.0 1.9 collective-permute-start.1
  25.9 14.0 %collective-permute-done.1 = bf16[256,512]{1,0:T(8,128)(2,1)S(1)} collective-permute-done((bf16[256,512]{1,0:T(8,128)(2,1)S(1)}, bf16[256,512]{1,0:T(8,128)(2,1)S(1)}, u32[]{:S(2)}, u32[]{:S(2)}) %collective-permute-start.1) | collective-permute-done | bytes 262176 | tf_op jit(solution)/shard_map/ppermute | solution.py:90
  40.0 3.3 collective-permute-start.2
  43.3 13.2 %collective-permute-done.2 = bf16[512,512]{1,0:T(8,128)(2,1)S(1)} collective-permute-done((bf16[512,512]{1,0:T(8,128)(2,1)S(1)}, bf16[512,512]{1,0:T(8,128)(2,1)S(1)}, u32[]{:S(2)}, u32[]{:S(2)}) %collective-permute-start.2) | collective-permute-done | bytes 524320 | tf_op jit(solution)/shard_map/ppermute | solution.py:90
  56.6 2.7 collective-permute-start.3
  60.0 0.7 constant_dynamic-update-slice_fusion.4
  60.7 0.9 constant_dynamic-update-slice_fusion.3
  61.6 11.7 %collective-permute-done.3 = bf16[1024,512]{1,0:T(8,128)(2,1)S(1)} collective-permute-done((bf16[1024,512]{1,0:T(8,128)(2,1)S(1)}, bf16[1024,512]{1,0:T(8,128)(2,1)S(1)}, u32[]{:S(2)}, u32[]{:S(2)}) %collective-permute-start.3) | collective-permute-done | bytes 1048608 | tf_op jit(solution)/shard_map/ppermute | solution.py:90
  73.3 1.1 constant_dynamic-update-slice_fusion.2
  74.4 1.9 copy-done.5
  76.3 2.0 collective-permute-start.4
  78.4 1.2 sort.34
  80.6 1.6 sort.35
  83.0 21.6 %collective-permute-done.4 = bf16[2048,512]{1,0:T(8,128)(2,1)S(1)} collective-permute-done((bf16[2048,512]{1,0:T(8,128)(2,1)}, bf16[2048,512]{1,0:T(8,128)(2,1)S(1)}, u32[]{:S(2)}, u32[]{:S(2)}) %collective-permute-start.4) | collective-permute-done | bytes 2097184 | tf_op jit(solution)/shard_map/ppermute | solution.py:90
  104.6 1.4 constant_dynamic-update-slice_fusion.8.kv_ref
  106.1 7.1 %shard_map.91 = (f32[128,256]{1,0:T(8,128)S(1)}, bf16[4096,512]{1,0:T(8,128)(2,1)S(1)}) custom-call(f32[8,4096]{1,0:T(8,128)S(1)} %broadcast_in_dim.30.mask_ref, bf16[128,256]{1,0:T(8,128)(2,1)S(1)} %copy-done.2, bf16[128,256]{1,0:T(8,128)(2,1)S(1)} %copy-done.3, bf16[128,256]{1,0:T(8,128)(2,1)S(1)} %copy-done.4, ...), custom_call_target="tpu_custom_call" | custom-call | flops 1342177280 | bytes 8388608 | tf_op jit(solution)/shard_map/pallas_call | solution.py:66
  113.3 1.9 collective-permute-start.5
  115.3 26.0 %collective-permute-done.5 = bf16[2048,512]{1,0:T(8,128)(2,1)S(1)} collective-permute-done((bf16[2048,512]{1,0:T(8,128)(2,1)S(1)}, bf16[2048,512]{1,0:T(8,128)(2,1)S(1)}, u32[]{:S(2)}, u32[]{:S(2)}) %collective-permute-start.5) | collective-permute-done | bytes 2097184 | tf_op jit(solution)/shard_map/ppermute | solution.py:90
  142.0 2.7 collective-permute-start.6
  144.8 14.6 %collective-permute-done.6 = bf16[1024,512]{1,0:T(8,128)(2,1)S(1)} collective-permute-done((bf16[1024,512]{1,0:T(8,128)(2,1)S(1)}, bf16[1024,512]{1,0:T(8,128)(2,1)S(1)}, u32[]{:S(2)}, u32[]{:S(2)}) %collective-permute-start.6) | collective-permute-done | bytes 1048608 | tf_op jit(solution)/shard_map/ppermute | solution.py:90
  159.8 2.6 collective-permute-start.7
  162.4 9.9 %collective-permute-done.7 = bf16[512,512]{1,0:T(8,128)(2,1)S(1)} collective-permute-done((bf16[512,512]{1,0:T(8,128)(2,1)S(1)}, bf16[512,512]{1,0:T(8,128)(2,1)S(1)}, u32[]{:S(2)}, u32[]{:S(2)}) %collective-permute-start.7) | collective-permute-done | bytes 524320 | tf_op jit(solution)/shard_map/ppermute | solution.py:90
  172.6 2.4 collective-permute-start.8
  175.0 8.8 %collective-permute-done.8 = bf16[256,512]{1,0:T(8,128)(2,1)S(1)} collective-permute-done((bf16[256,512]{1,0:T(8,128)(2,1)S(1)}, bf16[256,512]{1,0:T(8,128)(2,1)S(1)}, u32[]{:S(2)}, u32[]{:S(2)}) %collective-permute-start.8) | collective-permute-done | bytes 262176 | tf_op jit(solution)/shard_map/ppermute | solution.py:90
  183.9 11.1 %collective-permute-start.9 = (bf16[128,1280]{1,0:T(8,128)(2,1)S(1)}, bf16[128,1280]{1,0:T(8,128)(2,1)S(1)}, u32[]{:S(2)}, u32[]{:S(2)}) collective-permute-start(bf16[128,1280]{1,0:T(8,128)(2,1)S(1)} %pad_maximum_fusion.4), channel_id=1, source_target_pairs={{0,64},{1,65},{2,66},{3,67},{4,68},{5,69},{6,70},{7,71},{8,72},{9,... | collective-permute-start | bytes 983048 | tf_op jit(solution)/shard_map/ppermute | solution.py:90
  195.0 18.2 %collective-permute-done.9 = bf16[128,1280]{1,0:T(8,128)(2,1)S(1)} collective-permute-done((bf16[128,1280]{1,0:T(8,128)(2,1)S(1)}, bf16[128,1280]{1,0:T(8,128)(2,1)S(1)}, u32[]{:S(2)}, u32[]{:S(2)}) %collective-permute-start.9) | collective-permute-done | bytes 327712 | tf_op jit(solution)/shard_map/ppermute | solution.py:90
  213.3 1.9 collective-permute-start.10
  215.2 17.6 %collective-permute-done.10 = bf16[256,768]{1,0:T(8,128)(2,1)S(1)} collective-permute-done((bf16[256,768]{1,0:T(8,128)(2,1)S(1)}, bf16[256,768]{1,0:T(8,128)(2,1)S(1)}, u32[]{:S(2)}, u32[]{:S(2)}) %collective-permute-start.10) | collective-permute-done | bytes 393248 | tf_op jit(solution)/shard_map/ppermute | solution.py:90
  232.9 3.3 collective-permute-start.11
  236.2 19.5 %collective-permute-done.11 = bf16[512,768]{1,0:T(8,128)(2,1)S(1)} collective-permute-done((bf16[512,768]{1,0:T(8,128)(2,1)S(1)}, bf16[512,768]{1,0:T(8,128)(2,1)S(1)}, u32[]{:S(2)}, u32[]{:S(2)}) %collective-permute-start.11) | collective-permute-done | bytes 786464 | tf_op jit(solution)/shard_map/ppermute | solution.py:90
  255.8 2.8 collective-permute-start.12
  258.8 19.3 %collective-permute-done.12 = bf16[1024,768]{1,0:T(8,128)(2,1)S(1)} collective-permute-done((bf16[1024,768]{1,0:T(8,128)(2,1)S(1)}, bf16[1024,768]{1,0:T(8,128)(2,1)S(1)}, u32[]{:S(2)}, u32[]{:S(2)}) %collective-permute-start.12) | collective-permute-done | bytes 1572896 | tf_op jit(solution)/shard_map/ppermute | solution.py:90
  278.4 2.1 collective-permute-start.13
  280.5 37.0 %collective-permute-done.13 = bf16[2048,768]{1,0:T(8,128)(2,1)S(1)} collective-permute-done((bf16[2048,768]{1,0:T(8,128)(2,1)S(1)}, bf16[2048,768]{1,0:T(8,128)(2,1)S(1)}, u32[]{:S(2)}, u32[]{:S(2)}) %collective-permute-start.13) | collective-permute-done | bytes 3145760 | tf_op jit(solution)/shard_map/ppermute | solution.py:90
  318.5 3.2 convolution_convert_fusion
  321.7 2.3 gather_fusion.2
  324.5 1.9 collective-permute-start.14
  326.4 2.6 collective-permute-done.14
  329.4 3.5 collective-permute-start.15
  332.9 12.4 %collective-permute-done.15 = bf16[1024,256]{1,0:T(8,128)(2,1)S(1)} collective-permute-done((bf16[1024,256]{1,0:T(8,128)(2,1)S(1)}, bf16[1024,256]{1,0:T(8,128)(2,1)S(1)}, u32[]{:S(2)}, u32[]{:S(2)}) %collective-permute-start.15) | collective-permute-done | bytes 524320 | tf_op jit(solution)/shard_map/ppermute | solution.py:129
  345.4 5.1 %collective-permute-start.16 = (bf16[512,256]{1,0:T(8,128)(2,1)S(1)}, bf16[512,256]{1,0:T(8,128)(2,1)S(1)}, u32[]{:S(2)}, u32[]{:S(2)}) collective-permute-start(bf16[512,256]{1,0:T(8,128)(2,1)S(1)} %slice.144), channel_id=1, source_target_pairs={{0,8},{1,9},{2,10},{3,11},{4,12},{5,13},{6,14},{7,15},{8,0},{9,1},... | collective-permute-start | bytes 786440 | tf_op jit(solution)/shard_map/ppermute | solution.py:129
  350.6 5.8 %collective-permute-done.16 = bf16[512,256]{1,0:T(8,128)(2,1)S(1)} collective-permute-done((bf16[512,256]{1,0:T(8,128)(2,1)S(1)}, bf16[512,256]{1,0:T(8,128)(2,1)S(1)}, u32[]{:S(2)}, u32[]{:S(2)}) %collective-permute-start.16) | collective-permute-done | bytes 262176 | tf_op jit(solution)/shard_map/ppermute | solution.py:129
  356.4 10.9 %collective-permute-start.17 = (bf16[256,256]{1,0:T(8,128)(2,1)S(1)}, bf16[256,256]{1,0:T(8,128)(2,1)S(1)}, u32[]{:S(2)}, u32[]{:S(2)}) collective-permute-start(bf16[256,256]{1,0:T(8,128)(2,1)S(1)} %slice.146), channel_id=1, source_target_pairs={{0,2},{1,3},{2,0},{3,1},{4,6},{5,7},{6,4},{7,5},{8,10},{9,11},{10,... | collective-permute-start | bytes 393224 | tf_op jit(solution)/shard_map/ppermute | solution.py:129
  367.3 4.9 %collective-permute-done.17 = bf16[256,256]{1,0:T(8,128)(2,1)S(1)} collective-permute-done((bf16[256,256]{1,0:T(8,128)(2,1)S(1)}, bf16[256,256]{1,0:T(8,128)(2,1)S(1)}, u32[]{:S(2)}, u32[]{:S(2)}) %collective-permute-start.17) | collective-permute-done | bytes 131104 | tf_op jit(solution)/shard_map/ppermute | solution.py:129
  (71 shorter events, 7.6 us)
Async XLA Ops:
  0.0 82.2 %copy-start = (s32[32,32]{1,0:T(8,128)S(1)}, s32[32,32]{1,0:T(8,128)}, u32[]{:S(2)}) copy-start(s32[32,32]{1,0:T(8,128)} %param.14) | copy-start | bytes 12292
  3.0 21.0 %collective-permute-start = (bf16[128,512]{1,0:T(8,128)(2,1)S(1)}, bf16[128,512]{1,0:T(8,128)(2,1)S(1)}, u32[]{:S(2)}, u32[]{:S(2)}) collective-permute-start(bf16[128,512]{1,0:T(8,128)(2,1)S(1)} %get-tuple-element.39), channel_id=1, source_target_pairs={{0,64},{1,65},{2,66},{3,67},{4,68},{5,69},{6,70},{7,71},{8,72},{9,... | collective-permute-start | bytes 393224 | tf_op jit(solution)/shard_map/ppermute | solution.py:90
  24.0 15.9 %collective-permute-start.1 = (bf16[256,512]{1,0:T(8,128)(2,1)S(1)}, bf16[256,512]{1,0:T(8,128)(2,1)S(1)}, u32[]{:S(2)}, u32[]{:S(2)}) collective-permute-start(bf16[256,512]{1,0:T(8,128)(2,1)S(1)} %pad_maximum_fusion.5), channel_id=1, source_target_pairs={{0,32},{1,33},{2,34},{3,35},{4,36},{5,37},{6,38},{7,39},{8,40},{9,... | collective-permute-start | bytes 786440 | tf_op jit(solution)/shard_map/ppermute | solution.py:90
  40.0 16.6 %collective-permute-start.2 = (bf16[512,512]{1,0:T(8,128)(2,1)S(1)}, bf16[512,512]{1,0:T(8,128)(2,1)S(1)}, u32[]{:S(2)}, u32[]{:S(2)}) collective-permute-start(bf16[512,512]{1,0:T(8,128)(2,1)S(1)} %pad_maximum_fusion.3), channel_id=1, source_target_pairs={{0,256},{1,257},{2,258},{3,259},{4,260},{5,261},{6,262},{7,263},{8... | collective-permute-start | bytes 1572872 | tf_op jit(solution)/shard_map/ppermute | solution.py:90
  56.6 16.7 %collective-permute-start.3 = (bf16[1024,512]{1,0:T(8,128)(2,1)S(1)}, bf16[1024,512]{1,0:T(8,128)(2,1)S(1)}, u32[]{:S(2)}, u32[]{:S(2)}) collective-permute-start(bf16[1024,512]{1,0:T(8,128)(2,1)S(1)} %pad_maximum_fusion.1), channel_id=1, source_target_pairs={{0,128},{1,17},{2,130},{3,19},{4,132},{5,21},{6,134},{7,23},{8,136... | collective-permute-start | bytes 3145736 | tf_op jit(solution)/shard_map/ppermute | solution.py:90
  74.4 1.9 copy-start.5
  76.3 29.7 %copy-start.2 = (bf16[128,256]{1,0:T(8,128)(2,1)S(1)}, bf16[128,256]{1,0:T(8,128)(2,1)}, u32[]{:S(2)}) copy-start(bf16[128,256]{1,0:T(8,128)(2,1)} %q_ref.1) | copy-start | bytes 196612
  76.3 29.7 %copy-start.3 = (bf16[128,256]{1,0:T(8,128)(2,1)S(1)}, bf16[128,256]{1,0:T(8,128)(2,1)}, u32[]{:S(2)}) copy-start(bf16[128,256]{1,0:T(8,128)(2,1)} %do_ref.1) | copy-start | bytes 196612
  76.3 29.7 %copy-start.4 = (bf16[128,256]{1,0:T(8,128)(2,1)S(1)}, bf16[128,256]{1,0:T(8,128)(2,1)}, u32[]{:S(2)}) copy-start(bf16[128,256]{1,0:T(8,128)(2,1)} %o_ref.1) | copy-start | bytes 196612
  76.3 28.3 %collective-permute-start.4 = (bf16[2048,512]{1,0:T(8,128)(2,1)}, bf16[2048,512]{1,0:T(8,128)(2,1)S(1)}, u32[]{:S(2)}, u32[]{:S(2)}) collective-permute-start(bf16[2048,512]{1,0:T(8,128)(2,1)} %get-tuple-element.17), channel_id=1, source_target_pairs={{0,16},{1,129},{2,18},{3,131},{4,20},{5,133},{6,22},{7,135},{8,24}... | collective-permute-start | bytes 6291464 | tf_op jit(solution)/shard_map/ppermute | solution.py:90
  113.3 27.9 %collective-permute-start.5 = (bf16[2048,512]{1,0:T(8,128)(2,1)S(1)}, bf16[2048,512]{1,0:T(8,128)(2,1)S(1)}, u32[]{:S(2)}, u32[]{:S(2)}) collective-permute-start(bf16[2048,512]{1,0:T(8,128)(2,1)S(1)} %slice.74), channel_id=1, source_target_pairs={{0,16},{1,129},{2,18},{3,131},{4,20},{5,133},{6,22},{7,135},{8,24}... | collective-permute-start | bytes 6291464 | tf_op jit(solution)/shard_map/ppermute | solution.py:90
  142.0 17.4 %collective-permute-start.6 = (bf16[1024,512]{1,0:T(8,128)(2,1)S(1)}, bf16[1024,512]{1,0:T(8,128)(2,1)S(1)}, u32[]{:S(2)}, u32[]{:S(2)}) collective-permute-start(bf16[1024,512]{1,0:T(8,128)(2,1)S(1)} %slice.141), channel_id=1, source_target_pairs={{0,128},{1,17},{2,130},{3,19},{4,132},{5,21},{6,134},{7,23},{8,136... | collective-permute-start | bytes 3145736 | tf_op jit(solution)/shard_map/ppermute | solution.py:90
  159.8 12.6 %collective-permute-start.7 = (bf16[512,512]{1,0:T(8,128)(2,1)S(1)}, bf16[512,512]{1,0:T(8,128)(2,1)S(1)}, u32[]{:S(2)}, u32[]{:S(2)}) collective-permute-start(bf16[512,512]{1,0:T(8,128)(2,1)S(1)} %slice.143), channel_id=1, source_target_pairs={{0,256},{1,257},{2,258},{3,259},{4,260},{5,261},{6,262},{7,263},{8... | collective-permute-start | bytes 1572872 | tf_op jit(solution)/shard_map/ppermute | solution.py:90
  172.6 11.1 %collective-permute-start.8 = (bf16[256,512]{1,0:T(8,128)(2,1)S(1)}, bf16[256,512]{1,0:T(8,128)(2,1)S(1)}, u32[]{:S(2)}, u32[]{:S(2)}) collective-permute-start(bf16[256,512]{1,0:T(8,128)(2,1)S(1)} %slice.145), channel_id=1, source_target_pairs={{0,32},{1,33},{2,34},{3,35},{4,36},{5,37},{6,38},{7,39},{8,40},{9,... | collective-permute-start | bytes 786440 | tf_op jit(solution)/shard_map/ppermute | solution.py:90
  183.9 29.3 %collective-permute-start.9 = (bf16[128,1280]{1,0:T(8,128)(2,1)S(1)}, bf16[128,1280]{1,0:T(8,128)(2,1)S(1)}, u32[]{:S(2)}, u32[]{:S(2)}) collective-permute-start(bf16[128,1280]{1,0:T(8,128)(2,1)S(1)} %pad_maximum_fusion.4), channel_id=1, source_target_pairs={{0,64},{1,65},{2,66},{3,67},{4,68},{5,69},{6,70},{7,71},{8,72},{9,... | collective-permute-start | bytes 983048 | tf_op jit(solution)/shard_map/ppermute | solution.py:90
  213.3 19.5 %collective-permute-start.10 = (bf16[256,768]{1,0:T(8,128)(2,1)S(1)}, bf16[256,768]{1,0:T(8,128)(2,1)S(1)}, u32[]{:S(2)}, u32[]{:S(2)}) collective-permute-start(bf16[256,768]{1,0:T(8,128)(2,1)S(1)} %maximum_maximum_fusion), channel_id=1, source_target_pairs={{0,32},{1,33},{2,34},{3,35},{4,36},{5,37},{6,38},{7,39},{8,40},{9,... | collective-permute-start | bytes 1179656 | tf_op jit(solution)/shard_map/ppermute | solution.py:90
  232.9 22.9 %collective-permute-start.11 = (bf16[512,768]{1,0:T(8,128)(2,1)S(1)}, bf16[512,768]{1,0:T(8,128)(2,1)S(1)}, u32[]{:S(2)}, u32[]{:S(2)}) collective-permute-start(bf16[512,768]{1,0:T(8,128)(2,1)S(1)} %pad_maximum_fusion.2), channel_id=1, source_target_pairs={{0,256},{1,257},{2,258},{3,259},{4,260},{5,261},{6,262},{7,263},{8... | collective-permute-start | bytes 2359304 | tf_op jit(solution)/shard_map/ppermute | solution.py:90
  255.8 22.3 %collective-permute-start.12 = (bf16[1024,768]{1,0:T(8,128)(2,1)S(1)}, bf16[1024,768]{1,0:T(8,128)(2,1)S(1)}, u32[]{:S(2)}, u32[]{:S(2)}) collective-permute-start(bf16[1024,768]{1,0:T(8,128)(2,1)S(1)} %pad_maximum_fusion), channel_id=1, source_target_pairs={{0,128},{1,17},{2,130},{3,19},{4,132},{5,21},{6,134},{7,23},{8,136... | collective-permute-start | bytes 4718600 | tf_op jit(solution)/shard_map/ppermute | solution.py:90
  278.4 39.2 %collective-permute-start.13 = (bf16[2048,768]{1,0:T(8,128)(2,1)S(1)}, bf16[2048,768]{1,0:T(8,128)(2,1)S(1)}, u32[]{:S(2)}, u32[]{:S(2)}) collective-permute-start(bf16[2048,768]{1,0:T(8,128)(2,1)S(1)} %get-tuple-element.15), channel_id=1, source_target_pairs={{0,16},{1,129},{2,18},{3,131},{4,20},{5,133},{6,22},{7,135},{8,24}... | collective-permute-start | bytes 9437192 | tf_op jit(solution)/shard_map/ppermute | solution.py:90
  317.5 0.9 copy-start.6
  317.5 1.0 copy-start.7
  317.5 1.0 copy-start.8
  324.5 4.6 %collective-permute-start.14 = (bf16[2048,256]{1,0:T(8,128)(2,1)S(1)}, bf16[2048,256]{1,0:T(8,128)(2,1)S(1)}, u32[]{:S(2)}, u32[]{:S(2)}) collective-permute-start(bf16[2048,256]{1,0:T(8,128)(2,1)S(1)} %bitcast.17), channel_id=1, source_target_pairs={{0,1},{1,0},{2,3},{3,2},{4,5},{5,4},{6,7},{7,6},{8,9},{9,8},{10,11... | collective-permute-start | bytes 3145736 | tf_op jit(solution)/shard_map/ppermute | solution.py:129
  329.0 43.9 %copy-start.1 = (s32[32,32]{1,0:T(8,128)S(1)}, s32[32,32]{1,0:T(8,128)}, u32[]{:S(2)}) copy-start(s32[32,32]{1,0:T(8,128)} %param.14) | copy-start | bytes 12292
  329.4 15.9 %collective-permute-start.15 = (bf16[1024,256]{1,0:T(8,128)(2,1)S(1)}, bf16[1024,256]{1,0:T(8,128)(2,1)S(1)}, u32[]{:S(2)}, u32[]{:S(2)}) collective-permute-start(bf16[1024,256]{1,0:T(8,128)(2,1)S(1)} %slice.142), channel_id=1, source_target_pairs={{0,4},{1,5},{2,6},{3,7},{4,0},{5,1},{6,2},{7,3},{8,12},{9,13},{10,... | collective-permute-start | bytes 1572872 | tf_op jit(solution)/shard_map/ppermute | solution.py:129
  345.4 10.9 %collective-permute-start.16 = (bf16[512,256]{1,0:T(8,128)(2,1)S(1)}, bf16[512,256]{1,0:T(8,128)(2,1)S(1)}, u32[]{:S(2)}, u32[]{:S(2)}) collective-permute-start(bf16[512,256]{1,0:T(8,128)(2,1)S(1)} %slice.144), channel_id=1, source_target_pairs={{0,8},{1,9},{2,10},{3,11},{4,12},{5,13},{6,14},{7,15},{8,0},{9,1},... | collective-permute-start | bytes 786440 | tf_op jit(solution)/shard_map/ppermute | solution.py:129
  356.4 15.8 %collective-permute-start.17 = (bf16[256,256]{1,0:T(8,128)(2,1)S(1)}, bf16[256,256]{1,0:T(8,128)(2,1)S(1)}, u32[]{:S(2)}, u32[]{:S(2)}) collective-permute-start(bf16[256,256]{1,0:T(8,128)(2,1)S(1)} %slice.146), channel_id=1, source_target_pairs={{0,2},{1,3},{2,0},{3,1},{4,6},{5,7},{6,4},{7,5},{8,10},{9,11},{10,... | collective-permute-start | bytes 393224 | tf_op jit(solution)/shard_map/ppermute | solution.py:129

commit v8 on v6

--- a/solution.py
+++ b/solution.py
@@ -13,8 +13,8 @@
 
 
 NEG_FILL = -1e30
-GATHER_ORDERS = ((4, 2, 16, 8, 1), (4, 2, 16, 1, 8))
-SCATTER_ORDERS = ((1, 8, 16, 2, 4), (8, 1, 16, 2, 4))
+GATHER_ORDERS = ((4, 2, 16, 8, 1), (4, 16, 2, 1, 8))
+SCATTER_ORDERS = tuple(tuple(reversed(order)) for order in GATHER_ORDERS)
 TP_ORDER = (1, 4, 8, 2)
 
 

time: 379 us -> 363 us (0.958)
  the two profiles are of different devices: /device:TPU:6 before, /device:TPU:172 now
where the time goes in v8:
time: 363 us; the launch traced here: 362 us
  waiting for transfers between devices  248 us (68%)
  starting transfers between devices  81.2 us (22%)
  local copies, waits for them, and re-layouts  15.7 us (4%)
  Pallas kernels  7.12 us (2%)
  other arithmetic  5.96 us (2%)
    ppermute x15, waiting for transfers between devices, _pair_permute(): return lax.ppermute(value, ('ctx', 'tp'), pairs)  207 us
    ppermute x15, starting transfers between devices, _pair_permute(): return lax.ppermute(value, ('ctx', 'tp'), pairs)  70.1 us
    ppermute x4, waiting for transfers between devices, tp_halving_reduce(): lax.ppermute(held[:half].astype(wire), 'tp', [(i, i ^ distance) for i in...  41.6 us
    ppermute x4, starting transfers between devices, tp_halving_reduce(): lax.ppermute(held[:half].astype(wire), 'tp', [(i, i ^ distance) for i in...  11.1 us
    unnamed x26, local copies, waits for them, and re-layouts  8.23 us
  transfers between devices with their start and end apart: 19, of which 19 were waited for; matrix products, arithmetic and copies ran while one was open for 2% of the time, Pallas kernels for 0%

profile of v8, /device:TPU:172, one launch (start us, length us, event | category | flops | bytes accessed | tf_op | source)
XLA Modules:
  0.0 362.0 jit_solution(11047083573128560092)
XLA Ops:
  0.0 1.5 constant_dynamic-update-slice_fusion.7
  1.5 1.5 constant_dynamic-update-slice_fusion.6
  3.0 1.9 collective-permute-start
  4.9 11.7 %collective-permute-done = bf16[128,512]{1,0:T(8,128)(2,1)S(1)} collective-permute-done((bf16[128,512]{1,0:T(8,128)(2,1)S(1)}, bf16[128,512]{1,0:T(8,128)(2,1)S(1)}, u32[]{:S(2)}, u32[]{:S(2)}) %collective-permute-start) | collective-permute-done | bytes 131104 | tf_op jit(solution)/shard_map/ppermute | solution.py:90
  16.6 9.7 %collective-permute-start.1 = (bf16[256,512]{1,0:T(8,128)(2,1)S(1)}, bf16[256,512]{1,0:T(8,128)(2,1)S(1)}, u32[]{:S(2)}, u32[]{:S(2)}) collective-permute-start(bf16[256,512]{1,0:T(8,128)(2,1)S(1)} %pad_maximum_fusion.5), channel_id=1, source_target_pairs={{0,32},{1,257},{2,34},{3,259},{4,36},{5,261},{6,38},{7,263},{8,40}... | collective-permute-start | bytes 786440 | tf_op jit(solution)/shard_map/ppermute | solution.py:90
  26.3 4.3 %collective-permute-done.1 = bf16[256,512]{1,0:T(8,128)(2,1)S(1)} collective-permute-done((bf16[256,512]{1,0:T(8,128)(2,1)S(1)}, bf16[256,512]{1,0:T(8,128)(2,1)S(1)}, u32[]{:S(2)}, u32[]{:S(2)}) %collective-permute-start.1) | collective-permute-done | bytes 262176 | tf_op jit(solution)/shard_map/ppermute | solution.py:90
  30.7 2.4 collective-permute-start.2
  33.1 10.2 %collective-permute-done.2 = bf16[512,512]{1,0:T(8,128)(2,1)S(1)} collective-permute-done((bf16[512,512]{1,0:T(8,128)(2,1)S(1)}, bf16[512,512]{1,0:T(8,128)(2,1)S(1)}, u32[]{:S(2)}, u32[]{:S(2)}) %collective-permute-start.2) | collective-permute-done | bytes 524320 | tf_op jit(solution)/shard_map/ppermute | solution.py:90
  43.3 3.1 collective-permute-start.3
  48.7 11.3 %collective-permute-done.3 = bf16[1024,512]{1,0:T(8,128)(2,1)S(1)} collective-permute-done((bf16[1024,512]{1,0:T(8,128)(2,1)S(1)}, bf16[1024,512]{1,0:T(8,128)(2,1)S(1)}, u32[]{:S(2)}, u32[]{:S(2)}) %collective-permute-start.3) | collective-permute-done | bytes 1048608 | tf_op jit(solution)/shard_map/ppermute | solution.py:90
  60.0 1.1 constant_dynamic-update-slice_fusion.2
  61.1 1.9 copy-done.5
  63.1 2.0 collective-permute-start.4
  65.2 1.2 sort.34
  66.6 1.6 sort.35
  69.8 21.6 %collective-permute-done.4 = bf16[2048,512]{1,0:T(8,128)(2,1)S(1)} collective-permute-done((bf16[2048,512]{1,0:T(8,128)(2,1)}, bf16[2048,512]{1,0:T(8,128)(2,1)S(1)}, u32[]{:S(2)}, u32[]{:S(2)}) %collective-permute-start.4) | collective-permute-done | bytes 2097184 | tf_op jit(solution)/shard_map/ppermute | solution.py:90
  91.3 1.4 constant_dynamic-update-slice_fusion.8.kv_ref
  92.8 7.1 %shard_map.91 = (f32[128,256]{1,0:T(8,128)S(1)}, bf16[4096,512]{1,0:T(8,128)(2,1)S(1)}) custom-call(f32[8,4096]{1,0:T(8,128)S(1)} %broadcast_in_dim.30.mask_ref, bf16[128,256]{1,0:T(8,128)(2,1)S(1)} %copy-done.2, bf16[128,256]{1,0:T(8,128)(2,1)S(1)} %copy-done.3, bf16[128,256]{1,0:T(8,128)(2,1)S(1)} %copy-done.4, ...), custom_call_target="tpu_custom_call" | custom-call | flops 1342177280 | bytes 8388608 | tf_op jit(solution)/shard_map/pallas_call | solution.py:66
  100.1 1.9 collective-permute-start.5
  102.0 26.0 %collective-permute-done.5 = bf16[2048,512]{1,0:T(8,128)(2,1)S(1)} collective-permute-done((bf16[2048,512]{1,0:T(8,128)(2,1)S(1)}, bf16[2048,512]{1,0:T(8,128)(2,1)S(1)}, u32[]{:S(2)}, u32[]{:S(2)}) %collective-permute-start.5) | collective-permute-done | bytes 2097184 | tf_op jit(solution)/shard_map/ppermute | solution.py:90
  128.7 3.1 collective-permute-start.6
  131.9 13.6 %collective-permute-done.6 = bf16[1024,512]{1,0:T(8,128)(2,1)S(1)} collective-permute-done((bf16[1024,512]{1,0:T(8,128)(2,1)S(1)}, bf16[1024,512]{1,0:T(8,128)(2,1)S(1)}, u32[]{:S(2)}, u32[]{:S(2)}) %collective-permute-start.6) | collective-permute-done | bytes 1048608 | tf_op jit(solution)/shard_map/ppermute | solution.py:90
  145.8 2.4 collective-permute-start.7
  148.3 10.2 %collective-permute-done.7 = bf16[512,512]{1,0:T(8,128)(2,1)S(1)} collective-permute-done((bf16[512,512]{1,0:T(8,128)(2,1)S(1)}, bf16[512,512]{1,0:T(8,128)(2,1)S(1)}, u32[]{:S(2)}, u32[]{:S(2)}) %collective-permute-start.7) | collective-permute-done | bytes 524320 | tf_op jit(solution)/shard_map/ppermute | solution.py:90
  158.6 4.9 %collective-permute-start.8 = (bf16[256,512]{1,0:T(8,128)(2,1)S(1)}, bf16[256,512]{1,0:T(8,128)(2,1)S(1)}, u32[]{:S(2)}, u32[]{:S(2)}) collective-permute-start(bf16[256,512]{1,0:T(8,128)(2,1)S(1)} %slice.129), channel_id=1, source_target_pairs={{0,32},{1,257},{2,34},{3,259},{4,36},{5,261},{6,38},{7,263},{8,40}... | collective-permute-start | bytes 786440 | tf_op jit(solution)/shard_map/ppermute | solution.py:90
  163.5 6.1 %collective-permute-done.8 = bf16[256,512]{1,0:T(8,128)(2,1)S(1)} collective-permute-done((bf16[256,512]{1,0:T(8,128)(2,1)S(1)}, bf16[256,512]{1,0:T(8,128)(2,1)S(1)}, u32[]{:S(2)}, u32[]{:S(2)}) %collective-permute-start.8) | collective-permute-done | bytes 262176 | tf_op jit(solution)/shard_map/ppermute | solution.py:90
  169.8 2.7 collective-permute-start.9
  172.5 9.9 %collective-permute-done.9 = bf16[128,512]{1,0:T(8,128)(2,1)S(1)} collective-permute-done((bf16[128,512]{1,0:T(8,128)(2,1)S(1)}, bf16[128,512]{1,0:T(8,128)(2,1)S(1)}, u32[]{:S(2)}, u32[]{:S(2)}) %collective-permute-start.9) | collective-permute-done | bytes 131104 | tf_op jit(solution)/shard_map/ppermute | solution.py:90
  182.5 5.4 %collective-permute-start.10 = (bf16[128,768]{1,0:T(8,128)(2,1)S(1)}, bf16[128,768]{1,0:T(8,128)(2,1)S(1)}, u32[]{:S(2)}, u32[]{:S(2)}) collective-permute-start(bf16[128,768]{1,0:T(8,128)(2,1)S(1)} %get-tuple-element.31), channel_id=1, source_target_pairs={{0,64},{1,65},{2,66},{3,67},{4,68},{5,69},{6,70},{7,71},{8,72},{9,... | collective-permute-start | bytes 589832 | tf_op jit(solution)/shard_map/ppermute | solution.py:90
  187.9 6.1 %collective-permute-done.10 = bf16[128,768]{1,0:T(8,128)(2,1)S(1)} collective-permute-done((bf16[128,768]{1,0:T(8,128)(2,1)S(1)}, bf16[128,768]{1,0:T(8,128)(2,1)S(1)}, u32[]{:S(2)}, u32[]{:S(2)}) %collective-permute-start.10) | collective-permute-done | bytes 196640 | tf_op jit(solution)/shard_map/ppermute | solution.py:90
  194.1 14.7 %collective-permute-start.11 = (bf16[256,768]{1,0:T(8,128)(2,1)S(1)}, bf16[256,768]{1,0:T(8,128)(2,1)S(1)}, u32[]{:S(2)}, u32[]{:S(2)}) collective-permute-start(bf16[256,768]{1,0:T(8,128)(2,1)S(1)} %pad_maximum_fusion.4), channel_id=1, source_target_pairs={{0,32},{1,257},{2,34},{3,259},{4,36},{5,261},{6,38},{7,263},{8,40}... | collective-permute-start | bytes 1179656 | tf_op jit(solution)/shard_map/ppermute | solution.py:90
  208.8 5.8 %collective-permute-done.11 = bf16[256,768]{1,0:T(8,128)(2,1)S(1)} collective-permute-done((bf16[256,768]{1,0:T(8,128)(2,1)S(1)}, bf16[256,768]{1,0:T(8,128)(2,1)S(1)}, u32[]{:S(2)}, u32[]{:S(2)}) %collective-permute-start.11) | collective-permute-done | bytes 393248 | tf_op jit(solution)/shard_map/ppermute | solution.py:90
  214.7 2.2 collective-permute-start.12
  216.9 13.2 %collective-permute-done.12 = bf16[512,768]{1,0:T(8,128)(2,1)S(1)} collective-permute-done((bf16[512,768]{1,0:T(8,128)(2,1)S(1)}, bf16[512,768]{1,0:T(8,128)(2,1)S(1)}, u32[]{:S(2)}, u32[]{:S(2)}) %collective-permute-start.12) | collective-permute-done | bytes 786464 | tf_op jit(solution)/shard_map/ppermute | solution.py:90
  230.2 11.5 %collective-permute-start.13 = (bf16[1024,768]{1,0:T(8,128)(2,1)S(1)}, bf16[1024,768]{1,0:T(8,128)(2,1)S(1)}, u32[]{:S(2)}, u32[]{:S(2)}) collective-permute-start(bf16[1024,768]{1,0:T(8,128)(2,1)S(1)} %pad_maximum_fusion), channel_id=1, source_target_pairs={{0,128},{1,17},{2,130},{3,19},{4,132},{5,21},{6,134},{7,23},{8,136... | collective-permute-start | bytes 4718600 | tf_op jit(solution)/shard_map/ppermute | solution.py:90
  241.9 19.8 %collective-permute-done.13 = bf16[1024,768]{1,0:T(8,128)(2,1)S(1)} collective-permute-done((bf16[1024,768]{1,0:T(8,128)(2,1)S(1)}, bf16[1024,768]{1,0:T(8,128)(2,1)S(1)}, u32[]{:S(2)}, u32[]{:S(2)}) %collective-permute-start.13) | collective-permute-done | bytes 1572896 | tf_op jit(solution)/shard_map/ppermute | solution.py:90
  261.8 2.1 collective-permute-start.14
  264.0 37.0 %collective-permute-done.14 = bf16[2048,768]{1,0:T(8,128)(2,1)S(1)} collective-permute-done((bf16[2048,768]{1,0:T(8,128)(2,1)S(1)}, bf16[2048,768]{1,0:T(8,128)(2,1)S(1)}, u32[]{:S(2)}, u32[]{:S(2)}) %collective-permute-start.14) | collective-permute-done | bytes 3145760 | tf_op jit(solution)/shard_map/ppermute | solution.py:90
  302.0 3.2 convolution_convert_fusion
  305.2 2.3 gather_fusion.2
  308.0 1.9 collective-permute-start.15
  309.9 2.6 collective-permute-done.15
  312.9 2.4 collective-permute-start.16
  315.3 13.5 %collective-permute-done.16 = bf16[1024,256]{1,0:T(8,128)(2,1)S(1)} collective-permute-done((bf16[1024,256]{1,0:T(8,128)(2,1)S(1)}, bf16[1024,256]{1,0:T(8,128)(2,1)S(1)}, u32[]{:S(2)}, u32[]{:S(2)}) %collective-permute-start.16) | collective-permute-done | bytes 524320 | tf_op jit(solution)/shard_map/ppermute | solution.py:129
  328.9 4.2 %collective-permute-start.17 = (bf16[512,256]{1,0:T(8,128)(2,1)S(1)}, bf16[512,256]{1,0:T(8,128)(2,1)S(1)}, u32[]{:S(2)}, u32[]{:S(2)}) collective-permute-start(bf16[512,256]{1,0:T(8,128)(2,1)S(1)} %slice.128), channel_id=1, source_target_pairs={{0,8},{1,9},{2,10},{3,11},{4,12},{5,13},{6,14},{7,15},{8,0},{9,1},... | collective-permute-start | bytes 786440 | tf_op jit(solution)/shard_map/ppermute | solution.py:129
  333.1 6.7 %collective-permute-done.17 = bf16[512,256]{1,0:T(8,128)(2,1)S(1)} collective-permute-done((bf16[512,256]{1,0:T(8,128)(2,1)S(1)}, bf16[512,256]{1,0:T(8,128)(2,1)S(1)}, u32[]{:S(2)}, u32[]{:S(2)}) %collective-permute-start.17) | collective-permute-done | bytes 262176 | tf_op jit(solution)/shard_map/ppermute | solution.py:129
  339.9 2.6 collective-permute-start.18
  342.5 18.7 %collective-permute-done.18 = bf16[256,256]{1,0:T(8,128)(2,1)S(1)} collective-permute-done((bf16[256,256]{1,0:T(8,128)(2,1)S(1)}, bf16[256,256]{1,0:T(8,128)(2,1)S(1)}, u32[]{:S(2)}, u32[]{:S(2)}) %collective-permute-start.18) | collective-permute-done | bytes 131104 | tf_op jit(solution)/shard_map/ppermute | solution.py:129
  (71 shorter events, 9.1 us)
Async XLA Ops:
  0.0 68.9 %copy-start = (s32[32,32]{1,0:T(8,128)S(1)}, s32[32,32]{1,0:T(8,128)}, u32[]{:S(2)}) copy-start(s32[32,32]{1,0:T(8,128)} %param.14) | copy-start | bytes 12292
  3.0 13.6 %collective-permute-start = (bf16[128,512]{1,0:T(8,128)(2,1)S(1)}, bf16[128,512]{1,0:T(8,128)(2,1)S(1)}, u32[]{:S(2)}, u32[]{:S(2)}) collective-permute-start(bf16[128,512]{1,0:T(8,128)(2,1)S(1)} %get-tuple-element.36), channel_id=1, source_target_pairs={{0,64},{1,65},{2,66},{3,67},{4,68},{5,69},{6,70},{7,71},{8,72},{9,... | collective-permute-start | bytes 393224 | tf_op jit(solution)/shard_map/ppermute | solution.py:90
  16.6 14.0 %collective-permute-start.1 = (bf16[256,512]{1,0:T(8,128)(2,1)S(1)}, bf16[256,512]{1,0:T(8,128)(2,1)S(1)}, u32[]{:S(2)}, u32[]{:S(2)}) collective-permute-start(bf16[256,512]{1,0:T(8,128)(2,1)S(1)} %pad_maximum_fusion.5), channel_id=1, source_target_pairs={{0,32},{1,257},{2,34},{3,259},{4,36},{5,261},{6,38},{7,263},{8,40}... | collective-permute-start | bytes 786440 | tf_op jit(solution)/shard_map/ppermute | solution.py:90
  30.7 12.6 %collective-permute-start.2 = (bf16[512,512]{1,0:T(8,128)(2,1)S(1)}, bf16[512,512]{1,0:T(8,128)(2,1)S(1)}, u32[]{:S(2)}, u32[]{:S(2)}) collective-permute-start(bf16[512,512]{1,0:T(8,128)(2,1)S(1)} %pad_maximum_fusion.3), channel_id=1, source_target_pairs={{0,256},{1,33},{2,258},{3,35},{4,260},{5,37},{6,262},{7,39},{8,264... | collective-permute-start | bytes 1572872 | tf_op jit(solution)/shard_map/ppermute | solution.py:90
  43.3 16.7 %collective-permute-start.3 = (bf16[1024,512]{1,0:T(8,128)(2,1)S(1)}, bf16[1024,512]{1,0:T(8,128)(2,1)S(1)}, u32[]{:S(2)}, u32[]{:S(2)}) collective-permute-start(bf16[1024,512]{1,0:T(8,128)(2,1)S(1)} %pad_maximum_fusion.1), channel_id=1, source_target_pairs={{0,128},{1,17},{2,130},{3,19},{4,132},{5,21},{6,134},{7,23},{8,136... | collective-permute-start | bytes 3145736 | tf_op jit(solution)/shard_map/ppermute | solution.py:90
  61.1 1.9 copy-start.5
  63.0 29.7 %copy-start.2 = (bf16[128,256]{1,0:T(8,128)(2,1)S(1)}, bf16[128,256]{1,0:T(8,128)(2,1)}, u32[]{:S(2)}) copy-start(bf16[128,256]{1,0:T(8,128)(2,1)} %q_ref.1) | copy-start | bytes 196612
  63.1 29.7 %copy-start.3 = (bf16[128,256]{1,0:T(8,128)(2,1)S(1)}, bf16[128,256]{1,0:T(8,128)(2,1)}, u32[]{:S(2)}) copy-start(bf16[128,256]{1,0:T(8,128)(2,1)} %do_ref.1) | copy-start | bytes 196612
  63.1 29.7 %copy-start.4 = (bf16[128,256]{1,0:T(8,128)(2,1)S(1)}, bf16[128,256]{1,0:T(8,128)(2,1)}, u32[]{:S(2)}) copy-start(bf16[128,256]{1,0:T(8,128)(2,1)} %o_ref.1) | copy-start | bytes 196612
  63.1 28.3 %collective-permute-start.4 = (bf16[2048,512]{1,0:T(8,128)(2,1)}, bf16[2048,512]{1,0:T(8,128)(2,1)S(1)}, u32[]{:S(2)}, u32[]{:S(2)}) collective-permute-start(bf16[2048,512]{1,0:T(8,128)(2,1)} %get-tuple-element.17), channel_id=1, source_target_pairs={{0,16},{1,129},{2,18},{3,131},{4,20},{5,133},{6,22},{7,135},{8,24}... | collective-permute-start | bytes 6291464 | tf_op jit(solution)/shard_map/ppermute | solution.py:90
  100.1 27.9 %collective-permute-start.5 = (bf16[2048,512]{1,0:T(8,128)(2,1)S(1)}, bf16[2048,512]{1,0:T(8,128)(2,1)S(1)}, u32[]{:S(2)}, u32[]{:S(2)}) collective-permute-start(bf16[2048,512]{1,0:T(8,128)(2,1)S(1)} %slice.66), channel_id=1, source_target_pairs={{0,16},{1,129},{2,18},{3,131},{4,20},{5,133},{6,22},{7,135},{8,24}... | collective-permute-start | bytes 6291464 | tf_op jit(solution)/shard_map/ppermute | solution.py:90
  128.7 16.7 %collective-permute-start.6 = (bf16[1024,512]{1,0:T(8,128)(2,1)S(1)}, bf16[1024,512]{1,0:T(8,128)(2,1)S(1)}, u32[]{:S(2)}, u32[]{:S(2)}) collective-permute-start(bf16[1024,512]{1,0:T(8,128)(2,1)S(1)} %slice.125), channel_id=1, source_target_pairs={{0,128},{1,17},{2,130},{3,19},{4,132},{5,21},{6,134},{7,23},{8,136... | collective-permute-start | bytes 3145736 | tf_op jit(solution)/shard_map/ppermute | solution.py:90
  145.8 12.6 %collective-permute-start.7 = (bf16[512,512]{1,0:T(8,128)(2,1)S(1)}, bf16[512,512]{1,0:T(8,128)(2,1)S(1)}, u32[]{:S(2)}, u32[]{:S(2)}) collective-permute-start(bf16[512,512]{1,0:T(8,128)(2,1)S(1)} %slice.127), channel_id=1, source_target_pairs={{0,256},{1,33},{2,258},{3,35},{4,260},{5,37},{6,262},{7,39},{8,264... | collective-permute-start | bytes 1572872 | tf_op jit(solution)/shard_map/ppermute | solution.py:90
  158.6 11.1 %collective-permute-start.8 = (bf16[256,512]{1,0:T(8,128)(2,1)S(1)}, bf16[256,512]{1,0:T(8,128)(2,1)S(1)}, u32[]{:S(2)}, u32[]{:S(2)}) collective-permute-start(bf16[256,512]{1,0:T(8,128)(2,1)S(1)} %slice.129), channel_id=1, source_target_pairs={{0,32},{1,257},{2,34},{3,259},{4,36},{5,261},{6,38},{7,263},{8,40}... | collective-permute-start | bytes 786440 | tf_op jit(solution)/shard_map/ppermute | solution.py:90
  169.8 12.6 %collective-permute-start.9 = (bf16[128,512]{1,0:T(8,128)(2,1)S(1)}, bf16[128,512]{1,0:T(8,128)(2,1)S(1)}, u32[]{:S(2)}, u32[]{:S(2)}) collective-permute-start(bf16[128,512]{1,0:T(8,128)(2,1)S(1)} %slice.131), channel_id=1, source_target_pairs={{0,64},{1,65},{2,66},{3,67},{4,68},{5,69},{6,70},{7,71},{8,72},{9,... | collective-permute-start | bytes 393224 | tf_op jit(solution)/shard_map/ppermute | solution.py:90
  182.5 11.6 %collective-permute-start.10 = (bf16[128,768]{1,0:T(8,128)(2,1)S(1)}, bf16[128,768]{1,0:T(8,128)(2,1)S(1)}, u32[]{:S(2)}, u32[]{:S(2)}) collective-permute-start(bf16[128,768]{1,0:T(8,128)(2,1)S(1)} %get-tuple-element.31), channel_id=1, source_target_pairs={{0,64},{1,65},{2,66},{3,67},{4,68},{5,69},{6,70},{7,71},{8,72},{9,... | collective-permute-start | bytes 589832 | tf_op jit(solution)/shard_map/ppermute | solution.py:90
  194.1 20.6 %collective-permute-start.11 = (bf16[256,768]{1,0:T(8,128)(2,1)S(1)}, bf16[256,768]{1,0:T(8,128)(2,1)S(1)}, u32[]{:S(2)}, u32[]{:S(2)}) collective-permute-start(bf16[256,768]{1,0:T(8,128)(2,1)S(1)} %pad_maximum_fusion.4), channel_id=1, source_target_pairs={{0,32},{1,257},{2,34},{3,259},{4,36},{5,261},{6,38},{7,263},{8,40}... | collective-permute-start | bytes 1179656 | tf_op jit(solution)/shard_map/ppermute | solution.py:90
  214.7 15.4 %collective-permute-start.12 = (bf16[512,768]{1,0:T(8,128)(2,1)S(1)}, bf16[512,768]{1,0:T(8,128)(2,1)S(1)}, u32[]{:S(2)}, u32[]{:S(2)}) collective-permute-start(bf16[512,768]{1,0:T(8,128)(2,1)S(1)} %pad_maximum_fusion.2), channel_id=1, source_target_pairs={{0,256},{1,33},{2,258},{3,35},{4,260},{5,37},{6,262},{7,39},{8,264... | collective-permute-start | bytes 2359304 | tf_op jit(solution)/shard_map/ppermute | solution.py:90
  230.2 31.4 %collective-permute-start.13 = (bf16[1024,768]{1,0:T(8,128)(2,1)S(1)}, bf16[1024,768]{1,0:T(8,128)(2,1)S(1)}, u32[]{:S(2)}, u32[]{:S(2)}) collective-permute-start(bf16[1024,768]{1,0:T(8,128)(2,1)S(1)} %pad_maximum_fusion), channel_id=1, source_target_pairs={{0,128},{1,17},{2,130},{3,19},{4,132},{5,21},{6,134},{7,23},{8,136... | collective-permute-start | bytes 4718600 | tf_op jit(solution)/shard_map/ppermute | solution.py:90
  261.8 39.2 %collective-permute-start.14 = (bf16[2048,768]{1,0:T(8,128)(2,1)S(1)}, bf16[2048,768]{1,0:T(8,128)(2,1)S(1)}, u32[]{:S(2)}, u32[]{:S(2)}) collective-permute-start(bf16[2048,768]{1,0:T(8,128)(2,1)S(1)} %get-tuple-element.15), channel_id=1, source_target_pairs={{0,16},{1,129},{2,18},{3,131},{4,20},{5,133},{6,22},{7,135},{8,24}... | collective-permute-start | bytes 9437192 | tf_op jit(solution)/shard_map/ppermute | solution.py:90
  301.0 0.9 copy-start.6
  301.0 1.0 copy-start.7
  301.0 1.0 copy-start.8
  308.0 4.6 %collective-permute-start.15 = (bf16[2048,256]{1,0:T(8,128)(2,1)S(1)}, bf16[2048,256]{1,0:T(8,128)(2,1)S(1)}, u32[]{:S(2)}, u32[]{:S(2)}) collective-permute-start(bf16[2048,256]{1,0:T(8,128)(2,1)S(1)} %bitcast.17), channel_id=1, source_target_pairs={{0,1},{1,0},{2,3},{3,2},{4,5},{5,4},{6,7},{7,6},{8,9},{9,8},{10,11... | collective-permute-start | bytes 3145736 | tf_op jit(solution)/shard_map/ppermute | solution.py:129
  312.5 49.5 %copy-start.1 = (s32[32,32]{1,0:T(8,128)S(1)}, s32[32,32]{1,0:T(8,128)}, u32[]{:S(2)}) copy-start(s32[32,32]{1,0:T(8,128)} %param.14) | copy-start | bytes 12292
  312.9 15.9 %collective-permute-start.16 = (bf16[1024,256]{1,0:T(8,128)(2,1)S(1)}, bf16[1024,256]{1,0:T(8,128)(2,1)S(1)}, u32[]{:S(2)}, u32[]{:S(2)}) collective-permute-start(bf16[1024,256]{1,0:T(8,128)(2,1)S(1)} %slice.126), channel_id=1, source_target_pairs={{0,4},{1,5},{2,6},{3,7},{4,0},{5,1},{6,2},{7,3},{8,12},{9,13},{10,... | collective-permute-start | bytes 1572872 | tf_op jit(solution)/shard_map/ppermute | solution.py:129
  328.9 10.9 %collective-permute-start.17 = (bf16[512,256]{1,0:T(8,128)(2,1)S(1)}, bf16[512,256]{1,0:T(8,128)(2,1)S(1)}, u32[]{:S(2)}, u32[]{:S(2)}) collective-permute-start(bf16[512,256]{1,0:T(8,128)(2,1)S(1)} %slice.128), channel_id=1, source_target_pairs={{0,8},{1,9},{2,10},{3,11},{4,12},{5,13},{6,14},{7,15},{8,0},{9,1},... | collective-permute-start | bytes 786440 | tf_op jit(solution)/shard_map/ppermute | solution.py:129
  339.9 21.4 %collective-permute-start.18 = (bf16[256,256]{1,0:T(8,128)(2,1)S(1)}, bf16[256,256]{1,0:T(8,128)(2,1)S(1)}, u32[]{:S(2)}, u32[]{:S(2)}) collective-permute-start(bf16[256,256]{1,0:T(8,128)(2,1)S(1)} %slice.130), channel_id=1, source_target_pairs={{0,2},{1,3},{2,0},{3,1},{4,6},{5,7},{6,4},{7,5},{8,10},{9,11},{10,... | collective-permute-start | bytes 393224 | tf_op jit(solution)/shard_map/ppermute | solution.py:129

commit v9 on v8

--- a/solution.py
+++ b/solution.py
@@ -15,6 +15,8 @@
 NEG_FILL = -1e30
 GATHER_ORDERS = ((4, 2, 16, 8, 1), (4, 16, 2, 1, 8))
 SCATTER_ORDERS = tuple(tuple(reversed(order)) for order in GATHER_ORDERS)
+HEAD_GATHER_ORDERS = ((4, 2, 16, 8), (4, 16, 2, 8))
+HEAD_SCATTER_ORDERS = tuple(tuple(reversed(order)) for order in HEAD_GATHER_ORDERS)
 TP_ORDER = (1, 4, 8, 2)
 
 
@@ -26,16 +28,19 @@
     return lax.dot_general(a, b, (((0,), (0,)), ((), ())), preferred_element_type=jnp.float32)
 
 
-def attention_kernel(head_count, score_scale, mask_ref, q_ref, do_ref, o_ref, kv_ref, dq_ref, dkdv_ref):
-    width = head_count * HD
+def attention_kernel(slab_count, score_scale, mask_ref, q_ref, do_ref, o_ref, kv_ref, dq_ref, dkdv_ref):
     key_rows = kv_ref.shape[0]
-    block_count = key_rows // BLK
-    allowed = mask_ref[0:1, :] > 0
-    for h in range(head_count):
-        cols = slice(h * HD, (h + 1) * HD)
-        q_h = q_ref[:, cols]
-        do_h = do_ref[:, cols]
-        k_h = kv_ref[:, cols]
+    rows = q_ref.shape[0] // slab_count
+    block = rows * slab_count
+    block_count = key_rows // block
+    k_h = kv_ref[:, 0:HD]
+    dk_total = jnp.zeros((key_rows, HD), jnp.float32)
+    dv_total = jnp.zeros((key_rows, HD), jnp.float32)
+    for a in range(slab_count):
+        mine = slice(a * rows, (a + 1) * rows)
+        allowed = mask_ref[a : a + 1, :] > 0
+        q_h = q_ref[mine, :]
+        do_h = do_ref[mine, :]
         scores = _nt(q_h, k_h) * score_scale
         masked = jnp.where(allowed, scores, NEG_FILL)
         row_max = jnp.max(masked, axis=1, keepdims=True)
@@ -43,39 +48,40 @@
         log_total = row_max + jnp.log(row_sum)
         probs = jnp.where(allowed, jnp.exp(masked - log_total), 0.0)
         row_delta = jnp.sum(
-            do_h.astype(jnp.float32) * o_ref[:, cols].astype(jnp.float32), axis=1, keepdims=True
+            do_h.astype(jnp.float32) * o_ref[mine, :].astype(jnp.float32), axis=1, keepdims=True
         )
-        dprobs = _nt(do_h, kv_ref[:, pl.ds(width + h * HD, HD)])
+        dprobs = _nt(do_h, kv_ref[:, HD : 2 * HD])
         score_gradient = (probs * (dprobs - row_delta) * score_scale).astype(jnp.bfloat16)
-        dq_ref[:, cols] = jnp.dot(score_gradient, k_h, preferred_element_type=jnp.float32)
-        dk = _tn(score_gradient, q_h).astype(jnp.bfloat16)
-        dv = _tn(probs.astype(jnp.bfloat16), do_h).astype(jnp.bfloat16)
-        for p in range(block_count):
-            src = slice(p * BLK, (p + 1) * BLK)
-            dst = slice((block_count - 1 - p) * BLK, (block_count - p) * BLK)
-            dkdv_ref[dst, cols] = dk[src]
-            dkdv_ref[dst, pl.ds(width + h * HD, HD)] = dv[src]
-
-
-def slab_attention(mask, queries, output_grad, attn_output, key_value):
-    slab_rows, width = queries.shape
-    head_count = width // HD
+        dq_ref[mine, :] = jnp.dot(score_gradient, k_h, preferred_element_type=jnp.float32)
+        dk_total = dk_total + _tn(score_gradient, q_h)
+        dv_total = dv_total + _tn(probs.astype(jnp.bfloat16), do_h)
+    dk = dk_total.astype(jnp.bfloat16)
+    dv = dv_total.astype(jnp.bfloat16)
+    for p in range(block_count):
+        src = slice(p * block, (p + 1) * block)
+        dst = slice((block_count - 1 - p) * block, (block_count - p) * block)
+        dkdv_ref[dst, 0:HD] = dk[src]
+        dkdv_ref[dst, HD : 2 * HD] = dv[src]
+
+
+def slab_attention(mask, queries, output_grad, attn_output, key_value, slab_count):
+    query_rows = queries.shape[0]
     key_rows = key_value.shape[0]
     vmem = pl.BlockSpec(memory_space=pltpu.VMEM)
-    flops = 2 * slab_rows * key_rows * width * 5
+    flops = 2 * query_rows * key_rows * HD * 5
     return pl.pallas_call(
-        functools.partial(attention_kernel, head_count, 1.0 / math.sqrt(HD)),
+        functools.partial(attention_kernel, slab_count, 1.0 / math.sqrt(HD)),
         out_shape=(
-            jax.ShapeDtypeStruct((slab_rows, width), jnp.float32),
-            jax.ShapeDtypeStruct((key_rows, 2 * width), jnp.bfloat16),
+            jax.ShapeDtypeStruct((query_rows, HD), jnp.float32),
+            jax.ShapeDtypeStruct((key_rows, 2 * HD), jnp.bfloat16),
         ),
         in_specs=[vmem] * 5,
         out_specs=(vmem, vmem),
         compiler_params=pltpu.CompilerParams(vmem_limit_bytes=48 * 1024 * 1024),
         cost_estimate=pl.CostEstimate(
             flops=flops,
-            transcendentals=2 * slab_rows * key_rows * head_count,
-            bytes_accessed=key_rows * width * 2 * 4,
+            transcendentals=2 * query_rows * key_rows,
+            bytes_accessed=key_rows * HD * 2 * 4,
         ),
     )(mask, queries, output_grad, attn_output, key_value)
 
@@ -133,25 +139,56 @@
     return held
 
 
+def xor_of_position(distances, count):
+    position = jnp.arange(count, dtype=jnp.int32)
+    return sum(((position >> r) & 1) * d for r, d in enumerate(distances))
+
+
 def per_device(
     queries, key_states, value_states, attn_output, output_grad, block_map, w_query, w_key, w_value
 ):
     slab_rows, width = queries.shape
-    ctx_count, tp_count = lax.axis_size("ctx"), lax.axis_size("tp")
+    ctx_count = lax.axis_size("ctx")
     me = lax.axis_index("ctx")
+    tp_count = lax.axis_size("tp")
     me_tp = lax.axis_index("tp")
     core = me_tp % 2
-    row_map = lax.dynamic_index_in_dim(block_map, me * slab_rows // BLK, axis=0, keepdims=False)
+    odd = me % 2
+    low = odd == 0
+    stacked = jnp.stack([queries, output_grad, attn_output, key_states, value_states])
+    head_0, head_1 = stacked[:, :, :HD], stacked[:, :, HD : 2 * HD]
+    kept = jnp.where(low, head_0, head_1)
+    given = jnp.where(low, head_1, head_0)
+    got = _pair_permute(given, (1, 1))
+    both = jnp.where(low, jnp.concatenate([kept, got], 1), jnp.concatenate([got, kept], 1))
+    pair_q, pair_do, pair_o, pair_k, pair_v = (both[i] for i in range(5))
+    pair_kv = jnp.concatenate([pair_k, pair_v], axis=1)
+    gathered = concat_gather(pair_kv, HEAD_GATHER_ORDERS)
+    group_count = ctx_count // 2
+    holder = me ^ per_core(core, [xor_of_position(o, group_count) for o in HEAD_GATHER_ORDERS])
+    base = holder - holder % 2
+    key_slabs = jnp.stack([base, base + 1], axis=1).reshape(-1) * slab_rows // BLK
+    first = (me - odd) * slab_rows // BLK
+    mask_rows = jnp.stack([block_map[first][key_slabs], block_map[first + 1][key_slabs]])
+    mask = jnp.repeat(mask_rows.astype(jnp.float32), BLK, axis=1)
+    mask = jnp.concatenate([mask, jnp.zeros((6, mask.shape[1]), jnp.float32)], axis=0)
+    pair_dq, part_grads = slab_attention(mask, pair_q, pair_do, pair_o, gathered, 2)
+    finished = halving_reduce(part_grads, HEAD_SCATTER_ORDERS).astype(jnp.bfloat16)
+    pair_grads = jnp.concatenate([pair_dq.astype(jnp.bfloat16), finished], axis=1)
+    lower, upper = pair_grads[:slab_rows], pair_grads[slab_rows:]
+    mine = jnp.where(low, lower, upper)
+    back = _pair_permute(jnp.where(low, upper, lower), (1, 1))
+    first_head = jnp.where(low, mine, back)
+    second_head = jnp.where(low, back, mine)
+    own_grads = jnp.concatenate(
+        [
+            first_head[:, 0:HD], second_head[:, 0:HD],
+            first_head[:, HD : 2 * HD], second_head[:, HD : 2 * HD],
+            first_head[:, 2 * HD : 3 * HD], second_head[:, 2 * HD : 3 * HD],
+        ],
+        axis=1,
+    )
     gather_at = per_core(core, [gather_positions(me, o, ctx_count) for o in GATHER_ORDERS])
-    slab_at = jnp.argsort(gather_at)
-    mask = jnp.broadcast_to(
-        jnp.repeat(row_map[slab_at].astype(jnp.float32), BLK)[None, :], (8, ctx_count * slab_rows)
-    )
-    key_value = jnp.concatenate([key_states, value_states], axis=1)
-    gathered = concat_gather(key_value, GATHER_ORDERS)
-    dq_total, part_grads = slab_attention(mask, queries, output_grad, attn_output, gathered)
-    finished = halving_reduce(part_grads, SCATTER_ORDERS).astype(jnp.bfloat16)
-    own_grads = jnp.concatenate([dq_total.astype(jnp.bfloat16), finished], axis=1)
     gradients = concat_gather(own_grads, GATHER_ORDERS)
     projections = jnp.concatenate([w_query, w_key, w_value], axis=1)
     term = lax.dot_general(

time: 363 us -> 347 us (0.956)
  the two profiles are of different devices: /device:TPU:172 before, /device:TPU:6 now
where the time goes in v9:
time: 347 us; the launch traced here: 340 us
  waiting for transfers between devices  233 us (67%)
  starting transfers between devices  69.2 us (20%)
  local copies, waits for them, and re-layouts  21.7 us (6%)
  matrix products  6.02 us (2%)
  Pallas kernels  5.06 us (1%)
  other arithmetic  4.82 us (1%)
    ppermute x15, waiting for transfers between devices, _pair_permute(): return lax.ppermute(value, ('ctx', 'tp'), pairs)  208 us
    ppermute x15, starting transfers between devices, _pair_permute(): return lax.ppermute(value, ('ctx', 'tp'), pairs)  46.8 us
    ppermute x4, waiting for transfers between devices, tp_halving_reduce(): lax.ppermute(held[:half].astype(wire), 'tp', [(i, i ^ distance) for i in...  24.8 us
    ppermute x4, starting transfers between devices, tp_halving_reduce(): lax.ppermute(held[:half].astype(wire), 'tp', [(i, i ^ distance) for i in...  22.4 us
    unnamed x30, local copies, waits for them, and re-layouts  10.3 us
  transfers between devices with their start and end apart: 19, of which 19 were waited for; matrix products, arithmetic and copies ran while one was open for 2% of the time, Pallas kernels for 0%

profile of v9, /device:TPU:6, one launch (start us, length us, event | category | flops | bytes accessed | tf_op | source)
XLA Modules:
  0.0 340.5 jit_solution(13557721041378057802)
XLA Ops:
  0.8 0.8 constant_dynamic-update-slice_fusion.3
  4.3 3.8 %collective-permute-start = (bf16[5,128,128]{2,1,0:T(8,128)(2,1)S(1)}, bf16[5,128,128]{2,1,0:T(8,128)(2,1)S(1)}, u32[]{:S(2)}, u32[]{:S(2)}) collective-permute-start(bf16[5,128,128]{2,1,0:T(8,128)(2,1)S(1)} %get-tuple-element.27), channel_id=1, source_target_pairs={{0,16},{1,17},{2,18},{3,19},{4,20},{5,21},{6,22},{7,23},{8,24},{9,... | collective-permute-start | bytes 491528 | tf_op jit(solution)/shard_map/ppermute | solution.py:96
  8.1 4.2 %collective-permute-done = bf16[5,128,128]{2,1,0:T(8,128)(2,1)S(1)} collective-permute-done((bf16[5,128,128]{2,1,0:T(8,128)(2,1)S(1)}, bf16[5,128,128]{2,1,0:T(8,128)(2,1)S(1)}, u32[]{:S(2)}, u32[]{:S(2)}) %collective-permute-start) | collective-permute-done | bytes 163872 | tf_op jit(solution)/shard_map/ppermute | solution.py:96
  12.4 9.1 %collective-permute-start.1 = (bf16[256,256]{1,0:T(8,128)(2,1)S(1)}, bf16[256,256]{1,0:T(8,128)(2,1)S(1)}, u32[]{:S(2)}, u32[]{:S(2)}) collective-permute-start(bf16[256,256]{1,0:T(8,128)(2,1)S(1)} %get-tuple-element.32), channel_id=1, source_target_pairs={{0,64},{1,65},{2,66},{3,67},{4,68},{5,69},{6,70},{7,71},{8,72},{9,... | collective-permute-start | bytes 393224 | tf_op jit(solution)/shard_map/ppermute | solution.py:96
  21.5 11.2 %collective-permute-done.1 = bf16[256,256]{1,0:T(8,128)(2,1)S(1)} collective-permute-done((bf16[256,256]{1,0:T(8,128)(2,1)S(1)}, bf16[256,256]{1,0:T(8,128)(2,1)S(1)}, u32[]{:S(2)}, u32[]{:S(2)}) %collective-permute-start.1) | collective-permute-done | bytes 131104 | tf_op jit(solution)/shard_map/ppermute | solution.py:96
  32.8 1.9 collective-permute-start.2
  34.8 1.2 sort.17
  36.1 8.3 %collective-permute-done.2 = bf16[512,256]{1,0:T(8,128)(2,1)S(1)} collective-permute-done((bf16[512,256]{1,0:T(8,128)(2,1)S(1)}, bf16[512,256]{1,0:T(8,128)(2,1)S(1)}, u32[]{:S(2)}, u32[]{:S(2)}) %collective-permute-start.2) | collective-permute-done | bytes 262176 | tf_op jit(solution)/shard_map/ppermute | solution.py:96
  44.4 3.3 collective-permute-start.3
  47.8 9.2 %collective-permute-done.3 = bf16[1024,256]{1,0:T(8,128)(2,1)S(1)} collective-permute-done((bf16[1024,256]{1,0:T(8,128)(2,1)S(1)}, bf16[1024,256]{1,0:T(8,128)(2,1)S(1)}, u32[]{:S(2)}, u32[]{:S(2)}) %collective-permute-start.3) | collective-permute-done | bytes 524320 | tf_op jit(solution)/shard_map/ppermute | solution.py:96
  57.0 1.1 pad_maximum_fusion.1
  58.1 2.7 collective-permute-start.4
  63.5 21.9 %collective-permute-done.4 = bf16[2048,256]{1,0:T(8,128)(2,1)} collective-permute-done((bf16[2048,256]{1,0:T(8,128)(2,1)}, bf16[2048,256]{1,0:T(8,128)(2,1)}, u32[]{:S(2)}, u32[]{:S(2)}) %collective-permute-start.4) | collective-permute-done | bytes 1048608 | tf_op jit(solution)/shard_map/ppermute | solution.py:96
  85.4 1.3 constant_dynamic-update-slice_fusion.5.kv_ref
  86.7 5.1 %shard_map.91 = (f32[256,128]{1,0:T(8,128)S(1)}, bf16[4096,256]{1,0:T(8,128)(2,1)S(1)}) custom-call(f32[8,4096]{1,0:T(8,128)S(1)} %concatenate.55.mask_ref, bf16[256,128]{1,0:T(8,128)(2,1)S(1)} %get-tuple-element.25.q_ref, bf16[256,128]{1,0:T(8,128)(2,1)S(1)} %get-tuple-element.24.do_ref, bf16[256,128]{1,0:T(8,128)(2,1)S(1)} %get-tuple-element.23.o_ref, ...), custom_call_target="tpu_custom_call" | custom-call | flops 1342177280 | bytes 4194304 | tf_op jit(solution)/shard_map/pallas_call | solution.py:72
  91.9 2.8 collective-permute-start.5
  94.7 23.4 %collective-permute-done.5 = bf16[2048,256]{1,0:T(8,128)(2,1)S(1)} collective-permute-done((bf16[2048,256]{1,0:T(8,128)(2,1)S(1)}, bf16[2048,256]{1,0:T(8,128)(2,1)S(1)}, u32[]{:S(2)}, u32[]{:S(2)}) %collective-permute-start.5) | collective-permute-done | bytes 1048608 | tf_op jit(solution)/shard_map/ppermute | solution.py:96
  118.4 3.5 %collective-permute-start.6 = (bf16[1024,256]{1,0:T(8,128)(2,1)S(1)}, bf16[1024,256]{1,0:T(8,128)(2,1)S(1)}, u32[]{:S(2)}, u32[]{:S(2)}) collective-permute-start(bf16[1024,256]{1,0:T(8,128)(2,1)S(1)} %slice.235), channel_id=1, source_target_pairs={{0,256},{1,33},{2,258},{3,35},{4,260},{5,37},{6,262},{7,39},{8,264... | collective-permute-start | bytes 1572872 | tf_op jit(solution)/shard_map/ppermute | solution.py:96
  121.9 9.1 %collective-permute-done.6 = bf16[1024,256]{1,0:T(8,128)(2,1)S(1)} collective-permute-done((bf16[1024,256]{1,0:T(8,128)(2,1)S(1)}, bf16[1024,256]{1,0:T(8,128)(2,1)S(1)}, u32[]{:S(2)}, u32[]{:S(2)}) %collective-permute-start.6) | collective-permute-done | bytes 524320 | tf_op jit(solution)/shard_map/ppermute | solution.py:96
  131.1 1.9 collective-permute-start.7
  133.1 8.3 %collective-permute-done.7 = bf16[512,256]{1,0:T(8,128)(2,1)S(1)} collective-permute-done((bf16[512,256]{1,0:T(8,128)(2,1)S(1)}, bf16[512,256]{1,0:T(8,128)(2,1)S(1)}, u32[]{:S(2)}, u32[]{:S(2)}) %collective-permute-start.7) | collective-permute-done | bytes 262176 | tf_op jit(solution)/shard_map/ppermute | solution.py:96
  141.5 1.9 collective-permute-start.8
  143.4 16.1 %collective-permute-done.8 = bf16[256,256]{1,0:T(8,128)(2,1)S(1)} collective-permute-done((bf16[256,256]{1,0:T(8,128)(2,1)S(1)}, bf16[256,256]{1,0:T(8,128)(2,1)S(1)}, u32[]{:S(2)}, u32[]{:S(2)}) %collective-permute-start.8) | collective-permute-done | bytes 131104 | tf_op jit(solution)/shard_map/ppermute | solution.py:96
  159.6 1.9 collective-permute-start.9
  161.5 4.7 %collective-permute-done.9 = bf16[128,384]{1,0:T(8,128)(2,1)S(1)} collective-permute-done((bf16[128,384]{1,0:T(8,128)(2,1)S(1)}, bf16[128,384]{1,0:T(8,128)(2,1)S(1)}, u32[]{:S(2)}, u32[]{:S(2)}) %collective-permute-start.9) | collective-permute-done | bytes 98336 | tf_op jit(solution)/shard_map/ppermute | solution.py:96
  170.0 1.9 collective-permute-start.10
  171.9 19.9 %collective-permute-done.10 = bf16[128,768]{1,0:T(8,128)(2,1)S(1)} collective-permute-done((bf16[128,768]{1,0:T(8,128)(2,1)S(1)}, bf16[128,768]{1,0:T(8,128)(2,1)S(1)}, u32[]{:S(2)}, u32[]{:S(2)}) %collective-permute-start.10) | collective-permute-done | bytes 196640 | tf_op jit(solution)/shard_map/ppermute | solution.py:96
  191.8 1.9 collective-permute-start.11
  193.8 8.8 %collective-permute-done.11 = bf16[256,768]{1,0:T(8,128)(2,1)S(1)} collective-permute-done((bf16[256,768]{1,0:T(8,128)(2,1)S(1)}, bf16[256,768]{1,0:T(8,128)(2,1)S(1)}, u32[]{:S(2)}, u32[]{:S(2)}) %collective-permute-start.11) | collective-permute-done | bytes 393248 | tf_op jit(solution)/shard_map/ppermute | solution.py:96
  202.7 4.2 %collective-permute-start.12 = (bf16[512,768]{1,0:T(8,128)(2,1)S(1)}, bf16[512,768]{1,0:T(8,128)(2,1)S(1)}, u32[]{:S(2)}, u32[]{:S(2)}) collective-permute-start(bf16[512,768]{1,0:T(8,128)(2,1)S(1)} %pad_maximum_fusion.2), channel_id=1, source_target_pairs={{0,256},{1,33},{2,258},{3,35},{4,260},{5,37},{6,262},{7,39},{8,264... | collective-permute-start | bytes 2359304 | tf_op jit(solution)/shard_map/ppermute | solution.py:96
  206.9 11.2 %collective-permute-done.12 = bf16[512,768]{1,0:T(8,128)(2,1)S(1)} collective-permute-done((bf16[512,768]{1,0:T(8,128)(2,1)S(1)}, bf16[512,768]{1,0:T(8,128)(2,1)S(1)}, u32[]{:S(2)}, u32[]{:S(2)}) %collective-permute-start.12) | collective-permute-done | bytes 786464 | tf_op jit(solution)/shard_map/ppermute | solution.py:96
  218.2 3.7 %collective-permute-start.13 = (bf16[1024,768]{1,0:T(8,128)(2,1)S(1)}, bf16[1024,768]{1,0:T(8,128)(2,1)S(1)}, u32[]{:S(2)}, u32[]{:S(2)}) collective-permute-start(bf16[1024,768]{1,0:T(8,128)(2,1)S(1)} %pad_maximum_fusion), channel_id=1, source_target_pairs={{0,128},{1,17},{2,130},{3,19},{4,132},{5,21},{6,134},{7,23},{8,136... | collective-permute-start | bytes 4718600 | tf_op jit(solution)/shard_map/ppermute | solution.py:96
  223.4 1.0 constant_dynamic-update-slice_fusion.17
  224.4 16.1 %collective-permute-done.13 = bf16[1024,768]{1,0:T(8,128)(2,1)S(1)} collective-permute-done((bf16[1024,768]{1,0:T(8,128)(2,1)S(1)}, bf16[1024,768]{1,0:T(8,128)(2,1)S(1)}, u32[]{:S(2)}, u32[]{:S(2)}) %collective-permute-start.13) | collective-permute-done | bytes 1572896 | tf_op jit(solution)/shard_map/ppermute | solution.py:96
  240.5 1.4 constant_dynamic-update-slice_fusion.16
  241.9 2.2 collective-permute-start.14
  245.3 36.0 %collective-permute-done.14 = bf16[2048,768]{1,0:T(8,128)(2,1)S(1)} collective-permute-done((bf16[2048,768]{1,0:T(8,128)(2,1)}, bf16[2048,768]{1,0:T(8,128)(2,1)S(1)}, u32[]{:S(2)}, u32[]{:S(2)}) %collective-permute-start.14) | collective-permute-done | bytes 3145760 | tf_op jit(solution)/shard_map/ppermute | solution.py:96
  281.3 1.9 constant_dynamic-update-slice_fusion.26
  283.2 6.0 %convolution_convert_fusion = bf16[4096,256]{1,0:T(8,128)(2,1)} fusion(bf16[4096,768]{1,0:T(8,128)(2,1)} %constant_dynamic-update-slice_fusion.26, bf16[256,256]{1,0:T(8,128)(2,1)S(1)} %copy-done.1, bf16[256,256]{1,0:T(8,128)(2,1)S(1)} %copy-done.2, bf16[256,256]{1,0:T(8,128)(2,1)S(1)} %copy-done.3), kind=kOutput, calls=%fused_computation.4 | convolution fusion | flops 1612840960 | bytes 8781824 | tf_op jit(solution)/shard_map/dot_general | solution.py:194
  289.2 2.3 gather_fusion.3
  292.0 2.0 collective-permute-start.15
  294.0 2.5 collective-permute-done.15
  296.9 3.5 %collective-permute-start.16 = (bf16[1024,256]{1,0:T(8,128)(2,1)S(1)}, bf16[1024,256]{1,0:T(8,128)(2,1)S(1)}, u32[]{:S(2)}, u32[]{:S(2)}) collective-permute-start(bf16[1024,256]{1,0:T(8,128)(2,1)S(1)} %slice.234), channel_id=1, source_target_pairs={{0,4},{1,5},{2,6},{3,7},{4,0},{5,1},{6,2},{7,3},{8,12},{9,13},{10,... | collective-permute-start | bytes 1572872 | tf_op jit(solution)/shard_map/ppermute | solution.py:135
  300.4 12.4 %collective-permute-done.16 = bf16[1024,256]{1,0:T(8,128)(2,1)S(1)} collective-permute-done((bf16[1024,256]{1,0:T(8,128)(2,1)S(1)}, bf16[1024,256]{1,0:T(8,128)(2,1)S(1)}, u32[]{:S(2)}, u32[]{:S(2)}) %collective-permute-start.16) | collective-permute-done | bytes 524320 | tf_op jit(solution)/shard_map/ppermute | solution.py:135
  312.9 5.1 %collective-permute-start.17 = (bf16[512,256]{1,0:T(8,128)(2,1)S(1)}, bf16[512,256]{1,0:T(8,128)(2,1)S(1)}, u32[]{:S(2)}, u32[]{:S(2)}) collective-permute-start(bf16[512,256]{1,0:T(8,128)(2,1)S(1)} %slice.236), channel_id=1, source_target_pairs={{0,8},{1,9},{2,10},{3,11},{4,12},{5,13},{6,14},{7,15},{8,0},{9,1},... | collective-permute-start | bytes 786440 | tf_op jit(solution)/shard_map/ppermute | solution.py:135
  318.0 5.8 %collective-permute-done.17 = bf16[512,256]{1,0:T(8,128)(2,1)S(1)} collective-permute-done((bf16[512,256]{1,0:T(8,128)(2,1)S(1)}, bf16[512,256]{1,0:T(8,128)(2,1)S(1)}, u32[]{:S(2)}, u32[]{:S(2)}) %collective-permute-start.17) | collective-permute-done | bytes 262176 | tf_op jit(solution)/shard_map/ppermute | solution.py:135
  323.9 11.8 %collective-permute-start.18 = (bf16[256,256]{1,0:T(8,128)(2,1)S(1)}, bf16[256,256]{1,0:T(8,128)(2,1)S(1)}, u32[]{:S(2)}, u32[]{:S(2)}) collective-permute-start(bf16[256,256]{1,0:T(8,128)(2,1)S(1)} %slice.238), channel_id=1, source_target_pairs={{0,2},{1,3},{2,0},{3,1},{4,6},{5,7},{6,4},{7,5},{8,10},{9,11},{10,... | collective-permute-start | bytes 393224 | tf_op jit(solution)/shard_map/ppermute | solution.py:135
  335.8 4.0 %collective-permute-done.18 = bf16[256,256]{1,0:T(8,128)(2,1)S(1)} collective-permute-done((bf16[256,256]{1,0:T(8,128)(2,1)S(1)}, bf16[256,256]{1,0:T(8,128)(2,1)S(1)}, u32[]{:S(2)}, u32[]{:S(2)}) %collective-permute-start.18) | collective-permute-done | bytes 131104 | tf_op jit(solution)/shard_map/ppermute | solution.py:135
  (80 shorter events, 15.5 us)
Async XLA Ops:
  4.3 8.0 %collective-permute-start = (bf16[5,128,128]{2,1,0:T(8,128)(2,1)S(1)}, bf16[5,128,128]{2,1,0:T(8,128)(2,1)S(1)}, u32[]{:S(2)}, u32[]{:S(2)}) collective-permute-start(bf16[5,128,128]{2,1,0:T(8,128)(2,1)S(1)} %get-tuple-element.27), channel_id=1, source_target_pairs={{0,16},{1,17},{2,18},{3,19},{4,20},{5,21},{6,22},{7,23},{8,24},{9,... | collective-permute-start | bytes 491528 | tf_op jit(solution)/shard_map/ppermute | solution.py:96
  12.4 20.3 %collective-permute-start.1 = (bf16[256,256]{1,0:T(8,128)(2,1)S(1)}, bf16[256,256]{1,0:T(8,128)(2,1)S(1)}, u32[]{:S(2)}, u32[]{:S(2)}) collective-permute-start(bf16[256,256]{1,0:T(8,128)(2,1)S(1)} %get-tuple-element.32), channel_id=1, source_target_pairs={{0,64},{1,65},{2,66},{3,67},{4,68},{5,69},{6,70},{7,71},{8,72},{9,... | collective-permute-start | bytes 393224 | tf_op jit(solution)/shard_map/ppermute | solution.py:96
  32.8 11.6 %collective-permute-start.2 = (bf16[512,256]{1,0:T(8,128)(2,1)S(1)}, bf16[512,256]{1,0:T(8,128)(2,1)S(1)}, u32[]{:S(2)}, u32[]{:S(2)}) collective-permute-start(bf16[512,256]{1,0:T(8,128)(2,1)S(1)} %pad_maximum_fusion.5), channel_id=1, source_target_pairs={{0,32},{1,257},{2,34},{3,259},{4,36},{5,261},{6,38},{7,263},{8,40}... | collective-permute-start | bytes 786440 | tf_op jit(solution)/shard_map/ppermute | solution.py:96
  44.4 12.6 %collective-permute-start.3 = (bf16[1024,256]{1,0:T(8,128)(2,1)S(1)}, bf16[1024,256]{1,0:T(8,128)(2,1)S(1)}, u32[]{:S(2)}, u32[]{:S(2)}) collective-permute-start(bf16[1024,256]{1,0:T(8,128)(2,1)S(1)} %pad_maximum_fusion.3), channel_id=1, source_target_pairs={{0,256},{1,33},{2,258},{3,35},{4,260},{5,37},{6,262},{7,39},{8,264... | collective-permute-start | bytes 1572872 | tf_op jit(solution)/shard_map/ppermute | solution.py:96
  58.1 27.4 %collective-permute-start.4 = (bf16[2048,256]{1,0:T(8,128)(2,1)}, bf16[2048,256]{1,0:T(8,128)(2,1)}, u32[]{:S(2)}, u32[]{:S(2)}) collective-permute-start(bf16[2048,256]{1,0:T(8,128)(2,1)} %pad_maximum_fusion.1), channel_id=1, source_target_pairs={{0,128},{1,129},{2,130},{3,131},{4,132},{5,133},{6,134},{7,135},{8... | collective-permute-start | bytes 3145736 | tf_op jit(solution)/shard_map/ppermute | solution.py:96
  91.9 26.2 %collective-permute-start.5 = (bf16[2048,256]{1,0:T(8,128)(2,1)S(1)}, bf16[2048,256]{1,0:T(8,128)(2,1)S(1)}, u32[]{:S(2)}, u32[]{:S(2)}) collective-permute-start(bf16[2048,256]{1,0:T(8,128)(2,1)S(1)} %slice.111), channel_id=1, source_target_pairs={{0,128},{1,129},{2,130},{3,131},{4,132},{5,133},{6,134},{7,135},{8... | collective-permute-start | bytes 3145736 | tf_op jit(solution)/shard_map/ppermute | solution.py:96
  118.4 12.6 %collective-permute-start.6 = (bf16[1024,256]{1,0:T(8,128)(2,1)S(1)}, bf16[1024,256]{1,0:T(8,128)(2,1)S(1)}, u32[]{:S(2)}, u32[]{:S(2)}) collective-permute-start(bf16[1024,256]{1,0:T(8,128)(2,1)S(1)} %slice.235), channel_id=1, source_target_pairs={{0,256},{1,33},{2,258},{3,35},{4,260},{5,37},{6,262},{7,39},{8,264... | collective-permute-start | bytes 1572872 | tf_op jit(solution)/shard_map/ppermute | solution.py:96
  131.1 10.3 %collective-permute-start.7 = (bf16[512,256]{1,0:T(8,128)(2,1)S(1)}, bf16[512,256]{1,0:T(8,128)(2,1)S(1)}, u32[]{:S(2)}, u32[]{:S(2)}) collective-permute-start(bf16[512,256]{1,0:T(8,128)(2,1)S(1)} %slice.237), channel_id=1, source_target_pairs={{0,32},{1,257},{2,34},{3,259},{4,36},{5,261},{6,38},{7,263},{8,40}... | collective-permute-start | bytes 786440 | tf_op jit(solution)/shard_map/ppermute | solution.py:96
  141.5 18.0 %collective-permute-start.8 = (bf16[256,256]{1,0:T(8,128)(2,1)S(1)}, bf16[256,256]{1,0:T(8,128)(2,1)S(1)}, u32[]{:S(2)}, u32[]{:S(2)}) collective-permute-start(bf16[256,256]{1,0:T(8,128)(2,1)S(1)} %slice.239), channel_id=1, source_target_pairs={{0,64},{1,65},{2,66},{3,67},{4,68},{5,69},{6,70},{7,71},{8,72},{9,... | collective-permute-start | bytes 393224 | tf_op jit(solution)/shard_map/ppermute | solution.py:96
  159.6 6.6 %collective-permute-start.9 = (bf16[128,384]{1,0:T(8,128)(2,1)S(1)}, bf16[128,384]{1,0:T(8,128)(2,1)S(1)}, u32[]{:S(2)}, u32[]{:S(2)}) collective-permute-start(bf16[128,384]{1,0:T(8,128)(2,1)S(1)} %broadcast_select_fusion.5), channel_id=1, source_target_pairs={{0,16},{1,17},{2,18},{3,19},{4,20},{5,21},{6,22},{7,23},{8,24},{9,... | collective-permute-start | bytes 294920 | tf_op jit(solution)/shard_map/ppermute | solution.py:96
  170.0 21.8 %collective-permute-start.10 = (bf16[128,768]{1,0:T(8,128)(2,1)S(1)}, bf16[128,768]{1,0:T(8,128)(2,1)S(1)}, u32[]{:S(2)}, u32[]{:S(2)}) collective-permute-start(bf16[128,768]{1,0:T(8,128)(2,1)S(1)} %get-tuple-element.36), channel_id=1, source_target_pairs={{0,64},{1,65},{2,66},{3,67},{4,68},{5,69},{6,70},{7,71},{8,72},{9,... | collective-permute-start | bytes 589832 | tf_op jit(solution)/shard_map/ppermute | solution.py:96
  191.8 10.8 %collective-permute-start.11 = (bf16[256,768]{1,0:T(8,128)(2,1)S(1)}, bf16[256,768]{1,0:T(8,128)(2,1)S(1)}, u32[]{:S(2)}, u32[]{:S(2)}) collective-permute-start(bf16[256,768]{1,0:T(8,128)(2,1)S(1)} %pad_maximum_fusion.4), channel_id=1, source_target_pairs={{0,32},{1,257},{2,34},{3,259},{4,36},{5,261},{6,38},{7,263},{8,40}... | collective-permute-start | bytes 1179656 | tf_op jit(solution)/shard_map/ppermute | solution.py:96
  202.7 15.4 %collective-permute-start.12 = (bf16[512,768]{1,0:T(8,128)(2,1)S(1)}, bf16[512,768]{1,0:T(8,128)(2,1)S(1)}, u32[]{:S(2)}, u32[]{:S(2)}) collective-permute-start(bf16[512,768]{1,0:T(8,128)(2,1)S(1)} %pad_maximum_fusion.2), channel_id=1, source_target_pairs={{0,256},{1,33},{2,258},{3,35},{4,260},{5,37},{6,262},{7,39},{8,264... | collective-permute-start | bytes 2359304 | tf_op jit(solution)/shard_map/ppermute | solution.py:96
  218.2 22.3 %collective-permute-start.13 = (bf16[1024,768]{1,0:T(8,128)(2,1)S(1)}, bf16[1024,768]{1,0:T(8,128)(2,1)S(1)}, u32[]{:S(2)}, u32[]{:S(2)}) collective-permute-start(bf16[1024,768]{1,0:T(8,128)(2,1)S(1)} %pad_maximum_fusion), channel_id=1, source_target_pairs={{0,128},{1,17},{2,130},{3,19},{4,132},{5,21},{6,134},{7,23},{8,136... | collective-permute-start | bytes 4718600 | tf_op jit(solution)/shard_map/ppermute | solution.py:96
  241.9 2.6 copy-start
  241.9 39.4 %collective-permute-start.14 = (bf16[2048,768]{1,0:T(8,128)(2,1)}, bf16[2048,768]{1,0:T(8,128)(2,1)S(1)}, u32[]{:S(2)}, u32[]{:S(2)}) collective-permute-start(bf16[2048,768]{1,0:T(8,128)(2,1)} %get-tuple-element.15), channel_id=1, source_target_pairs={{0,16},{1,129},{2,18},{3,131},{4,20},{5,133},{6,22},{7,135},{8,24}... | collective-permute-start | bytes 9437192 | tf_op jit(solution)/shard_map/ppermute | solution.py:96
  281.3 1.9 copy-start.1
  281.3 1.9 copy-start.2
  281.3 1.9 copy-start.3
  292.0 4.6 %collective-permute-start.15 = (bf16[2048,256]{1,0:T(8,128)(2,1)S(1)}, bf16[2048,256]{1,0:T(8,128)(2,1)S(1)}, u32[]{:S(2)}, u32[]{:S(2)}) collective-permute-start(bf16[2048,256]{1,0:T(8,128)(2,1)S(1)} %bitcast.46), channel_id=1, source_target_pairs={{0,1},{1,0},{2,3},{3,2},{4,5},{5,4},{6,7},{7,6},{8,9},{9,8},{10,11... | collective-permute-start | bytes 3145736 | tf_op jit(solution)/shard_map/ppermute | solution.py:135
  296.9 15.9 %collective-permute-start.16 = (bf16[1024,256]{1,0:T(8,128)(2,1)S(1)}, bf16[1024,256]{1,0:T(8,128)(2,1)S(1)}, u32[]{:S(2)}, u32[]{:S(2)}) collective-permute-start(bf16[1024,256]{1,0:T(8,128)(2,1)S(1)} %slice.234), channel_id=1, source_target_pairs={{0,4},{1,5},{2,6},{3,7},{4,0},{5,1},{6,2},{7,3},{8,12},{9,13},{10,... | collective-permute-start | bytes 1572872 | tf_op jit(solution)/shard_map/ppermute | solution.py:135
  312.9 10.9 %collective-permute-start.17 = (bf16[512,256]{1,0:T(8,128)(2,1)S(1)}, bf16[512,256]{1,0:T(8,128)(2,1)S(1)}, u32[]{:S(2)}, u32[]{:S(2)}) collective-permute-start(bf16[512,256]{1,0:T(8,128)(2,1)S(1)} %slice.236), channel_id=1, source_target_pairs={{0,8},{1,9},{2,10},{3,11},{4,12},{5,13},{6,14},{7,15},{8,0},{9,1},... | collective-permute-start | bytes 786440 | tf_op jit(solution)/shard_map/ppermute | solution.py:135
  323.9 15.9 %collective-permute-start.18 = (bf16[256,256]{1,0:T(8,128)(2,1)S(1)}, bf16[256,256]{1,0:T(8,128)(2,1)S(1)}, u32[]{:S(2)}, u32[]{:S(2)}) collective-permute-start(bf16[256,256]{1,0:T(8,128)(2,1)S(1)} %slice.238), channel_id=1, source_target_pairs={{0,2},{1,3},{2,0},{3,1},{4,6},{5,7},{6,4},{7,5},{8,10},{9,11},{10,... | collective-permute-start | bytes 393224 | tf_op jit(solution)/shard_map/ppermute | solution.py:135

commit v10 on v9

--- a/solution.py
+++ b/solution.py
@@ -155,14 +155,15 @@
     core = me_tp % 2
     odd = me % 2
     low = odd == 0
-    stacked = jnp.stack([queries, output_grad, attn_output, key_states, value_states])
-    head_0, head_1 = stacked[:, :, :HD], stacked[:, :, HD : 2 * HD]
-    kept = jnp.where(low, head_0, head_1)
-    given = jnp.where(low, head_1, head_0)
+    arrays = (queries, output_grad, attn_output, key_states, value_states)
+    kept = jnp.concatenate([lax.dynamic_slice_in_dim(x, odd * HD, HD, 1) for x in arrays], axis=1)
+    given = jnp.concatenate(
+        [lax.dynamic_slice_in_dim(x, (1 - odd) * HD, HD, 1) for x in arrays], axis=1
+    )
     got = _pair_permute(given, (1, 1))
-    both = jnp.where(low, jnp.concatenate([kept, got], 1), jnp.concatenate([got, kept], 1))
-    pair_q, pair_do, pair_o, pair_k, pair_v = (both[i] for i in range(5))
-    pair_kv = jnp.concatenate([pair_k, pair_v], axis=1)
+    both = jnp.where(low, jnp.concatenate([kept, got], 0), jnp.concatenate([got, kept], 0))
+    pair_q, pair_do, pair_o = both[:, 0:HD], both[:, HD : 2 * HD], both[:, 2 * HD : 3 * HD]
+    pair_kv = both[:, 3 * HD : 5 * HD]
     gathered = concat_gather(pair_kv, HEAD_GATHER_ORDERS)
     group_count = ctx_count // 2
     holder = me ^ per_core(core, [xor_of_position(o, group_count) for o in HEAD_GATHER_ORDERS])
@@ -189,11 +190,16 @@
         axis=1,
     )
     gather_at = per_core(core, [gather_positions(me, o, ctx_count) for o in GATHER_ORDERS])
-    gradients = concat_gather(own_grads, GATHER_ORDERS)
+    held = concat_gather(own_grads, tuple(order[:-1] for order in GATHER_ORDERS))
+    other = _pair_permute(held, tuple(order[-1] for order in GATHER_ORDERS))
     projections = jnp.concatenate([w_query, w_key, w_value], axis=1)
-    term = lax.dot_general(
-        gradients, projections, (((1,), (1,)), ((), ())), preferred_element_type=jnp.float32
-    ).astype(jnp.bfloat16)
+
+    def project(rows):
+        return lax.dot_general(
+            rows, projections, (((1,), (1,)), ((), ())), preferred_element_type=jnp.float32
+        ).astype(jnp.bfloat16)
+
+    term = jnp.concatenate([project(held), project(other)], axis=0)
     tp_at = scatter_positions(me_tp, TP_ORDER, tp_count)
     owner = jnp.argsort(tp_at)
     per_owner = ctx_count // tp_count

time: 347 us -> 342 us (0.986)
  waiting for transfers between devices: 233 us -> 229 us
    ppermute x15, waiting for transfers between devices: 208 us -> 204 us  [_pair_permute(): return lax.ppermute(value, ('ctx', 'tp'), pairs)]
    unnamed x30 -> x29, local copies, waits for them, and re-layouts: 10.3 us -> 9.03 us
  transfers between devices with their start and end apart: 19 -> 19, of which waited for: 19 -> 19; matrix products, arithmetic and copies ran while one was open for 2% -> 4% of each run, Pallas kernels for 0% -> 0%
where the time goes in v10:
time: 342 us; the launch traced here: 335 us
  waiting for transfers between devices  229 us (67%)
  starting transfers between devices  69.1 us (20%)
  local copies, waits for them, and re-layouts  18.6 us (5%)
  other arithmetic  7.3 us (2%)
  matrix products  5.81 us (2%)
  Pallas kernels  4.88 us (1%)
    ppermute x15, waiting for transfers between devices, _pair_permute(): return lax.ppermute(value, ('ctx', 'tp'), pairs)  204 us
    ppermute x15, starting transfers between devices, _pair_permute(): return lax.ppermute(value, ('ctx', 'tp'), pairs)  46.8 us
    ppermute x4, waiting for transfers between devices, tp_halving_reduce(): lax.ppermute(held[:half].astype(wire), 'tp', [(i, i ^ distance) for i in...  24.8 us
    ppermute x4, starting transfers between devices, tp_halving_reduce(): lax.ppermute(held[:half].astype(wire), 'tp', [(i, i ^ distance) for i in...  22.3 us
    unnamed x29, local copies, waits for them, and re-layouts  9.03 us
  transfers between devices with their start and end apart: 19, of which 19 were waited for; matrix products, arithmetic and copies ran while one was open for 4% of the time, Pallas kernels for 0%

profile of v10, /device:TPU:6, one launch (start us, length us, event | category | flops | bytes accessed | tf_op | source)
XLA Modules:
  0.0 335.1 jit_solution(17439237559608537600)
XLA Ops:
  4.0 3.8 %collective-permute-start = (bf16[128,640]{1,0:T(8,128)(2,1)S(1)}, bf16[128,640]{1,0:T(8,128)(2,1)S(1)}, u32[]{:S(2)}, u32[]{:S(2)}) collective-permute-start(bf16[128,640]{1,0:T(8,128)(2,1)S(1)} %get-tuple-element.27), channel_id=1, source_target_pairs={{0,16},{1,17},{2,18},{3,19},{4,20},{5,21},{6,22},{7,23},{8,24},{9,... | collective-permute-start | bytes 491528 | tf_op jit(solution)/shard_map/ppermute | solution.py:96
  7.8 4.2 %collective-permute-done = bf16[128,640]{1,0:T(8,128)(2,1)S(1)} collective-permute-done((bf16[128,640]{1,0:T(8,128)(2,1)S(1)}, bf16[128,640]{1,0:T(8,128)(2,1)S(1)}, u32[]{:S(2)}, u32[]{:S(2)}) %collective-permute-start) | collective-permute-done | bytes 163872 | tf_op jit(solution)/shard_map/ppermute | solution.py:96
  12.1 9.1 %collective-permute-start.1 = (bf16[256,256]{1,0:T(8,128)(2,1)S(1)}, bf16[256,256]{1,0:T(8,128)(2,1)S(1)}, u32[]{:S(2)}, u32[]{:S(2)}) collective-permute-start(bf16[256,256]{1,0:T(8,128)(2,1)S(1)} %get-tuple-element.15), channel_id=1, source_target_pairs={{0,64},{1,65},{2,66},{3,67},{4,68},{5,69},{6,70},{7,71},{8,72},{9,... | collective-permute-start | bytes 393224 | tf_op jit(solution)/shard_map/ppermute | solution.py:96
  21.2 11.2 %collective-permute-done.1 = bf16[256,256]{1,0:T(8,128)(2,1)S(1)} collective-permute-done((bf16[256,256]{1,0:T(8,128)(2,1)S(1)}, bf16[256,256]{1,0:T(8,128)(2,1)S(1)}, u32[]{:S(2)}, u32[]{:S(2)}) %collective-permute-start.1) | collective-permute-done | bytes 131104 | tf_op jit(solution)/shard_map/ppermute | solution.py:96
  32.5 1.9 collective-permute-start.2
  34.5 1.2 sort.17
  35.7 8.4 %collective-permute-done.2 = bf16[512,256]{1,0:T(8,128)(2,1)S(1)} collective-permute-done((bf16[512,256]{1,0:T(8,128)(2,1)S(1)}, bf16[512,256]{1,0:T(8,128)(2,1)S(1)}, u32[]{:S(2)}, u32[]{:S(2)}) %collective-permute-start.2) | collective-permute-done | bytes 262176 | tf_op jit(solution)/shard_map/ppermute | solution.py:96
  44.9 3.3 collective-permute-start.3
  48.6 9.1 %collective-permute-done.3 = bf16[1024,256]{1,0:T(8,128)(2,1)S(1)} collective-permute-done((bf16[1024,256]{1,0:T(8,128)(2,1)}, bf16[1024,256]{1,0:T(8,128)(2,1)S(1)}, u32[]{:S(2)}, u32[]{:S(2)}) %collective-permute-start.3) | collective-permute-done | bytes 524320 | tf_op jit(solution)/shard_map/ppermute | solution.py:96
  57.7 1.1 pad_maximum_fusion.2
  58.7 2.7 collective-permute-start.4
  64.0 22.2 %collective-permute-done.4 = bf16[2048,256]{1,0:T(8,128)(2,1)} collective-permute-done((bf16[2048,256]{1,0:T(8,128)(2,1)}, bf16[2048,256]{1,0:T(8,128)(2,1)}, u32[]{:S(2)}, u32[]{:S(2)}) %collective-permute-start.4) | collective-permute-done | bytes 1048608 | tf_op jit(solution)/shard_map/ppermute | solution.py:96
  86.1 1.3 constant_dynamic-update-slice_fusion.10.kv_ref
  87.4 4.9 %shard_map.91 = (f32[256,128]{1,0:T(8,128)S(1)}, bf16[4096,256]{1,0:T(8,128)(2,1)S(1)}) custom-call(f32[8,4096]{1,0:T(8,128)S(1)} %concatenate.57.mask_ref, bf16[256,128]{1,0:T(8,128)(2,1)S(1)} %get-tuple-element.19.q_ref, bf16[256,128]{1,0:T(8,128)(2,1)S(1)} %get-tuple-element.18.do_ref, bf16[256,128]{1,0:T(8,128)(2,1)S(1)} %get-tuple-element.17.o_ref, ...), custom_call_target="tpu_custom_call" | custom-call | flops 1342177280 | bytes 4194304 | tf_op jit(solution)/shard_map/pallas_call | solution.py:72
  92.4 2.8 collective-permute-start.5
  95.2 23.4 %collective-permute-done.5 = bf16[2048,256]{1,0:T(8,128)(2,1)S(1)} collective-permute-done((bf16[2048,256]{1,0:T(8,128)(2,1)S(1)}, bf16[2048,256]{1,0:T(8,128)(2,1)S(1)}, u32[]{:S(2)}, u32[]{:S(2)}) %collective-permute-start.5) | collective-permute-done | bytes 1048608 | tf_op jit(solution)/shard_map/ppermute | solution.py:96
  119.0 3.5 %collective-permute-start.6 = (bf16[1024,256]{1,0:T(8,128)(2,1)S(1)}, bf16[1024,256]{1,0:T(8,128)(2,1)S(1)}, u32[]{:S(2)}, u32[]{:S(2)}) collective-permute-start(bf16[1024,256]{1,0:T(8,128)(2,1)S(1)} %slice.206), channel_id=1, source_target_pairs={{0,256},{1,33},{2,258},{3,35},{4,260},{5,37},{6,262},{7,39},{8,264... | collective-permute-start | bytes 1572872 | tf_op jit(solution)/shard_map/ppermute | solution.py:96
  122.4 9.1 %collective-permute-done.6 = bf16[1024,256]{1,0:T(8,128)(2,1)S(1)} collective-permute-done((bf16[1024,256]{1,0:T(8,128)(2,1)S(1)}, bf16[1024,256]{1,0:T(8,128)(2,1)S(1)}, u32[]{:S(2)}, u32[]{:S(2)}) %collective-permute-start.6) | collective-permute-done | bytes 524320 | tf_op jit(solution)/shard_map/ppermute | solution.py:96
  131.7 1.9 collective-permute-start.7
  133.6 8.3 %collective-permute-done.7 = bf16[512,256]{1,0:T(8,128)(2,1)S(1)} collective-permute-done((bf16[512,256]{1,0:T(8,128)(2,1)S(1)}, bf16[512,256]{1,0:T(8,128)(2,1)S(1)}, u32[]{:S(2)}, u32[]{:S(2)}) %collective-permute-start.7) | collective-permute-done | bytes 262176 | tf_op jit(solution)/shard_map/ppermute | solution.py:96
  142.0 1.9 collective-permute-start.8
  144.0 16.0 %collective-permute-done.8 = bf16[256,256]{1,0:T(8,128)(2,1)S(1)} collective-permute-done((bf16[256,256]{1,0:T(8,128)(2,1)S(1)}, bf16[256,256]{1,0:T(8,128)(2,1)S(1)}, u32[]{:S(2)}, u32[]{:S(2)}) %collective-permute-start.8) | collective-permute-done | bytes 131104 | tf_op jit(solution)/shard_map/ppermute | solution.py:96
  160.1 1.9 collective-permute-start.9
  162.0 4.7 %collective-permute-done.9 = bf16[128,384]{1,0:T(8,128)(2,1)S(1)} collective-permute-done((bf16[128,384]{1,0:T(8,128)(2,1)S(1)}, bf16[128,384]{1,0:T(8,128)(2,1)S(1)}, u32[]{:S(2)}, u32[]{:S(2)}) %collective-permute-start.9) | collective-permute-done | bytes 98336 | tf_op jit(solution)/shard_map/ppermute | solution.py:96
  168.1 1.9 collective-permute-start.10
  170.0 20.2 %collective-permute-done.10 = bf16[128,768]{1,0:T(8,128)(2,1)S(1)} collective-permute-done((bf16[128,768]{1,0:T(8,128)(2,1)S(1)}, bf16[128,768]{1,0:T(8,128)(2,1)S(1)}, u32[]{:S(2)}, u32[]{:S(2)}) %collective-permute-start.10) | collective-permute-done | bytes 196640 | tf_op jit(solution)/shard_map/ppermute | solution.py:96
  190.3 1.9 collective-permute-start.11
  192.2 8.7 %collective-permute-done.11 = bf16[256,768]{1,0:T(8,128)(2,1)S(1)} collective-permute-done((bf16[256,768]{1,0:T(8,128)(2,1)S(1)}, bf16[256,768]{1,0:T(8,128)(2,1)S(1)}, u32[]{:S(2)}, u32[]{:S(2)}) %collective-permute-start.11) | collective-permute-done | bytes 393248 | tf_op jit(solution)/shard_map/ppermute | solution.py:96
  201.0 4.4 %collective-permute-start.12 = (bf16[512,768]{1,0:T(8,128)(2,1)S(1)}, bf16[512,768]{1,0:T(8,128)(2,1)S(1)}, u32[]{:S(2)}, u32[]{:S(2)}) collective-permute-start(bf16[512,768]{1,0:T(8,128)(2,1)S(1)} %pad_maximum_fusion.3), channel_id=1, source_target_pairs={{0,256},{1,33},{2,258},{3,35},{4,260},{5,37},{6,262},{7,39},{8,264... | collective-permute-start | bytes 2359304 | tf_op jit(solution)/shard_map/ppermute | solution.py:96
  205.4 11.0 %collective-permute-done.12 = bf16[512,768]{1,0:T(8,128)(2,1)S(1)} collective-permute-done((bf16[512,768]{1,0:T(8,128)(2,1)S(1)}, bf16[512,768]{1,0:T(8,128)(2,1)S(1)}, u32[]{:S(2)}, u32[]{:S(2)}) %collective-permute-start.12) | collective-permute-done | bytes 786464 | tf_op jit(solution)/shard_map/ppermute | solution.py:96
  216.5 3.8 %collective-permute-start.13 = (bf16[1024,768]{1,0:T(8,128)(2,1)S(1)}, bf16[1024,768]{1,0:T(8,128)(2,1)S(1)}, u32[]{:S(2)}, u32[]{:S(2)}) collective-permute-start(bf16[1024,768]{1,0:T(8,128)(2,1)S(1)} %pad_maximum_fusion.1), channel_id=1, source_target_pairs={{0,128},{1,17},{2,130},{3,19},{4,132},{5,21},{6,134},{7,23},{8,136... | collective-permute-start | bytes 4718600 | tf_op jit(solution)/shard_map/ppermute | solution.py:96
  224.2 1.0 constant_dynamic-update-slice_fusion.22
  225.2 13.6 %collective-permute-done.13 = bf16[1024,768]{1,0:T(8,128)(2,1)S(1)} collective-permute-done((bf16[1024,768]{1,0:T(8,128)(2,1)S(1)}, bf16[1024,768]{1,0:T(8,128)(2,1)S(1)}, u32[]{:S(2)}, u32[]{:S(2)}) %collective-permute-start.13) | collective-permute-done | bytes 1572896 | tf_op jit(solution)/shard_map/ppermute | solution.py:96
  238.8 1.2 constant_dynamic-update-slice_fusion.21
  240.0 1.9 collective-permute-start.14
  242.8 2.9 convolution_convert_fusion.1
  245.7 33.8 %collective-permute-done.14 = bf16[2048,768]{1,0:T(8,128)(2,1)} collective-permute-done((bf16[2048,768]{1,0:T(8,128)(2,1)}, bf16[2048,768]{1,0:T(8,128)(2,1)}, u32[]{:S(2)}, u32[]{:S(2)}) %collective-permute-start.14) | collective-permute-done | bytes 3145760 | tf_op jit(solution)/shard_map/ppermute | solution.py:96
  279.5 2.9 convolution_convert_fusion
  282.6 2.0 gather_fusion.3
  284.6 1.8 broadcast_select_fusion
  286.6 2.0 collective-permute-start.15
  288.6 2.5 collective-permute-done.15
  291.5 3.5 %collective-permute-start.16 = (bf16[1024,256]{1,0:T(8,128)(2,1)S(1)}, bf16[1024,256]{1,0:T(8,128)(2,1)S(1)}, u32[]{:S(2)}, u32[]{:S(2)}) collective-permute-start(bf16[1024,256]{1,0:T(8,128)(2,1)S(1)} %slice.205), channel_id=1, source_target_pairs={{0,4},{1,5},{2,6},{3,7},{4,0},{5,1},{6,2},{7,3},{8,12},{9,13},{10,... | collective-permute-start | bytes 1572872 | tf_op jit(solution)/shard_map/ppermute | solution.py:135
  295.0 12.4 %collective-permute-done.16 = bf16[1024,256]{1,0:T(8,128)(2,1)S(1)} collective-permute-done((bf16[1024,256]{1,0:T(8,128)(2,1)S(1)}, bf16[1024,256]{1,0:T(8,128)(2,1)S(1)}, u32[]{:S(2)}, u32[]{:S(2)}) %collective-permute-start.16) | collective-permute-done | bytes 524320 | tf_op jit(solution)/shard_map/ppermute | solution.py:135
  307.5 5.1 %collective-permute-start.17 = (bf16[512,256]{1,0:T(8,128)(2,1)S(1)}, bf16[512,256]{1,0:T(8,128)(2,1)S(1)}, u32[]{:S(2)}, u32[]{:S(2)}) collective-permute-start(bf16[512,256]{1,0:T(8,128)(2,1)S(1)} %slice.207), channel_id=1, source_target_pairs={{0,8},{1,9},{2,10},{3,11},{4,12},{5,13},{6,14},{7,15},{8,0},{9,1},... | collective-permute-start | bytes 786440 | tf_op jit(solution)/shard_map/ppermute | solution.py:135
  312.7 5.8 %collective-permute-done.17 = bf16[512,256]{1,0:T(8,128)(2,1)S(1)} collective-permute-done((bf16[512,256]{1,0:T(8,128)(2,1)S(1)}, bf16[512,256]{1,0:T(8,128)(2,1)S(1)}, u32[]{:S(2)}, u32[]{:S(2)}) %collective-permute-start.17) | collective-permute-done | bytes 262176 | tf_op jit(solution)/shard_map/ppermute | solution.py:135
  318.5 11.7 %collective-permute-start.18 = (bf16[256,256]{1,0:T(8,128)(2,1)S(1)}, bf16[256,256]{1,0:T(8,128)(2,1)S(1)}, u32[]{:S(2)}, u32[]{:S(2)}) collective-permute-start(bf16[256,256]{1,0:T(8,128)(2,1)S(1)} %slice.209), channel_id=1, source_target_pairs={{0,2},{1,3},{2,0},{3,1},{4,6},{5,7},{6,4},{7,5},{8,10},{9,11},{10,... | collective-permute-start | bytes 393224 | tf_op jit(solution)/shard_map/ppermute | solution.py:135
  330.3 4.1 %collective-permute-done.18 = bf16[256,256]{1,0:T(8,128)(2,1)S(1)} collective-permute-done((bf16[256,256]{1,0:T(8,128)(2,1)S(1)}, bf16[256,256]{1,0:T(8,128)(2,1)S(1)}, u32[]{:S(2)}, u32[]{:S(2)}) %collective-permute-start.18) | collective-permute-done | bytes 131104 | tf_op jit(solution)/shard_map/ppermute | solution.py:135
  (81 shorter events, 16.2 us)
Async XLA Ops:
  4.0 8.0 %collective-permute-start = (bf16[128,640]{1,0:T(8,128)(2,1)S(1)}, bf16[128,640]{1,0:T(8,128)(2,1)S(1)}, u32[]{:S(2)}, u32[]{:S(2)}) collective-permute-start(bf16[128,640]{1,0:T(8,128)(2,1)S(1)} %get-tuple-element.27), channel_id=1, source_target_pairs={{0,16},{1,17},{2,18},{3,19},{4,20},{5,21},{6,22},{7,23},{8,24},{9,... | collective-permute-start | bytes 491528 | tf_op jit(solution)/shard_map/ppermute | solution.py:96
  12.1 20.3 %collective-permute-start.1 = (bf16[256,256]{1,0:T(8,128)(2,1)S(1)}, bf16[256,256]{1,0:T(8,128)(2,1)S(1)}, u32[]{:S(2)}, u32[]{:S(2)}) collective-permute-start(bf16[256,256]{1,0:T(8,128)(2,1)S(1)} %get-tuple-element.15), channel_id=1, source_target_pairs={{0,64},{1,65},{2,66},{3,67},{4,68},{5,69},{6,70},{7,71},{8,72},{9,... | collective-permute-start | bytes 393224 | tf_op jit(solution)/shard_map/ppermute | solution.py:96
  32.5 11.6 %collective-permute-start.2 = (bf16[512,256]{1,0:T(8,128)(2,1)S(1)}, bf16[512,256]{1,0:T(8,128)(2,1)S(1)}, u32[]{:S(2)}, u32[]{:S(2)}) collective-permute-start(bf16[512,256]{1,0:T(8,128)(2,1)S(1)} %pad_maximum_fusion.6), channel_id=1, source_target_pairs={{0,32},{1,257},{2,34},{3,259},{4,36},{5,261},{6,38},{7,263},{8,40}... | collective-permute-start | bytes 786440 | tf_op jit(solution)/shard_map/ppermute | solution.py:96
  44.9 12.8 %collective-permute-start.3 = (bf16[1024,256]{1,0:T(8,128)(2,1)}, bf16[1024,256]{1,0:T(8,128)(2,1)S(1)}, u32[]{:S(2)}, u32[]{:S(2)}) collective-permute-start(bf16[1024,256]{1,0:T(8,128)(2,1)} %pad_maximum_fusion.4), channel_id=1, source_target_pairs={{0,256},{1,33},{2,258},{3,35},{4,260},{5,37},{6,262},{7,39},{8,264... | collective-permute-start | bytes 1572872 | tf_op jit(solution)/shard_map/ppermute | solution.py:96
  58.7 27.4 %collective-permute-start.4 = (bf16[2048,256]{1,0:T(8,128)(2,1)}, bf16[2048,256]{1,0:T(8,128)(2,1)}, u32[]{:S(2)}, u32[]{:S(2)}) collective-permute-start(bf16[2048,256]{1,0:T(8,128)(2,1)} %pad_maximum_fusion.2), channel_id=1, source_target_pairs={{0,128},{1,129},{2,130},{3,131},{4,132},{5,133},{6,134},{7,135},{8... | collective-permute-start | bytes 3145736 | tf_op jit(solution)/shard_map/ppermute | solution.py:96
  92.4 26.2 %collective-permute-start.5 = (bf16[2048,256]{1,0:T(8,128)(2,1)S(1)}, bf16[2048,256]{1,0:T(8,128)(2,1)S(1)}, u32[]{:S(2)}, u32[]{:S(2)}) collective-permute-start(bf16[2048,256]{1,0:T(8,128)(2,1)S(1)} %slice.99), channel_id=1, source_target_pairs={{0,128},{1,129},{2,130},{3,131},{4,132},{5,133},{6,134},{7,135},{8... | collective-permute-start | bytes 3145736 | tf_op jit(solution)/shard_map/ppermute | solution.py:96
  119.0 12.6 %collective-permute-start.6 = (bf16[1024,256]{1,0:T(8,128)(2,1)S(1)}, bf16[1024,256]{1,0:T(8,128)(2,1)S(1)}, u32[]{:S(2)}, u32[]{:S(2)}) collective-permute-start(bf16[1024,256]{1,0:T(8,128)(2,1)S(1)} %slice.206), channel_id=1, source_target_pairs={{0,256},{1,33},{2,258},{3,35},{4,260},{5,37},{6,262},{7,39},{8,264... | collective-permute-start | bytes 1572872 | tf_op jit(solution)/shard_map/ppermute | solution.py:96
  131.7 10.3 %collective-permute-start.7 = (bf16[512,256]{1,0:T(8,128)(2,1)S(1)}, bf16[512,256]{1,0:T(8,128)(2,1)S(1)}, u32[]{:S(2)}, u32[]{:S(2)}) collective-permute-start(bf16[512,256]{1,0:T(8,128)(2,1)S(1)} %slice.208), channel_id=1, source_target_pairs={{0,32},{1,257},{2,34},{3,259},{4,36},{5,261},{6,38},{7,263},{8,40}... | collective-permute-start | bytes 786440 | tf_op jit(solution)/shard_map/ppermute | solution.py:96
  142.0 18.0 %collective-permute-start.8 = (bf16[256,256]{1,0:T(8,128)(2,1)S(1)}, bf16[256,256]{1,0:T(8,128)(2,1)S(1)}, u32[]{:S(2)}, u32[]{:S(2)}) collective-permute-start(bf16[256,256]{1,0:T(8,128)(2,1)S(1)} %slice.210), channel_id=1, source_target_pairs={{0,64},{1,65},{2,66},{3,67},{4,68},{5,69},{6,70},{7,71},{8,72},{9,... | collective-permute-start | bytes 393224 | tf_op jit(solution)/shard_map/ppermute | solution.py:96
  160.1 6.6 %collective-permute-start.9 = (bf16[128,384]{1,0:T(8,128)(2,1)S(1)}, bf16[128,384]{1,0:T(8,128)(2,1)S(1)}, u32[]{:S(2)}, u32[]{:S(2)}) collective-permute-start(bf16[128,384]{1,0:T(8,128)(2,1)S(1)} %broadcast_select_fusion.3), channel_id=1, source_target_pairs={{0,16},{1,17},{2,18},{3,19},{4,20},{5,21},{6,22},{7,23},{8,24},{9,... | collective-permute-start | bytes 294920 | tf_op jit(solution)/shard_map/ppermute | solution.py:96
  168.1 22.2 %collective-permute-start.10 = (bf16[128,768]{1,0:T(8,128)(2,1)S(1)}, bf16[128,768]{1,0:T(8,128)(2,1)S(1)}, u32[]{:S(2)}, u32[]{:S(2)}) collective-permute-start(bf16[128,768]{1,0:T(8,128)(2,1)S(1)} %get-tuple-element.22), channel_id=1, source_target_pairs={{0,64},{1,65},{2,66},{3,67},{4,68},{5,69},{6,70},{7,71},{8,72},{9,... | collective-permute-start | bytes 589832 | tf_op jit(solution)/shard_map/ppermute | solution.py:96
  190.3 10.7 %collective-permute-start.11 = (bf16[256,768]{1,0:T(8,128)(2,1)S(1)}, bf16[256,768]{1,0:T(8,128)(2,1)S(1)}, u32[]{:S(2)}, u32[]{:S(2)}) collective-permute-start(bf16[256,768]{1,0:T(8,128)(2,1)S(1)} %pad_maximum_fusion.5), channel_id=1, source_target_pairs={{0,32},{1,257},{2,34},{3,259},{4,36},{5,261},{6,38},{7,263},{8,40}... | collective-permute-start | bytes 1179656 | tf_op jit(solution)/shard_map/ppermute | solution.py:96
  201.0 15.4 %collective-permute-start.12 = (bf16[512,768]{1,0:T(8,128)(2,1)S(1)}, bf16[512,768]{1,0:T(8,128)(2,1)S(1)}, u32[]{:S(2)}, u32[]{:S(2)}) collective-permute-start(bf16[512,768]{1,0:T(8,128)(2,1)S(1)} %pad_maximum_fusion.3), channel_id=1, source_target_pairs={{0,256},{1,33},{2,258},{3,35},{4,260},{5,37},{6,262},{7,39},{8,264... | collective-permute-start | bytes 2359304 | tf_op jit(solution)/shard_map/ppermute | solution.py:96
  216.5 22.3 %collective-permute-start.13 = (bf16[1024,768]{1,0:T(8,128)(2,1)S(1)}, bf16[1024,768]{1,0:T(8,128)(2,1)S(1)}, u32[]{:S(2)}, u32[]{:S(2)}) collective-permute-start(bf16[1024,768]{1,0:T(8,128)(2,1)S(1)} %pad_maximum_fusion.1), channel_id=1, source_target_pairs={{0,128},{1,17},{2,130},{3,19},{4,132},{5,21},{6,134},{7,23},{8,136... | collective-permute-start | bytes 4718600 | tf_op jit(solution)/shard_map/ppermute | solution.py:96
  225.2 17.5 %copy-start = (bf16[256,256]{1,0:T(8,128)(2,1)S(1)}, bf16[256,256]{1,0:T(8,128)(2,1)}, u32[]{:S(2)}) copy-start(bf16[256,256]{1,0:T(8,128)(2,1)} %param.15) | copy-start | bytes 393220
  225.2 17.5 %copy-start.1 = (bf16[256,256]{1,0:T(8,128)(2,1)S(1)}, bf16[256,256]{1,0:T(8,128)(2,1)}, u32[]{:S(2)}) copy-start(bf16[256,256]{1,0:T(8,128)(2,1)} %param.16) | copy-start | bytes 393220
  225.2 17.5 %copy-start.2 = (bf16[256,256]{1,0:T(8,128)(2,1)S(1)}, bf16[256,256]{1,0:T(8,128)(2,1)}, u32[]{:S(2)}) copy-start(bf16[256,256]{1,0:T(8,128)(2,1)} %param.17) | copy-start | bytes 393220
  240.0 39.5 %collective-permute-start.14 = (bf16[2048,768]{1,0:T(8,128)(2,1)}, bf16[2048,768]{1,0:T(8,128)(2,1)}, u32[]{:S(2)}, u32[]{:S(2)}) collective-permute-start(bf16[2048,768]{1,0:T(8,128)(2,1)} %constant_dynamic-update-slice_fusion.21), channel_id=1, source_target_pairs={{0,16},{1,129},{2,18},{3,131},{4,20},{5,133},{6,22},{7,135},{8,24}... | collective-permute-start | bytes 9437192 | tf_op jit(solution)/shard_map/ppermute | solution.py:96
  286.6 4.6 %collective-permute-start.15 = (bf16[2048,256]{1,0:T(8,128)(2,1)S(1)}, bf16[2048,256]{1,0:T(8,128)(2,1)S(1)}, u32[]{:S(2)}, u32[]{:S(2)}) collective-permute-start(bf16[2048,256]{1,0:T(8,128)(2,1)S(1)} %bitcast.29), channel_id=1, source_target_pairs={{0,1},{1,0},{2,3},{3,2},{4,5},{5,4},{6,7},{7,6},{8,9},{9,8},{10,11... | collective-permute-start | bytes 3145736 | tf_op jit(solution)/shard_map/ppermute | solution.py:135
  291.5 15.9 %collective-permute-start.16 = (bf16[1024,256]{1,0:T(8,128)(2,1)S(1)}, bf16[1024,256]{1,0:T(8,128)(2,1)S(1)}, u32[]{:S(2)}, u32[]{:S(2)}) collective-permute-start(bf16[1024,256]{1,0:T(8,128)(2,1)S(1)} %slice.205), channel_id=1, source_target_pairs={{0,4},{1,5},{2,6},{3,7},{4,0},{5,1},{6,2},{7,3},{8,12},{9,13},{10,... | collective-permute-start | bytes 1572872 | tf_op jit(solution)/shard_map/ppermute | solution.py:135
  307.5 10.9 %collective-permute-start.17 = (bf16[512,256]{1,0:T(8,128)(2,1)S(1)}, bf16[512,256]{1,0:T(8,128)(2,1)S(1)}, u32[]{:S(2)}, u32[]{:S(2)}) collective-permute-start(bf16[512,256]{1,0:T(8,128)(2,1)S(1)} %slice.207), channel_id=1, source_target_pairs={{0,8},{1,9},{2,10},{3,11},{4,12},{5,13},{6,14},{7,15},{8,0},{9,1},... | collective-permute-start | bytes 786440 | tf_op jit(solution)/shard_map/ppermute | solution.py:135
  318.5 15.9 %collective-permute-start.18 = (bf16[256,256]{1,0:T(8,128)(2,1)S(1)}, bf16[256,256]{1,0:T(8,128)(2,1)S(1)}, u32[]{:S(2)}, u32[]{:S(2)}) collective-permute-start(bf16[256,256]{1,0:T(8,128)(2,1)S(1)} %slice.209), channel_id=1, source_target_pairs={{0,2},{1,3},{2,0},{3,1},{4,6},{5,7},{6,4},{7,5},{8,10},{9,11},{10,... | collective-permute-start | bytes 393224 | tf_op jit(solution)/shard_map/ppermute | solution.py:135

commit v11 on v10

--- a/solution.py
+++ b/solution.py
@@ -17,7 +17,7 @@
 SCATTER_ORDERS = tuple(tuple(reversed(order)) for order in GATHER_ORDERS)
 HEAD_GATHER_ORDERS = ((4, 2, 16, 8), (4, 16, 2, 8))
 HEAD_SCATTER_ORDERS = tuple(tuple(reversed(order)) for order in HEAD_GATHER_ORDERS)
-TP_ORDER = (1, 4, 8, 2)
+TP_ORDERS = ((1, 4, 12, 2), (1, 12, 4, 2))
 
 
 def _nt(a, b):
@@ -101,10 +101,24 @@
     return sum(((offset & d) != 0).astype(jnp.int32) << r for r, d in enumerate(distances))
 
 
+def _coefficient_masks(distances):
+    width = max(distances).bit_length()
+    masks = []
+    for r in range(len(distances)):
+        for m in range(1 << width):
+            if all(bin(d & m).count("1") % 2 == (r == s) for s, d in enumerate(distances)):
+                masks.append(m)
+                break
+    return masks
+
+
 def scatter_positions(me, distances, count):
     offset = me ^ jnp.arange(count, dtype=jnp.int32)
     top = len(distances) - 1
-    return sum(((offset & d) == 0).astype(jnp.int32) << (top - r) for r, d in enumerate(distances))
+    return sum(
+        ((lax.population_count(offset & m) & 1) == 0).astype(jnp.int32) << (top - r)
+        for r, m in enumerate(_coefficient_masks(distances))
+    )
 
 
 def per_core(core, tables):
@@ -127,14 +141,32 @@
     return held
 
 
-def tp_halving_reduce(x, order, wire=jnp.bfloat16):
+def tp_positions(me, core, count):
+    first, rest = TP_ORDERS[0][0], [order[1:] for order in TP_ORDERS]
+    assert all(order[0] == first for order in TP_ORDERS)
+    offset = me ^ jnp.arange(count, dtype=jnp.int32)
+    sent = (lax.population_count(offset & _coefficient_masks(TP_ORDERS[0])[0]) & 1) == 1
+
+    def later(off, order):
+        masks = _coefficient_masks((first,) + tuple(order))[1:]
+        top = len(masks) - 1
+        return sum(
+            ((lax.population_count(off & m) & 1) == 0).astype(jnp.int32) << (top - r)
+            for r, m in enumerate(masks)
+        )
+
+    mine = per_core(core, [later(offset, o) for o in rest])
+    theirs = per_core(core, [later(offset ^ first, o) for o in reversed(rest)])
+    return jnp.where(sent, theirs, count // 2 + mine)
+
+
+def tp_halving_reduce(x, orders, wire=jnp.bfloat16):
     count = lax.axis_size("tp")
     held = x
-    for distance in order:
+    for distances in zip(*orders):
         half = held.shape[0] // 2
-        sent = lax.ppermute(
-            held[:half].astype(wire), "tp", [(i, i ^ distance) for i in range(count)]
-        )
+        pairs = [(i, i ^ distances[i % 2]) for i in range(count)]
+        sent = lax.ppermute(held[:half].astype(wire), "tp", pairs)
         held = held[half:].astype(jnp.float32) + sent.astype(jnp.float32)
     return held
 
@@ -200,13 +232,13 @@
         ).astype(jnp.bfloat16)
 
     term = jnp.concatenate([project(held), project(other)], axis=0)
-    tp_at = scatter_positions(me_tp, TP_ORDER, tp_count)
+    tp_at = tp_positions(me_tp, core, tp_count)
     owner = jnp.argsort(tp_at)
     per_owner = ctx_count // tp_count
     wanted = (owner[:, None] * per_owner + jnp.arange(per_owner)[None, :]).reshape(-1)
     source = gather_at[wanted]
     ordered = jnp.take(term.reshape(ctx_count, slab_rows, -1), source, axis=0)
-    return tp_halving_reduce(ordered.reshape(ctx_count * slab_rows, -1), TP_ORDER).astype(
+    return tp_halving_reduce(ordered.reshape(ctx_count * slab_rows, -1), TP_ORDERS).astype(
         jnp.bfloat16
     )
 

time: 342 us -> 335 us (0.980)
  waiting for transfers between devices: 229 us -> 223 us
    ppermute x4, waiting for transfers between devices: 24.8 us -> 18.8 us  [tp_halving_reduce(): sent = lax.ppermute(held[:half].astype(wire), 'tp', pairs)]
where the time goes in v11:
time: 335 us; the launch traced here: 329 us
  waiting for transfers between devices  223 us (67%)
  starting transfers between devices  68.9 us (21%)
  local copies, waits for them, and re-layouts  18.6 us (6%)
  other arithmetic  7.3 us (2%)
  matrix products  5.81 us (2%)
  Pallas kernels  4.88 us (1%)
    ppermute x15, waiting for transfers between devices, _pair_permute(): return lax.ppermute(value, ('ctx', 'tp'), pairs)  204 us
    ppermute x15, starting transfers between devices, _pair_permute(): return lax.ppermute(value, ('ctx', 'tp'), pairs)  46.8 us
    ppermute x4, starting transfers between devices, tp_halving_reduce(): sent = lax.ppermute(held[:half].astype(wire), 'tp', pairs)  22.2 us
    ppermute x4, waiting for transfers between devices, tp_halving_reduce(): sent = lax.ppermute(held[:half].astype(wire), 'tp', pairs)  18.8 us
    unnamed x29, local copies, waits for them, and re-layouts  9.03 us
  transfers between devices with their start and end apart: 19, of which 19 were waited for; matrix products, arithmetic and copies ran while one was open for 4% of the time, Pallas kernels for 0%

profile of v11, /device:TPU:6, one launch (start us, length us, event | category | flops | bytes accessed | tf_op | source)
XLA Modules:
  0.0 328.9 jit_solution(6113636194228434170)
XLA Ops:
  4.0 3.8 %collective-permute-start = (bf16[128,640]{1,0:T(8,128)(2,1)S(1)}, bf16[128,640]{1,0:T(8,128)(2,1)S(1)}, u32[]{:S(2)}, u32[]{:S(2)}) collective-permute-start(bf16[128,640]{1,0:T(8,128)(2,1)S(1)} %get-tuple-element.27), channel_id=1, source_target_pairs={{0,16},{1,17},{2,18},{3,19},{4,20},{5,21},{6,22},{7,23},{8,24},{9,... | collective-permute-start | bytes 491528 | tf_op jit(solution)/shard_map/ppermute | solution.py:96
  7.8 4.2 %collective-permute-done = bf16[128,640]{1,0:T(8,128)(2,1)S(1)} collective-permute-done((bf16[128,640]{1,0:T(8,128)(2,1)S(1)}, bf16[128,640]{1,0:T(8,128)(2,1)S(1)}, u32[]{:S(2)}, u32[]{:S(2)}) %collective-permute-start) | collective-permute-done | bytes 163872 | tf_op jit(solution)/shard_map/ppermute | solution.py:96
  12.1 9.1 %collective-permute-start.1 = (bf16[256,256]{1,0:T(8,128)(2,1)S(1)}, bf16[256,256]{1,0:T(8,128)(2,1)S(1)}, u32[]{:S(2)}, u32[]{:S(2)}) collective-permute-start(bf16[256,256]{1,0:T(8,128)(2,1)S(1)} %get-tuple-element.15), channel_id=1, source_target_pairs={{0,64},{1,65},{2,66},{3,67},{4,68},{5,69},{6,70},{7,71},{8,72},{9,... | collective-permute-start | bytes 393224 | tf_op jit(solution)/shard_map/ppermute | solution.py:96
  21.2 11.2 %collective-permute-done.1 = bf16[256,256]{1,0:T(8,128)(2,1)S(1)} collective-permute-done((bf16[256,256]{1,0:T(8,128)(2,1)S(1)}, bf16[256,256]{1,0:T(8,128)(2,1)S(1)}, u32[]{:S(2)}, u32[]{:S(2)}) %collective-permute-start.1) | collective-permute-done | bytes 131104 | tf_op jit(solution)/shard_map/ppermute | solution.py:96
  32.5 1.9 collective-permute-start.2
  34.5 1.2 sort.17
  35.7 8.4 %collective-permute-done.2 = bf16[512,256]{1,0:T(8,128)(2,1)S(1)} collective-permute-done((bf16[512,256]{1,0:T(8,128)(2,1)S(1)}, bf16[512,256]{1,0:T(8,128)(2,1)S(1)}, u32[]{:S(2)}, u32[]{:S(2)}) %collective-permute-start.2) | collective-permute-done | bytes 262176 | tf_op jit(solution)/shard_map/ppermute | solution.py:96
  44.9 3.3 %collective-permute-start.3 = (bf16[1024,256]{1,0:T(8,128)(2,1)}, bf16[1024,256]{1,0:T(8,128)(2,1)S(1)}, u32[]{:S(2)}, u32[]{:S(2)}) collective-permute-start(bf16[1024,256]{1,0:T(8,128)(2,1)} %pad_maximum_fusion.4), channel_id=1, source_target_pairs={{0,256},{1,33},{2,258},{3,35},{4,260},{5,37},{6,262},{7,39},{8,264... | collective-permute-start | bytes 1572872 | tf_op jit(solution)/shard_map/ppermute | solution.py:96
  48.6 9.1 %collective-permute-done.3 = bf16[1024,256]{1,0:T(8,128)(2,1)S(1)} collective-permute-done((bf16[1024,256]{1,0:T(8,128)(2,1)}, bf16[1024,256]{1,0:T(8,128)(2,1)S(1)}, u32[]{:S(2)}, u32[]{:S(2)}) %collective-permute-start.3) | collective-permute-done | bytes 524320 | tf_op jit(solution)/shard_map/ppermute | solution.py:96
  57.7 1.1 pad_maximum_fusion.2
  58.7 2.7 collective-permute-start.4
  64.0 22.2 %collective-permute-done.4 = bf16[2048,256]{1,0:T(8,128)(2,1)} collective-permute-done((bf16[2048,256]{1,0:T(8,128)(2,1)}, bf16[2048,256]{1,0:T(8,128)(2,1)}, u32[]{:S(2)}, u32[]{:S(2)}) %collective-permute-start.4) | collective-permute-done | bytes 1048608 | tf_op jit(solution)/shard_map/ppermute | solution.py:96
  86.1 1.3 constant_dynamic-update-slice_fusion.10.kv_ref
  87.4 4.9 %shard_map.91 = (f32[256,128]{1,0:T(8,128)S(1)}, bf16[4096,256]{1,0:T(8,128)(2,1)S(1)}) custom-call(f32[8,4096]{1,0:T(8,128)S(1)} %concatenate.57.mask_ref, bf16[256,128]{1,0:T(8,128)(2,1)S(1)} %get-tuple-element.19.q_ref, bf16[256,128]{1,0:T(8,128)(2,1)S(1)} %get-tuple-element.18.do_ref, bf16[256,128]{1,0:T(8,128)(2,1)S(1)} %get-tuple-element.17.o_ref, ...), custom_call_target="tpu_custom_call" | custom-call | flops 1342177280 | bytes 4194304 | tf_op jit(solution)/shard_map/pallas_call | solution.py:72
  92.4 2.8 collective-permute-start.5
  95.2 23.4 %collective-permute-done.5 = bf16[2048,256]{1,0:T(8,128)(2,1)S(1)} collective-permute-done((bf16[2048,256]{1,0:T(8,128)(2,1)S(1)}, bf16[2048,256]{1,0:T(8,128)(2,1)S(1)}, u32[]{:S(2)}, u32[]{:S(2)}) %collective-permute-start.5) | collective-permute-done | bytes 1048608 | tf_op jit(solution)/shard_map/ppermute | solution.py:96
  119.0 3.5 %collective-permute-start.6 = (bf16[1024,256]{1,0:T(8,128)(2,1)S(1)}, bf16[1024,256]{1,0:T(8,128)(2,1)S(1)}, u32[]{:S(2)}, u32[]{:S(2)}) collective-permute-start(bf16[1024,256]{1,0:T(8,128)(2,1)S(1)} %slice.206), channel_id=1, source_target_pairs={{0,256},{1,33},{2,258},{3,35},{4,260},{5,37},{6,262},{7,39},{8,264... | collective-permute-start | bytes 1572872 | tf_op jit(solution)/shard_map/ppermute | solution.py:96
  122.4 9.1 %collective-permute-done.6 = bf16[1024,256]{1,0:T(8,128)(2,1)S(1)} collective-permute-done((bf16[1024,256]{1,0:T(8,128)(2,1)S(1)}, bf16[1024,256]{1,0:T(8,128)(2,1)S(1)}, u32[]{:S(2)}, u32[]{:S(2)}) %collective-permute-start.6) | collective-permute-done | bytes 524320 | tf_op jit(solution)/shard_map/ppermute | solution.py:96
  131.7 1.9 collective-permute-start.7
  133.6 8.3 %collective-permute-done.7 = bf16[512,256]{1,0:T(8,128)(2,1)S(1)} collective-permute-done((bf16[512,256]{1,0:T(8,128)(2,1)S(1)}, bf16[512,256]{1,0:T(8,128)(2,1)S(1)}, u32[]{:S(2)}, u32[]{:S(2)}) %collective-permute-start.7) | collective-permute-done | bytes 262176 | tf_op jit(solution)/shard_map/ppermute | solution.py:96
  142.0 1.9 collective-permute-start.8
  144.0 16.0 %collective-permute-done.8 = bf16[256,256]{1,0:T(8,128)(2,1)S(1)} collective-permute-done((bf16[256,256]{1,0:T(8,128)(2,1)S(1)}, bf16[256,256]{1,0:T(8,128)(2,1)S(1)}, u32[]{:S(2)}, u32[]{:S(2)}) %collective-permute-start.8) | collective-permute-done | bytes 131104 | tf_op jit(solution)/shard_map/ppermute | solution.py:96
  160.1 1.9 collective-permute-start.9
  162.0 4.7 %collective-permute-done.9 = bf16[128,384]{1,0:T(8,128)(2,1)S(1)} collective-permute-done((bf16[128,384]{1,0:T(8,128)(2,1)S(1)}, bf16[128,384]{1,0:T(8,128)(2,1)S(1)}, u32[]{:S(2)}, u32[]{:S(2)}) %collective-permute-start.9) | collective-permute-done | bytes 98336 | tf_op jit(solution)/shard_map/ppermute | solution.py:96
  168.1 1.9 collective-permute-start.10
  170.0 20.2 %collective-permute-done.10 = bf16[128,768]{1,0:T(8,128)(2,1)S(1)} collective-permute-done((bf16[128,768]{1,0:T(8,128)(2,1)S(1)}, bf16[128,768]{1,0:T(8,128)(2,1)S(1)}, u32[]{:S(2)}, u32[]{:S(2)}) %collective-permute-start.10) | collective-permute-done | bytes 196640 | tf_op jit(solution)/shard_map/ppermute | solution.py:96
  190.3 1.9 collective-permute-start.11
  192.2 8.7 %collective-permute-done.11 = bf16[256,768]{1,0:T(8,128)(2,1)S(1)} collective-permute-done((bf16[256,768]{1,0:T(8,128)(2,1)S(1)}, bf16[256,768]{1,0:T(8,128)(2,1)S(1)}, u32[]{:S(2)}, u32[]{:S(2)}) %collective-permute-start.11) | collective-permute-done | bytes 393248 | tf_op jit(solution)/shard_map/ppermute | solution.py:96
  201.0 4.4 %collective-permute-start.12 = (bf16[512,768]{1,0:T(8,128)(2,1)S(1)}, bf16[512,768]{1,0:T(8,128)(2,1)S(1)}, u32[]{:S(2)}, u32[]{:S(2)}) collective-permute-start(bf16[512,768]{1,0:T(8,128)(2,1)S(1)} %pad_maximum_fusion.3), channel_id=1, source_target_pairs={{0,256},{1,33},{2,258},{3,35},{4,260},{5,37},{6,262},{7,39},{8,264... | collective-permute-start | bytes 2359304 | tf_op jit(solution)/shard_map/ppermute | solution.py:96
  205.4 11.0 %collective-permute-done.12 = bf16[512,768]{1,0:T(8,128)(2,1)S(1)} collective-permute-done((bf16[512,768]{1,0:T(8,128)(2,1)S(1)}, bf16[512,768]{1,0:T(8,128)(2,1)S(1)}, u32[]{:S(2)}, u32[]{:S(2)}) %collective-permute-start.12) | collective-permute-done | bytes 786464 | tf_op jit(solution)/shard_map/ppermute | solution.py:96
  216.5 3.8 %collective-permute-start.13 = (bf16[1024,768]{1,0:T(8,128)(2,1)S(1)}, bf16[1024,768]{1,0:T(8,128)(2,1)S(1)}, u32[]{:S(2)}, u32[]{:S(2)}) collective-permute-start(bf16[1024,768]{1,0:T(8,128)(2,1)S(1)} %pad_maximum_fusion.1), channel_id=1, source_target_pairs={{0,128},{1,17},{2,130},{3,19},{4,132},{5,21},{6,134},{7,23},{8,136... | collective-permute-start | bytes 4718600 | tf_op jit(solution)/shard_map/ppermute | solution.py:96
  224.2 1.0 constant_dynamic-update-slice_fusion.22
  225.2 13.6 %collective-permute-done.13 = bf16[1024,768]{1,0:T(8,128)(2,1)S(1)} collective-permute-done((bf16[1024,768]{1,0:T(8,128)(2,1)S(1)}, bf16[1024,768]{1,0:T(8,128)(2,1)S(1)}, u32[]{:S(2)}, u32[]{:S(2)}) %collective-permute-start.13) | collective-permute-done | bytes 1572896 | tf_op jit(solution)/shard_map/ppermute | solution.py:96
  238.8 1.2 constant_dynamic-update-slice_fusion.21
  240.0 1.9 collective-permute-start.14
  242.8 2.9 convolution_convert_fusion.1
  245.7 33.8 %collective-permute-done.14 = bf16[2048,768]{1,0:T(8,128)(2,1)} collective-permute-done((bf16[2048,768]{1,0:T(8,128)(2,1)}, bf16[2048,768]{1,0:T(8,128)(2,1)}, u32[]{:S(2)}, u32[]{:S(2)}) %collective-permute-start.14) | collective-permute-done | bytes 3145760 | tf_op jit(solution)/shard_map/ppermute | solution.py:96
  279.5 2.9 convolution_convert_fusion
  282.6 2.0 gather_fusion.3
  284.6 1.8 broadcast_select_fusion
  286.6 2.0 collective-permute-start.15
  288.6 2.5 collective-permute-done.15
  291.5 3.5 %collective-permute-start.16 = (bf16[1024,256]{1,0:T(8,128)(2,1)S(1)}, bf16[1024,256]{1,0:T(8,128)(2,1)S(1)}, u32[]{:S(2)}, u32[]{:S(2)}) collective-permute-start(bf16[1024,256]{1,0:T(8,128)(2,1)S(1)} %slice.205), channel_id=1, source_target_pairs={{0,4},{1,13},{2,6},{3,15},{4,0},{5,9},{6,2},{7,11},{8,12},{9,5},{1... | collective-permute-start | bytes 1572872 | tf_op jit(solution)/shard_map/ppermute | solution.py:169
  295.0 7.6 %collective-permute-done.16 = bf16[1024,256]{1,0:T(8,128)(2,1)S(1)} collective-permute-done((bf16[1024,256]{1,0:T(8,128)(2,1)S(1)}, bf16[1024,256]{1,0:T(8,128)(2,1)S(1)}, u32[]{:S(2)}, u32[]{:S(2)}) %collective-permute-start.16) | collective-permute-done | bytes 524320 | tf_op jit(solution)/shard_map/ppermute | solution.py:169
  302.8 4.9 %collective-permute-start.17 = (bf16[512,256]{1,0:T(8,128)(2,1)S(1)}, bf16[512,256]{1,0:T(8,128)(2,1)S(1)}, u32[]{:S(2)}, u32[]{:S(2)}) collective-permute-start(bf16[512,256]{1,0:T(8,128)(2,1)S(1)} %slice.207), channel_id=1, source_target_pairs={{0,12},{1,5},{2,14},{3,7},{4,8},{5,1},{6,10},{7,3},{8,4},{9,13},{1... | collective-permute-start | bytes 786440 | tf_op jit(solution)/shard_map/ppermute | solution.py:169
  307.7 4.5 %collective-permute-done.17 = bf16[512,256]{1,0:T(8,128)(2,1)S(1)} collective-permute-done((bf16[512,256]{1,0:T(8,128)(2,1)S(1)}, bf16[512,256]{1,0:T(8,128)(2,1)S(1)}, u32[]{:S(2)}, u32[]{:S(2)}) %collective-permute-start.17) | collective-permute-done | bytes 262176 | tf_op jit(solution)/shard_map/ppermute | solution.py:169
  312.3 11.7 %collective-permute-start.18 = (bf16[256,256]{1,0:T(8,128)(2,1)S(1)}, bf16[256,256]{1,0:T(8,128)(2,1)S(1)}, u32[]{:S(2)}, u32[]{:S(2)}) collective-permute-start(bf16[256,256]{1,0:T(8,128)(2,1)S(1)} %slice.209), channel_id=1, source_target_pairs={{0,2},{1,3},{2,0},{3,1},{4,6},{5,7},{6,4},{7,5},{8,10},{9,11},{10,... | collective-permute-start | bytes 393224 | tf_op jit(solution)/shard_map/ppermute | solution.py:169
  324.1 4.1 %collective-permute-done.18 = bf16[256,256]{1,0:T(8,128)(2,1)S(1)} collective-permute-done((bf16[256,256]{1,0:T(8,128)(2,1)S(1)}, bf16[256,256]{1,0:T(8,128)(2,1)S(1)}, u32[]{:S(2)}, u32[]{:S(2)}) %collective-permute-start.18) | collective-permute-done | bytes 131104 | tf_op jit(solution)/shard_map/ppermute | solution.py:169
  (81 shorter events, 16.2 us)
Async XLA Ops:
  4.0 8.0 %collective-permute-start = (bf16[128,640]{1,0:T(8,128)(2,1)S(1)}, bf16[128,640]{1,0:T(8,128)(2,1)S(1)}, u32[]{:S(2)}, u32[]{:S(2)}) collective-permute-start(bf16[128,640]{1,0:T(8,128)(2,1)S(1)} %get-tuple-element.27), channel_id=1, source_target_pairs={{0,16},{1,17},{2,18},{3,19},{4,20},{5,21},{6,22},{7,23},{8,24},{9,... | collective-permute-start | bytes 491528 | tf_op jit(solution)/shard_map/ppermute | solution.py:96
  12.1 20.3 %collective-permute-start.1 = (bf16[256,256]{1,0:T(8,128)(2,1)S(1)}, bf16[256,256]{1,0:T(8,128)(2,1)S(1)}, u32[]{:S(2)}, u32[]{:S(2)}) collective-permute-start(bf16[256,256]{1,0:T(8,128)(2,1)S(1)} %get-tuple-element.15), channel_id=1, source_target_pairs={{0,64},{1,65},{2,66},{3,67},{4,68},{5,69},{6,70},{7,71},{8,72},{9,... | collective-permute-start | bytes 393224 | tf_op jit(solution)/shard_map/ppermute | solution.py:96
  32.5 11.6 %collective-permute-start.2 = (bf16[512,256]{1,0:T(8,128)(2,1)S(1)}, bf16[512,256]{1,0:T(8,128)(2,1)S(1)}, u32[]{:S(2)}, u32[]{:S(2)}) collective-permute-start(bf16[512,256]{1,0:T(8,128)(2,1)S(1)} %pad_maximum_fusion.6), channel_id=1, source_target_pairs={{0,32},{1,257},{2,34},{3,259},{4,36},{5,261},{6,38},{7,263},{8,40}... | collective-permute-start | bytes 786440 | tf_op jit(solution)/shard_map/ppermute | solution.py:96
  44.9 12.8 %collective-permute-start.3 = (bf16[1024,256]{1,0:T(8,128)(2,1)}, bf16[1024,256]{1,0:T(8,128)(2,1)S(1)}, u32[]{:S(2)}, u32[]{:S(2)}) collective-permute-start(bf16[1024,256]{1,0:T(8,128)(2,1)} %pad_maximum_fusion.4), channel_id=1, source_target_pairs={{0,256},{1,33},{2,258},{3,35},{4,260},{5,37},{6,262},{7,39},{8,264... | collective-permute-start | bytes 1572872 | tf_op jit(solution)/shard_map/ppermute | solution.py:96
  58.7 27.4 %collective-permute-start.4 = (bf16[2048,256]{1,0:T(8,128)(2,1)}, bf16[2048,256]{1,0:T(8,128)(2,1)}, u32[]{:S(2)}, u32[]{:S(2)}) collective-permute-start(bf16[2048,256]{1,0:T(8,128)(2,1)} %pad_maximum_fusion.2), channel_id=1, source_target_pairs={{0,128},{1,129},{2,130},{3,131},{4,132},{5,133},{6,134},{7,135},{8... | collective-permute-start | bytes 3145736 | tf_op jit(solution)/shard_map/ppermute | solution.py:96
  92.4 26.2 %collective-permute-start.5 = (bf16[2048,256]{1,0:T(8,128)(2,1)S(1)}, bf16[2048,256]{1,0:T(8,128)(2,1)S(1)}, u32[]{:S(2)}, u32[]{:S(2)}) collective-permute-start(bf16[2048,256]{1,0:T(8,128)(2,1)S(1)} %slice.99), channel_id=1, source_target_pairs={{0,128},{1,129},{2,130},{3,131},{4,132},{5,133},{6,134},{7,135},{8... | collective-permute-start | bytes 3145736 | tf_op jit(solution)/shard_map/ppermute | solution.py:96
  119.0 12.6 %collective-permute-start.6 = (bf16[1024,256]{1,0:T(8,128)(2,1)S(1)}, bf16[1024,256]{1,0:T(8,128)(2,1)S(1)}, u32[]{:S(2)}, u32[]{:S(2)}) collective-permute-start(bf16[1024,256]{1,0:T(8,128)(2,1)S(1)} %slice.206), channel_id=1, source_target_pairs={{0,256},{1,33},{2,258},{3,35},{4,260},{5,37},{6,262},{7,39},{8,264... | collective-permute-start | bytes 1572872 | tf_op jit(solution)/shard_map/ppermute | solution.py:96
  131.7 10.3 %collective-permute-start.7 = (bf16[512,256]{1,0:T(8,128)(2,1)S(1)}, bf16[512,256]{1,0:T(8,128)(2,1)S(1)}, u32[]{:S(2)}, u32[]{:S(2)}) collective-permute-start(bf16[512,256]{1,0:T(8,128)(2,1)S(1)} %slice.208), channel_id=1, source_target_pairs={{0,32},{1,257},{2,34},{3,259},{4,36},{5,261},{6,38},{7,263},{8,40}... | collective-permute-start | bytes 786440 | tf_op jit(solution)/shard_map/ppermute | solution.py:96
  142.0 18.0 %collective-permute-start.8 = (bf16[256,256]{1,0:T(8,128)(2,1)S(1)}, bf16[256,256]{1,0:T(8,128)(2,1)S(1)}, u32[]{:S(2)}, u32[]{:S(2)}) collective-permute-start(bf16[256,256]{1,0:T(8,128)(2,1)S(1)} %slice.210), channel_id=1, source_target_pairs={{0,64},{1,65},{2,66},{3,67},{4,68},{5,69},{6,70},{7,71},{8,72},{9,... | collective-permute-start | bytes 393224 | tf_op jit(solution)/shard_map/ppermute | solution.py:96
  160.1 6.6 %collective-permute-start.9 = (bf16[128,384]{1,0:T(8,128)(2,1)S(1)}, bf16[128,384]{1,0:T(8,128)(2,1)S(1)}, u32[]{:S(2)}, u32[]{:S(2)}) collective-permute-start(bf16[128,384]{1,0:T(8,128)(2,1)S(1)} %broadcast_select_fusion.3), channel_id=1, source_target_pairs={{0,16},{1,17},{2,18},{3,19},{4,20},{5,21},{6,22},{7,23},{8,24},{9,... | collective-permute-start | bytes 294920 | tf_op jit(solution)/shard_map/ppermute | solution.py:96
  168.1 22.2 %collective-permute-start.10 = (bf16[128,768]{1,0:T(8,128)(2,1)S(1)}, bf16[128,768]{1,0:T(8,128)(2,1)S(1)}, u32[]{:S(2)}, u32[]{:S(2)}) collective-permute-start(bf16[128,768]{1,0:T(8,128)(2,1)S(1)} %get-tuple-element.22), channel_id=1, source_target_pairs={{0,64},{1,65},{2,66},{3,67},{4,68},{5,69},{6,70},{7,71},{8,72},{9,... | collective-permute-start | bytes 589832 | tf_op jit(solution)/shard_map/ppermute | solution.py:96
  190.3 10.7 %collective-permute-start.11 = (bf16[256,768]{1,0:T(8,128)(2,1)S(1)}, bf16[256,768]{1,0:T(8,128)(2,1)S(1)}, u32[]{:S(2)}, u32[]{:S(2)}) collective-permute-start(bf16[256,768]{1,0:T(8,128)(2,1)S(1)} %pad_maximum_fusion.5), channel_id=1, source_target_pairs={{0,32},{1,257},{2,34},{3,259},{4,36},{5,261},{6,38},{7,263},{8,40}... | collective-permute-start | bytes 1179656 | tf_op jit(solution)/shard_map/ppermute | solution.py:96
  201.0 15.4 %collective-permute-start.12 = (bf16[512,768]{1,0:T(8,128)(2,1)S(1)}, bf16[512,768]{1,0:T(8,128)(2,1)S(1)}, u32[]{:S(2)}, u32[]{:S(2)}) collective-permute-start(bf16[512,768]{1,0:T(8,128)(2,1)S(1)} %pad_maximum_fusion.3), channel_id=1, source_target_pairs={{0,256},{1,33},{2,258},{3,35},{4,260},{5,37},{6,262},{7,39},{8,264... | collective-permute-start | bytes 2359304 | tf_op jit(solution)/shard_map/ppermute | solution.py:96
  216.5 22.3 %collective-permute-start.13 = (bf16[1024,768]{1,0:T(8,128)(2,1)S(1)}, bf16[1024,768]{1,0:T(8,128)(2,1)S(1)}, u32[]{:S(2)}, u32[]{:S(2)}) collective-permute-start(bf16[1024,768]{1,0:T(8,128)(2,1)S(1)} %pad_maximum_fusion.1), channel_id=1, source_target_pairs={{0,128},{1,17},{2,130},{3,19},{4,132},{5,21},{6,134},{7,23},{8,136... | collective-permute-start | bytes 4718600 | tf_op jit(solution)/shard_map/ppermute | solution.py:96
  225.2 17.5 %copy-start = (bf16[256,256]{1,0:T(8,128)(2,1)S(1)}, bf16[256,256]{1,0:T(8,128)(2,1)}, u32[]{:S(2)}) copy-start(bf16[256,256]{1,0:T(8,128)(2,1)} %param.15) | copy-start | bytes 393220
  225.2 17.5 %copy-start.1 = (bf16[256,256]{1,0:T(8,128)(2,1)S(1)}, bf16[256,256]{1,0:T(8,128)(2,1)}, u32[]{:S(2)}) copy-start(bf16[256,256]{1,0:T(8,128)(2,1)} %param.16) | copy-start | bytes 393220
  225.2 17.5 %copy-start.2 = (bf16[256,256]{1,0:T(8,128)(2,1)S(1)}, bf16[256,256]{1,0:T(8,128)(2,1)}, u32[]{:S(2)}) copy-start(bf16[256,256]{1,0:T(8,128)(2,1)} %param.17) | copy-start | bytes 393220
  240.0 39.5 %collective-permute-start.14 = (bf16[2048,768]{1,0:T(8,128)(2,1)}, bf16[2048,768]{1,0:T(8,128)(2,1)}, u32[]{:S(2)}, u32[]{:S(2)}) collective-permute-start(bf16[2048,768]{1,0:T(8,128)(2,1)} %constant_dynamic-update-slice_fusion.21), channel_id=1, source_target_pairs={{0,16},{1,129},{2,18},{3,131},{4,20},{5,133},{6,22},{7,135},{8,24}... | collective-permute-start | bytes 9437192 | tf_op jit(solution)/shard_map/ppermute | solution.py:96
  286.6 4.6 %collective-permute-start.15 = (bf16[2048,256]{1,0:T(8,128)(2,1)S(1)}, bf16[2048,256]{1,0:T(8,128)(2,1)S(1)}, u32[]{:S(2)}, u32[]{:S(2)}) collective-permute-start(bf16[2048,256]{1,0:T(8,128)(2,1)S(1)} %bitcast.29), channel_id=1, source_target_pairs={{0,1},{1,0},{2,3},{3,2},{4,5},{5,4},{6,7},{7,6},{8,9},{9,8},{10,11... | collective-permute-start | bytes 3145736 | tf_op jit(solution)/shard_map/ppermute | solution.py:169
  291.5 11.1 %collective-permute-start.16 = (bf16[1024,256]{1,0:T(8,128)(2,1)S(1)}, bf16[1024,256]{1,0:T(8,128)(2,1)S(1)}, u32[]{:S(2)}, u32[]{:S(2)}) collective-permute-start(bf16[1024,256]{1,0:T(8,128)(2,1)S(1)} %slice.205), channel_id=1, source_target_pairs={{0,4},{1,13},{2,6},{3,15},{4,0},{5,9},{6,2},{7,11},{8,12},{9,5},{1... | collective-permute-start | bytes 1572872 | tf_op jit(solution)/shard_map/ppermute | solution.py:169
  302.8 9.5 %collective-permute-start.17 = (bf16[512,256]{1,0:T(8,128)(2,1)S(1)}, bf16[512,256]{1,0:T(8,128)(2,1)S(1)}, u32[]{:S(2)}, u32[]{:S(2)}) collective-permute-start(bf16[512,256]{1,0:T(8,128)(2,1)S(1)} %slice.207), channel_id=1, source_target_pairs={{0,12},{1,5},{2,14},{3,7},{4,8},{5,1},{6,10},{7,3},{8,4},{9,13},{1... | collective-permute-start | bytes 786440 | tf_op jit(solution)/shard_map/ppermute | solution.py:169
  312.3 15.9 %collective-permute-start.18 = (bf16[256,256]{1,0:T(8,128)(2,1)S(1)}, bf16[256,256]{1,0:T(8,128)(2,1)S(1)}, u32[]{:S(2)}, u32[]{:S(2)}) collective-permute-start(bf16[256,256]{1,0:T(8,128)(2,1)S(1)} %slice.209), channel_id=1, source_target_pairs={{0,2},{1,3},{2,0},{3,1},{4,6},{5,7},{6,4},{7,5},{8,10},{9,11},{10,... | collective-permute-start | bytes 393224 | tf_op jit(solution)/shard_map/ppermute | solution.py:169

commit v12 on v11

--- a/solution.py
+++ b/solution.py
@@ -13,9 +13,9 @@
 
 
 NEG_FILL = -1e30
-GATHER_ORDERS = ((4, 2, 16, 8, 1), (4, 16, 2, 1, 8))
+GATHER_ORDERS = ((4, 2, 24, 8, 1), (4, 24, 2, 1, 8))
 SCATTER_ORDERS = tuple(tuple(reversed(order)) for order in GATHER_ORDERS)
-HEAD_GATHER_ORDERS = ((4, 2, 16, 8), (4, 16, 2, 8))
+HEAD_GATHER_ORDERS = ((4, 2, 24, 8), (4, 24, 2, 8))
 HEAD_SCATTER_ORDERS = tuple(tuple(reversed(order)) for order in HEAD_GATHER_ORDERS)
 TP_ORDERS = ((1, 4, 12, 2), (1, 12, 4, 2))
 
@@ -98,7 +98,10 @@
 
 def gather_positions(me, distances, count):
     offset = me ^ jnp.arange(count, dtype=jnp.int32)
-    return sum(((offset & d) != 0).astype(jnp.int32) << r for r, d in enumerate(distances))
+    return sum(
+        (lax.population_count(offset & m) & 1) << r
+        for r, m in enumerate(_coefficient_masks(distances))
+    )
 
 
 def _coefficient_masks(distances):
@@ -173,7 +176,10 @@
 
 def xor_of_position(distances, count):
     position = jnp.arange(count, dtype=jnp.int32)
-    return sum(((position >> r) & 1) * d for r, d in enumerate(distances))
+    total = jnp.zeros_like(position)
+    for r, d in enumerate(distances):
+        total = total ^ (((position >> r) & 1) * d)
+    return total
 
 
 def per_device(

time: 335 us -> 342 us (1.021)
  waiting for transfers between devices: 223 us -> 233 us
    ppermute x4, waiting for transfers between devices: 18.8 us -> 24.2 us  [tp_halving_reduce(): sent = lax.ppermute(held[:half].astype(wire), 'tp', pairs)]
    ppermute x15, waiting for transfers between devices: 204 us -> 209 us  [_pair_permute(): return lax.ppermute(value, ('ctx', 'tp'), pairs)]
where the time goes in v12:
time: 342 us; the launch traced here: 339 us
  waiting for transfers between devices  233 us (68%)
  starting transfers between devices  68.8 us (20%)
  local copies, waits for them, and re-layouts  18.6 us (5%)
  other arithmetic  7.31 us (2%)
  matrix products  5.81 us (2%)
  Pallas kernels  4.89 us (1%)
    ppermute x15, waiting for transfers between devices, _pair_permute(): return lax.ppermute(value, ('ctx', 'tp'), pairs)  209 us
    ppermute x15, starting transfers between devices, _pair_permute(): return lax.ppermute(value, ('ctx', 'tp'), pairs)  47 us
    ppermute x4, waiting for transfers between devices, tp_halving_reduce(): sent = lax.ppermute(held[:half].astype(wire), 'tp', pairs)  24.2 us
    ppermute x4, starting transfers between devices, tp_halving_reduce(): sent = lax.ppermute(held[:half].astype(wire), 'tp', pairs)  21.8 us
    unnamed x29, local copies, waits for them, and re-layouts  9.03 us
  transfers between devices with their start and end apart: 19, of which 19 were waited for; matrix products, arithmetic and copies ran while one was open for 4% of the time, Pallas kernels for 0%

profile of v12, /device:TPU:6, one launch (start us, length us, event | category | flops | bytes accessed | tf_op | source)
XLA Modules:
  0.0 338.7 jit_solution(977829380365030376)
XLA Ops:
  4.0 3.8 %collective-permute-start = (bf16[128,640]{1,0:T(8,128)(2,1)S(1)}, bf16[128,640]{1,0:T(8,128)(2,1)S(1)}, u32[]{:S(2)}, u32[]{:S(2)}) collective-permute-start(bf16[128,640]{1,0:T(8,128)(2,1)S(1)} %get-tuple-element.27), channel_id=1, source_target_pairs={{0,16},{1,17},{2,18},{3,19},{4,20},{5,21},{6,22},{7,23},{8,24},{9,... | collective-permute-start | bytes 491528 | tf_op jit(solution)/shard_map/ppermute | solution.py:96
  7.8 4.2 %collective-permute-done = bf16[128,640]{1,0:T(8,128)(2,1)S(1)} collective-permute-done((bf16[128,640]{1,0:T(8,128)(2,1)S(1)}, bf16[128,640]{1,0:T(8,128)(2,1)S(1)}, u32[]{:S(2)}, u32[]{:S(2)}) %collective-permute-start) | collective-permute-done | bytes 163872 | tf_op jit(solution)/shard_map/ppermute | solution.py:96
  12.1 9.1 %collective-permute-start.1 = (bf16[256,256]{1,0:T(8,128)(2,1)S(1)}, bf16[256,256]{1,0:T(8,128)(2,1)S(1)}, u32[]{:S(2)}, u32[]{:S(2)}) collective-permute-start(bf16[256,256]{1,0:T(8,128)(2,1)S(1)} %get-tuple-element.15), channel_id=1, source_target_pairs={{0,64},{1,65},{2,66},{3,67},{4,68},{5,69},{6,70},{7,71},{8,72},{9,... | collective-permute-start | bytes 393224 | tf_op jit(solution)/shard_map/ppermute | solution.py:96
  21.2 11.2 %collective-permute-done.1 = bf16[256,256]{1,0:T(8,128)(2,1)S(1)} collective-permute-done((bf16[256,256]{1,0:T(8,128)(2,1)S(1)}, bf16[256,256]{1,0:T(8,128)(2,1)S(1)}, u32[]{:S(2)}, u32[]{:S(2)}) %collective-permute-start.1) | collective-permute-done | bytes 131104 | tf_op jit(solution)/shard_map/ppermute | solution.py:96
  32.5 1.9 collective-permute-start.2
  34.5 1.2 sort.17
  35.7 8.4 %collective-permute-done.2 = bf16[512,256]{1,0:T(8,128)(2,1)S(1)} collective-permute-done((bf16[512,256]{1,0:T(8,128)(2,1)S(1)}, bf16[512,256]{1,0:T(8,128)(2,1)S(1)}, u32[]{:S(2)}, u32[]{:S(2)}) %collective-permute-start.2) | collective-permute-done | bytes 262176 | tf_op jit(solution)/shard_map/ppermute | solution.py:96
  44.9 2.4 collective-permute-start.3
  47.7 9.7 %collective-permute-done.3 = bf16[1024,256]{1,0:T(8,128)(2,1)S(1)} collective-permute-done((bf16[1024,256]{1,0:T(8,128)(2,1)}, bf16[1024,256]{1,0:T(8,128)(2,1)S(1)}, u32[]{:S(2)}, u32[]{:S(2)}) %collective-permute-start.3) | collective-permute-done | bytes 524320 | tf_op jit(solution)/shard_map/ppermute | solution.py:96
  57.4 1.1 pad_maximum_fusion.2
  58.5 1.9 collective-permute-start.4
  62.8 23.0 %collective-permute-done.4 = bf16[2048,256]{1,0:T(8,128)(2,1)} collective-permute-done((bf16[2048,256]{1,0:T(8,128)(2,1)}, bf16[2048,256]{1,0:T(8,128)(2,1)}, u32[]{:S(2)}, u32[]{:S(2)}) %collective-permute-start.4) | collective-permute-done | bytes 1048608 | tf_op jit(solution)/shard_map/ppermute | solution.py:96
  85.8 1.3 constant_dynamic-update-slice_fusion.10.kv_ref
  87.1 4.9 %shard_map.91 = (f32[256,128]{1,0:T(8,128)S(1)}, bf16[4096,256]{1,0:T(8,128)(2,1)S(1)}) custom-call(f32[8,4096]{1,0:T(8,128)S(1)} %concatenate.57.mask_ref, bf16[256,128]{1,0:T(8,128)(2,1)S(1)} %get-tuple-element.19.q_ref, bf16[256,128]{1,0:T(8,128)(2,1)S(1)} %get-tuple-element.18.do_ref, bf16[256,128]{1,0:T(8,128)(2,1)S(1)} %get-tuple-element.17.o_ref, ...), custom_call_target="tpu_custom_call" | custom-call | flops 1342177280 | bytes 4194304 | tf_op jit(solution)/shard_map/pallas_call | solution.py:72
  92.1 2.2 collective-permute-start.5
  94.3 24.0 %collective-permute-done.5 = bf16[2048,256]{1,0:T(8,128)(2,1)S(1)} collective-permute-done((bf16[2048,256]{1,0:T(8,128)(2,1)S(1)}, bf16[2048,256]{1,0:T(8,128)(2,1)S(1)}, u32[]{:S(2)}, u32[]{:S(2)}) %collective-permute-start.5) | collective-permute-done | bytes 1048608 | tf_op jit(solution)/shard_map/ppermute | solution.py:96
  118.7 2.4 collective-permute-start.6
  121.1 9.9 %collective-permute-done.6 = bf16[1024,256]{1,0:T(8,128)(2,1)S(1)} collective-permute-done((bf16[1024,256]{1,0:T(8,128)(2,1)S(1)}, bf16[1024,256]{1,0:T(8,128)(2,1)S(1)}, u32[]{:S(2)}, u32[]{:S(2)}) %collective-permute-start.6) | collective-permute-done | bytes 524320 | tf_op jit(solution)/shard_map/ppermute | solution.py:96
  131.1 2.1 collective-permute-start.7
  133.2 8.2 %collective-permute-done.7 = bf16[512,256]{1,0:T(8,128)(2,1)S(1)} collective-permute-done((bf16[512,256]{1,0:T(8,128)(2,1)S(1)}, bf16[512,256]{1,0:T(8,128)(2,1)S(1)}, u32[]{:S(2)}, u32[]{:S(2)}) %collective-permute-start.7) | collective-permute-done | bytes 262176 | tf_op jit(solution)/shard_map/ppermute | solution.py:96
  141.5 1.9 collective-permute-start.8
  143.5 16.2 %collective-permute-done.8 = bf16[256,256]{1,0:T(8,128)(2,1)S(1)} collective-permute-done((bf16[256,256]{1,0:T(8,128)(2,1)S(1)}, bf16[256,256]{1,0:T(8,128)(2,1)S(1)}, u32[]{:S(2)}, u32[]{:S(2)}) %collective-permute-start.8) | collective-permute-done | bytes 131104 | tf_op jit(solution)/shard_map/ppermute | solution.py:96
  159.8 1.9 collective-permute-start.9
  161.7 4.7 %collective-permute-done.9 = bf16[128,384]{1,0:T(8,128)(2,1)S(1)} collective-permute-done((bf16[128,384]{1,0:T(8,128)(2,1)S(1)}, bf16[128,384]{1,0:T(8,128)(2,1)S(1)}, u32[]{:S(2)}, u32[]{:S(2)}) %collective-permute-start.9) | collective-permute-done | bytes 98336 | tf_op jit(solution)/shard_map/ppermute | solution.py:96
  167.8 1.9 collective-permute-start.10
  169.7 20.3 %collective-permute-done.10 = bf16[128,768]{1,0:T(8,128)(2,1)S(1)} collective-permute-done((bf16[128,768]{1,0:T(8,128)(2,1)S(1)}, bf16[128,768]{1,0:T(8,128)(2,1)S(1)}, u32[]{:S(2)}, u32[]{:S(2)}) %collective-permute-start.10) | collective-permute-done | bytes 196640 | tf_op jit(solution)/shard_map/ppermute | solution.py:96
  190.1 1.9 collective-permute-start.11
  192.0 8.7 %collective-permute-done.11 = bf16[256,768]{1,0:T(8,128)(2,1)S(1)} collective-permute-done((bf16[256,768]{1,0:T(8,128)(2,1)S(1)}, bf16[256,768]{1,0:T(8,128)(2,1)S(1)}, u32[]{:S(2)}, u32[]{:S(2)}) %collective-permute-start.11) | collective-permute-done | bytes 393248 | tf_op jit(solution)/shard_map/ppermute | solution.py:96
  200.8 2.4 collective-permute-start.12
  203.2 12.7 %collective-permute-done.12 = bf16[512,768]{1,0:T(8,128)(2,1)S(1)} collective-permute-done((bf16[512,768]{1,0:T(8,128)(2,1)S(1)}, bf16[512,768]{1,0:T(8,128)(2,1)S(1)}, u32[]{:S(2)}, u32[]{:S(2)}) %collective-permute-start.12) | collective-permute-done | bytes 786464 | tf_op jit(solution)/shard_map/ppermute | solution.py:96
  216.0 9.2 %collective-permute-start.13 = (bf16[1024,768]{1,0:T(8,128)(2,1)S(1)}, bf16[1024,768]{1,0:T(8,128)(2,1)S(1)}, u32[]{:S(2)}, u32[]{:S(2)}) collective-permute-start(bf16[1024,768]{1,0:T(8,128)(2,1)S(1)} %pad_maximum_fusion.1), channel_id=1, source_target_pairs={{0,128},{1,17},{2,130},{3,19},{4,132},{5,21},{6,134},{7,23},{8,136... | collective-permute-start | bytes 4718600 | tf_op jit(solution)/shard_map/ppermute | solution.py:96
  229.2 1.0 constant_dynamic-update-slice_fusion.22
  230.2 13.4 %collective-permute-done.13 = bf16[1024,768]{1,0:T(8,128)(2,1)S(1)} collective-permute-done((bf16[1024,768]{1,0:T(8,128)(2,1)S(1)}, bf16[1024,768]{1,0:T(8,128)(2,1)S(1)}, u32[]{:S(2)}, u32[]{:S(2)}) %collective-permute-start.13) | collective-permute-done | bytes 1572896 | tf_op jit(solution)/shard_map/ppermute | solution.py:96
  243.6 1.2 constant_dynamic-update-slice_fusion.21
  244.9 1.9 collective-permute-start.14
  247.6 2.9 convolution_convert_fusion.1
  250.5 33.8 %collective-permute-done.14 = bf16[2048,768]{1,0:T(8,128)(2,1)} collective-permute-done((bf16[2048,768]{1,0:T(8,128)(2,1)}, bf16[2048,768]{1,0:T(8,128)(2,1)}, u32[]{:S(2)}, u32[]{:S(2)}) %collective-permute-start.14) | collective-permute-done | bytes 3145760 | tf_op jit(solution)/shard_map/ppermute | solution.py:96
  284.3 2.9 convolution_convert_fusion
  287.4 2.0 gather_fusion.3
  289.4 1.8 broadcast_select_fusion
  291.4 1.9 collective-permute-start.15
  293.3 2.6 collective-permute-done.15
  296.4 3.5 %collective-permute-start.16 = (bf16[1024,256]{1,0:T(8,128)(2,1)S(1)}, bf16[1024,256]{1,0:T(8,128)(2,1)S(1)}, u32[]{:S(2)}, u32[]{:S(2)}) collective-permute-start(bf16[1024,256]{1,0:T(8,128)(2,1)S(1)} %slice.205), channel_id=1, source_target_pairs={{0,4},{1,13},{2,6},{3,15},{4,0},{5,9},{6,2},{7,11},{8,12},{9,5},{1... | collective-permute-start | bytes 1572872 | tf_op jit(solution)/shard_map/ppermute | solution.py:172
  299.8 7.6 %collective-permute-done.16 = bf16[1024,256]{1,0:T(8,128)(2,1)S(1)} collective-permute-done((bf16[1024,256]{1,0:T(8,128)(2,1)S(1)}, bf16[1024,256]{1,0:T(8,128)(2,1)S(1)}, u32[]{:S(2)}, u32[]{:S(2)}) %collective-permute-start.16) | collective-permute-done | bytes 524320 | tf_op jit(solution)/shard_map/ppermute | solution.py:172
  307.6 4.9 %collective-permute-start.17 = (bf16[512,256]{1,0:T(8,128)(2,1)S(1)}, bf16[512,256]{1,0:T(8,128)(2,1)S(1)}, u32[]{:S(2)}, u32[]{:S(2)}) collective-permute-start(bf16[512,256]{1,0:T(8,128)(2,1)S(1)} %slice.207), channel_id=1, source_target_pairs={{0,12},{1,5},{2,14},{3,7},{4,8},{5,1},{6,10},{7,3},{8,4},{9,13},{1... | collective-permute-start | bytes 786440 | tf_op jit(solution)/shard_map/ppermute | solution.py:172
  312.5 4.5 %collective-permute-done.17 = bf16[512,256]{1,0:T(8,128)(2,1)S(1)} collective-permute-done((bf16[512,256]{1,0:T(8,128)(2,1)S(1)}, bf16[512,256]{1,0:T(8,128)(2,1)S(1)}, u32[]{:S(2)}, u32[]{:S(2)}) %collective-permute-start.17) | collective-permute-done | bytes 262176 | tf_op jit(solution)/shard_map/ppermute | solution.py:172
  317.1 11.5 %collective-permute-start.18 = (bf16[256,256]{1,0:T(8,128)(2,1)S(1)}, bf16[256,256]{1,0:T(8,128)(2,1)S(1)}, u32[]{:S(2)}, u32[]{:S(2)}) collective-permute-start(bf16[256,256]{1,0:T(8,128)(2,1)S(1)} %slice.209), channel_id=1, source_target_pairs={{0,2},{1,3},{2,0},{3,1},{4,6},{5,7},{6,4},{7,5},{8,10},{9,11},{10,... | collective-permute-start | bytes 393224 | tf_op jit(solution)/shard_map/ppermute | solution.py:172
  328.6 9.4 %collective-permute-done.18 = bf16[256,256]{1,0:T(8,128)(2,1)S(1)} collective-permute-done((bf16[256,256]{1,0:T(8,128)(2,1)S(1)}, bf16[256,256]{1,0:T(8,128)(2,1)S(1)}, u32[]{:S(2)}, u32[]{:S(2)}) %collective-permute-start.18) | collective-permute-done | bytes 131104 | tf_op jit(solution)/shard_map/ppermute | solution.py:172
  (81 shorter events, 16.2 us)
Async XLA Ops:
  4.0 8.0 %collective-permute-start = (bf16[128,640]{1,0:T(8,128)(2,1)S(1)}, bf16[128,640]{1,0:T(8,128)(2,1)S(1)}, u32[]{:S(2)}, u32[]{:S(2)}) collective-permute-start(bf16[128,640]{1,0:T(8,128)(2,1)S(1)} %get-tuple-element.27), channel_id=1, source_target_pairs={{0,16},{1,17},{2,18},{3,19},{4,20},{5,21},{6,22},{7,23},{8,24},{9,... | collective-permute-start | bytes 491528 | tf_op jit(solution)/shard_map/ppermute | solution.py:96
  12.1 20.3 %collective-permute-start.1 = (bf16[256,256]{1,0:T(8,128)(2,1)S(1)}, bf16[256,256]{1,0:T(8,128)(2,1)S(1)}, u32[]{:S(2)}, u32[]{:S(2)}) collective-permute-start(bf16[256,256]{1,0:T(8,128)(2,1)S(1)} %get-tuple-element.15), channel_id=1, source_target_pairs={{0,64},{1,65},{2,66},{3,67},{4,68},{5,69},{6,70},{7,71},{8,72},{9,... | collective-permute-start | bytes 393224 | tf_op jit(solution)/shard_map/ppermute | solution.py:96
  32.5 11.6 %collective-permute-start.2 = (bf16[512,256]{1,0:T(8,128)(2,1)S(1)}, bf16[512,256]{1,0:T(8,128)(2,1)S(1)}, u32[]{:S(2)}, u32[]{:S(2)}) collective-permute-start(bf16[512,256]{1,0:T(8,128)(2,1)S(1)} %pad_maximum_fusion.6), channel_id=1, source_target_pairs={{0,32},{1,385},{2,34},{3,387},{4,36},{5,389},{6,38},{7,391},{8,40}... | collective-permute-start | bytes 786440 | tf_op jit(solution)/shard_map/ppermute | solution.py:96
  44.9 12.5 %collective-permute-start.3 = (bf16[1024,256]{1,0:T(8,128)(2,1)}, bf16[1024,256]{1,0:T(8,128)(2,1)S(1)}, u32[]{:S(2)}, u32[]{:S(2)}) collective-permute-start(bf16[1024,256]{1,0:T(8,128)(2,1)} %pad_maximum_fusion.4), channel_id=1, source_target_pairs={{0,384},{1,33},{2,386},{3,35},{4,388},{5,37},{6,390},{7,39},{8,392... | collective-permute-start | bytes 1572872 | tf_op jit(solution)/shard_map/ppermute | solution.py:96
  58.5 27.4 %collective-permute-start.4 = (bf16[2048,256]{1,0:T(8,128)(2,1)}, bf16[2048,256]{1,0:T(8,128)(2,1)}, u32[]{:S(2)}, u32[]{:S(2)}) collective-permute-start(bf16[2048,256]{1,0:T(8,128)(2,1)} %pad_maximum_fusion.2), channel_id=1, source_target_pairs={{0,128},{1,129},{2,130},{3,131},{4,132},{5,133},{6,134},{7,135},{8... | collective-permute-start | bytes 3145736 | tf_op jit(solution)/shard_map/ppermute | solution.py:96
  92.1 26.2 %collective-permute-start.5 = (bf16[2048,256]{1,0:T(8,128)(2,1)S(1)}, bf16[2048,256]{1,0:T(8,128)(2,1)S(1)}, u32[]{:S(2)}, u32[]{:S(2)}) collective-permute-start(bf16[2048,256]{1,0:T(8,128)(2,1)S(1)} %slice.99), channel_id=1, source_target_pairs={{0,128},{1,129},{2,130},{3,131},{4,132},{5,133},{6,134},{7,135},{8... | collective-permute-start | bytes 3145736 | tf_op jit(solution)/shard_map/ppermute | solution.py:96
  118.7 12.3 %collective-permute-start.6 = (bf16[1024,256]{1,0:T(8,128)(2,1)S(1)}, bf16[1024,256]{1,0:T(8,128)(2,1)S(1)}, u32[]{:S(2)}, u32[]{:S(2)}) collective-permute-start(bf16[1024,256]{1,0:T(8,128)(2,1)S(1)} %slice.206), channel_id=1, source_target_pairs={{0,384},{1,33},{2,386},{3,35},{4,388},{5,37},{6,390},{7,39},{8,392... | collective-permute-start | bytes 1572872 | tf_op jit(solution)/shard_map/ppermute | solution.py:96
  131.1 10.4 %collective-permute-start.7 = (bf16[512,256]{1,0:T(8,128)(2,1)S(1)}, bf16[512,256]{1,0:T(8,128)(2,1)S(1)}, u32[]{:S(2)}, u32[]{:S(2)}) collective-permute-start(bf16[512,256]{1,0:T(8,128)(2,1)S(1)} %slice.208), channel_id=1, source_target_pairs={{0,32},{1,385},{2,34},{3,387},{4,36},{5,389},{6,38},{7,391},{8,40}... | collective-permute-start | bytes 786440 | tf_op jit(solution)/shard_map/ppermute | solution.py:96
  141.5 18.2 %collective-permute-start.8 = (bf16[256,256]{1,0:T(8,128)(2,1)S(1)}, bf16[256,256]{1,0:T(8,128)(2,1)S(1)}, u32[]{:S(2)}, u32[]{:S(2)}) collective-permute-start(bf16[256,256]{1,0:T(8,128)(2,1)S(1)} %slice.210), channel_id=1, source_target_pairs={{0,64},{1,65},{2,66},{3,67},{4,68},{5,69},{6,70},{7,71},{8,72},{9,... | collective-permute-start | bytes 393224 | tf_op jit(solution)/shard_map/ppermute | solution.py:96
  159.8 6.6 %collective-permute-start.9 = (bf16[128,384]{1,0:T(8,128)(2,1)S(1)}, bf16[128,384]{1,0:T(8,128)(2,1)S(1)}, u32[]{:S(2)}, u32[]{:S(2)}) collective-permute-start(bf16[128,384]{1,0:T(8,128)(2,1)S(1)} %broadcast_select_fusion.3), channel_id=1, source_target_pairs={{0,16},{1,17},{2,18},{3,19},{4,20},{5,21},{6,22},{7,23},{8,24},{9,... | collective-permute-start | bytes 294920 | tf_op jit(solution)/shard_map/ppermute | solution.py:96
  167.8 22.3 %collective-permute-start.10 = (bf16[128,768]{1,0:T(8,128)(2,1)S(1)}, bf16[128,768]{1,0:T(8,128)(2,1)S(1)}, u32[]{:S(2)}, u32[]{:S(2)}) collective-permute-start(bf16[128,768]{1,0:T(8,128)(2,1)S(1)} %get-tuple-element.22), channel_id=1, source_target_pairs={{0,64},{1,65},{2,66},{3,67},{4,68},{5,69},{6,70},{7,71},{8,72},{9,... | collective-permute-start | bytes 589832 | tf_op jit(solution)/shard_map/ppermute | solution.py:96
  190.1 10.7 %collective-permute-start.11 = (bf16[256,768]{1,0:T(8,128)(2,1)S(1)}, bf16[256,768]{1,0:T(8,128)(2,1)S(1)}, u32[]{:S(2)}, u32[]{:S(2)}) collective-permute-start(bf16[256,768]{1,0:T(8,128)(2,1)S(1)} %pad_maximum_fusion.5), channel_id=1, source_target_pairs={{0,32},{1,385},{2,34},{3,387},{4,36},{5,389},{6,38},{7,391},{8,40}... | collective-permute-start | bytes 1179656 | tf_op jit(solution)/shard_map/ppermute | solution.py:96
  200.8 15.1 %collective-permute-start.12 = (bf16[512,768]{1,0:T(8,128)(2,1)S(1)}, bf16[512,768]{1,0:T(8,128)(2,1)S(1)}, u32[]{:S(2)}, u32[]{:S(2)}) collective-permute-start(bf16[512,768]{1,0:T(8,128)(2,1)S(1)} %pad_maximum_fusion.3), channel_id=1, source_target_pairs={{0,384},{1,33},{2,386},{3,35},{4,388},{5,37},{6,390},{7,39},{8,392... | collective-permute-start | bytes 2359304 | tf_op jit(solution)/shard_map/ppermute | solution.py:96
  216.0 27.6 %collective-permute-start.13 = (bf16[1024,768]{1,0:T(8,128)(2,1)S(1)}, bf16[1024,768]{1,0:T(8,128)(2,1)S(1)}, u32[]{:S(2)}, u32[]{:S(2)}) collective-permute-start(bf16[1024,768]{1,0:T(8,128)(2,1)S(1)} %pad_maximum_fusion.1), channel_id=1, source_target_pairs={{0,128},{1,17},{2,130},{3,19},{4,132},{5,21},{6,134},{7,23},{8,136... | collective-permute-start | bytes 4718600 | tf_op jit(solution)/shard_map/ppermute | solution.py:96
  230.2 17.3 %copy-start = (bf16[256,256]{1,0:T(8,128)(2,1)S(1)}, bf16[256,256]{1,0:T(8,128)(2,1)}, u32[]{:S(2)}) copy-start(bf16[256,256]{1,0:T(8,128)(2,1)} %param.15) | copy-start | bytes 393220
  230.2 17.4 %copy-start.1 = (bf16[256,256]{1,0:T(8,128)(2,1)S(1)}, bf16[256,256]{1,0:T(8,128)(2,1)}, u32[]{:S(2)}) copy-start(bf16[256,256]{1,0:T(8,128)(2,1)} %param.16) | copy-start | bytes 393220
  230.2 17.4 %copy-start.2 = (bf16[256,256]{1,0:T(8,128)(2,1)S(1)}, bf16[256,256]{1,0:T(8,128)(2,1)}, u32[]{:S(2)}) copy-start(bf16[256,256]{1,0:T(8,128)(2,1)} %param.17) | copy-start | bytes 393220
  244.9 39.5 %collective-permute-start.14 = (bf16[2048,768]{1,0:T(8,128)(2,1)}, bf16[2048,768]{1,0:T(8,128)(2,1)}, u32[]{:S(2)}, u32[]{:S(2)}) collective-permute-start(bf16[2048,768]{1,0:T(8,128)(2,1)} %constant_dynamic-update-slice_fusion.21), channel_id=1, source_target_pairs={{0,16},{1,129},{2,18},{3,131},{4,20},{5,133},{6,22},{7,135},{8,24}... | collective-permute-start | bytes 9437192 | tf_op jit(solution)/shard_map/ppermute | solution.py:96
  291.4 4.6 %collective-permute-start.15 = (bf16[2048,256]{1,0:T(8,128)(2,1)S(1)}, bf16[2048,256]{1,0:T(8,128)(2,1)S(1)}, u32[]{:S(2)}, u32[]{:S(2)}) collective-permute-start(bf16[2048,256]{1,0:T(8,128)(2,1)S(1)} %bitcast.29), channel_id=1, source_target_pairs={{0,1},{1,0},{2,3},{3,2},{4,5},{5,4},{6,7},{7,6},{8,9},{9,8},{10,11... | collective-permute-start | bytes 3145736 | tf_op jit(solution)/shard_map/ppermute | solution.py:172
  296.4 11.1 %collective-permute-start.16 = (bf16[1024,256]{1,0:T(8,128)(2,1)S(1)}, bf16[1024,256]{1,0:T(8,128)(2,1)S(1)}, u32[]{:S(2)}, u32[]{:S(2)}) collective-permute-start(bf16[1024,256]{1,0:T(8,128)(2,1)S(1)} %slice.205), channel_id=1, source_target_pairs={{0,4},{1,13},{2,6},{3,15},{4,0},{5,9},{6,2},{7,11},{8,12},{9,5},{1... | collective-permute-start | bytes 1572872 | tf_op jit(solution)/shard_map/ppermute | solution.py:172
  307.6 9.5 %collective-permute-start.17 = (bf16[512,256]{1,0:T(8,128)(2,1)S(1)}, bf16[512,256]{1,0:T(8,128)(2,1)S(1)}, u32[]{:S(2)}, u32[]{:S(2)}) collective-permute-start(bf16[512,256]{1,0:T(8,128)(2,1)S(1)} %slice.207), channel_id=1, source_target_pairs={{0,12},{1,5},{2,14},{3,7},{4,8},{5,1},{6,10},{7,3},{8,4},{9,13},{1... | collective-permute-start | bytes 786440 | tf_op jit(solution)/shard_map/ppermute | solution.py:172
  317.1 20.9 %collective-permute-start.18 = (bf16[256,256]{1,0:T(8,128)(2,1)S(1)}, bf16[256,256]{1,0:T(8,128)(2,1)S(1)}, u32[]{:S(2)}, u32[]{:S(2)}) collective-permute-start(bf16[256,256]{1,0:T(8,128)(2,1)S(1)} %slice.209), channel_id=1, source_target_pairs={{0,2},{1,3},{2,0},{3,1},{4,6},{5,7},{6,4},{7,5},{8,10},{9,11},{10,... | collective-permute-start | bytes 393224 | tf_op jit(solution)/shard_map/ppermute | solution.py:172

commit v13 on v11

--- a/solution.py
+++ b/solution.py
@@ -15,7 +15,7 @@
 NEG_FILL = -1e30
 GATHER_ORDERS = ((4, 2, 16, 8, 1), (4, 16, 2, 1, 8))
 SCATTER_ORDERS = tuple(tuple(reversed(order)) for order in GATHER_ORDERS)
-HEAD_GATHER_ORDERS = ((4, 2, 16, 8), (4, 16, 2, 8))
+HEAD_GATHER_ORDERS = ((4, 2, 8, 16), (4, 16, 8, 2))
 HEAD_SCATTER_ORDERS = tuple(tuple(reversed(order)) for order in HEAD_GATHER_ORDERS)
 TP_ORDERS = ((1, 4, 12, 2), (1, 12, 4, 2))
 

time: 335 us -> 324 us (0.967)
  the two profiles are of different devices: /device:TPU:6 before, /device:TPU:26 now
where the time goes in v13:
time: 324 us; the launch traced here: 323 us
  waiting for transfers between devices  211 us (65%)
  starting transfers between devices  74.3 us (23%)
  local copies, waits for them, and re-layouts  18.6 us (6%)
  other arithmetic  7.3 us (2%)
  matrix products  5.81 us (2%)
  Pallas kernels  4.89 us (2%)
    ppermute x15, waiting for transfers between devices, _pair_permute(): return lax.ppermute(value, ('ctx', 'tp'), pairs)  181 us
    ppermute x15, starting transfers between devices, _pair_permute(): return lax.ppermute(value, ('ctx', 'tp'), pairs)  48.6 us
    ppermute x4, waiting for transfers between devices, tp_halving_reduce(): sent = lax.ppermute(held[:half].astype(wire), 'tp', pairs)  30.1 us
    ppermute x4, starting transfers between devices, tp_halving_reduce(): sent = lax.ppermute(held[:half].astype(wire), 'tp', pairs)  25.6 us
    unnamed x29, local copies, waits for them, and re-layouts  9.03 us
  transfers between devices with their start and end apart: 19, of which 19 were waited for; matrix products, arithmetic and copies ran while one was open for 4% of the time, Pallas kernels for 0%

profile of v13, /device:TPU:26, one launch (start us, length us, event | category | flops | bytes accessed | tf_op | source)
XLA Modules:
  0.0 322.5 jit_solution(3331641301202944932)
XLA Ops:
  4.0 3.8 %collective-permute-start = (bf16[128,640]{1,0:T(8,128)(2,1)S(1)}, bf16[128,640]{1,0:T(8,128)(2,1)S(1)}, u32[]{:S(2)}, u32[]{:S(2)}) collective-permute-start(bf16[128,640]{1,0:T(8,128)(2,1)S(1)} %get-tuple-element.27), channel_id=1, source_target_pairs={{0,16},{1,17},{2,18},{3,19},{4,20},{5,21},{6,22},{7,23},{8,24},{9,... | collective-permute-start | bytes 491528 | tf_op jit(solution)/shard_map/ppermute | solution.py:96
  7.8 4.2 %collective-permute-done = bf16[128,640]{1,0:T(8,128)(2,1)S(1)} collective-permute-done((bf16[128,640]{1,0:T(8,128)(2,1)S(1)}, bf16[128,640]{1,0:T(8,128)(2,1)S(1)}, u32[]{:S(2)}, u32[]{:S(2)}) %collective-permute-start) | collective-permute-done | bytes 163872 | tf_op jit(solution)/shard_map/ppermute | solution.py:96
  12.1 9.1 %collective-permute-start.1 = (bf16[256,256]{1,0:T(8,128)(2,1)S(1)}, bf16[256,256]{1,0:T(8,128)(2,1)S(1)}, u32[]{:S(2)}, u32[]{:S(2)}) collective-permute-start(bf16[256,256]{1,0:T(8,128)(2,1)S(1)} %get-tuple-element.15), channel_id=1, source_target_pairs={{0,64},{1,65},{2,66},{3,67},{4,68},{5,69},{6,70},{7,71},{8,72},{9,... | collective-permute-start | bytes 393224 | tf_op jit(solution)/shard_map/ppermute | solution.py:96
  21.2 11.2 %collective-permute-done.1 = bf16[256,256]{1,0:T(8,128)(2,1)S(1)} collective-permute-done((bf16[256,256]{1,0:T(8,128)(2,1)S(1)}, bf16[256,256]{1,0:T(8,128)(2,1)S(1)}, u32[]{:S(2)}, u32[]{:S(2)}) %collective-permute-start.1) | collective-permute-done | bytes 131104 | tf_op jit(solution)/shard_map/ppermute | solution.py:96
  32.5 1.9 collective-permute-start.2
  34.5 1.2 sort.17
  35.7 8.4 %collective-permute-done.2 = bf16[512,256]{1,0:T(8,128)(2,1)S(1)} collective-permute-done((bf16[512,256]{1,0:T(8,128)(2,1)S(1)}, bf16[512,256]{1,0:T(8,128)(2,1)S(1)}, u32[]{:S(2)}, u32[]{:S(2)}) %collective-permute-start.2) | collective-permute-done | bytes 262176 | tf_op jit(solution)/shard_map/ppermute | solution.py:96
  44.9 2.4 collective-permute-start.3
  47.8 9.4 %collective-permute-done.3 = bf16[1024,256]{1,0:T(8,128)(2,1)S(1)} collective-permute-done((bf16[1024,256]{1,0:T(8,128)(2,1)}, bf16[1024,256]{1,0:T(8,128)(2,1)S(1)}, u32[]{:S(2)}, u32[]{:S(2)}) %collective-permute-start.3) | collective-permute-done | bytes 524320 | tf_op jit(solution)/shard_map/ppermute | solution.py:96
  57.2 1.1 pad_maximum_fusion.2
  58.2 3.7 %collective-permute-start.4 = (bf16[2048,256]{1,0:T(8,128)(2,1)}, bf16[2048,256]{1,0:T(8,128)(2,1)}, u32[]{:S(2)}, u32[]{:S(2)}) collective-permute-start(bf16[2048,256]{1,0:T(8,128)(2,1)} %pad_maximum_fusion.2), channel_id=1, source_target_pairs={{0,256},{1,33},{2,258},{3,35},{4,260},{5,37},{6,262},{7,39},{8,264... | collective-permute-start | bytes 3145736 | tf_op jit(solution)/shard_map/ppermute | solution.py:96
  64.4 12.3 %collective-permute-done.4 = bf16[2048,256]{1,0:T(8,128)(2,1)} collective-permute-done((bf16[2048,256]{1,0:T(8,128)(2,1)}, bf16[2048,256]{1,0:T(8,128)(2,1)}, u32[]{:S(2)}, u32[]{:S(2)}) %collective-permute-start.4) | collective-permute-done | bytes 1048608 | tf_op jit(solution)/shard_map/ppermute | solution.py:96
  76.7 1.3 constant_dynamic-update-slice_fusion.10.kv_ref
  78.0 4.9 %shard_map.91 = (f32[256,128]{1,0:T(8,128)S(1)}, bf16[4096,256]{1,0:T(8,128)(2,1)S(1)}) custom-call(f32[8,4096]{1,0:T(8,128)S(1)} %concatenate.57.mask_ref, bf16[256,128]{1,0:T(8,128)(2,1)S(1)} %get-tuple-element.19.q_ref, bf16[256,128]{1,0:T(8,128)(2,1)S(1)} %get-tuple-element.18.do_ref, bf16[256,128]{1,0:T(8,128)(2,1)S(1)} %get-tuple-element.17.o_ref, ...), custom_call_target="tpu_custom_call" | custom-call | flops 1342177280 | bytes 4194304 | tf_op jit(solution)/shard_map/pallas_call | solution.py:72
  83.0 3.7 %collective-permute-start.5 = (bf16[2048,256]{1,0:T(8,128)(2,1)S(1)}, bf16[2048,256]{1,0:T(8,128)(2,1)S(1)}, u32[]{:S(2)}, u32[]{:S(2)}) collective-permute-start(bf16[2048,256]{1,0:T(8,128)(2,1)S(1)} %slice.99), channel_id=1, source_target_pairs={{0,256},{1,33},{2,258},{3,35},{4,260},{5,37},{6,262},{7,39},{8,264... | collective-permute-start | bytes 3145736 | tf_op jit(solution)/shard_map/ppermute | solution.py:96
  86.7 14.5 %collective-permute-done.5 = bf16[2048,256]{1,0:T(8,128)(2,1)S(1)} collective-permute-done((bf16[2048,256]{1,0:T(8,128)(2,1)S(1)}, bf16[2048,256]{1,0:T(8,128)(2,1)S(1)}, u32[]{:S(2)}, u32[]{:S(2)}) %collective-permute-start.5) | collective-permute-done | bytes 1048608 | tf_op jit(solution)/shard_map/ppermute | solution.py:96
  101.5 2.2 collective-permute-start.6
  103.7 8.9 %collective-permute-done.6 = bf16[1024,256]{1,0:T(8,128)(2,1)S(1)} collective-permute-done((bf16[1024,256]{1,0:T(8,128)(2,1)S(1)}, bf16[1024,256]{1,0:T(8,128)(2,1)S(1)}, u32[]{:S(2)}, u32[]{:S(2)}) %collective-permute-start.6) | collective-permute-done | bytes 524320 | tf_op jit(solution)/shard_map/ppermute | solution.py:96
  112.7 1.9 collective-permute-start.7
  114.7 10.0 %collective-permute-done.7 = bf16[512,256]{1,0:T(8,128)(2,1)S(1)} collective-permute-done((bf16[512,256]{1,0:T(8,128)(2,1)S(1)}, bf16[512,256]{1,0:T(8,128)(2,1)S(1)}, u32[]{:S(2)}, u32[]{:S(2)}) %collective-permute-start.7) | collective-permute-done | bytes 262176 | tf_op jit(solution)/shard_map/ppermute | solution.py:96
  124.8 2.8 collective-permute-start.8
  127.6 10.5 %collective-permute-done.8 = bf16[256,256]{1,0:T(8,128)(2,1)S(1)} collective-permute-done((bf16[256,256]{1,0:T(8,128)(2,1)S(1)}, bf16[256,256]{1,0:T(8,128)(2,1)S(1)}, u32[]{:S(2)}, u32[]{:S(2)}) %collective-permute-start.8) | collective-permute-done | bytes 131104 | tf_op jit(solution)/shard_map/ppermute | solution.py:96
  138.1 1.9 collective-permute-start.9
  140.1 4.6 %collective-permute-done.9 = bf16[128,384]{1,0:T(8,128)(2,1)S(1)} collective-permute-done((bf16[128,384]{1,0:T(8,128)(2,1)S(1)}, bf16[128,384]{1,0:T(8,128)(2,1)S(1)}, u32[]{:S(2)}, u32[]{:S(2)}) %collective-permute-start.9) | collective-permute-done | bytes 98336 | tf_op jit(solution)/shard_map/ppermute | solution.py:96
  146.0 5.9 %collective-permute-start.10 = (bf16[128,768]{1,0:T(8,128)(2,1)S(1)}, bf16[128,768]{1,0:T(8,128)(2,1)S(1)}, u32[]{:S(2)}, u32[]{:S(2)}) collective-permute-start(bf16[128,768]{1,0:T(8,128)(2,1)S(1)} %get-tuple-element.22), channel_id=1, source_target_pairs={{0,64},{1,65},{2,66},{3,67},{4,68},{5,69},{6,70},{7,71},{8,72},{9,... | collective-permute-start | bytes 589832 | tf_op jit(solution)/shard_map/ppermute | solution.py:96
  151.9 9.8 %collective-permute-done.10 = bf16[128,768]{1,0:T(8,128)(2,1)S(1)} collective-permute-done((bf16[128,768]{1,0:T(8,128)(2,1)S(1)}, bf16[128,768]{1,0:T(8,128)(2,1)S(1)}, u32[]{:S(2)}, u32[]{:S(2)}) %collective-permute-start.10) | collective-permute-done | bytes 196640 | tf_op jit(solution)/shard_map/ppermute | solution.py:96
  161.7 1.9 collective-permute-start.11
  163.7 12.8 %collective-permute-done.11 = bf16[256,768]{1,0:T(8,128)(2,1)S(1)} collective-permute-done((bf16[256,768]{1,0:T(8,128)(2,1)S(1)}, bf16[256,768]{1,0:T(8,128)(2,1)S(1)}, u32[]{:S(2)}, u32[]{:S(2)}) %collective-permute-start.11) | collective-permute-done | bytes 393248 | tf_op jit(solution)/shard_map/ppermute | solution.py:96
  176.5 3.2 collective-permute-start.12
  179.7 12.2 %collective-permute-done.12 = bf16[512,768]{1,0:T(8,128)(2,1)S(1)} collective-permute-done((bf16[512,768]{1,0:T(8,128)(2,1)S(1)}, bf16[512,768]{1,0:T(8,128)(2,1)S(1)}, u32[]{:S(2)}, u32[]{:S(2)}) %collective-permute-start.12) | collective-permute-done | bytes 786464 | tf_op jit(solution)/shard_map/ppermute | solution.py:96
  192.0 2.2 collective-permute-start.13
  198.1 1.0 constant_dynamic-update-slice_fusion.22
  199.1 15.2 %collective-permute-done.13 = bf16[1024,768]{1,0:T(8,128)(2,1)S(1)} collective-permute-done((bf16[1024,768]{1,0:T(8,128)(2,1)S(1)}, bf16[1024,768]{1,0:T(8,128)(2,1)S(1)}, u32[]{:S(2)}, u32[]{:S(2)}) %collective-permute-start.13) | collective-permute-done | bytes 1572896 | tf_op jit(solution)/shard_map/ppermute | solution.py:96
  214.3 1.2 constant_dynamic-update-slice_fusion.21
  215.5 1.9 collective-permute-start.14
  218.3 2.9 convolution_convert_fusion.1
  221.2 37.1 %collective-permute-done.14 = bf16[2048,768]{1,0:T(8,128)(2,1)} collective-permute-done((bf16[2048,768]{1,0:T(8,128)(2,1)}, bf16[2048,768]{1,0:T(8,128)(2,1)}, u32[]{:S(2)}, u32[]{:S(2)}) %collective-permute-start.14) | collective-permute-done | bytes 3145760 | tf_op jit(solution)/shard_map/ppermute | solution.py:96
  258.3 2.9 convolution_convert_fusion
  261.4 2.0 gather_fusion.3
  263.4 1.8 broadcast_select_fusion
  265.4 11.1 %collective-permute-start.15 = (bf16[2048,256]{1,0:T(8,128)(2,1)S(1)}, bf16[2048,256]{1,0:T(8,128)(2,1)S(1)}, u32[]{:S(2)}, u32[]{:S(2)}) collective-permute-start(bf16[2048,256]{1,0:T(8,128)(2,1)S(1)} %bitcast.29), channel_id=1, source_target_pairs={{0,1},{1,0},{2,3},{3,2},{4,5},{5,4},{6,7},{7,6},{8,9},{9,8},{10,11... | collective-permute-start | bytes 3145736 | tf_op jit(solution)/shard_map/ppermute | solution.py:169
  276.5 2.3 collective-permute-done.15
  279.2 2.7 collective-permute-start.16
  281.9 8.4 %collective-permute-done.16 = bf16[1024,256]{1,0:T(8,128)(2,1)S(1)} collective-permute-done((bf16[1024,256]{1,0:T(8,128)(2,1)S(1)}, bf16[1024,256]{1,0:T(8,128)(2,1)S(1)}, u32[]{:S(2)}, u32[]{:S(2)}) %collective-permute-start.16) | collective-permute-done | bytes 524320 | tf_op jit(solution)/shard_map/ppermute | solution.py:169
  290.4 2.1 collective-permute-start.17
  292.6 7.4 %collective-permute-done.17 = bf16[512,256]{1,0:T(8,128)(2,1)S(1)} collective-permute-done((bf16[512,256]{1,0:T(8,128)(2,1)S(1)}, bf16[512,256]{1,0:T(8,128)(2,1)S(1)}, u32[]{:S(2)}, u32[]{:S(2)}) %collective-permute-start.17) | collective-permute-done | bytes 262176 | tf_op jit(solution)/shard_map/ppermute | solution.py:169
  300.0 9.7 %collective-permute-start.18 = (bf16[256,256]{1,0:T(8,128)(2,1)S(1)}, bf16[256,256]{1,0:T(8,128)(2,1)S(1)}, u32[]{:S(2)}, u32[]{:S(2)}) collective-permute-start(bf16[256,256]{1,0:T(8,128)(2,1)S(1)} %slice.209), channel_id=1, source_target_pairs={{0,2},{1,3},{2,0},{3,1},{4,6},{5,7},{6,4},{7,5},{8,10},{9,11},{10,... | collective-permute-start | bytes 393224 | tf_op jit(solution)/shard_map/ppermute | solution.py:169
  309.7 12.1 %collective-permute-done.18 = bf16[256,256]{1,0:T(8,128)(2,1)S(1)} collective-permute-done((bf16[256,256]{1,0:T(8,128)(2,1)S(1)}, bf16[256,256]{1,0:T(8,128)(2,1)S(1)}, u32[]{:S(2)}, u32[]{:S(2)}) %collective-permute-start.18) | collective-permute-done | bytes 131104 | tf_op jit(solution)/shard_map/ppermute | solution.py:169
  (81 shorter events, 16.2 us)
Async XLA Ops:
  4.0 8.0 %collective-permute-start = (bf16[128,640]{1,0:T(8,128)(2,1)S(1)}, bf16[128,640]{1,0:T(8,128)(2,1)S(1)}, u32[]{:S(2)}, u32[]{:S(2)}) collective-permute-start(bf16[128,640]{1,0:T(8,128)(2,1)S(1)} %get-tuple-element.27), channel_id=1, source_target_pairs={{0,16},{1,17},{2,18},{3,19},{4,20},{5,21},{6,22},{7,23},{8,24},{9,... | collective-permute-start | bytes 491528 | tf_op jit(solution)/shard_map/ppermute | solution.py:96
  12.1 20.3 %collective-permute-start.1 = (bf16[256,256]{1,0:T(8,128)(2,1)S(1)}, bf16[256,256]{1,0:T(8,128)(2,1)S(1)}, u32[]{:S(2)}, u32[]{:S(2)}) collective-permute-start(bf16[256,256]{1,0:T(8,128)(2,1)S(1)} %get-tuple-element.15), channel_id=1, source_target_pairs={{0,64},{1,65},{2,66},{3,67},{4,68},{5,69},{6,70},{7,71},{8,72},{9,... | collective-permute-start | bytes 393224 | tf_op jit(solution)/shard_map/ppermute | solution.py:96
  32.5 11.6 %collective-permute-start.2 = (bf16[512,256]{1,0:T(8,128)(2,1)S(1)}, bf16[512,256]{1,0:T(8,128)(2,1)S(1)}, u32[]{:S(2)}, u32[]{:S(2)}) collective-permute-start(bf16[512,256]{1,0:T(8,128)(2,1)S(1)} %pad_maximum_fusion.6), channel_id=1, source_target_pairs={{0,32},{1,257},{2,34},{3,259},{4,36},{5,261},{6,38},{7,263},{8,40}... | collective-permute-start | bytes 786440 | tf_op jit(solution)/shard_map/ppermute | solution.py:96
  44.9 12.2 %collective-permute-start.3 = (bf16[1024,256]{1,0:T(8,128)(2,1)}, bf16[1024,256]{1,0:T(8,128)(2,1)S(1)}, u32[]{:S(2)}, u32[]{:S(2)}) collective-permute-start(bf16[1024,256]{1,0:T(8,128)(2,1)} %pad_maximum_fusion.4), channel_id=1, source_target_pairs={{0,128},{1,129},{2,130},{3,131},{4,132},{5,133},{6,134},{7,135},{8... | collective-permute-start | bytes 1572872 | tf_op jit(solution)/shard_map/ppermute | solution.py:96
  58.2 18.5 %collective-permute-start.4 = (bf16[2048,256]{1,0:T(8,128)(2,1)}, bf16[2048,256]{1,0:T(8,128)(2,1)}, u32[]{:S(2)}, u32[]{:S(2)}) collective-permute-start(bf16[2048,256]{1,0:T(8,128)(2,1)} %pad_maximum_fusion.2), channel_id=1, source_target_pairs={{0,256},{1,33},{2,258},{3,35},{4,260},{5,37},{6,262},{7,39},{8,264... | collective-permute-start | bytes 3145736 | tf_op jit(solution)/shard_map/ppermute | solution.py:96
  83.0 18.2 %collective-permute-start.5 = (bf16[2048,256]{1,0:T(8,128)(2,1)S(1)}, bf16[2048,256]{1,0:T(8,128)(2,1)S(1)}, u32[]{:S(2)}, u32[]{:S(2)}) collective-permute-start(bf16[2048,256]{1,0:T(8,128)(2,1)S(1)} %slice.99), channel_id=1, source_target_pairs={{0,256},{1,33},{2,258},{3,35},{4,260},{5,37},{6,262},{7,39},{8,264... | collective-permute-start | bytes 3145736 | tf_op jit(solution)/shard_map/ppermute | solution.py:96
  101.5 11.1 %collective-permute-start.6 = (bf16[1024,256]{1,0:T(8,128)(2,1)S(1)}, bf16[1024,256]{1,0:T(8,128)(2,1)S(1)}, u32[]{:S(2)}, u32[]{:S(2)}) collective-permute-start(bf16[1024,256]{1,0:T(8,128)(2,1)S(1)} %slice.206), channel_id=1, source_target_pairs={{0,128},{1,129},{2,130},{3,131},{4,132},{5,133},{6,134},{7,135},{8... | collective-permute-start | bytes 1572872 | tf_op jit(solution)/shard_map/ppermute | solution.py:96
  112.7 12.0 %collective-permute-start.7 = (bf16[512,256]{1,0:T(8,128)(2,1)S(1)}, bf16[512,256]{1,0:T(8,128)(2,1)S(1)}, u32[]{:S(2)}, u32[]{:S(2)}) collective-permute-start(bf16[512,256]{1,0:T(8,128)(2,1)S(1)} %slice.208), channel_id=1, source_target_pairs={{0,32},{1,257},{2,34},{3,259},{4,36},{5,261},{6,38},{7,263},{8,40}... | collective-permute-start | bytes 786440 | tf_op jit(solution)/shard_map/ppermute | solution.py:96
  124.8 13.3 %collective-permute-start.8 = (bf16[256,256]{1,0:T(8,128)(2,1)S(1)}, bf16[256,256]{1,0:T(8,128)(2,1)S(1)}, u32[]{:S(2)}, u32[]{:S(2)}) collective-permute-start(bf16[256,256]{1,0:T(8,128)(2,1)S(1)} %slice.210), channel_id=1, source_target_pairs={{0,64},{1,65},{2,66},{3,67},{4,68},{5,69},{6,70},{7,71},{8,72},{9,... | collective-permute-start | bytes 393224 | tf_op jit(solution)/shard_map/ppermute | solution.py:96
  138.1 6.5 %collective-permute-start.9 = (bf16[128,384]{1,0:T(8,128)(2,1)S(1)}, bf16[128,384]{1,0:T(8,128)(2,1)S(1)}, u32[]{:S(2)}, u32[]{:S(2)}) collective-permute-start(bf16[128,384]{1,0:T(8,128)(2,1)S(1)} %broadcast_select_fusion.3), channel_id=1, source_target_pairs={{0,16},{1,17},{2,18},{3,19},{4,20},{5,21},{6,22},{7,23},{8,24},{9,... | collective-permute-start | bytes 294920 | tf_op jit(solution)/shard_map/ppermute | solution.py:96
  146.0 15.7 %collective-permute-start.10 = (bf16[128,768]{1,0:T(8,128)(2,1)S(1)}, bf16[128,768]{1,0:T(8,128)(2,1)S(1)}, u32[]{:S(2)}, u32[]{:S(2)}) collective-permute-start(bf16[128,768]{1,0:T(8,128)(2,1)S(1)} %get-tuple-element.22), channel_id=1, source_target_pairs={{0,64},{1,65},{2,66},{3,67},{4,68},{5,69},{6,70},{7,71},{8,72},{9,... | collective-permute-start | bytes 589832 | tf_op jit(solution)/shard_map/ppermute | solution.py:96
  161.7 14.7 %collective-permute-start.11 = (bf16[256,768]{1,0:T(8,128)(2,1)S(1)}, bf16[256,768]{1,0:T(8,128)(2,1)S(1)}, u32[]{:S(2)}, u32[]{:S(2)}) collective-permute-start(bf16[256,768]{1,0:T(8,128)(2,1)S(1)} %pad_maximum_fusion.5), channel_id=1, source_target_pairs={{0,32},{1,257},{2,34},{3,259},{4,36},{5,261},{6,38},{7,263},{8,40}... | collective-permute-start | bytes 1179656 | tf_op jit(solution)/shard_map/ppermute | solution.py:96
  176.5 15.4 %collective-permute-start.12 = (bf16[512,768]{1,0:T(8,128)(2,1)S(1)}, bf16[512,768]{1,0:T(8,128)(2,1)S(1)}, u32[]{:S(2)}, u32[]{:S(2)}) collective-permute-start(bf16[512,768]{1,0:T(8,128)(2,1)S(1)} %pad_maximum_fusion.3), channel_id=1, source_target_pairs={{0,256},{1,33},{2,258},{3,35},{4,260},{5,37},{6,262},{7,39},{8,264... | collective-permute-start | bytes 2359304 | tf_op jit(solution)/shard_map/ppermute | solution.py:96
  192.0 22.3 %collective-permute-start.13 = (bf16[1024,768]{1,0:T(8,128)(2,1)S(1)}, bf16[1024,768]{1,0:T(8,128)(2,1)S(1)}, u32[]{:S(2)}, u32[]{:S(2)}) collective-permute-start(bf16[1024,768]{1,0:T(8,128)(2,1)S(1)} %pad_maximum_fusion.1), channel_id=1, source_target_pairs={{0,128},{1,17},{2,130},{3,19},{4,132},{5,21},{6,134},{7,23},{8,136... | collective-permute-start | bytes 4718600 | tf_op jit(solution)/shard_map/ppermute | solution.py:96
  199.1 19.1 %copy-start = (bf16[256,256]{1,0:T(8,128)(2,1)S(1)}, bf16[256,256]{1,0:T(8,128)(2,1)}, u32[]{:S(2)}) copy-start(bf16[256,256]{1,0:T(8,128)(2,1)} %param.15) | copy-start | bytes 393220
  199.1 19.1 %copy-start.1 = (bf16[256,256]{1,0:T(8,128)(2,1)S(1)}, bf16[256,256]{1,0:T(8,128)(2,1)}, u32[]{:S(2)}) copy-start(bf16[256,256]{1,0:T(8,128)(2,1)} %param.16) | copy-start | bytes 393220
  199.1 19.1 %copy-start.2 = (bf16[256,256]{1,0:T(8,128)(2,1)S(1)}, bf16[256,256]{1,0:T(8,128)(2,1)}, u32[]{:S(2)}) copy-start(bf16[256,256]{1,0:T(8,128)(2,1)} %param.17) | copy-start | bytes 393220
  215.5 42.8 %collective-permute-start.14 = (bf16[2048,768]{1,0:T(8,128)(2,1)}, bf16[2048,768]{1,0:T(8,128)(2,1)}, u32[]{:S(2)}, u32[]{:S(2)}) collective-permute-start(bf16[2048,768]{1,0:T(8,128)(2,1)} %constant_dynamic-update-slice_fusion.21), channel_id=1, source_target_pairs={{0,16},{1,129},{2,18},{3,131},{4,20},{5,133},{6,22},{7,135},{8,24}... | collective-permute-start | bytes 9437192 | tf_op jit(solution)/shard_map/ppermute | solution.py:96
  265.4 13.4 %collective-permute-start.15 = (bf16[2048,256]{1,0:T(8,128)(2,1)S(1)}, bf16[2048,256]{1,0:T(8,128)(2,1)S(1)}, u32[]{:S(2)}, u32[]{:S(2)}) collective-permute-start(bf16[2048,256]{1,0:T(8,128)(2,1)S(1)} %bitcast.29), channel_id=1, source_target_pairs={{0,1},{1,0},{2,3},{3,2},{4,5},{5,4},{6,7},{7,6},{8,9},{9,8},{10,11... | collective-permute-start | bytes 3145736 | tf_op jit(solution)/shard_map/ppermute | solution.py:169
  279.2 11.1 %collective-permute-start.16 = (bf16[1024,256]{1,0:T(8,128)(2,1)S(1)}, bf16[1024,256]{1,0:T(8,128)(2,1)S(1)}, u32[]{:S(2)}, u32[]{:S(2)}) collective-permute-start(bf16[1024,256]{1,0:T(8,128)(2,1)S(1)} %slice.205), channel_id=1, source_target_pairs={{0,4},{1,13},{2,6},{3,15},{4,0},{5,9},{6,2},{7,11},{8,12},{9,5},{1... | collective-permute-start | bytes 1572872 | tf_op jit(solution)/shard_map/ppermute | solution.py:169
  290.4 9.5 %collective-permute-start.17 = (bf16[512,256]{1,0:T(8,128)(2,1)S(1)}, bf16[512,256]{1,0:T(8,128)(2,1)S(1)}, u32[]{:S(2)}, u32[]{:S(2)}) collective-permute-start(bf16[512,256]{1,0:T(8,128)(2,1)S(1)} %slice.207), channel_id=1, source_target_pairs={{0,12},{1,5},{2,14},{3,7},{4,8},{5,1},{6,10},{7,3},{8,4},{9,13},{1... | collective-permute-start | bytes 786440 | tf_op jit(solution)/shard_map/ppermute | solution.py:169
  300.0 21.8 %collective-permute-start.18 = (bf16[256,256]{1,0:T(8,128)(2,1)S(1)}, bf16[256,256]{1,0:T(8,128)(2,1)S(1)}, u32[]{:S(2)}, u32[]{:S(2)}) collective-permute-start(bf16[256,256]{1,0:T(8,128)(2,1)S(1)} %slice.209), channel_id=1, source_target_pairs={{0,2},{1,3},{2,0},{3,1},{4,6},{5,7},{6,4},{7,5},{8,10},{9,11},{10,... | collective-permute-start | bytes 393224 | tf_op jit(solution)/shard_map/ppermute | solution.py:169

commit v14 on v13

--- a/solution.py
+++ b/solution.py
@@ -15,7 +15,7 @@
 NEG_FILL = -1e30
 GATHER_ORDERS = ((4, 2, 16, 8, 1), (4, 16, 2, 1, 8))
 SCATTER_ORDERS = tuple(tuple(reversed(order)) for order in GATHER_ORDERS)
-HEAD_GATHER_ORDERS = ((4, 2, 8, 16), (4, 16, 8, 2))
+HEAD_GATHER_ORDERS = ((4, 8, 2, 16), (4, 8, 16, 2))
 HEAD_SCATTER_ORDERS = tuple(tuple(reversed(order)) for order in HEAD_GATHER_ORDERS)
 TP_ORDERS = ((1, 4, 12, 2), (1, 12, 4, 2))
 

time: 324 us -> 333 us (1.028)
  the two profiles are of different devices: /device:TPU:26 before, /device:TPU:6 now
where the time goes in v14:
time: 333 us; the launch traced here: 330 us
  waiting for transfers between devices  231 us (69%)
  starting transfers between devices  62.6 us (19%)
  local copies, waits for them, and re-layouts  18.6 us (6%)
  other arithmetic  7.31 us (2%)
  matrix products  5.8 us (2%)
  Pallas kernels  4.87 us (1%)
    ppermute x15, waiting for transfers between devices, _pair_permute(): return lax.ppermute(value, ('ctx', 'tp'), pairs)  206 us
    ppermute x15, starting transfers between devices, _pair_permute(): return lax.ppermute(value, ('ctx', 'tp'), pairs)  43.1 us
    ppermute x4, waiting for transfers between devices, tp_halving_reduce(): sent = lax.ppermute(held[:half].astype(wire), 'tp', pairs)  24.7 us
    ppermute x4, starting transfers between devices, tp_halving_reduce(): sent = lax.ppermute(held[:half].astype(wire), 'tp', pairs)  19.5 us
    unnamed x29, local copies, waits for them, and re-layouts  9.03 us
  transfers between devices with their start and end apart: 19, of which 19 were waited for; matrix products, arithmetic and copies ran while one was open for 4% of the time, Pallas kernels for 0%

profile of v14, /device:TPU:6, one launch (start us, length us, event | category | flops | bytes accessed | tf_op | source)
XLA Modules:
  0.0 330.3 jit_solution(374690979777271544)
XLA Ops:
  4.0 3.8 %collective-permute-start = (bf16[128,640]{1,0:T(8,128)(2,1)S(1)}, bf16[128,640]{1,0:T(8,128)(2,1)S(1)}, u32[]{:S(2)}, u32[]{:S(2)}) collective-permute-start(bf16[128,640]{1,0:T(8,128)(2,1)S(1)} %get-tuple-element.27), channel_id=1, source_target_pairs={{0,16},{1,17},{2,18},{3,19},{4,20},{5,21},{6,22},{7,23},{8,24},{9,... | collective-permute-start | bytes 491528 | tf_op jit(solution)/shard_map/ppermute | solution.py:96
  7.8 4.2 %collective-permute-done = bf16[128,640]{1,0:T(8,128)(2,1)S(1)} collective-permute-done((bf16[128,640]{1,0:T(8,128)(2,1)S(1)}, bf16[128,640]{1,0:T(8,128)(2,1)S(1)}, u32[]{:S(2)}, u32[]{:S(2)}) %collective-permute-start) | collective-permute-done | bytes 163872 | tf_op jit(solution)/shard_map/ppermute | solution.py:96
  12.1 9.1 %collective-permute-start.1 = (bf16[256,256]{1,0:T(8,128)(2,1)S(1)}, bf16[256,256]{1,0:T(8,128)(2,1)S(1)}, u32[]{:S(2)}, u32[]{:S(2)}) collective-permute-start(bf16[256,256]{1,0:T(8,128)(2,1)S(1)} %get-tuple-element.15), channel_id=1, source_target_pairs={{0,64},{1,65},{2,66},{3,67},{4,68},{5,69},{6,70},{7,71},{8,72},{9,... | collective-permute-start | bytes 393224 | tf_op jit(solution)/shard_map/ppermute | solution.py:96
  21.2 11.2 %collective-permute-done.1 = bf16[256,256]{1,0:T(8,128)(2,1)S(1)} collective-permute-done((bf16[256,256]{1,0:T(8,128)(2,1)S(1)}, bf16[256,256]{1,0:T(8,128)(2,1)S(1)}, u32[]{:S(2)}, u32[]{:S(2)}) %collective-permute-start.1) | collective-permute-done | bytes 131104 | tf_op jit(solution)/shard_map/ppermute | solution.py:96
  32.5 2.7 collective-permute-start.2
  35.3 1.2 sort.17
  36.5 5.1 %collective-permute-done.2 = bf16[512,256]{1,0:T(8,128)(2,1)S(1)} collective-permute-done((bf16[512,256]{1,0:T(8,128)(2,1)S(1)}, bf16[512,256]{1,0:T(8,128)(2,1)S(1)}, u32[]{:S(2)}, u32[]{:S(2)}) %collective-permute-start.2) | collective-permute-done | bytes 262176 | tf_op jit(solution)/shard_map/ppermute | solution.py:96
  42.4 1.9 collective-permute-start.3
  44.8 28.1 %collective-permute-done.3 = bf16[1024,256]{1,0:T(8,128)(2,1)S(1)} collective-permute-done((bf16[1024,256]{1,0:T(8,128)(2,1)}, bf16[1024,256]{1,0:T(8,128)(2,1)S(1)}, u32[]{:S(2)}, u32[]{:S(2)}) %collective-permute-start.3) | collective-permute-done | bytes 524320 | tf_op jit(solution)/shard_map/ppermute | solution.py:96
  72.8 1.1 pad_maximum_fusion.2
  73.9 3.0 collective-permute-start.4
  79.4 13.0 %collective-permute-done.4 = bf16[2048,256]{1,0:T(8,128)(2,1)} collective-permute-done((bf16[2048,256]{1,0:T(8,128)(2,1)}, bf16[2048,256]{1,0:T(8,128)(2,1)}, u32[]{:S(2)}, u32[]{:S(2)}) %collective-permute-start.4) | collective-permute-done | bytes 1048608 | tf_op jit(solution)/shard_map/ppermute | solution.py:96
  92.4 1.3 constant_dynamic-update-slice_fusion.10.kv_ref
  93.7 4.9 %shard_map.91 = (f32[256,128]{1,0:T(8,128)S(1)}, bf16[4096,256]{1,0:T(8,128)(2,1)S(1)}) custom-call(f32[8,4096]{1,0:T(8,128)S(1)} %concatenate.57.mask_ref, bf16[256,128]{1,0:T(8,128)(2,1)S(1)} %get-tuple-element.19.q_ref, bf16[256,128]{1,0:T(8,128)(2,1)S(1)} %get-tuple-element.18.do_ref, bf16[256,128]{1,0:T(8,128)(2,1)S(1)} %get-tuple-element.17.o_ref, ...), custom_call_target="tpu_custom_call" | custom-call | flops 1342177280 | bytes 4194304 | tf_op jit(solution)/shard_map/pallas_call | solution.py:72
  98.7 3.0 collective-permute-start.5
  101.7 15.2 %collective-permute-done.5 = bf16[2048,256]{1,0:T(8,128)(2,1)S(1)} collective-permute-done((bf16[2048,256]{1,0:T(8,128)(2,1)S(1)}, bf16[2048,256]{1,0:T(8,128)(2,1)S(1)}, u32[]{:S(2)}, u32[]{:S(2)}) %collective-permute-start.5) | collective-permute-done | bytes 1048608 | tf_op jit(solution)/shard_map/ppermute | solution.py:96
  117.2 1.9 collective-permute-start.6
  119.1 12.6 %collective-permute-done.6 = bf16[1024,256]{1,0:T(8,128)(2,1)S(1)} collective-permute-done((bf16[1024,256]{1,0:T(8,128)(2,1)S(1)}, bf16[1024,256]{1,0:T(8,128)(2,1)S(1)}, u32[]{:S(2)}, u32[]{:S(2)}) %collective-permute-start.6) | collective-permute-done | bytes 524320 | tf_op jit(solution)/shard_map/ppermute | solution.py:96
  131.8 2.4 collective-permute-start.7
  134.3 5.8 %collective-permute-done.7 = bf16[512,256]{1,0:T(8,128)(2,1)S(1)} collective-permute-done((bf16[512,256]{1,0:T(8,128)(2,1)S(1)}, bf16[512,256]{1,0:T(8,128)(2,1)S(1)}, u32[]{:S(2)}, u32[]{:S(2)}) %collective-permute-start.7) | collective-permute-done | bytes 262176 | tf_op jit(solution)/shard_map/ppermute | solution.py:96
  140.2 1.9 collective-permute-start.8
  142.1 16.2 %collective-permute-done.8 = bf16[256,256]{1,0:T(8,128)(2,1)S(1)} collective-permute-done((bf16[256,256]{1,0:T(8,128)(2,1)S(1)}, bf16[256,256]{1,0:T(8,128)(2,1)S(1)}, u32[]{:S(2)}, u32[]{:S(2)}) %collective-permute-start.8) | collective-permute-done | bytes 131104 | tf_op jit(solution)/shard_map/ppermute | solution.py:96
  158.4 1.9 collective-permute-start.9
  160.3 4.8 %collective-permute-done.9 = bf16[128,384]{1,0:T(8,128)(2,1)S(1)} collective-permute-done((bf16[128,384]{1,0:T(8,128)(2,1)S(1)}, bf16[128,384]{1,0:T(8,128)(2,1)S(1)}, u32[]{:S(2)}, u32[]{:S(2)}) %collective-permute-start.9) | collective-permute-done | bytes 98336 | tf_op jit(solution)/shard_map/ppermute | solution.py:96
  166.5 1.9 collective-permute-start.10
  168.4 19.8 %collective-permute-done.10 = bf16[128,768]{1,0:T(8,128)(2,1)S(1)} collective-permute-done((bf16[128,768]{1,0:T(8,128)(2,1)S(1)}, bf16[128,768]{1,0:T(8,128)(2,1)S(1)}, u32[]{:S(2)}, u32[]{:S(2)}) %collective-permute-start.10) | collective-permute-done | bytes 196640 | tf_op jit(solution)/shard_map/ppermute | solution.py:96
  188.2 1.9 collective-permute-start.11
  190.1 9.1 %collective-permute-done.11 = bf16[256,768]{1,0:T(8,128)(2,1)S(1)} collective-permute-done((bf16[256,768]{1,0:T(8,128)(2,1)S(1)}, bf16[256,768]{1,0:T(8,128)(2,1)S(1)}, u32[]{:S(2)}, u32[]{:S(2)}) %collective-permute-start.11) | collective-permute-done | bytes 393248 | tf_op jit(solution)/shard_map/ppermute | solution.py:96
  199.3 3.0 collective-permute-start.12
  202.2 12.4 %collective-permute-done.12 = bf16[512,768]{1,0:T(8,128)(2,1)S(1)} collective-permute-done((bf16[512,768]{1,0:T(8,128)(2,1)S(1)}, bf16[512,768]{1,0:T(8,128)(2,1)S(1)}, u32[]{:S(2)}, u32[]{:S(2)}) %collective-permute-start.12) | collective-permute-done | bytes 786464 | tf_op jit(solution)/shard_map/ppermute | solution.py:96
  214.8 2.5 collective-permute-start.13
  221.2 1.0 constant_dynamic-update-slice_fusion.22
  222.2 14.9 %collective-permute-done.13 = bf16[1024,768]{1,0:T(8,128)(2,1)S(1)} collective-permute-done((bf16[1024,768]{1,0:T(8,128)(2,1)S(1)}, bf16[1024,768]{1,0:T(8,128)(2,1)S(1)}, u32[]{:S(2)}, u32[]{:S(2)}) %collective-permute-start.13) | collective-permute-done | bytes 1572896 | tf_op jit(solution)/shard_map/ppermute | solution.py:96
  237.1 1.2 constant_dynamic-update-slice_fusion.21
  238.3 2.0 collective-permute-start.14
  241.2 2.9 convolution_convert_fusion.1
  244.1 33.7 %collective-permute-done.14 = bf16[2048,768]{1,0:T(8,128)(2,1)} collective-permute-done((bf16[2048,768]{1,0:T(8,128)(2,1)}, bf16[2048,768]{1,0:T(8,128)(2,1)}, u32[]{:S(2)}, u32[]{:S(2)}) %collective-permute-start.14) | collective-permute-done | bytes 3145760 | tf_op jit(solution)/shard_map/ppermute | solution.py:96
  277.8 2.9 convolution_convert_fusion
  280.8 2.0 gather_fusion.3
  282.8 1.8 broadcast_select_fusion
  284.8 2.0 collective-permute-start.15
  286.9 2.5 collective-permute-done.15
  289.8 3.5 %collective-permute-start.16 = (bf16[1024,256]{1,0:T(8,128)(2,1)S(1)}, bf16[1024,256]{1,0:T(8,128)(2,1)S(1)}, u32[]{:S(2)}, u32[]{:S(2)}) collective-permute-start(bf16[1024,256]{1,0:T(8,128)(2,1)S(1)} %slice.205), channel_id=1, source_target_pairs={{0,4},{1,13},{2,6},{3,15},{4,0},{5,9},{6,2},{7,11},{8,12},{9,5},{1... | collective-permute-start | bytes 1572872 | tf_op jit(solution)/shard_map/ppermute | solution.py:169
  293.3 7.6 %collective-permute-done.16 = bf16[1024,256]{1,0:T(8,128)(2,1)S(1)} collective-permute-done((bf16[1024,256]{1,0:T(8,128)(2,1)S(1)}, bf16[1024,256]{1,0:T(8,128)(2,1)S(1)}, u32[]{:S(2)}, u32[]{:S(2)}) %collective-permute-start.16) | collective-permute-done | bytes 524320 | tf_op jit(solution)/shard_map/ppermute | solution.py:169
  301.0 4.9 %collective-permute-start.17 = (bf16[512,256]{1,0:T(8,128)(2,1)S(1)}, bf16[512,256]{1,0:T(8,128)(2,1)S(1)}, u32[]{:S(2)}, u32[]{:S(2)}) collective-permute-start(bf16[512,256]{1,0:T(8,128)(2,1)S(1)} %slice.207), channel_id=1, source_target_pairs={{0,12},{1,5},{2,14},{3,7},{4,8},{5,1},{6,10},{7,3},{8,4},{9,13},{1... | collective-permute-start | bytes 786440 | tf_op jit(solution)/shard_map/ppermute | solution.py:169
  305.9 4.6 %collective-permute-done.17 = bf16[512,256]{1,0:T(8,128)(2,1)S(1)} collective-permute-done((bf16[512,256]{1,0:T(8,128)(2,1)S(1)}, bf16[512,256]{1,0:T(8,128)(2,1)S(1)}, u32[]{:S(2)}, u32[]{:S(2)}) %collective-permute-start.17) | collective-permute-done | bytes 262176 | tf_op jit(solution)/shard_map/ppermute | solution.py:169
  310.6 9.1 %collective-permute-start.18 = (bf16[256,256]{1,0:T(8,128)(2,1)S(1)}, bf16[256,256]{1,0:T(8,128)(2,1)S(1)}, u32[]{:S(2)}, u32[]{:S(2)}) collective-permute-start(bf16[256,256]{1,0:T(8,128)(2,1)S(1)} %slice.209), channel_id=1, source_target_pairs={{0,2},{1,3},{2,0},{3,1},{4,6},{5,7},{6,4},{7,5},{8,10},{9,11},{10,... | collective-permute-start | bytes 393224 | tf_op jit(solution)/shard_map/ppermute | solution.py:169
  319.6 10.0 %collective-permute-done.18 = bf16[256,256]{1,0:T(8,128)(2,1)S(1)} collective-permute-done((bf16[256,256]{1,0:T(8,128)(2,1)S(1)}, bf16[256,256]{1,0:T(8,128)(2,1)S(1)}, u32[]{:S(2)}, u32[]{:S(2)}) %collective-permute-start.18) | collective-permute-done | bytes 131104 | tf_op jit(solution)/shard_map/ppermute | solution.py:169
  (81 shorter events, 16.2 us)
Async XLA Ops:
  4.0 8.0 %collective-permute-start = (bf16[128,640]{1,0:T(8,128)(2,1)S(1)}, bf16[128,640]{1,0:T(8,128)(2,1)S(1)}, u32[]{:S(2)}, u32[]{:S(2)}) collective-permute-start(bf16[128,640]{1,0:T(8,128)(2,1)S(1)} %get-tuple-element.27), channel_id=1, source_target_pairs={{0,16},{1,17},{2,18},{3,19},{4,20},{5,21},{6,22},{7,23},{8,24},{9,... | collective-permute-start | bytes 491528 | tf_op jit(solution)/shard_map/ppermute | solution.py:96
  12.1 20.3 %collective-permute-start.1 = (bf16[256,256]{1,0:T(8,128)(2,1)S(1)}, bf16[256,256]{1,0:T(8,128)(2,1)S(1)}, u32[]{:S(2)}, u32[]{:S(2)}) collective-permute-start(bf16[256,256]{1,0:T(8,128)(2,1)S(1)} %get-tuple-element.15), channel_id=1, source_target_pairs={{0,64},{1,65},{2,66},{3,67},{4,68},{5,69},{6,70},{7,71},{8,72},{9,... | collective-permute-start | bytes 393224 | tf_op jit(solution)/shard_map/ppermute | solution.py:96
  32.5 9.1 %collective-permute-start.2 = (bf16[512,256]{1,0:T(8,128)(2,1)S(1)}, bf16[512,256]{1,0:T(8,128)(2,1)S(1)}, u32[]{:S(2)}, u32[]{:S(2)}) collective-permute-start(bf16[512,256]{1,0:T(8,128)(2,1)S(1)} %pad_maximum_fusion.6), channel_id=1, source_target_pairs={{0,128},{1,129},{2,130},{3,131},{4,132},{5,133},{6,134},{7,135},{8... | collective-permute-start | bytes 786440 | tf_op jit(solution)/shard_map/ppermute | solution.py:96
  42.4 30.4 %collective-permute-start.3 = (bf16[1024,256]{1,0:T(8,128)(2,1)}, bf16[1024,256]{1,0:T(8,128)(2,1)S(1)}, u32[]{:S(2)}, u32[]{:S(2)}) collective-permute-start(bf16[1024,256]{1,0:T(8,128)(2,1)} %pad_maximum_fusion.4), channel_id=1, source_target_pairs={{0,32},{1,257},{2,34},{3,259},{4,36},{5,261},{6,38},{7,263},{8,40}... | collective-permute-start | bytes 1572872 | tf_op jit(solution)/shard_map/ppermute | solution.py:96
  73.9 18.5 %collective-permute-start.4 = (bf16[2048,256]{1,0:T(8,128)(2,1)}, bf16[2048,256]{1,0:T(8,128)(2,1)}, u32[]{:S(2)}, u32[]{:S(2)}) collective-permute-start(bf16[2048,256]{1,0:T(8,128)(2,1)} %pad_maximum_fusion.2), channel_id=1, source_target_pairs={{0,256},{1,33},{2,258},{3,35},{4,260},{5,37},{6,262},{7,39},{8,264... | collective-permute-start | bytes 3145736 | tf_op jit(solution)/shard_map/ppermute | solution.py:96
  98.7 18.2 %collective-permute-start.5 = (bf16[2048,256]{1,0:T(8,128)(2,1)S(1)}, bf16[2048,256]{1,0:T(8,128)(2,1)S(1)}, u32[]{:S(2)}, u32[]{:S(2)}) collective-permute-start(bf16[2048,256]{1,0:T(8,128)(2,1)S(1)} %slice.99), channel_id=1, source_target_pairs={{0,256},{1,33},{2,258},{3,35},{4,260},{5,37},{6,262},{7,39},{8,264... | collective-permute-start | bytes 3145736 | tf_op jit(solution)/shard_map/ppermute | solution.py:96
  117.2 14.5 %collective-permute-start.6 = (bf16[1024,256]{1,0:T(8,128)(2,1)S(1)}, bf16[1024,256]{1,0:T(8,128)(2,1)S(1)}, u32[]{:S(2)}, u32[]{:S(2)}) collective-permute-start(bf16[1024,256]{1,0:T(8,128)(2,1)S(1)} %slice.206), channel_id=1, source_target_pairs={{0,32},{1,257},{2,34},{3,259},{4,36},{5,261},{6,38},{7,263},{8,40}... | collective-permute-start | bytes 1572872 | tf_op jit(solution)/shard_map/ppermute | solution.py:96
  131.8 8.3 %collective-permute-start.7 = (bf16[512,256]{1,0:T(8,128)(2,1)S(1)}, bf16[512,256]{1,0:T(8,128)(2,1)S(1)}, u32[]{:S(2)}, u32[]{:S(2)}) collective-permute-start(bf16[512,256]{1,0:T(8,128)(2,1)S(1)} %slice.208), channel_id=1, source_target_pairs={{0,128},{1,129},{2,130},{3,131},{4,132},{5,133},{6,134},{7,135},{8... | collective-permute-start | bytes 786440 | tf_op jit(solution)/shard_map/ppermute | solution.py:96
  140.2 18.1 %collective-permute-start.8 = (bf16[256,256]{1,0:T(8,128)(2,1)S(1)}, bf16[256,256]{1,0:T(8,128)(2,1)S(1)}, u32[]{:S(2)}, u32[]{:S(2)}) collective-permute-start(bf16[256,256]{1,0:T(8,128)(2,1)S(1)} %slice.210), channel_id=1, source_target_pairs={{0,64},{1,65},{2,66},{3,67},{4,68},{5,69},{6,70},{7,71},{8,72},{9,... | collective-permute-start | bytes 393224 | tf_op jit(solution)/shard_map/ppermute | solution.py:96
  158.4 6.7 %collective-permute-start.9 = (bf16[128,384]{1,0:T(8,128)(2,1)S(1)}, bf16[128,384]{1,0:T(8,128)(2,1)S(1)}, u32[]{:S(2)}, u32[]{:S(2)}) collective-permute-start(bf16[128,384]{1,0:T(8,128)(2,1)S(1)} %broadcast_select_fusion.3), channel_id=1, source_target_pairs={{0,16},{1,17},{2,18},{3,19},{4,20},{5,21},{6,22},{7,23},{8,24},{9,... | collective-permute-start | bytes 294920 | tf_op jit(solution)/shard_map/ppermute | solution.py:96
  166.5 21.7 %collective-permute-start.10 = (bf16[128,768]{1,0:T(8,128)(2,1)S(1)}, bf16[128,768]{1,0:T(8,128)(2,1)S(1)}, u32[]{:S(2)}, u32[]{:S(2)}) collective-permute-start(bf16[128,768]{1,0:T(8,128)(2,1)S(1)} %get-tuple-element.22), channel_id=1, source_target_pairs={{0,64},{1,65},{2,66},{3,67},{4,68},{5,69},{6,70},{7,71},{8,72},{9,... | collective-permute-start | bytes 589832 | tf_op jit(solution)/shard_map/ppermute | solution.py:96
  188.2 11.0 %collective-permute-start.11 = (bf16[256,768]{1,0:T(8,128)(2,1)S(1)}, bf16[256,768]{1,0:T(8,128)(2,1)S(1)}, u32[]{:S(2)}, u32[]{:S(2)}) collective-permute-start(bf16[256,768]{1,0:T(8,128)(2,1)S(1)} %pad_maximum_fusion.5), channel_id=1, source_target_pairs={{0,32},{1,257},{2,34},{3,259},{4,36},{5,261},{6,38},{7,263},{8,40}... | collective-permute-start | bytes 1179656 | tf_op jit(solution)/shard_map/ppermute | solution.py:96
  199.3 15.4 %collective-permute-start.12 = (bf16[512,768]{1,0:T(8,128)(2,1)S(1)}, bf16[512,768]{1,0:T(8,128)(2,1)S(1)}, u32[]{:S(2)}, u32[]{:S(2)}) collective-permute-start(bf16[512,768]{1,0:T(8,128)(2,1)S(1)} %pad_maximum_fusion.3), channel_id=1, source_target_pairs={{0,256},{1,33},{2,258},{3,35},{4,260},{5,37},{6,262},{7,39},{8,264... | collective-permute-start | bytes 2359304 | tf_op jit(solution)/shard_map/ppermute | solution.py:96
  214.8 22.3 %collective-permute-start.13 = (bf16[1024,768]{1,0:T(8,128)(2,1)S(1)}, bf16[1024,768]{1,0:T(8,128)(2,1)S(1)}, u32[]{:S(2)}, u32[]{:S(2)}) collective-permute-start(bf16[1024,768]{1,0:T(8,128)(2,1)S(1)} %pad_maximum_fusion.1), channel_id=1, source_target_pairs={{0,128},{1,17},{2,130},{3,19},{4,132},{5,21},{6,134},{7,23},{8,136... | collective-permute-start | bytes 4718600 | tf_op jit(solution)/shard_map/ppermute | solution.py:96
  222.2 18.9 %copy-start = (bf16[256,256]{1,0:T(8,128)(2,1)S(1)}, bf16[256,256]{1,0:T(8,128)(2,1)}, u32[]{:S(2)}) copy-start(bf16[256,256]{1,0:T(8,128)(2,1)} %param.15) | copy-start | bytes 393220
  222.2 18.9 %copy-start.1 = (bf16[256,256]{1,0:T(8,128)(2,1)S(1)}, bf16[256,256]{1,0:T(8,128)(2,1)}, u32[]{:S(2)}) copy-start(bf16[256,256]{1,0:T(8,128)(2,1)} %param.16) | copy-start | bytes 393220
  222.2 18.9 %copy-start.2 = (bf16[256,256]{1,0:T(8,128)(2,1)S(1)}, bf16[256,256]{1,0:T(8,128)(2,1)}, u32[]{:S(2)}) copy-start(bf16[256,256]{1,0:T(8,128)(2,1)} %param.17) | copy-start | bytes 393220
  238.3 39.5 %collective-permute-start.14 = (bf16[2048,768]{1,0:T(8,128)(2,1)}, bf16[2048,768]{1,0:T(8,128)(2,1)}, u32[]{:S(2)}, u32[]{:S(2)}) collective-permute-start(bf16[2048,768]{1,0:T(8,128)(2,1)} %constant_dynamic-update-slice_fusion.21), channel_id=1, source_target_pairs={{0,16},{1,129},{2,18},{3,131},{4,20},{5,133},{6,22},{7,135},{8,24}... | collective-permute-start | bytes 9437192 | tf_op jit(solution)/shard_map/ppermute | solution.py:96
  284.8 4.6 %collective-permute-start.15 = (bf16[2048,256]{1,0:T(8,128)(2,1)S(1)}, bf16[2048,256]{1,0:T(8,128)(2,1)S(1)}, u32[]{:S(2)}, u32[]{:S(2)}) collective-permute-start(bf16[2048,256]{1,0:T(8,128)(2,1)S(1)} %bitcast.29), channel_id=1, source_target_pairs={{0,1},{1,0},{2,3},{3,2},{4,5},{5,4},{6,7},{7,6},{8,9},{9,8},{10,11... | collective-permute-start | bytes 3145736 | tf_op jit(solution)/shard_map/ppermute | solution.py:169
  289.8 11.1 %collective-permute-start.16 = (bf16[1024,256]{1,0:T(8,128)(2,1)S(1)}, bf16[1024,256]{1,0:T(8,128)(2,1)S(1)}, u32[]{:S(2)}, u32[]{:S(2)}) collective-permute-start(bf16[1024,256]{1,0:T(8,128)(2,1)S(1)} %slice.205), channel_id=1, source_target_pairs={{0,4},{1,13},{2,6},{3,15},{4,0},{5,9},{6,2},{7,11},{8,12},{9,5},{1... | collective-permute-start | bytes 1572872 | tf_op jit(solution)/shard_map/ppermute | solution.py:169
  301.0 9.5 %collective-permute-start.17 = (bf16[512,256]{1,0:T(8,128)(2,1)S(1)}, bf16[512,256]{1,0:T(8,128)(2,1)S(1)}, u32[]{:S(2)}, u32[]{:S(2)}) collective-permute-start(bf16[512,256]{1,0:T(8,128)(2,1)S(1)} %slice.207), channel_id=1, source_target_pairs={{0,12},{1,5},{2,14},{3,7},{4,8},{5,1},{6,10},{7,3},{8,4},{9,13},{1... | collective-permute-start | bytes 786440 | tf_op jit(solution)/shard_map/ppermute | solution.py:169
  310.6 19.1 %collective-permute-start.18 = (bf16[256,256]{1,0:T(8,128)(2,1)S(1)}, bf16[256,256]{1,0:T(8,128)(2,1)S(1)}, u32[]{:S(2)}, u32[]{:S(2)}) collective-permute-start(bf16[256,256]{1,0:T(8,128)(2,1)S(1)} %slice.209), channel_id=1, source_target_pairs={{0,2},{1,3},{2,0},{3,1},{4,6},{5,7},{6,4},{7,5},{8,10},{9,11},{10,... | collective-permute-start | bytes 393224 | tf_op jit(solution)/shard_map/ppermute | solution.py:169
